TPU v7x, 128 devices: a whole 4x4x4 slice. The times are simulated.
128 devices in a mesh: dp: 8 (over z_lo, x), seq: 16 (over z_hi, y, core).
Axes of the slice: x: 4, y: 4, z: 4 (z_hi: 2, z_lo: 2; z = z_hi * 2 + z_lo), core: 2. Of those that a mesh axis runs over, the one named last changes fastest.
Arguments:
- series: bfloat16 [8, 8192, 128], P('dp', 'seq'), may hold values from -6 to 6
- cotangent: bfloat16 [8, 8192, 128], P('dp', 'seq'), may hold values from -6 to 6
- w_in: bfloat16 [128, 384], replicated, may hold values from -0.5 to 0.5
- w_out: bfloat16 [128, 128], replicated, may hold values from -0.5 to 0.5
- taps: float32 [3, 384], replicated, may hold values from -3 to 3
- skip_one: float32 [128], replicated, may hold values from 0.5 to 1.5
- skip_two: float32 [128], replicated, may hold values from 0.5 to 1.5
- filter_one: float32 [8, 8192], P(None, 'seq'), may hold values from -0.0625 to 0.0625
- filter_two: float32 [8, 8192], P(None, 'seq'), may hold values from -0.0625 to 0.0625
Outputs:
- output: bfloat16 [8, 8192, 128], P('dp', 'seq')
- d_series: bfloat16 [8, 8192, 128], P('dp', 'seq')
- grad_w_in: float32 [128, 384], replicated
- grad_w_out: float32 [128, 128], replicated
- grad_taps: float32 [3, 384], replicated
- grad_skip_one: float32 [128], replicated
- grad_skip_two: float32 [128], replicated
- grad_filter_one: float32 [8, 8192], P(None, 'seq')
- grad_filter_two: float32 [8, 8192], P(None, 'seq')
All inputs are finite; a program needn't handle non-finite values.
Results may differ from a plain program's by a relative error of at most 0.015.
Values may be sent and summed in bfloat16 or wider, within the bound.
A program may use at most 128 MiB of HBM per device.

v0:
```python
import math

import jax
import jax.numpy as jnp
from jax import lax
from jax.sharding import PartitionSpec as P

FACTOR = 32


def passed_along(block, axis, distance):
    devices = range(lax.axis_size(axis))
    route = [(i - distance, i) for i in devices if i - distance in devices]
    return lax.ppermute(block, axis, route)


def grid_index(shape_pair, along):
    return lax.broadcasted_iota(jnp.int32, shape_pair, along)


def twiddle(row_index, col_index, period, direction):
    angle = (
        direction * 2.0 * math.pi / period * (row_index * col_index % period).astype(jnp.float32)
    )
    return (jnp.cos(angle), jnp.sin(angle))


def complex_mul(left_real, left_imag, right_real, right_imag):
    return (
        left_real * right_real - left_imag * right_imag,
        left_real * right_imag + left_imag * right_real,
    )


def complex_dft(real_part, imag_part, table_real, table_imag, pattern):
    highest = lax.Precision.HIGHEST
    first = jnp.einsum(pattern, table_real, real_part, precision=highest)
    second = jnp.einsum(pattern, table_imag, imag_part, precision=highest)
    third = jnp.einsum(pattern, table_real, imag_part, precision=highest)
    fourth = jnp.einsum(pattern, table_imag, real_part, precision=highest)
    return (first - second, third + fourth)


def local_dft(pieces):
    real_part, imag_part = pieces
    series_count, pair_rows, block_rows, channels = real_part.shape
    inner = block_rows // FACTOR
    real_part = real_part.reshape(series_count, pair_rows, FACTOR, inner, channels)
    imag_part = imag_part.reshape(series_count, pair_rows, FACTOR, inner, channels)
    table_real, table_imag = twiddle(
        grid_index((FACTOR, FACTOR), 0), grid_index((FACTOR, FACTOR), 1), FACTOR, -1.0
    )
    real_part, imag_part = complex_dft(
        real_part, imag_part, table_real, table_imag, "ca,erabk->ercbk"
    )
    turn_real, turn_imag = twiddle(
        grid_index((FACTOR, inner), 0), grid_index((FACTOR, inner), 1), block_rows, -1.0
    )
    real_part, imag_part = complex_mul(
        real_part, imag_part, turn_real[:, :, None], turn_imag[:, :, None]
    )
    table_real, table_imag = twiddle(
        grid_index((inner, inner), 0), grid_index((inner, inner), 1), inner, -1.0
    )
    return complex_dft(real_part, imag_part, table_real, table_imag, "db,ercbk->ercdk")


def local_inverse(real_part, imag_part):
    series_count, pair_rows, outer, inner, channels = real_part.shape
    block_rows = outer * inner
    table_real, table_imag = twiddle(
        grid_index((inner, inner), 0), grid_index((inner, inner), 1), inner, 1.0
    )
    real_part, imag_part = complex_dft(
        real_part, imag_part, table_real, table_imag, "bd,ercdk->ercbk"
    )
    turn_real, turn_imag = twiddle(
        grid_index((outer, inner), 0), grid_index((outer, inner), 1), block_rows, 1.0
    )
    real_part, imag_part = complex_mul(
        real_part, imag_part, turn_real[:, :, None], turn_imag[:, :, None]
    )
    table_real, table_imag = twiddle(
        grid_index((outer, outer), 0), grid_index((outer, outer), 1), outer, 1.0
    )
    real_part, imag_part = complex_dft(
        real_part, imag_part, table_real, table_imag, "ac,ercbk->erabk"
    )
    return (
        real_part.reshape(series_count, pair_rows, block_rows, channels),
        imag_part.reshape(series_count, pair_rows, block_rows, channels),
    )


def first_section(columns):
    highest = lax.Precision.HIGHEST
    groups = lax.axis_size("seq")
    column_width = columns.shape[2]
    period = 2 * groups * groups * column_width
    offset = lax.axis_index("seq") * column_width
    table_real, table_imag = twiddle(
        grid_index((2 * groups, groups), 0), grid_index((2 * groups, groups), 1), 2 * groups, -1.0
    )
    real_part = jnp.einsum("kn,enjc->ekjc", table_real, columns, precision=highest)
    imag_part = jnp.einsum("kn,enjc->ekjc", table_imag, columns, precision=highest)
    turn_real, turn_imag = twiddle(
        grid_index((2 * groups, column_width), 0),
        grid_index((2 * groups, column_width), 1) + offset,
        period,
        -1.0,
    )
    return complex_mul(real_part, imag_part, turn_real[:, :, None], turn_imag[:, :, None])


def last_section(pieces):
    highest = lax.Precision.HIGHEST
    part_real, part_imag = pieces
    groups = lax.axis_size("seq")
    column_width = part_real.shape[2]
    period = 2 * groups * groups * column_width
    offset = lax.axis_index("seq") * column_width
    turn_real, turn_imag = twiddle(
        grid_index((2 * groups, column_width), 0),
        grid_index((2 * groups, column_width), 1) + offset,
        period,
        1.0,
    )
    part_real, part_imag = complex_mul(
        part_real, part_imag, turn_real[:, :, None], turn_imag[:, :, None]
    )
    table_real, table_imag = twiddle(
        grid_index((groups, 2 * groups), 0), grid_index((groups, 2 * groups), 1), 2 * groups, 1.0
    )
    summed = jnp.einsum("nk,ekjc->enjc", table_real, part_real, precision=highest) - jnp.einsum(
        "nk,ekjc->enjc", table_imag, part_imag, precision=highest
    )
    return summed * (1.0 / period)


def to_frequency(real_part, imag_part):
    return local_dft(
        (
            lax.all_to_all(real_part, "seq", split_axis=1, concat_axis=2, tiled=True),
            lax.all_to_all(imag_part, "seq", split_axis=1, concat_axis=2, tiled=True),
        )
    )


def spectrum(field):
    real_part, imag_part = first_section(
        lax.all_to_all(field, "seq", split_axis=2, concat_axis=1, tiled=True)
    )
    return to_frequency(real_part, imag_part)


def signal(real_part, imag_part):
    real_part, imag_part = local_inverse(real_part, imag_part)
    columns = last_section(
        (
            lax.all_to_all(real_part, "seq", split_axis=2, concat_axis=1, tiled=True),
            lax.all_to_all(imag_part, "seq", split_axis=2, concat_axis=1, tiled=True),
        )
    )
    return lax.all_to_all(columns, "seq", split_axis=1, concat_axis=2, tiled=True)


def order_spectrum(real_part, imag_part):
    series_count, pair_rows, outer, inner, channels = real_part.shape
    block_rows = outer * inner
    real_part = jnp.swapaxes(real_part, 2, 3).reshape(series_count, pair_rows, block_rows, channels)
    imag_part = jnp.swapaxes(imag_part, 2, 3).reshape(series_count, pair_rows, block_rows, channels)
    real_part, imag_part = (
        lax.all_to_all(real_part, "seq", split_axis=2, concat_axis=1, tiled=True),
        lax.all_to_all(imag_part, "seq", split_axis=2, concat_axis=1, tiled=True),
    )
    return (jnp.swapaxes(real_part, 1, 2), jnp.swapaxes(imag_part, 1, 2))


def restore_spectrum(real_part, imag_part):
    real_part = jnp.swapaxes(real_part, 1, 2)
    imag_part = jnp.swapaxes(imag_part, 1, 2)
    real_part, imag_part = (
        lax.all_to_all(real_part, "seq", split_axis=1, concat_axis=2, tiled=True),
        lax.all_to_all(imag_part, "seq", split_axis=1, concat_axis=2, tiled=True),
    )
    series_count, pair_rows, block_rows, channels = real_part.shape
    inner = block_rows // FACTOR
    real_part = jnp.swapaxes(
        real_part.reshape(series_count, pair_rows, inner, FACTOR, channels), 2, 3
    )
    imag_part = jnp.swapaxes(
        imag_part.reshape(series_count, pair_rows, inner, FACTOR, channels), 2, 3
    )
    return (real_part, imag_part)


def transform(field):
    real_part, imag_part = spectrum(field)
    real_part, imag_part = order_spectrum(real_part, imag_part)
    return (real_part, imag_part)


def untransform(real_part, imag_part, in_columns):
    real_part, imag_part = restore_spectrum(real_part, imag_part)
    return signal(real_part, imag_part)


def widen_groups(pieces, channels):
    real_part, imag_part = pieces
    repeat_count = channels // real_part.shape[-1]
    return (
        jnp.repeat(real_part, repeat_count, axis=-1),
        jnp.repeat(imag_part, repeat_count, axis=-1),
    )


def group_sum(pieces, filters):
    result = []
    for piece in pieces:
        channels = piece.shape[-1]
        reshaped = piece.reshape(piece.shape[:-1] + (filters, channels // filters))
        result.append(jnp.sum(jnp.sum(reshaped, axis=-1), axis=0, keepdims=True))
    return (result[0], result[1])


def rows_before(field):
    return passed_along(field[:, :, -2:], "seq", 1)


def rows_after(field):
    return passed_along(field[:, :, :2], "seq", -1)


def filter_blocks(filter_rows):
    return filter_rows.T.reshape(1, 1, filter_rows.shape[1], filter_rows.shape[0])


def shards(series, cotangent, w_in, w_out, taps, skip_one, skip_two, filter_one, filter_two):
    series_count, block_rows, width_d = series.shape
    filters = filter_one.shape[0]
    token_total = series_count * lax.axis_size("dp") * block_rows * lax.axis_size("seq")
    grad_scale = 1.0 / math.sqrt(token_total)
    series_four = series.reshape(series_count, 1, block_rows, width_d)
    cot_four = cotangent.reshape(series_count, 1, block_rows, width_d)
    series_here, cot_here = (series_four, cot_four)
    projected = jnp.einsum("entd,dc->entc", series_here, w_in, preferred_element_type=jnp.float32)
    before = rows_before(projected)
    extended = jnp.concatenate([before, projected], axis=2)
    run_rows = projected.shape[2]
    convolved = (
        taps[0] * extended[:, :, 2:]
        + taps[1] * extended[:, :, 1:-1]
        + taps[2] * extended[:, :, :-2]
    )
    value_part = convolved[..., :width_d]
    gate_one = convolved[..., width_d : 2 * width_d]
    gate_two = convolved[..., 2 * width_d :]
    spec_one = transform(filter_blocks(filter_one))
    spec_two = transform(filter_blocks(filter_two))
    one_real, one_imag = widen_groups(spec_one, width_d)
    two_real, two_imag = widen_groups(spec_two, width_d)
    value_real, value_imag = transform(value_part)
    y_one = (
        untransform(*complex_mul(one_real, one_imag, value_real, value_imag), False)
        + skip_one * value_part
    )
    gated_mid = gate_one * y_one
    mid_real, mid_imag = transform(gated_mid)
    y_two = (
        untransform(*complex_mul(two_real, two_imag, mid_real, mid_imag), False)
        + skip_two * gated_mid
    )
    product = (gate_two * y_two).astype(jnp.bfloat16)
    output = jnp.einsum("entc,cd->entd", product, w_out, preferred_element_type=jnp.float32).astype(
        jnp.bfloat16
    )
    d_product = jnp.einsum("entd,cd->entc", cot_here, w_out, preferred_element_type=jnp.float32)
    grad_two = d_product * gate_two
    d_gate_two = d_product * y_two
    gtwo_real, gtwo_imag = transform(grad_two)
    d_mid = (
        untransform(*complex_mul(two_real, -two_imag, gtwo_real, gtwo_imag), False)
        + skip_two * grad_two
    )
    filter_two_spec = group_sum(complex_mul(mid_real, -mid_imag, gtwo_real, gtwo_imag), filters)
    filter_two_time = untransform(filter_two_spec[0], filter_two_spec[1], False)[0, 0].T
    grad_one = d_mid * gate_one
    d_gate_one = d_mid * y_one
    gone_real, gone_imag = transform(grad_one)
    d_value = (
        untransform(*complex_mul(one_real, -one_imag, gone_real, gone_imag), False)
        + skip_one * grad_one
    )
    filter_one_spec = group_sum(complex_mul(value_real, -value_imag, gone_real, gone_imag), filters)
    filter_one_time = untransform(filter_one_spec[0], filter_one_spec[1], False)[0, 0].T
    d_convolved = jnp.concatenate([d_value, d_gate_one, d_gate_two], axis=3)
    after = rows_after(d_convolved)
    extended_back = jnp.concatenate([d_convolved, after], axis=2)
    d_projected = (
        taps[0] * extended_back[:, :, :-2]
        + taps[1] * extended_back[:, :, 1:-1]
        + taps[2] * extended_back[:, :, 2:]
    ).astype(jnp.bfloat16)
    d_series = jnp.einsum(
        "entc,dc->entd", d_projected, w_in, preferred_element_type=jnp.float32
    ).astype(jnp.bfloat16)
    local_w_in = jnp.einsum(
        "entd,entc->dc", series_here, d_projected, preferred_element_type=jnp.float32
    )
    local_w_out = jnp.einsum("entc,entd->cd", product, cot_here, preferred_element_type=jnp.float32)
    local_taps = jnp.stack(
        [
            jnp.sum(
                d_convolved * extended[:, :, 2 - offset : 2 - offset + run_rows], axis=(0, 1, 2)
            )
            for offset in range(3)
        ]
    )
    local_skip_one = jnp.sum(grad_one * value_part, axis=(0, 1, 2))
    local_skip_two = jnp.sum(grad_two * gated_mid, axis=(0, 1, 2))
    grad_w_in, grad_w_out, grad_taps, grad_skip_one, grad_skip_two = lax.psum(
        (local_w_in, local_w_out, local_taps, local_skip_one, local_skip_two), ("dp", "seq")
    )
    grad_filter_one, grad_filter_two = (
        lax.psum(filter_one_time.astype(jnp.bfloat16), "dp").astype(jnp.float32),
        lax.psum(filter_two_time.astype(jnp.bfloat16), "dp").astype(jnp.float32),
    )
    output = output.reshape(series_count, block_rows, width_d)
    d_series = d_series.reshape(series_count, block_rows, width_d)
    return (
        output,
        d_series,
        grad_scale * grad_w_in,
        grad_scale * grad_w_out,
        grad_scale * grad_taps,
        grad_scale * grad_skip_one,
        grad_scale * grad_skip_two,
        grad_scale * grad_filter_one,
        grad_scale * grad_filter_two,
    )


def solution(mesh):
    in_specs = (
        P("dp", "seq", None),
        P("dp", "seq", None),
        P(),
        P(),
        P(),
        P(),
        P(),
        P(None, "seq"),
        P(None, "seq"),
    )
    out_specs = (
        P("dp", "seq", None),
        P("dp", "seq", None),
        P(),
        P(),
        P(),
        P(),
        P(),
        P(None, "seq"),
        P(None, "seq"),
    )
    return jax.shard_map(shards, mesh=mesh, in_specs=in_specs, out_specs=out_specs, check_vma=False)
```

profile of v0, /device:TPU:1, one launch (start us, length us, event | category | flops | bytes accessed | tf_op | source)
XLA Modules:
  0.0 1293.6 jit_solution(11738205178397126315)
XLA Ops:
  10.7 9.3 all-to-all-start.4
  89.2 9.1 all-to-all-done.9
  144.8 8.3 all-to-all-done.11
  188.9 8.4 all-to-all-done.14
  231.7 7.3 all-to-all-done.16
  245.4 9.6 all-to-all-done.17
  263.8 7.9 all-to-all-done.18
  283.9 12.2 all_to_all.876
  316.0 7.3 all-to-all-start.2
  368.1 7.2 all-to-all-start.21
  379.5 7.3 all-to-all-done.21
  417.1 7.3 all-to-all-start.23
  457.0 7.4 all-to-all-done.34
  474.2 7.2 all-to-all-done.24
  516.8 10.7 fusion.14
  530.6 7.3 all-to-all-start.26
  540.9 8.3 all-to-all-done.26
  557.4 8.5 all-to-all-done.25
  635.3 7.5 all-to-all-done.38
  651.9 7.5 all-to-all-done.28
  693.9 12.0 all_to_all.877
  725.9 7.3 all-to-all-start.56
  835.4 8.3 fusion.12
  874.4 7.4 all-to-all-start.57
  933.1 7.3 all-to-all-start.46
  958.3 9.3 all-to-all-done.45
  998.8 8.4 all-to-all-done.47
  1015.1 27.4 %all-reduce.2 = (bf16[8,512]{1,0:T(8,128)(2,1)}, bf16[8,512]{1,0:T(8,128)(2,1)}) all-reduce(bf16[8,512]{1,0:T(8,128)(2,1)S(1)} %bitcast.1449, bf16[8,512]{1,0:T(8,128)(2,1)S(1)} %bitcast.1448), channel_id=1, replica_groups=mesh['dp'=8,'seq'=16] {'dp'}, use_global_device_ids=true, to_apply=%region_12.13 | all-reduce | flops 8192 | bytes 32768 | tf_op jit(solution)/shard_map/psum | solution.py:325
  1046.1 14.8 %all-to-all-start.49 = ((f32[1,16,32,128]{3,2,0,1:T(8,128)}), f32[1,16,32,128]{3,2,0,1:T(8,128)S(1)}, u32[]{:S(2)}, u32[]{:S(2)}) async-start(f32[1,16,32,128]{3,2,0,1:T(8,128)} %copy.829), calls=%async_computation.49 | async-start | bytes 524288 | tf_op jit(solution)/shard_map/all_to_all | solution.py:164
  1062.2 7.4 all-to-all-done.49
  1075.5 66.5 %all-reduce = (f32[3,384]{1,0:T(4,128)S(1)}, f32[128]{0:T(128)S(1)}, f32[128]{0:T(128)S(1)}) all-reduce(f32[3,384]{1,0:T(4,128)S(1)} %pad_maximum_fusion.3, f32[128]{0:T(128)S(1)} %copy-done.70, f32[128]{0:T(128)S(1)} %copy-done.69), channel_id=1, replica_groups=mesh['dp'=8,'seq'=16] {'dp','seq'}, use_global_device_ids=true, to_apply=%region_5.6 | all-reduce | flops 1408 | bytes 11264 | tf_op jit(solution)/shard_map/psum | solution.py:321
  1145.6 137.8 %all-reduce.5.cloned.1.call-done = (f32[128,384]{0,1:T(8,128)}, f32[128,128]{1,0:T(8,128)}) async-done(((f32[128,384]{0,1:T(8,128)}, f32[128,128]{1,0:T(8,128)}), (f32[128,384]{0,1:T(8,128)}, f32[128,128]{1,0:T(8,128)})) %all-reduce.5.cloned.1.call-update) | async-done | bytes 262160 | tf_op jit(solution)/shard_map/psum | solution.py:321
  (620 shorter events, 797.6 us)
Async XLA Ops:
  10.7 17.3 %all-to-all-start.4 = ((f32[16,1,256]{2,1,0:T(1,128)}), f32[16,1,256]{2,1,0:T(1,128)S(1)}, u32[]{:S(2)}, u32[]{:S(2)}) async-start(f32[16,1,256]{2,1,0:T(1,128)} %reshape.1187), calls=%async_computation.4 | async-start | bytes 32768 | tf_op jit(solution)/shard_map/all_to_all | solution.py:151
  21.2 27.8 %collective-permute-start = (f32[1,1,2,384]{3,2,1,0:T(2,128)S(1)}, f32[1,1,2,384]{3,2,1,0:T(2,128)S(1)}, u32[]{:S(2)}, u32[]{:S(2)}) collective-permute-start(f32[1,1,2,384]{3,2,1,0:T(2,128)S(1)} %slice.53), channel_id=1, source_target_pairs={{0,1},{1,2},{2,3},{3,4},{4,5},{5,6},{6,7},{7,8},{8,9},{9,10},{10,1... | collective-permute-start | bytes 9224 | tf_op jit(solution)/shard_map/ppermute | solution.py:14
  98.3 16.1 %all-to-all-start.10 = ((f32[1,32,32,128]{3,2,0,1:T(8,128)}), f32[1,32,32,128]{3,2,0,1:T(8,128)S(1)}, u32[]{:S(2)}, u32[]{:S(2)}) async-start(f32[1,32,32,128]{3,2,0,1:T(8,128)} %copy.650), calls=%async_computation.10 | async-start | bytes 1048576 | tf_op jit(solution)/shard_map/all_to_all | solution.py:144
  153.0 16.2 %all-to-all-start.13 = ((f32[1,2,512,128]{3,1,0,2:T(2,128)}), f32[1,2,512,128]{3,1,0,2:T(2,128)S(1)}, u32[]{:S(2)}, u32[]{:S(2)}) async-start(f32[1,2,512,128]{3,1,0,2:T(2,128)} %copy.669), calls=%async_computation.13 | async-start | bytes 1048576 | tf_op jit(solution)/shard_map/all_to_all | solution.py:174
  197.3 16.6 %all-to-all-start.15 = ((f32[1,32,32,128]{3,2,0,1:T(8,128)}), f32[1,32,32,128]{3,2,0,1:T(8,128)}, u32[]{:S(2)}, u32[]{:S(2)}) async-start(f32[1,32,32,128]{3,2,0,1:T(8,128)} %copy.675), calls=%async_computation.15 | async-start | bytes 1048576 | tf_op jit(solution)/shard_map/all_to_all | solution.py:184
  222.0 17.0 %all-to-all-start.16 = ((f32[1,2,512,128]{3,1,0,2:T(2,128)}), f32[1,2,512,128]{3,1,0,2:T(2,128)}, u32[]{:S(2)}, u32[]{:S(2)}) async-start(f32[1,2,512,128]{3,1,0,2:T(2,128)} %copy.682), calls=%async_computation.16 | async-start | bytes 1048576 | tf_op jit(solution)/shard_map/all_to_all | solution.py:160
  239.0 15.9 %all-to-all-start.17 = ((f32[1,2,512,128]{3,1,0,2:T(2,128)}), f32[1,2,512,128]{3,1,0,2:T(2,128)S(1)}, u32[]{:S(2)}, u32[]{:S(2)}) async-start(f32[1,2,512,128]{3,1,0,2:T(2,128)} %copy.688), calls=%async_computation.17 | async-start | bytes 1048576 | tf_op jit(solution)/shard_map/all_to_all | solution.py:161
  296.1 19.9 %all-to-all-start.30 = ((f32[1,1,512,128]{3,1,0,2:T(1,128)}), f32[1,1,512,128]{3,1,0,2:T(1,128)}, u32[]{:S(2)}, u32[]{:S(2)}) async-start(f32[1,1,512,128]{3,1,0,2:T(1,128)} %bitcast.259), calls=%async_computation.30 | async-start | bytes 524288 | tf_op jit(solution)/shard_map/all_to_all | solution.py:151
  330.7 17.8 %all-to-all-start.31 = ((f32[1,32,32,128]{3,2,0,1:T(8,128)}), f32[1,32,32,128]{3,2,0,1:T(8,128)}, u32[]{:S(2)}, u32[]{:S(2)}) async-start(f32[1,32,32,128]{3,2,0,1:T(8,128)} %copy.745), calls=%async_computation.31 | async-start | bytes 1048576 | tf_op jit(solution)/shard_map/all_to_all | solution.py:143
  348.5 19.5 %all-to-all-start.32 = ((f32[1,32,32,128]{3,2,0,1:T(8,128)}), f32[1,32,32,128]{3,2,0,1:T(8,128)}, u32[]{:S(2)}, u32[]{:S(2)}) async-start(f32[1,32,32,128]{3,2,0,1:T(8,128)} %copy.748), calls=%async_computation.32 | async-start | bytes 1048576 | tf_op jit(solution)/shard_map/all_to_all | solution.py:144
  368.1 18.7 %all-to-all-start.21 = ((f32[1,32,32,128]{3,2,0,1:T(8,128)}), f32[1,32,32,128]{3,2,0,1:T(8,128)}, u32[]{:S(2)}, u32[]{:S(2)}) async-start(f32[1,32,32,128]{3,2,0,1:T(8,128)} %copy.700), calls=%async_computation.21 | async-start | bytes 1048576 | tf_op jit(solution)/shard_map/all_to_all | solution.py:144
  386.8 16.6 %all-to-all-start.20 = ((f32[1,32,32,128]{3,2,0,1:T(8,128)}), f32[1,32,32,128]{3,2,0,1:T(8,128)}, u32[]{:S(2)}, u32[]{:S(2)}) async-start(f32[1,32,32,128]{3,2,0,1:T(8,128)} %copy.697), calls=%async_computation.20 | async-start | bytes 1048576 | tf_op jit(solution)/shard_map/all_to_all | solution.py:143
  431.8 15.9 %all-to-all-start.33 = ((f32[1,2,512,128]{3,1,0,2:T(2,128)}), f32[1,2,512,128]{3,1,0,2:T(2,128)}, u32[]{:S(2)}, u32[]{:S(2)}) async-start(f32[1,2,512,128]{3,1,0,2:T(2,128)} %copy.756), calls=%async_computation.33 | async-start | bytes 1048576 | tf_op jit(solution)/shard_map/all_to_all | solution.py:173
  447.7 16.6 %all-to-all-start.34 = ((f32[1,2,512,128]{3,1,0,2:T(2,128)}), f32[1,2,512,128]{3,1,0,2:T(2,128)}, u32[]{:S(2)}, u32[]{:S(2)}) async-start(f32[1,2,512,128]{3,1,0,2:T(2,128)} %copy.763), calls=%async_computation.34 | async-start | bytes 1048576 | tf_op jit(solution)/shard_map/all_to_all | solution.py:174
  464.3 17.0 %all-to-all-start.24 = ((f32[1,2,512,128]{3,1,0,2:T(2,128)}), f32[1,2,512,128]{3,1,0,2:T(2,128)}, u32[]{:S(2)}, u32[]{:S(2)}) async-start(f32[1,2,512,128]{3,1,0,2:T(2,128)} %copy.719), calls=%async_computation.24 | async-start | bytes 1048576 | tf_op jit(solution)/shard_map/all_to_all | solution.py:174
  481.4 22.5 %all-to-all-start.22 = ((f32[1,2,512,128]{3,1,0,2:T(2,128)}), f32[1,2,512,128]{3,1,0,2:T(2,128)}, u32[]{:S(2)}, u32[]{:S(2)}) async-start(f32[1,2,512,128]{3,1,0,2:T(2,128)} %copy.708), calls=%async_computation.22 | async-start | bytes 1048576 | tf_op jit(solution)/shard_map/all_to_all | solution.py:173
  530.6 18.7 %all-to-all-start.26 = ((f32[1,32,32,128]{3,2,0,1:T(8,128)}), f32[1,32,32,128]{3,2,0,1:T(8,128)S(1)}, u32[]{:S(2)}, u32[]{:S(2)}) async-start(f32[1,32,32,128]{3,2,0,1:T(8,128)} %copy.725), calls=%async_computation.26 | async-start | bytes 1048576 | tf_op jit(solution)/shard_map/all_to_all | solution.py:184
  549.3 16.6 %all-to-all-start.25 = ((f32[1,32,32,128]{3,2,0,1:T(8,128)}), f32[1,32,32,128]{3,2,0,1:T(8,128)}, u32[]{:S(2)}, u32[]{:S(2)}) async-start(f32[1,32,32,128]{3,2,0,1:T(8,128)} %copy.723), calls=%async_computation.25 | async-start | bytes 1048576 | tf_op jit(solution)/shard_map/all_to_all | solution.py:183
  565.9 16.8 %all-to-all-start.36 = ((f32[1,32,32,128]{3,2,0,1:T(8,128)}), f32[1,32,32,128]{3,2,0,1:T(8,128)}, u32[]{:S(2)}, u32[]{:S(2)}) async-start(f32[1,32,32,128]{3,2,0,1:T(8,128)} %copy.769), calls=%async_computation.36 | async-start | bytes 1048576 | tf_op jit(solution)/shard_map/all_to_all | solution.py:184
  609.3 16.8 %all-to-all-start.37 = ((f32[1,2,512,128]{3,1,0,2:T(2,128)}), f32[1,2,512,128]{3,1,0,2:T(2,128)}, u32[]{:S(2)}, u32[]{:S(2)}) async-start(f32[1,2,512,128]{3,1,0,2:T(2,128)} %copy.774), calls=%async_computation.37 | async-start | bytes 1048576 | tf_op jit(solution)/shard_map/all_to_all | solution.py:160
  626.1 16.6 %all-to-all-start.38 = ((f32[1,2,512,128]{3,1,0,2:T(2,128)}), f32[1,2,512,128]{3,1,0,2:T(2,128)}, u32[]{:S(2)}, u32[]{:S(2)}) async-start(f32[1,2,512,128]{3,1,0,2:T(2,128)} %copy.780), calls=%async_computation.38 | async-start | bytes 1048576 | tf_op jit(solution)/shard_map/all_to_all | solution.py:161
  642.7 16.6 %all-to-all-start.28 = ((f32[1,2,512,128]{3,1,0,2:T(2,128)}), f32[1,2,512,128]{3,1,0,2:T(2,128)}, u32[]{:S(2)}, u32[]{:S(2)}) async-start(f32[1,2,512,128]{3,1,0,2:T(2,128)} %copy.736), calls=%async_computation.28 | async-start | bytes 1048576 | tf_op jit(solution)/shard_map/all_to_all | solution.py:161
  708.8 17.2 %all-to-all-start.40 = ((f32[1,1,512,128]{3,1,0,2:T(1,128)}), f32[1,1,512,128]{3,1,0,2:T(1,128)}, u32[]{:S(2)}, u32[]{:S(2)}) async-start(f32[1,1,512,128]{3,1,0,2:T(1,128)} %bitcast.1339), calls=%async_computation.40 | async-start | bytes 524288 | tf_op jit(solution)/shard_map/all_to_all | solution.py:151
  752.4 15.9 %all-to-all-start.41 = ((f32[1,32,32,128]{3,2,0,1:T(8,128)}), f32[1,32,32,128]{3,2,0,1:T(8,128)}, u32[]{:S(2)}, u32[]{:S(2)}) async-start(f32[1,32,32,128]{3,2,0,1:T(8,128)} %copy.789), calls=%async_computation.41 | async-start | bytes 1048576 | tf_op jit(solution)/shard_map/all_to_all | solution.py:143
  768.3 16.6 %all-to-all-start.42 = ((f32[1,32,32,128]{3,2,0,1:T(8,128)}), f32[1,32,32,128]{3,2,0,1:T(8,128)}, u32[]{:S(2)}, u32[]{:S(2)}) async-start(f32[1,32,32,128]{3,2,0,1:T(8,128)} %copy.792), calls=%async_computation.42 | async-start | bytes 1048576 | tf_op jit(solution)/shard_map/all_to_all | solution.py:144
  792.6 18.3 %all-to-all-start.43 = ((f32[1,2,512,128]{3,1,0,2:T(2,128)}), f32[1,2,512,128]{3,1,0,2:T(2,128)}, u32[]{:S(2)}, u32[]{:S(2)}) async-start(f32[1,2,512,128]{3,1,0,2:T(2,128)} %copy.800), calls=%async_computation.43 | async-start | bytes 1048576 | tf_op jit(solution)/shard_map/all_to_all | solution.py:173
  810.9 16.6 %all-to-all-start.44 = ((f32[1,2,512,128]{3,1,0,2:T(2,128)}), f32[1,2,512,128]{3,1,0,2:T(2,128)}, u32[]{:S(2)}, u32[]{:S(2)}) async-start(f32[1,2,512,128]{3,1,0,2:T(2,128)} %copy.807), calls=%async_computation.44 | async-start | bytes 1048576 | tf_op jit(solution)/shard_map/all_to_all | solution.py:174
  911.1 21.9 %all-to-all-start.52 = ((f32[16,1,512]{2,1,0:T(1,128)}), f32[16,1,512]{2,1,0:T(1,128)}, u32[]{:S(2)}, u32[]{:S(2)}) async-start(f32[16,1,512]{2,1,0:T(1,128)} %reshape.1213), calls=%async_computation.52 | async-start | bytes 65536 | tf_op jit(solution)/shard_map/all_to_all | solution.py:160
  933.1 18.7 %all-to-all-start.46 = ((f32[1,32,32,128]{3,2,0,1:T(8,128)}), f32[1,32,32,128]{3,2,0,1:T(8,128)S(1)}, u32[]{:S(2)}, u32[]{:S(2)}) async-start(f32[1,32,32,128]{3,2,0,1:T(8,128)} %copy.813), calls=%async_computation.46 | async-start | bytes 1048576 | tf_op jit(solution)/shard_map/all_to_all | solution.py:184
  1007.2 35.4 %all-to-all-start.48 = ((f32[1,2,512,128]{3,1,0,2:T(2,128)}), f32[1,2,512,128]{3,1,0,2:T(2,128)S(1)}, u32[]{:S(2)}, u32[]{:S(2)}) async-start(f32[1,2,512,128]{3,1,0,2:T(2,128)} %copy.824), calls=%async_computation.48 | async-start | bytes 1048576 | tf_op jit(solution)/shard_map/all_to_all | solution.py:161
  1046.1 23.5 %all-to-all-start.49 = ((f32[1,16,32,128]{3,2,0,1:T(8,128)}), f32[1,16,32,128]{3,2,0,1:T(8,128)S(1)}, u32[]{:S(2)}, u32[]{:S(2)}) async-start(f32[1,16,32,128]{3,2,0,1:T(8,128)} %copy.829), calls=%async_computation.49 | async-start | bytes 524288 | tf_op jit(solution)/shard_map/all_to_all | solution.py:164
  1060.9 222.4 %all-reduce.5.cloned.1.call-start = ((), (), s32[]{:S(2)}) async-start(), calls=%async_computation.60 | async-start | bytes 524288 | tf_op jit(solution)/shard_map/psum | solution.py:321
  (100 other events, 1196.9 us)
Sparse Core Ops, SparseCore 0:
  1144.8 138.5 all-reduce.4
where the time goes:
time: 1310 us; the launch traced here: 1290 us
  waiting for transfers between devices  427 us (33%)
  starting transfers between devices  315 us (24%)
  local copies, waits for them, and re-layouts  193 us (15%)
  matrix products  149 us (11%)
  blocking collectives  118 us (9%)
  other arithmetic  75 us (6%)
  between operations  16.5 us (1%)
    psum x1, waiting for transfers between devices, shards(): lax.psum((local_w_in, local_w_out, local_taps, local_skip_one, local_skip...  138 us
    psum x1, blocking collectives, shards(): lax.psum((local_w_in, local_w_out, local_taps, local_skip_one, local_skip...  66.5 us
    unnamed x186, local copies, waits for them, and re-layouts  50.7 us
    all_to_all x6, waiting for transfers between devices, restore_spectrum(): lax.all_to_all(real_part, 'seq', split_axis=1, concat_axis=2, tiled=True)  38.3 us
    all_to_all x6, starting transfers between devices, restore_spectrum(): lax.all_to_all(imag_part, 'seq', split_axis=1, concat_axis=2, tiled=True)  37.1 us
    all_to_all x6, waiting for transfers between devices, signal(): lax.all_to_all(imag_part, 'seq', split_axis=2, concat_axis=1, tiled=True)  34.4 us
    all_to_all x5, starting transfers between devices, signal(): lax.all_to_all(columns, 'seq', split_axis=1, concat_axis=2, tiled=True)  34.3 us
    all_to_all x6, waiting for transfers between devices, order_spectrum(): lax.all_to_all(imag_part, 'seq', split_axis=2, concat_axis=1, tiled=True)  33.6 us
  transfers between devices with their start and end apart: 61, of which 52 were waited for; matrix products, arithmetic and copies ran while one was open for 23% of the time, Pallas kernels for 0%

commit v1 on v0

v1 whole, which is shorter than its diff:
```python
import math

import numpy as np

import jax
import jax.numpy as jnp
from jax import lax
from jax.sharding import PartitionSpec as P

HIGHEST = lax.Precision.HIGHEST
LANES = 128


def dft_tables(length):
    size = 2 * length
    rows = size // LANES
    half = length // LANES
    k1 = np.arange(rows)
    f1 = np.exp(-2j * np.pi * (np.outer(k1, np.arange(half)) % rows) / rows)
    turn = np.exp(-2j * np.pi * np.outer(k1, np.arange(LANES)) / size)
    f2 = np.exp(-2j * np.pi * (np.outer(np.arange(LANES), np.arange(LANES)) % LANES) / LANES)
    fwd1 = np.concatenate([f1.real, f1.imag], axis=0)
    fwd2 = np.block([[f2.real, f2.imag], [-f2.imag, f2.real]])
    inv2 = np.block([[f2.real, -f2.imag], [f2.imag, f2.real]])
    inv1 = np.concatenate([f1.real.T, f1.imag.T], axis=1) / size
    as32 = lambda a: jnp.asarray(np.asarray(a, np.float32))
    return {
        "rows": rows,
        "fwd1": as32(fwd1),
        "fwd2": as32(fwd2),
        "inv1": as32(inv1),
        "inv2": as32(inv2),
        "turn_r": as32(turn.real)[:, None, :],
        "turn_i": as32(turn.imag)[:, None, :],
    }


def spectrum(x, tab):
    rows = tab["rows"]
    a = jnp.einsum("kn,ncm->kcm", tab["fwd1"], x, precision=HIGHEST)
    ar, ai = a[:rows], a[rows:]
    tr, ti = tab["turn_r"], tab["turn_i"]
    cat = jnp.concatenate([ar * tr - ai * ti, ar * ti + ai * tr], axis=-1)
    return jnp.einsum("kcm,mj->kcj", cat, tab["fwd2"], precision=HIGHEST)


def signal(s, tab):
    b = jnp.einsum("kcj,jm->kcm", s, tab["inv2"], precision=HIGHEST)
    br, bi = b[..., :LANES], b[..., LANES:]
    tr, ti = tab["turn_r"], tab["turn_i"]
    stacked = jnp.concatenate([br * tr + bi * ti, bi * tr - br * ti], axis=0)
    return jnp.einsum("nk,kcm->ncm", tab["inv1"], stacked, precision=HIGHEST)


def cmul(a, b, conj=False):
    ar, ai = a[..., :LANES], a[..., LANES:]
    br, bi = b[..., :LANES], b[..., LANES:]
    if conj:
        bi = -bi
    return jnp.concatenate([ar * br - ai * bi, ar * bi + ai * br], axis=-1)


def fold(x):
    c, length = x.shape
    return jnp.swapaxes(x.reshape(c, length // LANES, LANES), 0, 1)


def unfold(x):
    half, c, lanes = x.shape
    return jnp.swapaxes(x, 0, 1).reshape(c, half * lanes)


def shards(series, cotangent, w_in, w_out, taps, skip_one, skip_two, filter_one, filter_two):
    _, block, width = series.shape
    seq_n = lax.axis_size("seq")
    dp_n = lax.axis_size("dp")
    length = block * seq_n
    half = length // LANES
    me = lax.axis_index("seq")
    per = width // seq_n
    filters = filter_one.shape[0]
    group_width = width // filters
    per_group = group_width // per
    group = me // per_group
    grad_scale = 1.0 / math.sqrt(dp_n * series.shape[0] * length)
    tab = dft_tables(length)

    series_full = lax.all_gather(series[0], "seq", axis=0, tiled=True)
    cot_full = lax.all_gather(cotangent[0], "seq", axis=0, tiled=True)
    filt = lax.all_gather(jnp.stack([filter_one, filter_two]), "seq", axis=2, tiled=True)
    h_rows = lax.dynamic_index_in_dim(filt, group, axis=1, keepdims=False)

    w_sel = lax.dynamic_index_in_dim(
        w_in.reshape(width, 3, seq_n, per), me, axis=2, keepdims=False
    ).reshape(width, 3 * per)
    taps_sel = lax.dynamic_index_in_dim(
        taps.reshape(3, 3, seq_n, per), me, axis=2, keepdims=False
    ).reshape(3, 3 * per)
    wout_sel = lax.dynamic_index_in_dim(
        w_out.reshape(seq_n, per, width), me, axis=0, keepdims=False
    )
    skip1 = lax.dynamic_index_in_dim(skip_one.reshape(seq_n, per), me, axis=0, keepdims=False)
    skip2 = lax.dynamic_index_in_dim(skip_two.reshape(seq_n, per), me, axis=0, keepdims=False)
    skip1 = skip1[None, :, None]
    skip2 = skip2[None, :, None]

    proj = jnp.einsum("td,dc->ct", series_full, w_sel, preferred_element_type=jnp.float32)
    prev1 = jnp.pad(proj, ((0, 0), (1, 0)))[:, :length]
    prev2 = jnp.pad(proj, ((0, 0), (2, 0)))[:, :length]
    conv = taps_sel[0][:, None] * proj + taps_sel[1][:, None] * prev1 + taps_sel[2][:, None] * prev2
    conv_f = fold(conv)
    value = conv_f[:, :per]
    gate_one = conv_f[:, per : 2 * per]
    gate_two = conv_f[:, 2 * per :]

    h_spec = spectrum(fold(h_rows), tab)
    h_one = h_spec[:, 0:1]
    h_two = h_spec[:, 1:2]

    v_spec = spectrum(value, tab)
    y_one = signal(cmul(v_spec, h_one), tab) + skip1 * value
    gated_mid = gate_one * y_one
    m_spec = spectrum(gated_mid, tab)
    y_two = signal(cmul(m_spec, h_two), tab) + skip2 * gated_mid
    product = (gate_two * y_two).astype(jnp.bfloat16)

    cot_folded = cot_full.reshape(half, LANES, width)
    d_product = jnp.einsum(
        "nmd,cd->ncm", cot_folded, wout_sel, preferred_element_type=jnp.float32
    )
    grad_two = d_product * gate_two
    d_gate_two = d_product * y_two
    g2_spec = spectrum(grad_two, tab)
    d_mid = signal(cmul(g2_spec, h_two, conj=True), tab) + skip2 * grad_two
    grad_one = d_mid * gate_one
    d_gate_one = d_mid * y_one
    g1_spec = spectrum(grad_one, tab)
    d_value = signal(cmul(g1_spec, h_one, conj=True), tab) + skip1 * grad_one

    corr = jnp.concatenate(
        [
            jnp.sum(cmul(g1_spec, v_spec, conj=True), axis=1, keepdims=True),
            jnp.sum(cmul(g2_spec, m_spec, conj=True), axis=1, keepdims=True),
        ],
        axis=1,
    )
    filt_grad = unfold(signal(corr, tab))

    d_conv = unfold(jnp.concatenate([d_value, d_gate_one, d_gate_two], axis=1))
    next1 = jnp.pad(d_conv, ((0, 0), (0, 1)))[:, 1:]
    next2 = jnp.pad(d_conv, ((0, 0), (0, 2)))[:, 2:]
    d_proj = (
        taps_sel[0][:, None] * d_conv + taps_sel[1][:, None] * next1 + taps_sel[2][:, None] * next2
    ).astype(jnp.bfloat16)

    local_taps = jnp.stack(
        [jnp.sum(d_conv * proj, axis=1), jnp.sum(d_conv * prev1, axis=1), jnp.sum(d_conv * prev2, axis=1)]
    )
    local_skip1 = jnp.sum(grad_one * value, axis=(0, 2))
    local_skip2 = jnp.sum(grad_two * gated_mid, axis=(0, 2))
    local_w_in = jnp.einsum("td,ct->dc", series_full, d_proj, preferred_element_type=jnp.float32)
    local_w_out = jnp.einsum(
        "ncm,nmd->cd", product, cot_folded, preferred_element_type=jnp.float32
    )

    prod_blocks = product.reshape(seq_n, half // seq_n, per, LANES)
    prod_blocks = lax.all_to_all(prod_blocks, "seq", 0, 0, tiled=True)
    output = jnp.einsum(
        "jnim,jid->nmd",
        prod_blocks,
        w_out.reshape(seq_n, per, width),
        preferred_element_type=jnp.float32,
    ).astype(jnp.bfloat16)
    output = output.reshape(1, block, width)

    dp_blocks = d_proj.reshape(3, per, seq_n, block)
    dp_blocks = lax.all_to_all(dp_blocks, "seq", 2, 2, tiled=True)
    d_series = jnp.einsum(
        "pijt,dpji->td",
        dp_blocks,
        w_in.reshape(width, 3, seq_n, per),
        preferred_element_type=jnp.float32,
    ).astype(jnp.bfloat16)
    d_series = d_series.reshape(1, block, width)

    fg_blocks = lax.all_to_all(filt_grad.reshape(2, seq_n, block), "seq", 1, 1, tiled=True)
    fg_blocks = jnp.sum(fg_blocks.reshape(2, filters, per_group, block), axis=2)

    flat = jnp.concatenate(
        [
            local_w_in.reshape(-1),
            local_w_out.reshape(-1),
            local_taps.reshape(-1),
            local_skip1,
            local_skip2,
        ]
    )
    flat, fg_blocks = lax.psum((flat, fg_blocks), "dp")
    gathered = lax.all_gather(flat, "seq", axis=0, tiled=False)
    sizes = [width * 3 * per, per * width, 3 * 3 * per, per, per]
    offsets = np.cumsum([0] + sizes)
    part = lambda i: gathered[:, offsets[i] : offsets[i + 1]]
    grad_w_in = jnp.transpose(part(0).reshape(seq_n, width, 3, per), (1, 2, 0, 3)).reshape(
        width, 3 * width
    )
    grad_w_out = part(1).reshape(width, width)
    grad_taps = jnp.transpose(part(2).reshape(seq_n, 3, 3, per), (1, 2, 0, 3)).reshape(3, 3 * width)
    grad_skip_one = part(3).reshape(width)
    grad_skip_two = part(4).reshape(width)

    return (
        output,
        d_series,
        grad_scale * grad_w_in,
        grad_scale * grad_w_out,
        grad_scale * grad_taps,
        grad_scale * grad_skip_one,
        grad_scale * grad_skip_two,
        grad_scale * fg_blocks[0],
        grad_scale * fg_blocks[1],
    )


def solution(mesh):
    in_specs = (
        P("dp", "seq", None),
        P("dp", "seq", None),
        P(),
        P(),
        P(),
        P(),
        P(),
        P(None, "seq"),
        P(None, "seq"),
    )
    out_specs = (
        P("dp", "seq", None),
        P("dp", "seq", None),
        P(),
        P(),
        P(),
        P(),
        P(),
        P(None, "seq"),
        P(None, "seq"),
    )
    return jax.shard_map(shards, mesh=mesh, in_specs=in_specs, out_specs=out_specs, check_vma=False)
```

time: 1310 us -> 242 us (0.18); the launches traced: 1290 us -> 241 us
  waiting for transfers between devices: 427 us -> 74.9 us
  starting transfers between devices: 315 us -> 11.3 us
  local copies, waits for them, and re-layouts: 193 us -> 13 us
  matrix products: 149 us -> 31.4 us
  other arithmetic: 75 us -> 6.73 us
  blocking collectives: 118 us -> 88.9 us
    all_to_all x58 -> x3, starting transfers between devices: 308 us -> 11.2 us  [the longest x1 3.99 us: shards(): lax.all_to_all(filt_grad.reshape(2, seq_n, block), 'seq', 1, 1, tiled=True)]
    all_to_all x58 -> x3, waiting for transfers between devices: 287 us -> 11 us  [the longest x1 6.55 us: shards(): dp_blocks = lax.all_to_all(dp_blocks, 'seq', 2, 2, tiled=True)]
    psum x1 -> x0, waiting for transfers between devices: 138 us -> none  [shards(): lax.psum((local_w_in, local_w_out, local_taps, local_skip_one, local_skip...]
    dot_general x126 -> x26, matrix products: 149 us -> 31.4 us  [the longest x5 8.24 us: spectrum(): return jnp.einsum('kcm,mj->kcj', cat, tab['fwd2'], precision=HIGHEST)]
    psum x2 -> x1, blocking collectives: 93.9 us -> 27.5 us  [shards(): flat, fg_blocks = lax.psum((flat, fg_blocks), 'dp')]
    all_gather x0 -> x2, waiting for transfers between devices: none -> 62.5 us  [the longest x1 44.9 us: shards(): cot_full = lax.all_gather(cotangent[0], 'seq', axis=0, tiled=True)]
    all_gather x0 -> x2, blocking collectives: none -> 61.4 us  [the longest x1 32.8 us: shards(): gathered = lax.all_gather(flat, 'seq', axis=0, tiled=False)]
    all_to_all x68 -> x0, local copies, waits for them, and re-layouts: 57.9 us -> none  [the longest x16 19.4 us: order_spectrum(): lax.all_to_all(imag_part, 'seq', split_axis=2, concat_axis=1, tiled=True)]
  transfers between devices with their start and end apart: 61 -> 5, of which waited for: 52 -> 4; matrix products, arithmetic and copies ran while one was open for 23% -> 9% of each run, Pallas kernels for 0% -> 0%
where the time goes in v1:
time: 242 us; the launch traced here: 241 us
  blocking collectives  88.9 us (37%)
  waiting for transfers between devices  74.9 us (31%)
  matrix products  31.4 us (13%)
  between operations  14.6 us (6%)
  local copies, waits for them, and re-layouts  13 us (5%)
  starting transfers between devices  11.3 us (5%)
  other arithmetic  6.73 us (3%)
    all_gather x1, waiting for transfers between devices, shards(): cot_full = lax.all_gather(cotangent[0], 'seq', axis=0, tiled=True)  44.9 us
    all_gather x1, blocking collectives, shards(): gathered = lax.all_gather(flat, 'seq', axis=0, tiled=False)  32.8 us
    all_gather x1, blocking collectives, shards(): lax.all_gather(jnp.stack([filter_one, filter_two]), 'seq', axis=2, tiled=...  28.6 us
    psum x1, blocking collectives, shards(): flat, fg_blocks = lax.psum((flat, fg_blocks), 'dp')  27.5 us
    all_gather x1, waiting for transfers between devices, shards(): series_full = lax.all_gather(series[0], 'seq', axis=0, tiled=True)  17.6 us
    dot_general x5, matrix products, spectrum(): return jnp.einsum('kcm,mj->kcj', cat, tab['fwd2'], precision=HIGHEST)  8.24 us
    all_to_all x1, waiting for transfers between devices, shards(): dp_blocks = lax.all_to_all(dp_blocks, 'seq', 2, 2, tiled=True)  6.55 us
    dot_general x5, matrix products, spectrum(): a = jnp.einsum('kn,ncm->kcm', tab['fwd1'], x, precision=HIGHEST)  5.4 us
  transfers between devices with their start and end apart: 5, of which 4 were waited for; matrix products, arithmetic and copies ran while one was open for 9% of the time, Pallas kernels for 0%

profile of v1, /device:TPU:1, one launch (start us, length us, event | category | flops | bytes accessed | tf_op | source)
XLA Modules:
  0.0 240.8 jit_solution(16323084366032261383)
XLA Ops:
  11.3 1.0 copy.192
  13.1 28.6 %all_gather.16 = f32[2,8,8192]{2,1,0:T(8,128)S(1)} all-gather(f32[2,8,512]{2,1,0:T(8,128)S(1)} %pad_maximum_fusion.1), channel_id=1, replica_groups=mesh['dp'=8,'seq'=16] {'seq'}, dimensions={2}, use_global_device_ids=true | all-gather | bytes 557056 | tf_op jit(solution)/shard_map/all_gather | solution.py:90
  41.7 1.3 fusion.105
  43.0 0.9 multiply_subtract_fusion.15
  45.2 17.6 %all-gather.6.cloned.1.call-done = bf16[1,8192,128]{2,1,0:T(8,128)(2,1)} async-done(((bf16[1,512,128]{2,1,0:T(8,128)(2,1)}), bf16[1,8192,128]{2,1,0:T(8,128)(2,1)}) %all-gather.6.cloned.1.call-update) | async-done | bytes 2097168 | tf_op jit(solution)/shard_map/all_gather | solution.py:88
  62.9 2.8 %fusion.2 = f32[24,8192]{1,0:T(8,128)S(1)} fusion(bf16[1,8192,128]{2,1,0:T(8,128)(2,1)} %all-gather.6.cloned.1.call-done, bf16[128,3,16,8]{0,3,2,1:T(8,128)(2,1)S(1)} %bitcast.175, s32[]{:T(128)S(6)} %select_n.20), kind=kOutput, calls=%fused_computation.2 | convolution fusion | flops 50331648 | bytes 2889732 | tf_op jit(solution)/shard_map/td,dc->ct/dot_general | solution.py:107
  66.5 1.0 fusion.70
  67.6 44.9 %all-gather.8.cloned.1.call-done = bf16[1,8192,128]{2,1,0:T(8,128)(2,1)} async-done(((bf16[1,512,128]{2,1,0:T(8,128)(2,1)}), bf16[1,8192,128]{2,1,0:T(8,128)(2,1)}) %all-gather.8.cloned.1.call-update) | async-done | bytes 2097168 | tf_op jit(solution)/shard_map/all_gather | solution.py:89
  112.4 2.2 fusion.77
  114.7 1.0 fusion.104
  115.9 1.8 fusion.32
  117.9 1.1 fusion.36
  119.2 1.1 convolution_add_fusion.1
  120.3 1.0 fusion.103
  121.7 1.9 fusion.43
  123.6 2.1 fusion.10
  126.2 1.1 fusion.14
  127.3 1.1 fusion.47
  128.8 1.1 convolution_add_fusion.3
  129.9 1.0 fusion.102
  131.1 1.9 fusion.21
  133.3 1.1 fusion.25
  134.6 1.1 convolution_add_fusion
  135.7 1.2 multiply_reduce_fusion.3
  140.8 4.0 %all-to-all-start.2 = ((f32[2,16,512]{2,0,1:T(2,128)}), f32[2,16,512]{2,0,1:T(2,128)S(1)}, u32[]{:S(2)}, u32[]{:S(2)}) async-start(f32[2,16,512]{2,0,1:T(2,128)} %copy.223), calls=%async_computation.2 | async-start | bytes 131072 | tf_op jit(solution)/shard_map/all_to_all | solution.py:186
  147.7 4.5 %all-to-all-done.2 = f32[2,16,512]{2,0,1:T(2,128)S(1)} async-done(((f32[2,16,512]{2,0,1:T(2,128)}), f32[2,16,512]{2,0,1:T(2,128)S(1)}, u32[]{:S(2)}, u32[]{:S(2)}) %all-to-all-start.2) | async-done | bytes 65568 | tf_op jit(solution)/shard_map/all_to_all | solution.py:186
  152.1 3.7 %all-to-all-start = ((bf16[16,4,8,128]{3,2,1,0:T(8,128)(2,1)}), bf16[16,4,8,128]{3,2,1,0:T(8,128)(2,1)S(1)}, u32[]{:S(2)}, u32[]{:S(2)}) async-start(bf16[16,4,8,128]{3,2,1,0:T(8,128)(2,1)} %copy.202), calls=%async_computation | async-start | bytes 262144 | tf_op jit(solution)/shard_map/all_to_all | solution.py:167
  155.8 27.5 %all-reduce.4 = (f32[1,4184]{1,0:T(1,128)S(1)}, f32[2,8,512]{2,0,1:T(2,128)S(1)}) all-reduce(f32[1,4184]{1,0:T(1,128)S(1)} %all_gather.18, f32[2,8,512]{2,0,1:T(2,128)S(1)} %bitcast_reduce_fusion), channel_id=1, replica_groups=mesh['dp'=8,'seq'=16] {'dp'}, use_global_device_ids=true, to_apply=%region_5.6 | all-reduce | flops 12376 | bytes 99008 | tf_op jit(solution)/shard_map/psum | solution.py:198
  183.4 32.8 %all-gather.2 = f32[16,1,4184]{2,1,0:T(1,128)S(1)} all-gather(f32[1,1,4184]{2,1,0:T(1,128)S(1)} %bitcast.177), channel_id=1, replica_groups=mesh['dp'=8,'seq'=16] {'seq'}, dimensions={0}, use_global_device_ids=true | all-gather | bytes 284512 | tf_op jit(solution)/shard_map/all_gather | solution.py:199
  219.6 3.5 %all-to-all-start.1 = ((bf16[3,8,16,512]{3,1,0,2:T(8,128)(2,1)}), bf16[3,8,16,512]{3,1,0,2:T(8,128)(2,1)S(1)}, u32[]{:S(2)}, u32[]{:S(2)}) async-start(bf16[3,8,16,512]{3,1,0,2:T(8,128)(2,1)} %copy.212), calls=%async_computation.1 | async-start | bytes 786432 | tf_op jit(solution)/shard_map/all_to_all | solution.py:177
  226.5 6.5 %all-to-all-done.1 = bf16[3,8,16,512]{3,1,0,2:T(8,128)(2,1)S(1)} async-done(((bf16[3,8,16,512]{3,1,0,2:T(8,128)(2,1)}), bf16[3,8,16,512]{3,1,0,2:T(8,128)(2,1)S(1)}, u32[]{:S(2)}, u32[]{:S(2)}) %all-to-all-start.1) | async-done | bytes 393248 | tf_op jit(solution)/shard_map/all_to_all | solution.py:177
  233.0 1.0 fusion.6
  (98 shorter events, 22.5 us)
Async XLA Ops:
  7.2 105.3 %copy-start = (bf16[128,128]{1,0:T(8,128)(2,1)S(1)}, bf16[128,128]{1,0:T(8,128)(2,1)}, u32[]{:S(2)}) copy-start(bf16[128,128]{1,0:T(8,128)(2,1)} %param.18) | copy-start | bytes 98308
  7.2 36.7 %copy-start.4 = (f32[256,256,1]{1,0,2:T(8,128)S(1)}, f32[256,256,1]{1,0,2:T(8,128)}, u32[]{:S(2)}) copy-start(f32[256,256,1]{1,0,2:T(8,128)} %constant.82) | copy-start | bytes 786436
  7.2 55.7 %all-gather.6.cloned.1.call-start = ((), (), s32[]{:S(2)}) async-start(), calls=%async_computation.3 | async-start | bytes 2228224 | tf_op jit(solution)/shard_map/all_gather | solution.py:88
  7.9 104.5 %all-gather.8.cloned.1.call-start = ((), (), s32[]{:S(2)}) async-start(), calls=%async_computation.4 | async-start | bytes 2228224 | tf_op jit(solution)/shard_map/all_gather | solution.py:89
  12.3 53.3 %copy-start.13 = (bf16[128,384]{0,1:T(8,128)(2,1)}, bf16[128,384]{0,1:T(8,128)(2,1)S(1)}, u32[]{:S(2)}) copy-start(bf16[128,384]{0,1:T(8,128)(2,1)S(1)} %copy.192) | copy-start | bytes 294916
  65.6 0.9 copy-start.8
  67.5 48.2 %copy-start.5 = (f32[128,128]{0,1:T(8,128)S(1)}, f32[128,128]{0,1:T(8,128)}, u32[]{:S(2)}) copy-start(f32[128,128]{0,1:T(8,128)} %constant.69.clone) | copy-start | bytes 196612
  67.5 48.2 %copy-start.6 = (f32[128,128]{0,1:T(8,128)S(1)}, f32[128,128]{0,1:T(8,128)}, u32[]{:S(2)}) copy-start(f32[128,128]{0,1:T(8,128)} %constant.68.clone) | copy-start | bytes 196612
  115.7 2.0 copy-start.12
  115.9 2.0 copy-start.3
  117.9 1.3 copy-start.7
  121.7 4.0 %copy-start.9 = (f32[128,128]{1,0:T(8,128)S(1)}, f32[128,128]{1,0:T(8,128)}, u32[]{:S(2)}) copy-start(f32[128,128]{1,0:T(8,128)} %get-tuple-element.107) | copy-start | bytes 196612
  121.7 4.0 %copy-start.10 = (f32[128,128]{1,0:T(8,128)S(1)}, f32[128,128]{1,0:T(8,128)}, u32[]{:S(2)}) copy-start(f32[128,128]{1,0:T(8,128)} %get-tuple-element.111) | copy-start | bytes 196612
  121.7 4.0 %copy-start.11 = (f32[128,128]{1,0:T(8,128)S(1)}, f32[128,128]{1,0:T(8,128)}, u32[]{:S(2)}) copy-start(f32[128,128]{1,0:T(8,128)} %get-tuple-element.112) | copy-start | bytes 196612
  136.9 1.6 copy-start.2
  139.1 7.7 %copy-start.1 = (bf16[1,8192,128]{2,1,0:T(8,128)(2,1)S(1)}, bf16[1,8192,128]{2,1,0:T(8,128)(2,1)}, u32[]{:S(2)}) copy-start(bf16[1,8192,128]{2,1,0:T(8,128)(2,1)} %all-gather.6.cloned.1.call-done) | copy-start | bytes 6291460
  140.8 11.3 %all-to-all-start.2 = ((f32[2,16,512]{2,0,1:T(2,128)}), f32[2,16,512]{2,0,1:T(2,128)S(1)}, u32[]{:S(2)}, u32[]{:S(2)}) async-start(f32[2,16,512]{2,0,1:T(2,128)} %copy.223), calls=%async_computation.2 | async-start | bytes 131072 | tf_op jit(solution)/shard_map/all_to_all | solution.py:186
  152.1 67.5 %all-to-all-start = ((bf16[16,4,8,128]{3,2,1,0:T(8,128)(2,1)}), bf16[16,4,8,128]{3,2,1,0:T(8,128)(2,1)S(1)}, u32[]{:S(2)}, u32[]{:S(2)}) async-start(bf16[16,4,8,128]{3,2,1,0:T(8,128)(2,1)} %copy.202), calls=%async_computation | async-start | bytes 262144 | tf_op jit(solution)/shard_map/all_to_all | solution.py:167
  219.6 13.4 %all-to-all-start.1 = ((bf16[3,8,16,512]{3,1,0,2:T(8,128)(2,1)}), bf16[3,8,16,512]{3,1,0,2:T(8,128)(2,1)S(1)}, u32[]{:S(2)}, u32[]{:S(2)}) async-start(bf16[3,8,16,512]{3,1,0,2:T(8,128)(2,1)} %copy.212), calls=%async_computation.1 | async-start | bytes 786432 | tf_op jit(solution)/shard_map/all_to_all | solution.py:177
  224.3 8.8 %copy-start.14 = (bf16[128,384]{0,1:T(8,128)(2,1)S(1)}, bf16[128,384]{0,1:T(8,128)(2,1)}, u32[]{:S(2)}) copy-start(bf16[128,384]{0,1:T(8,128)(2,1)} %copy-done.13) | copy-start | bytes 294916
Sparse Core Ops, SparseCore 0:
  10.5 52.3 all-gather.5
  65.3 47.0 all-gather.7

commit v2 on v1

--- a/solution.py
+++ b/solution.py
@@ -85,26 +85,21 @@
     grad_scale = 1.0 / math.sqrt(dp_n * series.shape[0] * length)
     tab = dft_tables(length)
 
-    series_full = lax.all_gather(series[0], "seq", axis=0, tiled=True)
-    cot_full = lax.all_gather(cotangent[0], "seq", axis=0, tiled=True)
-    filt = lax.all_gather(jnp.stack([filter_one, filter_two]), "seq", axis=2, tiled=True)
-    h_rows = lax.dynamic_index_in_dim(filt, group, axis=1, keepdims=False)
-
-    w_sel = lax.dynamic_index_in_dim(
-        w_in.reshape(width, 3, seq_n, per), me, axis=2, keepdims=False
-    ).reshape(width, 3 * per)
+    rows_sent = jnp.repeat(jnp.swapaxes(jnp.stack([filter_one, filter_two]), 0, 1), per_group, axis=0)
+    rows_got = lax.all_to_all(rows_sent, "seq", 0, 0, tiled=True)
+    h_rows = jnp.swapaxes(rows_got, 0, 1).reshape(2, length)
+
     taps_sel = lax.dynamic_index_in_dim(
         taps.reshape(3, 3, seq_n, per), me, axis=2, keepdims=False
     ).reshape(3, 3 * per)
-    wout_sel = lax.dynamic_index_in_dim(
-        w_out.reshape(seq_n, per, width), me, axis=0, keepdims=False
-    )
     skip1 = lax.dynamic_index_in_dim(skip_one.reshape(seq_n, per), me, axis=0, keepdims=False)
     skip2 = lax.dynamic_index_in_dim(skip_two.reshape(seq_n, per), me, axis=0, keepdims=False)
     skip1 = skip1[None, :, None]
     skip2 = skip2[None, :, None]
 
-    proj = jnp.einsum("td,dc->ct", series_full, w_sel, preferred_element_type=jnp.float32)
+    proj_blk = jnp.einsum("td,dc->ct", series[0], w_in, preferred_element_type=jnp.float32)
+    proj_blk = lax.all_to_all(proj_blk.reshape(3, seq_n, per, block), "seq", 1, 1, tiled=True)
+    proj = jnp.swapaxes(proj_blk, 1, 2).reshape(3 * per, length)
     prev1 = jnp.pad(proj, ((0, 0), (1, 0)))[:, :length]
     prev2 = jnp.pad(proj, ((0, 0), (2, 0)))[:, :length]
     conv = taps_sel[0][:, None] * proj + taps_sel[1][:, None] * prev1 + taps_sel[2][:, None] * prev2
@@ -124,10 +119,11 @@
     y_two = signal(cmul(m_spec, h_two), tab) + skip2 * gated_mid
     product = (gate_two * y_two).astype(jnp.bfloat16)
 
-    cot_folded = cot_full.reshape(half, LANES, width)
-    d_product = jnp.einsum(
-        "nmd,cd->ncm", cot_folded, wout_sel, preferred_element_type=jnp.float32
-    )
+    dprod_blk = jnp.einsum("td,cd->ct", cotangent[0], w_out, preferred_element_type=jnp.float32)
+    dprod_blk = lax.all_to_all(dprod_blk.reshape(seq_n, per, block), "seq", 0, 0, tiled=True)
+    d_product = jnp.swapaxes(
+        dprod_blk.reshape(seq_n, per, block // LANES, LANES), 1, 2
+    ).reshape(half, per, LANES)
     grad_two = d_product * gate_two
     d_gate_two = d_product * y_two
     g2_spec = spectrum(grad_two, tab)
@@ -158,11 +154,6 @@
     )
     local_skip1 = jnp.sum(grad_one * value, axis=(0, 2))
     local_skip2 = jnp.sum(grad_two * gated_mid, axis=(0, 2))
-    local_w_in = jnp.einsum("td,ct->dc", series_full, d_proj, preferred_element_type=jnp.float32)
-    local_w_out = jnp.einsum(
-        "ncm,nmd->cd", product, cot_folded, preferred_element_type=jnp.float32
-    )
-
     prod_blocks = product.reshape(seq_n, half // seq_n, per, LANES)
     prod_blocks = lax.all_to_all(prod_blocks, "seq", 0, 0, tiled=True)
     output = jnp.einsum(
@@ -186,27 +177,19 @@
     fg_blocks = lax.all_to_all(filt_grad.reshape(2, seq_n, block), "seq", 1, 1, tiled=True)
     fg_blocks = jnp.sum(fg_blocks.reshape(2, filters, per_group, block), axis=2)
 
-    flat = jnp.concatenate(
-        [
-            local_w_in.reshape(-1),
-            local_w_out.reshape(-1),
-            local_taps.reshape(-1),
-            local_skip1,
-            local_skip2,
-        ]
-    )
-    flat, fg_blocks = lax.psum((flat, fg_blocks), "dp")
-    gathered = lax.all_gather(flat, "seq", axis=0, tiled=False)
-    sizes = [width * 3 * per, per * width, 3 * 3 * per, per, per]
-    offsets = np.cumsum([0] + sizes)
-    part = lambda i: gathered[:, offsets[i] : offsets[i + 1]]
-    grad_w_in = jnp.transpose(part(0).reshape(seq_n, width, 3, per), (1, 2, 0, 3)).reshape(
-        width, 3 * width
-    )
-    grad_w_out = part(1).reshape(width, width)
-    grad_taps = jnp.transpose(part(2).reshape(seq_n, 3, 3, per), (1, 2, 0, 3)).reshape(3, 3 * width)
-    grad_skip_one = part(3).reshape(width)
-    grad_skip_two = part(4).reshape(width)
+    prod_rows = jnp.transpose(prod_blocks, (1, 3, 0, 2)).reshape(block, width)
+    dp_rows = jnp.transpose(dp_blocks, (3, 0, 2, 1)).reshape(block, 3 * width)
+    local_w_in = jnp.einsum("td,tc->dc", series[0], dp_rows, preferred_element_type=jnp.float32)
+    local_w_out = jnp.einsum("tc,td->cd", prod_rows, cotangent[0], preferred_element_type=jnp.float32)
+    small = jnp.concatenate([local_taps.reshape(3, 3, 1, per), jnp.stack([local_skip1, local_skip2, jnp.zeros_like(local_skip1)]).reshape(3, 1, 1, per)], axis=1)
+    small_full = jnp.zeros((3, 4, seq_n, per), jnp.float32)
+    small_full = lax.dynamic_update_slice(small_full, small, (0, 0, me, 0))
+    grad_w_in, grad_w_out, small_full = lax.psum((local_w_in, local_w_out, small_full), ("dp", "seq"))
+    fg_blocks = lax.psum(fg_blocks, "dp")
+    small_full = small_full.reshape(3, 4, width)
+    grad_taps = small_full[:, :3].reshape(3, 3 * width)
+    grad_skip_one = small_full[0, 3]
+    grad_skip_two = small_full[1, 3]
 
     return (
         output,

time: 242 us -> 365 us (1.51)
  waiting for transfers between devices: 74.9 us -> 168 us
  starting transfers between devices: 11.3 us -> 41.2 us
    psum x0 -> x1, waiting for transfers between devices: none -> 136 us  [shards(): lax.psum((local_w_in, local_w_out, small_full), ('dp', 'seq'))]
    psum x1 -> x2, blocking collectives: 27.5 us -> 92.2 us  [the longest x1 67 us: shards(): lax.psum((local_w_in, local_w_out, small_full), ('dp', 'seq'))]
    all_gather x2 -> x0, waiting for transfers between devices: 62.5 us -> none  [the longest x1 44.9 us: shards(): cot_full = lax.all_gather(cotangent[0], 'seq', axis=0, tiled=True)]
    all_gather x2 -> x0, blocking collectives: 61.4 us -> none  [the longest x1 32.8 us: shards(): gathered = lax.all_gather(flat, 'seq', axis=0, tiled=False)]
    all_to_all x0 -> x3, waiting for transfers between devices: none -> 23.5 us  [the longest x1 13.9 us: shards(): lax.all_to_all(proj_blk.reshape(3, seq_n, per, block), 'seq', 1, 1, tiled...]
    all_to_all x0 -> x3, starting transfers between devices: none -> 18.2 us  [the longest x1 9.43 us: shards(): rows_got = lax.all_to_all(rows_sent, 'seq', 0, 0, tiled=True)]
    all_to_all x1, starting transfers between devices: 3.51 us -> 14.6 us  [shards(): dp_blocks = lax.all_to_all(dp_blocks, 'seq', 2, 2, tiled=True)]
    unnamed x37, local copies, waits for them, and re-layouts: 4.1 us -> 8.79 us
  transfers between devices with their start and end apart: 5 -> 7, of which waited for: 4 -> 5; matrix products, arithmetic and copies ran while one was open for 9% -> 3% of each run, Pallas kernels for 0% -> 0%
where the time goes in v2:
time: 365 us; the launch traced here: 364 us
  waiting for transfers between devices  168 us (46%)
  blocking collectives  92.2 us (25%)
  starting transfers between devices  41.2 us (11%)
  matrix products  28.5 us (8%)
  between operations  14.5 us (4%)
  local copies, waits for them, and re-layouts  13.5 us (4%)
  other arithmetic  6.89 us (2%)
    psum x1, waiting for transfers between devices, shards(): lax.psum((local_w_in, local_w_out, small_full), ('dp', 'seq'))  136 us
    psum x1, blocking collectives, shards(): lax.psum((local_w_in, local_w_out, small_full), ('dp', 'seq'))  67 us
    psum x1, blocking collectives, shards(): fg_blocks = lax.psum(fg_blocks, 'dp')  25.2 us
    all_to_all x1, starting transfers between devices, shards(): dp_blocks = lax.all_to_all(dp_blocks, 'seq', 2, 2, tiled=True)  14.6 us
    all_to_all x1, waiting for transfers between devices, shards(): lax.all_to_all(proj_blk.reshape(3, seq_n, per, block), 'seq', 1, 1, tiled...  13.9 us
    all_to_all x1, starting transfers between devices, shards(): rows_got = lax.all_to_all(rows_sent, 'seq', 0, 0, tiled=True)  9.43 us
    unnamed x37, local copies, waits for them, and re-layouts  8.79 us
    dot_general x5, matrix products, spectrum(): return jnp.einsum('kcm,mj->kcj', cat, tab['fwd2'], precision=HIGHEST)  8.23 us
  transfers between devices with their start and end apart: 7, of which 5 were waited for; matrix products, arithmetic and copies ran while one was open for 3% of the time, Pallas kernels for 0%

profile of v2, /device:TPU:1, one launch (start us, length us, event | category | flops | bytes accessed | tf_op | source)
XLA Modules:
  0.0 364.3 jit_solution(12172871343249868817)
XLA Ops:
  8.6 9.4 %all-to-all-start.1 = ((f32[16,2,512]{2,1,0:T(2,128)}), f32[16,2,512]{2,1,0:T(2,128)S(1)}, u32[]{:S(2)}, u32[]{:S(2)}) async-start(f32[16,2,512]{2,1,0:T(2,128)} %bitcast.12), calls=%async_computation.1 | async-start | bytes 131072 | tf_op jit(solution)/shard_map/all_to_all | solution.py:89
  20.6 1.2 fusion.68
  22.7 2.7 all-to-all-done.1
  25.4 4.6 %all-to-all-start.3 = ((f32[16,8,512]{2,1,0:T(8,128)}), f32[16,8,512]{2,1,0:T(8,128)S(1)}, u32[]{:S(2)}, u32[]{:S(2)}) async-start(f32[16,8,512]{2,1,0:T(8,128)} %fusion.70), calls=%async_computation.3 | async-start | bytes 524288 | tf_op jit(solution)/shard_map/all_to_all | solution.py:123
  31.8 6.9 %all-to-all-done.3 = f32[16,8,512]{2,1,0:T(8,128)S(1)} async-done(((f32[16,8,512]{2,1,0:T(8,128)}), f32[16,8,512]{2,1,0:T(8,128)S(1)}, u32[]{:S(2)}, u32[]{:S(2)}) %all-to-all-start.3) | async-done | bytes 262176 | tf_op jit(solution)/shard_map/all_to_all | solution.py:123
  38.7 4.2 %all-to-all-start = ((f32[3,16,8,512]{3,2,0,1:T(8,128)}), f32[3,16,8,512]{3,2,0,1:T(8,128)S(1)}, u32[]{:S(2)}, u32[]{:S(2)}) async-start(f32[3,16,8,512]{3,2,0,1:T(8,128)} %fusion.68), calls=%async_computation | async-start | bytes 1572864 | tf_op jit(solution)/shard_map/all_to_all | solution.py:101
  43.6 13.9 %all-to-all-done = f32[3,16,8,512]{3,2,0,1:T(8,128)S(1)} async-done(((f32[3,16,8,512]{3,2,0,1:T(8,128)}), f32[3,16,8,512]{3,2,0,1:T(8,128)S(1)}, u32[]{:S(2)}, u32[]{:S(2)}) %all-to-all-start) | async-done | bytes 786464 | tf_op jit(solution)/shard_map/all_to_all | solution.py:101
  59.1 1.0 fusion.64
  60.2 1.0 fusion.102
  61.3 1.9 fusion.25
  64.1 1.1 fusion.29
  66.1 1.1 convolution_add_fusion.1
  67.3 1.0 fusion.101
  68.5 1.9 fusion.3
  70.4 2.0 fusion.36
  72.9 1.1 fusion.7
  74.0 1.1 fusion.40
  75.4 1.1 convolution_add_fusion.3
  76.5 1.0 fusion.100
  77.7 1.9 fusion.14
  79.8 1.1 fusion.18
  81.1 1.1 convolution_add_fusion
  82.2 1.2 multiply_reduce_fusion.3
  86.7 4.0 %all-to-all-start.5 = ((f32[2,16,512]{2,0,1:T(2,128)}), f32[2,16,512]{2,0,1:T(2,128)S(1)}, u32[]{:S(2)}, u32[]{:S(2)}) async-start(f32[2,16,512]{2,0,1:T(2,128)} %copy.198), calls=%async_computation.5 | async-start | bytes 131072 | tf_op jit(solution)/shard_map/all_to_all | solution.py:177
  91.5 67.0 %psum.30 = f32[3,4,128]{2,1,0:T(4,128)S(1)} all-reduce(f32[3,4,128]{2,1,0:T(4,128)S(1)} %reshape.136), channel_id=1, replica_groups=mesh['dp'=8,'seq'=16] {'dp','seq'}, use_global_device_ids=true, to_apply=%region_7.8 | all-reduce | flops 1536 | bytes 12288 | tf_op jit(solution)/shard_map/psum | solution.py:187
  160.2 1.0 copy.188
  161.9 4.3 %all-to-all-start.2 = ((bf16[16,4,8,128]{3,2,1,0:T(8,128)(2,1)}), bf16[16,4,8,128]{3,2,1,0:T(8,128)(2,1)S(1)}, u32[]{:S(2)}, u32[]{:S(2)}) async-start(bf16[16,4,8,128]{3,2,1,0:T(8,128)(2,1)} %copy.177), calls=%async_computation.2 | async-start | bytes 262144 | tf_op jit(solution)/shard_map/all_to_all | solution.py:158
  166.3 25.2 %psum.31 = f32[2,8,512]{2,0,1:T(2,128)S(1)} all-reduce(f32[2,8,512]{2,0,1:T(2,128)S(1)} %bitcast_reduce_fusion), channel_id=1, replica_groups=mesh['dp'=8,'seq'=16] {'dp'}, use_global_device_ids=true, to_apply=%region_11.12 | all-reduce | flops 8192 | bytes 65536 | tf_op jit(solution)/shard_map/psum | solution.py:188
  192.7 14.6 %all-to-all-start.4 = ((bf16[3,8,16,512]{3,1,0,2:T(8,128)(2,1)}), bf16[3,8,16,512]{3,1,0,2:T(8,128)(2,1)S(1)}, u32[]{:S(2)}, u32[]{:S(2)}) async-start(bf16[3,8,16,512]{3,1,0,2:T(8,128)(2,1)} %copy.188), calls=%async_computation.4 | async-start | bytes 786432 | tf_op jit(solution)/shard_map/all_to_all | solution.py:168
  209.0 8.0 %all-to-all-done.4 = bf16[3,8,16,512]{3,1,0,2:T(8,128)(2,1)S(1)} async-done(((bf16[3,8,16,512]{3,1,0,2:T(8,128)(2,1)}), bf16[3,8,16,512]{3,1,0,2:T(8,128)(2,1)S(1)}, u32[]{:S(2)}, u32[]{:S(2)}) %all-to-all-start.4) | async-done | bytes 393248 | tf_op jit(solution)/shard_map/all_to_all | solution.py:168
  218.1 1.0 fusion.2
  219.0 136.0 %all-reduce.7.cloned.1.call-done = (f32[128,384]{0,1:T(8,128)}, f32[128,128]{1,0:T(8,128)}) async-done(((f32[128,384]{0,1:T(8,128)}, f32[128,128]{1,0:T(8,128)}), (f32[128,384]{0,1:T(8,128)}, f32[128,128]{1,0:T(8,128)})) %all-reduce.7.cloned.1.call-update) | async-done | bytes 262160 | tf_op jit(solution)/shard_map/psum | solution.py:187
  (105 shorter events, 25.0 us)
Async XLA Ops:
  7.2 13.4 %copy-start = (bf16[1,512,128]{2,1,0:T(8,128)(2,1)S(1)}, bf16[1,512,128]{2,1,0:T(8,128)(2,1)}, u32[]{:S(2)}) copy-start(bf16[1,512,128]{2,1,0:T(8,128)(2,1)} %param.15) | copy-start | bytes 393220
  8.6 10.5 %copy-start.8 = (bf16[128,384]{1,0:T(8,128)(2,1)S(1)}, bf16[128,384]{1,0:T(8,128)(2,1)}, u32[]{:S(2)}) copy-start(bf16[128,384]{1,0:T(8,128)(2,1)} %param.17) | copy-start | bytes 294916
  8.6 16.8 %all-to-all-start.1 = ((f32[16,2,512]{2,1,0:T(2,128)}), f32[16,2,512]{2,1,0:T(2,128)S(1)}, u32[]{:S(2)}, u32[]{:S(2)}) async-start(f32[16,2,512]{2,1,0:T(2,128)} %bitcast.12), calls=%async_computation.1 | async-start | bytes 131072 | tf_op jit(solution)/shard_map/all_to_all | solution.py:89
  18.1 0.7 copy-start.11
  19.2 0.7 copy-start.12
  19.8 0.7 copy-start.13
  20.6 1.2 copy-start.7
  20.6 1.2 copy-start.10
  25.4 13.3 %all-to-all-start.3 = ((f32[16,8,512]{2,1,0:T(8,128)}), f32[16,8,512]{2,1,0:T(8,128)S(1)}, u32[]{:S(2)}, u32[]{:S(2)}) async-start(f32[16,8,512]{2,1,0:T(8,128)} %fusion.70), calls=%async_computation.3 | async-start | bytes 524288 | tf_op jit(solution)/shard_map/all_to_all | solution.py:123
  30.0 0.8 copy-start.6
  30.8 0.8 copy-start.3
  30.8 0.9 copy-start.4
  31.7 11.1 %copy-start.2 = (f32[256,256,1]{1,0,2:T(8,128)S(1)}, f32[256,256,1]{1,0,2:T(8,128)}, u32[]{:S(2)}) copy-start(f32[256,256,1]{1,0,2:T(8,128)} %constant.59) | copy-start | bytes 786436
  38.7 18.8 %all-to-all-start = ((f32[3,16,8,512]{3,2,0,1:T(8,128)}), f32[3,16,8,512]{3,2,0,1:T(8,128)S(1)}, u32[]{:S(2)}, u32[]{:S(2)}) async-start(f32[3,16,8,512]{3,2,0,1:T(8,128)} %fusion.68), calls=%async_computation | async-start | bytes 1572864 | tf_op jit(solution)/shard_map/all_to_all | solution.py:101
  63.2 1.0 copy-start.1
  65.3 0.8 copy-start.5
  86.7 75.3 %all-to-all-start.5 = ((f32[2,16,512]{2,0,1:T(2,128)}), f32[2,16,512]{2,0,1:T(2,128)S(1)}, u32[]{:S(2)}, u32[]{:S(2)}) async-start(f32[2,16,512]{2,0,1:T(2,128)} %copy.198), calls=%async_computation.5 | async-start | bytes 131072 | tf_op jit(solution)/shard_map/all_to_all | solution.py:177
  161.9 30.8 %all-to-all-start.2 = ((bf16[16,4,8,128]{3,2,1,0:T(8,128)(2,1)}), bf16[16,4,8,128]{3,2,1,0:T(8,128)(2,1)S(1)}, u32[]{:S(2)}, u32[]{:S(2)}) async-start(bf16[16,4,8,128]{3,2,1,0:T(8,128)(2,1)} %copy.177), calls=%async_computation.2 | async-start | bytes 262144 | tf_op jit(solution)/shard_map/all_to_all | solution.py:158
  192.7 24.4 %all-to-all-start.4 = ((bf16[3,8,16,512]{3,1,0,2:T(8,128)(2,1)}), bf16[3,8,16,512]{3,1,0,2:T(8,128)(2,1)S(1)}, u32[]{:S(2)}, u32[]{:S(2)}) async-start(bf16[3,8,16,512]{3,1,0,2:T(8,128)(2,1)} %copy.188), calls=%async_computation.4 | async-start | bytes 786432 | tf_op jit(solution)/shard_map/all_to_all | solution.py:168
  207.3 147.7 %all-reduce.7.cloned.1.call-start = ((), (), s32[]{:S(2)}) async-start(), calls=%async_computation.6 | async-start | bytes 524288 | tf_op jit(solution)/shard_map/psum | solution.py:187
  356.0 0.8 copy-start.9
Sparse Core Ops, SparseCore 0:
  218.2 136.7 all-reduce.6

commit v3 on v2

--- a/solution.py
+++ b/solution.py
@@ -85,10 +85,6 @@
     grad_scale = 1.0 / math.sqrt(dp_n * series.shape[0] * length)
     tab = dft_tables(length)
 
-    rows_sent = jnp.repeat(jnp.swapaxes(jnp.stack([filter_one, filter_two]), 0, 1), per_group, axis=0)
-    rows_got = lax.all_to_all(rows_sent, "seq", 0, 0, tiled=True)
-    h_rows = jnp.swapaxes(rows_got, 0, 1).reshape(2, length)
-
     taps_sel = lax.dynamic_index_in_dim(
         taps.reshape(3, 3, seq_n, per), me, axis=2, keepdims=False
     ).reshape(3, 3 * per)
@@ -98,8 +94,18 @@
     skip2 = skip2[None, :, None]
 
     proj_blk = jnp.einsum("td,dc->ct", series[0], w_in, preferred_element_type=jnp.float32)
-    proj_blk = lax.all_to_all(proj_blk.reshape(3, seq_n, per, block), "seq", 1, 1, tiled=True)
-    proj = jnp.swapaxes(proj_blk, 1, 2).reshape(3 * per, length)
+    proj_blk = jnp.swapaxes(proj_blk.reshape(3, seq_n, per, block), 0, 1).reshape(seq_n, 3 * per, block)
+    dprod_blk = jnp.einsum("td,cd->ct", cotangent[0], w_out, preferred_element_type=jnp.float32)
+    dprod_blk = dprod_blk.reshape(seq_n, per, block)
+    rows_sent = jnp.repeat(jnp.swapaxes(jnp.stack([filter_one, filter_two]), 0, 1), per_group, axis=0)
+    got = lax.all_to_all(
+        jnp.concatenate([proj_blk, dprod_blk, rows_sent], axis=1), "seq", 0, 0, tiled=True
+    )
+    proj = jnp.swapaxes(got[:, : 3 * per], 0, 1).reshape(3 * per, length)
+    d_product = jnp.swapaxes(
+        got[:, 3 * per : 4 * per].reshape(seq_n, per, block // LANES, LANES), 1, 2
+    ).reshape(half, per, LANES)
+    h_rows = jnp.swapaxes(got[:, 4 * per :], 0, 1).reshape(2, length)
     prev1 = jnp.pad(proj, ((0, 0), (1, 0)))[:, :length]
     prev2 = jnp.pad(proj, ((0, 0), (2, 0)))[:, :length]
     conv = taps_sel[0][:, None] * proj + taps_sel[1][:, None] * prev1 + taps_sel[2][:, None] * prev2
@@ -119,11 +125,6 @@
     y_two = signal(cmul(m_spec, h_two), tab) + skip2 * gated_mid
     product = (gate_two * y_two).astype(jnp.bfloat16)
 
-    dprod_blk = jnp.einsum("td,cd->ct", cotangent[0], w_out, preferred_element_type=jnp.float32)
-    dprod_blk = lax.all_to_all(dprod_blk.reshape(seq_n, per, block), "seq", 0, 0, tiled=True)
-    d_product = jnp.swapaxes(
-        dprod_blk.reshape(seq_n, per, block // LANES, LANES), 1, 2
-    ).reshape(half, per, LANES)
     grad_two = d_product * gate_two
     d_gate_two = d_product * y_two
     g2_spec = spectrum(grad_two, tab)
@@ -154,39 +155,53 @@
     )
     local_skip1 = jnp.sum(grad_one * value, axis=(0, 2))
     local_skip2 = jnp.sum(grad_two * gated_mid, axis=(0, 2))
-    prod_blocks = product.reshape(seq_n, half // seq_n, per, LANES)
-    prod_blocks = lax.all_to_all(prod_blocks, "seq", 0, 0, tiled=True)
-    output = jnp.einsum(
-        "jnim,jid->nmd",
-        prod_blocks,
-        w_out.reshape(seq_n, per, width),
-        preferred_element_type=jnp.float32,
-    ).astype(jnp.bfloat16)
+    prod_sent = jnp.swapaxes(product.reshape(seq_n, half // seq_n, per, LANES), 1, 2)
+    prod_sent = prod_sent.reshape(seq_n, per, block)
+    dp_sent = jnp.swapaxes(d_proj.reshape(3 * per, seq_n, block), 0, 1)
+    back = lax.all_to_all(jnp.concatenate([prod_sent, dp_sent], axis=1), "seq", 0, 0, tiled=True)
+    prod_rows = jnp.transpose(back[:, :per], (2, 0, 1)).reshape(block, width)
+    dp_rows = jnp.transpose(back[:, per:].reshape(seq_n, 3, per, block), (3, 1, 0, 2))
+    dp_rows = dp_rows.reshape(block, 3 * width)
+    output = jnp.dot(prod_rows, w_out, preferred_element_type=jnp.float32).astype(jnp.bfloat16)
     output = output.reshape(1, block, width)
-
-    dp_blocks = d_proj.reshape(3, per, seq_n, block)
-    dp_blocks = lax.all_to_all(dp_blocks, "seq", 2, 2, tiled=True)
     d_series = jnp.einsum(
-        "pijt,dpji->td",
-        dp_blocks,
-        w_in.reshape(width, 3, seq_n, per),
-        preferred_element_type=jnp.float32,
+        "tc,dc->td", dp_rows, w_in, preferred_element_type=jnp.float32
     ).astype(jnp.bfloat16)
     d_series = d_series.reshape(1, block, width)
 
-    fg_blocks = lax.all_to_all(filt_grad.reshape(2, seq_n, block), "seq", 1, 1, tiled=True)
-    fg_blocks = jnp.sum(fg_blocks.reshape(2, filters, per_group, block), axis=2)
-
-    prod_rows = jnp.transpose(prod_blocks, (1, 3, 0, 2)).reshape(block, width)
-    dp_rows = jnp.transpose(dp_blocks, (3, 0, 2, 1)).reshape(block, 3 * width)
     local_w_in = jnp.einsum("td,tc->dc", series[0], dp_rows, preferred_element_type=jnp.float32)
     local_w_out = jnp.einsum("tc,td->cd", prod_rows, cotangent[0], preferred_element_type=jnp.float32)
-    small = jnp.concatenate([local_taps.reshape(3, 3, 1, per), jnp.stack([local_skip1, local_skip2, jnp.zeros_like(local_skip1)]).reshape(3, 1, 1, per)], axis=1)
-    small_full = jnp.zeros((3, 4, seq_n, per), jnp.float32)
-    small_full = lax.dynamic_update_slice(small_full, small, (0, 0, me, 0))
-    grad_w_in, grad_w_out, small_full = lax.psum((local_w_in, local_w_out, small_full), ("dp", "seq"))
-    fg_blocks = lax.psum(fg_blocks, "dp")
-    small_full = small_full.reshape(3, 4, width)
+    small = jnp.concatenate(
+        [
+            local_taps.reshape(3, 3, 1, per),
+            jnp.stack([local_skip1, local_skip2, jnp.zeros_like(local_skip1)]).reshape(3, 1, 1, per),
+        ],
+        axis=1,
+    )
+    small_full = lax.dynamic_update_slice(
+        jnp.zeros((3, 4, seq_n, per), jnp.float32), small, (0, 0, me, 0)
+    )
+    params = jnp.concatenate([local_w_in.reshape(-1), local_w_out.reshape(-1), small_full.reshape(-1)])
+    n_params = params.shape[0]
+    chunk = -(-n_params // (seq_n * dp_n))
+    params = jnp.pad(params, (0, chunk * seq_n * dp_n - n_params)).reshape(seq_n, dp_n * chunk)
+
+    fg_sent = jnp.swapaxes(filt_grad.reshape(2, seq_n, block), 0, 1).reshape(seq_n, 2 * block)
+    got = lax.all_to_all(jnp.concatenate([params, fg_sent], axis=1), "seq", 0, 0, tiled=True)
+    p_part = jnp.sum(got[:, : dp_n * chunk], axis=0).reshape(dp_n, chunk)
+    f_part = jnp.sum(got[:, dp_n * chunk :].reshape(filters, per_group, 2 * block), axis=1)
+    got = lax.all_to_all(jnp.concatenate([p_part, f_part], axis=1), "dp", 0, 0, tiled=True)
+    mine = jnp.sum(got, axis=0)
+    got = lax.all_to_all(jnp.broadcast_to(mine, (dp_n,) + mine.shape), "dp", 0, 0, tiled=True)
+    fg_blocks = jnp.swapaxes(got[:, chunk:].reshape(filters, 2, block), 0, 1)
+    p_seq = got[:, :chunk].reshape(1, dp_n * chunk)
+    got = lax.all_to_all(jnp.broadcast_to(p_seq, (seq_n, dp_n * chunk)), "seq", 0, 0, tiled=True)
+    full = got.reshape(-1)
+    sizes = [width * 3 * width, width * width, 3 * 4 * width]
+    offsets = np.cumsum([0] + sizes)
+    grad_w_in = full[offsets[0] : offsets[1]].reshape(width, 3 * width)
+    grad_w_out = full[offsets[1] : offsets[2]].reshape(width, width)
+    small_full = full[offsets[2] : offsets[3]].reshape(3, 4, width)
     grad_taps = small_full[:, :3].reshape(3, 3 * width)
     grad_skip_one = small_full[0, 3]
     grad_skip_two = small_full[1, 3]

time: 365 us -> 143 us (0.39)
  waiting for transfers between devices: 168 us -> 39.9 us
  blocking collectives: 92.2 us -> 22.4 us
  starting transfers between devices: 41.2 us -> 23.9 us
  between operations: 14.5 us -> 1.48 us
  other arithmetic: 6.89 us -> 12.1 us
    psum x1 -> x0, waiting for transfers between devices: 136 us -> none  [shards(): lax.psum((local_w_in, local_w_out, small_full), ('dp', 'seq'))]
    psum x2 -> x0, blocking collectives: 92.2 us -> none  [the longest x1 67 us: shards(): lax.psum((local_w_in, local_w_out, small_full), ('dp', 'seq'))]
    all_to_all x0 -> x2, blocking collectives: none -> 22.4 us  [the longest x1 12.9 us: shards(): lax.all_to_all(jnp.concatenate([params, fg_sent], axis=1), 'seq', 0, 0, t...]
    all_to_all x6 -> x4, starting transfers between devices: 41.1 us -> 23.9 us  [the longest x1 9.43 us: shards(): lax.all_to_all(jnp.concatenate([proj_blk, dprod_blk, rows_sent], axis=1),...]
    all_to_all x6 -> x4, waiting for transfers between devices: 31.5 us -> 39.9 us  [the longest x1 18.5 us: shards(): lax.all_to_all(jnp.concatenate([proj_blk, dprod_blk, rows_sent], axis=1),...]
    unnamed x37 -> x66, local copies, waits for them, and re-layouts: 8.79 us -> 5.42 us
  transfers between devices with their start and end apart: 7 -> 4, of which waited for: 5 -> 4; matrix products, arithmetic and copies ran while one was open for 3% -> 4% of each run, Pallas kernels for 0% -> 0%
where the time goes in v3:
time: 143 us; the launch traced here: 142 us
  waiting for transfers between devices  39.9 us (28%)
  matrix products  28.1 us (20%)
  starting transfers between devices  23.9 us (17%)
  blocking collectives  22.4 us (16%)
  local copies, waits for them, and re-layouts  14.5 us (10%)
  other arithmetic  12.1 us (8%)
  between operations  1.48 us (1%)
    all_to_all x1, waiting for transfers between devices, shards(): lax.all_to_all(jnp.concatenate([proj_blk, dprod_blk, rows_sent], axis=1),...  18.5 us
    all_to_all x1, blocking collectives, shards(): lax.all_to_all(jnp.concatenate([params, fg_sent], axis=1), 'seq', 0, 0, t...  12.9 us
    all_to_all x1, waiting for transfers between devices, shards(): lax.all_to_all(jnp.concatenate([prod_sent, dp_sent], axis=1), 'seq', 0, 0...  10 us
    all_to_all x1, blocking collectives, shards(): lax.all_to_all(jnp.concatenate([p_part, f_part], axis=1), 'dp', 0, 0, til...  9.44 us
    all_to_all x1, starting transfers between devices, shards(): lax.all_to_all(jnp.concatenate([proj_blk, dprod_blk, rows_sent], axis=1),...  9.43 us
    dot_general x5, matrix products, spectrum(): return jnp.einsum('kcm,mj->kcj', cat, tab['fwd2'], precision=HIGHEST)  8.21 us
    all_to_all x1, waiting for transfers between devices, shards(): lax.all_to_all(jnp.broadcast_to(p_seq, (seq_n, dp_n * chunk)), 'seq', 0,...  7.23 us
    all_to_all x1, starting transfers between devices, shards(): lax.all_to_all(jnp.broadcast_to(p_seq, (seq_n, dp_n * chunk)), 'seq', 0,...  6.9 us
  transfers between devices with their start and end apart: 4, of which 4 were waited for; matrix products, arithmetic and copies ran while one was open for 4% of the time, Pallas kernels for 0%

profile of v3, /device:TPU:1, one launch (start us, length us, event | category | flops | bytes accessed | tf_op | source)
XLA Modules:
  0.0 142.3 jit_solution(14638630823367992940)
XLA Ops:
  0.7 1.0 copy.148
  2.9 1.2 pad_maximum_fusion
  4.1 9.4 %all-to-all-start = ((f32[16,34,512]{2,1,0:T(8,128)}), f32[16,34,512]{2,1,0:T(8,128)S(1)}, u32[]{:S(2)}, u32[]{:S(2)}) async-start(f32[16,34,512]{2,1,0:T(8,128)} %pad_maximum_fusion), calls=%async_computation | async-start | bytes 2621440 | tf_op jit(solution)/shard_map/all_to_all | solution.py:101
  15.2 18.5 %all-to-all-done = f32[16,34,512]{2,1,0:T(8,128)S(1)} async-done(((f32[16,34,512]{2,1,0:T(8,128)}), f32[16,34,512]{2,1,0:T(8,128)S(1)}, u32[]{:S(2)}, u32[]{:S(2)}) %all-to-all-start) | async-done | bytes 1114144 | tf_op jit(solution)/shard_map/all_to_all | solution.py:101
  33.7 1.1 slice_bitcast_fusion.1
  35.7 2.0 %fusion.63 = f32[256,8,128]{0,2,1:T(8,128)} fusion(f32[256,64,1]{0,1,2:T(8,128)S(1)} %copy-done.15, f32[64,24,128]{2,0,1:T(8,128)S(1)} %bitcast.169), kind=kOutput, calls=%fused_computation.131 | convolution fusion | flops 201326592 | bytes 1376256 | tf_op jit(solution)/shard_map/kn,ncm->kcm/dot_general | solution.py:40
  37.8 2.0 %fusion.97 = f32[256,8,128]{0,2,1:T(8,128)} fusion(f32[256,64,1]{0,1,2:T(8,128)S(1)} %copy-done.15, f32[64,24,128]{2,0,1:T(8,128)S(1)} %bitcast.170, f32[64,8,128]{2,1,0:T(8,128)S(1)} %bitcast.181), kind=kOutput, calls=%fused_computation.195 | convolution fusion | flops 201392128 | bytes 1638400 | tf_op jit(solution)/shard_map/kn,ncm->kcm/dot_general | solution.py:40
  40.3 1.4 multiply_subtract_fusion.7
  42.4 1.8 %fusion.24 = f32[128,8,256]{2,0,1:T(8,128)S(1)} fusion(f32[256,256,1]{1,0,2:T(8,128)S(1)} %copy-done.2, f32[128,8,128]{0,2,1:T(8,128)S(1)} %get-tuple-element.37, f32[128,8,128]{0,2,1:T(8,128)S(1)} %get-tuple-element.36), kind=kOutput, calls=%fused_computation.35 | convolution fusion | flops 805568512 | bytes 2359296 | tf_op jit(solution)/shard_map/kcm,mj->kcj/dot_general | solution.py:44
  45.2 1.1 fusion.28
  47.1 1.1 convolution_add_fusion.1
  49.6 1.9 %fusion.2 = f32[128,8,256]{2,0,1:T(8,128)S(1)} fusion(f32[256,256,1]{1,0,2:T(8,128)S(1)} %copy-done.2, f32[128,8,128]{0,2,1:T(8,128)S(1)} %get-tuple-element.73, f32[128,8,128]{0,2,1:T(8,128)S(1)} %get-tuple-element.74), kind=kOutput, calls=%fused_computation.13 | convolution fusion | flops 805568512 | bytes 2359296 | tf_op jit(solution)/shard_map/kcm,mj->kcj/dot_general | solution.py:44
  51.4 2.1 %fusion.35 = f32[128,8,256]{2,0,1:T(8,128)S(1)} fusion(f32[256,256,1]{1,0,2:T(8,128)S(1)} %copy-done.2, f32[128,8,128]{0,2,1:T(8,128)S(1)} %get-tuple-element.31, f32[128,8,128]{0,2,1:T(8,128)S(1)} %get-tuple-element.30), kind=kOutput, calls=%fused_computation.46 | convolution fusion | flops 805568512 | bytes 2359296 | tf_op jit(solution)/shard_map/kcm,mj->kcj/dot_general | solution.py:44
  53.5 1.3 multiply_subtract_fusion.1
  54.8 1.1 fusion.6
  55.9 1.1 fusion.39
  57.3 1.1 convolution_add_fusion.3
  59.6 1.9 %fusion.13 = f32[128,8,256]{2,0,1:T(8,128)S(1)} fusion(f32[256,256,1]{1,0,2:T(8,128)S(1)} %copy-done.2, f32[128,8,128]{0,2,1:T(8,128)S(1)} %get-tuple-element.43, f32[128,8,128]{0,2,1:T(8,128)S(1)} %get-tuple-element.42), kind=kOutput, calls=%fused_computation.24 | convolution fusion | flops 805568512 | bytes 2359296 | tf_op jit(solution)/shard_map/kcm,mj->kcj/dot_general | solution.py:44
  61.5 1.2 multiply_subtract_fusion
  62.7 1.1 fusion.17
  63.9 1.1 convolution_add_fusion
  65.1 1.9 %multiply_reduce_fusion.3 = (f32[8]{0:T(128)S(1)}, f32[8]{0:T(128)S(1)}, bf16[64,8,128]{2,0,1:T(8,128)(2,1)}, f32[64,8,128]{2,0,1:T(8,128)S(1)}, f32[64,8,128]{2,0,1:T(8,128)S(1)}) fusion(f32[64,24,128]{2,0,1:T(8,128)S(1)} %bitcast.176, f32[64,8,128]{2,0,1:T(8,128)S(1)} %convolution_add_fusion.1, f32[64,8,128]{2,0,1:T(8,128)S(1)} %convolution_add_fusion.3, ...), kind=kOutput, calls=%fused_computation.125 | convolution fusion | flops 202440688 | bytes 3342432 | tf_op jit(solution)/shard_map/nk,kcm->ncm/dot_general | solution.py:52
  69.1 1.2 fusion.51
  71.5 1.1 copy.172
  72.6 4.2 %all-to-all-start.1 = ((bf16[16,32,512]{2,1,0:T(8,128)(2,1)}), bf16[16,32,512]{2,1,0:T(8,128)(2,1)S(1)}, u32[]{:S(2)}, u32[]{:S(2)}) async-start(bf16[16,32,512]{2,1,0:T(8,128)(2,1)} %copy.172), calls=%async_computation.1 | async-start | bytes 1048576 | tf_op jit(solution)/shard_map/all_to_all | solution.py:161
  78.2 10.0 %all-to-all-done.1 = bf16[16,32,512]{2,1,0:T(8,128)(2,1)S(1)} async-done(((bf16[16,32,512]{2,1,0:T(8,128)(2,1)}), bf16[16,32,512]{2,1,0:T(8,128)(2,1)S(1)}, u32[]{:S(2)}, u32[]{:S(2)}) %all-to-all-start.1) | async-done | bytes 524320 | tf_op jit(solution)/shard_map/all_to_all | solution.py:161
  90.0 12.9 %all_to_all.46 = f32[16,1,5216]{2,1,0:T(1,128)S(1)} all-to-all(f32[16,1,5216]{2,1,0:T(1,128)S(1)} %all_to_all.32), channel_id=1, replica_groups=mesh['dp'=8,'seq'=16] {'seq'}, dimensions={0} | all-to-all | bytes 667648 | tf_op jit(solution)/shard_map/all_to_all | solution.py:190
  103.4 9.4 %all_to_all.47 = f32[8,1,1548]{2,1,0:T(1,128)S(1)} all-to-all(f32[8,1,1548]{2,1,0:T(1,128)S(1)} %all_to_all.35), channel_id=1, replica_groups=mesh['dp'=8,'seq'=16] {'dp'}, dimensions={0} | all-to-all | bytes 99072 | tf_op jit(solution)/shard_map/all_to_all | solution.py:193
  113.5 3.3 %all-to-all-start.4 = ((f32[8,1,1548]{2,1,0:T(1,128)}), f32[8,1,1548]{2,1,0:T(1,128)S(1)}, u32[]{:S(2)}, u32[]{:S(2)}) async-start(f32[8,1,1548]{2,1,0:T(1,128)} %broadcast_in_dim.30), calls=%async_computation.4 | async-start | bytes 106496 | tf_op jit(solution)/shard_map/all_to_all | solution.py:195
  117.8 4.1 %all-to-all-done.4 = f32[8,1,1548]{2,1,0:T(1,128)S(1)} async-done(((f32[8,1,1548]{2,1,0:T(1,128)}), f32[8,1,1548]{2,1,0:T(1,128)S(1)}, u32[]{:S(2)}, u32[]{:S(2)}) %all-to-all-start.4) | async-done | bytes 49568 | tf_op jit(solution)/shard_map/all_to_all | solution.py:195
  122.9 6.9 %all-to-all-start.5 = ((f32[16,1,4192]{2,1,0:T(1,128)}), f32[16,1,4192]{2,1,0:T(1,128)S(1)}, u32[]{:S(2)}, u32[]{:S(2)}) async-start(f32[16,1,4192]{2,1,0:T(1,128)} %broadcast_in_dim.32), calls=%async_computation.5 | async-start | bytes 540672 | tf_op jit(solution)/shard_map/all_to_all | solution.py:198
  131.4 7.2 %all-to-all-done.5 = f32[16,1,4192]{2,1,0:T(1,128)S(1)} async-done(((f32[16,1,4192]{2,1,0:T(1,128)}), f32[16,1,4192]{2,1,0:T(1,128)S(1)}, u32[]{:S(2)}, u32[]{:S(2)}) %all-to-all-start.5) | async-done | bytes 268320 | tf_op jit(solution)/shard_map/all_to_all | solution.py:198
  (157 shorter events, 23.8 us)
Async XLA Ops:
  0.6 1.1 copy-start
  1.7 0.7 copy-start.22
  1.7 0.7 copy-start.23
  1.7 0.9 copy-start.17
  1.8 0.9 copy-start.20
  4.1 9.4 %copy-start.24 = (f32[3,384]{1,0:T(4,128)S(1)}, f32[3,384]{1,0:T(4,128)}, u32[]{:S(2)}) copy-start(f32[3,384]{1,0:T(4,128)} %param.19) | copy-start | bytes 13828
  4.1 9.8 %copy-start.26 = (f32[128]{0:T(128)S(1)}, f32[128]{0:T(128)}, u32[]{:S(2)}) copy-start(f32[128]{0:T(128)} %param.20) | copy-start | bytes 1540
  4.1 9.9 %copy-start.27 = (f32[128]{0:T(128)S(1)}, f32[128]{0:T(128)}, u32[]{:S(2)}) copy-start(f32[128]{0:T(128)} %param.21) | copy-start | bytes 1540
  4.1 29.6 %all-to-all-start = ((f32[16,34,512]{2,1,0:T(8,128)}), f32[16,34,512]{2,1,0:T(8,128)S(1)}, u32[]{:S(2)}, u32[]{:S(2)}) async-start(f32[16,34,512]{2,1,0:T(8,128)} %pad_maximum_fusion), calls=%async_computation | async-start | bytes 2621440 | tf_op jit(solution)/shard_map/all_to_all | solution.py:101
  34.9 0.8 copy-start.15
  37.8 2.5 %copy-start.3 = (f32[128,128]{0,1:T(8,128)S(1)}, f32[128,128]{0,1:T(8,128)}, u32[]{:S(2)}) copy-start(f32[128,128]{0,1:T(8,128)} %constant.45.clone) | copy-start | bytes 196612
  37.8 2.5 %copy-start.4 = (f32[128,128]{0,1:T(8,128)S(1)}, f32[128,128]{0,1:T(8,128)}, u32[]{:S(2)}) copy-start(f32[128,128]{0,1:T(8,128)} %constant.46.clone) | copy-start | bytes 196612
  40.3 1.4 %copy-start.2 = (f32[256,256,1]{1,0,2:T(8,128)S(1)}, f32[256,256,1]{1,0,2:T(8,128)}, u32[]{:S(2)}) copy-start(f32[256,256,1]{1,0,2:T(8,128)} %constant.59) | copy-start | bytes 786436
  44.2 1.0 copy-start.1
  46.3 0.8 copy-start.14
  46.3 0.8 copy-start.25
  47.1 2.2 %copy-start.5 = (f32[256,8,128]{0,2,1:T(8,128)S(1)}, f32[256,8,128]{0,2,1:T(8,128)}, u32[]{:S(2)}) copy-start(f32[256,8,128]{0,2,1:T(8,128)} %fusion.63) | copy-start | bytes 3145732
  65.1 3.1 %copy-start.9 = (f32[64,8,128]{2,0,1:T(8,128)}, f32[64,8,128]{2,0,1:T(8,128)S(1)}, u32[]{:S(2)}) copy-start(f32[64,8,128]{2,0,1:T(8,128)S(1)} %convolution_add_fusion) | copy-start | bytes 786436
  67.0 1.2 copy-start.6
  68.2 0.9 copy-start.8
  68.9 1.7 %copy-start.28 = (f32[3]{0:T(128)S(1)}, f32[3]{0:T(128)}, u32[]{:S(2)}) copy-start(f32[3]{0:T(128)} %pad.41.clone) | copy-start | bytes 40
  70.4 1.0 copy-start.16
  71.4 5.3 %copy-start.12 = (f32[128,8,128]{2,0,1:T(8,128)S(1)}, f32[128,8,128]{2,0,1:T(8,128)}, u32[]{:S(2)}) copy-start(f32[128,8,128]{2,0,1:T(8,128)} %get-tuple-element.16) | copy-start | bytes 1572868
  71.5 5.3 %copy-start.13 = (f32[128,8,128]{2,0,1:T(8,128)S(1)}, f32[128,8,128]{2,0,1:T(8,128)}, u32[]{:S(2)}) copy-start(f32[128,8,128]{2,0,1:T(8,128)} %get-tuple-element.17) | copy-start | bytes 1572868
  72.6 4.3 %copy-start.10 = (f32[128,8,128]{2,0,1:T(8,128)S(1)}, f32[128,8,128]{2,0,1:T(8,128)}, u32[]{:S(2)}) copy-start(f32[128,8,128]{2,0,1:T(8,128)} %get-tuple-element.18) | copy-start | bytes 1572868
  72.6 4.3 %copy-start.11 = (f32[128,8,128]{2,0,1:T(8,128)S(1)}, f32[128,8,128]{2,0,1:T(8,128)}, u32[]{:S(2)}) copy-start(f32[128,8,128]{2,0,1:T(8,128)} %get-tuple-element.19) | copy-start | bytes 1572868
  72.6 15.7 %all-to-all-start.1 = ((bf16[16,32,512]{2,1,0:T(8,128)(2,1)}), bf16[16,32,512]{2,1,0:T(8,128)(2,1)S(1)}, u32[]{:S(2)}, u32[]{:S(2)}) async-start(bf16[16,32,512]{2,1,0:T(8,128)(2,1)} %copy.172), calls=%async_computation.1 | async-start | bytes 1048576 | tf_op jit(solution)/shard_map/all_to_all | solution.py:161
  88.3 0.9 copy-start.18
  89.9 26.9 %copy-start.19 = (bf16[128,384]{1,0:T(8,128)(2,1)S(1)}, bf16[128,384]{1,0:T(8,128)(2,1)}, u32[]{:S(2)}) copy-start(bf16[128,384]{1,0:T(8,128)(2,1)} %param.17) | copy-start | bytes 294916
  103.0 26.8 %copy-start.21 = (bf16[128,128]{1,0:T(8,128)(2,1)S(1)}, bf16[128,128]{1,0:T(8,128)(2,1)}, u32[]{:S(2)}) copy-start(bf16[128,128]{1,0:T(8,128)(2,1)} %param.18) | copy-start | bytes 98308
  113.5 8.5 %all-to-all-start.4 = ((f32[8,1,1548]{2,1,0:T(1,128)}), f32[8,1,1548]{2,1,0:T(1,128)S(1)}, u32[]{:S(2)}, u32[]{:S(2)}) async-start(f32[8,1,1548]{2,1,0:T(1,128)} %broadcast_in_dim.30), calls=%async_computation.4 | async-start | bytes 106496 | tf_op jit(solution)/shard_map/all_to_all | solution.py:195
  122.9 15.7 %all-to-all-start.5 = ((f32[16,1,4192]{2,1,0:T(1,128)}), f32[16,1,4192]{2,1,0:T(1,128)S(1)}, u32[]{:S(2)}, u32[]{:S(2)}) async-start(f32[16,1,4192]{2,1,0:T(1,128)} %broadcast_in_dim.32), calls=%async_computation.5 | async-start | bytes 540672 | tf_op jit(solution)/shard_map/all_to_all | solution.py:198
  (1 other events, 0.7 us)

commit v4 on v3

--- a/solution.py
+++ b/solution.py
@@ -186,16 +186,19 @@
     chunk = -(-n_params // (seq_n * dp_n))
     params = jnp.pad(params, (0, chunk * seq_n * dp_n - n_params)).reshape(seq_n, dp_n * chunk)
 
-    fg_sent = jnp.swapaxes(filt_grad.reshape(2, seq_n, block), 0, 1).reshape(seq_n, 2 * block)
-    got = lax.all_to_all(jnp.concatenate([params, fg_sent], axis=1), "seq", 0, 0, tiled=True)
-    p_part = jnp.sum(got[:, : dp_n * chunk], axis=0).reshape(dp_n, chunk)
-    f_part = jnp.sum(got[:, dp_n * chunk :].reshape(filters, per_group, 2 * block), axis=1)
-    got = lax.all_to_all(jnp.concatenate([p_part, f_part], axis=1), "dp", 0, 0, tiled=True)
-    mine = jnp.sum(got, axis=0)
-    got = lax.all_to_all(jnp.broadcast_to(mine, (dp_n,) + mine.shape), "dp", 0, 0, tiled=True)
-    fg_blocks = jnp.swapaxes(got[:, chunk:].reshape(filters, 2, block), 0, 1)
-    p_seq = got[:, :chunk].reshape(1, dp_n * chunk)
-    got = lax.all_to_all(jnp.broadcast_to(p_seq, (seq_n, dp_n * chunk)), "seq", 0, 0, tiled=True)
+    fg_sent = jnp.swapaxes(filt_grad.reshape(2, seq_n, block), 0, 1)
+    got = lax.all_to_all(fg_sent, "seq", 0, 0, tiled=True)
+    f_part = jnp.sum(got.reshape(filters, per_group, 2, block), axis=1)
+    params = params.reshape(seq_n * dp_n, chunk)
+    got = lax.all_to_all(params, ("dp", "seq"), 0, 0, tiled=True)
+    p_mine = jnp.sum(got, axis=0, keepdims=True)
+    got = lax.all_to_all(f_part, "dp", 0, 0, tiled=True)
+    f_mine = jnp.sum(got, axis=0, keepdims=True)
+    got = lax.all_to_all(jnp.broadcast_to(f_mine, (dp_n,) + f_mine.shape[1:]), "dp", 0, 0, tiled=True)
+    fg_blocks = jnp.swapaxes(got, 0, 1)
+    got = lax.all_to_all(
+        jnp.broadcast_to(p_mine, (seq_n * dp_n, chunk)), ("dp", "seq"), 0, 0, tiled=True
+    )
     full = got.reshape(-1)
     sizes = [width * 3 * width, width * width, 3 * 4 * width]
     offsets = np.cumsum([0] + sizes)

time: 143 us -> 154 us (1.077)
  blocking collectives: 22.4 us -> 0 us
  waiting for transfers between devices: 39.9 us -> 61.4 us
  starting transfers between devices: 23.9 us -> 36.4 us
  other arithmetic: 12.1 us -> 9.83 us
  local copies, waits for them, and re-layouts: 14.5 us -> 16.5 us
    all_to_all x2 -> x0, blocking collectives: 22.4 us -> none  [the longest x1 12.9 us: shards(): lax.all_to_all(jnp.concatenate([params, fg_sent], axis=1), 'seq', 0, 0, t...]
    all_to_all x2 -> x5, waiting for transfers between devices: 11.4 us -> 31.8 us  [the longest x1 11.6 us: shards(): got = lax.all_to_all(params, ('dp', 'seq'), 0, 0, tiled=True)]
    all_to_all x2 -> x5, starting transfers between devices: 10.2 us -> 23.2 us  [the longest x1 5.89 us: shards(): got = lax.all_to_all(params, ('dp', 'seq'), 0, 0, tiled=True)]
    sub x3, other arithmetic: 2.7 us -> 0.92 us  [cmul(): return jnp.concatenate([ar * br - ai * bi, ar * bi + ai * br], axis=-1)]
    unnamed x66 -> x43, local copies, waits for them, and re-layouts: 5.42 us -> 7.19 us
  transfers between devices with their start and end apart: 4 -> 7, of which waited for: 4 -> 7; matrix products, arithmetic and copies ran while one was open for 4% -> 5% of each run, Pallas kernels for 0% -> 0%
where the time goes in v4:
time: 154 us; the launch traced here: 153 us
  waiting for transfers between devices  61.4 us (40%)
  starting transfers between devices  36.4 us (24%)
  matrix products  27.5 us (18%)
  local copies, waits for them, and re-layouts  16.5 us (11%)
  other arithmetic  9.83 us (6%)
    all_to_all x1, waiting for transfers between devices, shards(): lax.all_to_all(jnp.concatenate([proj_blk, dprod_blk, rows_sent], axis=1),...  19.5 us
    all_to_all x1, waiting for transfers between devices, shards(): got = lax.all_to_all(params, ('dp', 'seq'), 0, 0, tiled=True)  11.6 us
    all_to_all x1, waiting for transfers between devices, shards(): lax.all_to_all(jnp.concatenate([prod_sent, dp_sent], axis=1), 'seq', 0, 0...  10.1 us
    all_to_all x1, starting transfers between devices, shards(): lax.all_to_all(jnp.concatenate([proj_blk, dprod_blk, rows_sent], axis=1),...  9.43 us
    all_to_all x1, waiting for transfers between devices, shards(): lax.all_to_all(jnp.broadcast_to(p_mine, (seq_n * dp_n, chunk)), ('dp', 's...  8.45 us
    dot_general x5, matrix products, spectrum(): return jnp.einsum('kcm,mj->kcj', cat, tab['fwd2'], precision=HIGHEST)  8.2 us
    unnamed x43, local copies, waits for them, and re-layouts  7.19 us
    dot_general x5, matrix products, spectrum(): a = jnp.einsum('kn,ncm->kcm', tab['fwd1'], x, precision=HIGHEST)  6.53 us
  transfers between devices with their start and end apart: 7, of which 7 were waited for; matrix products, arithmetic and copies ran while one was open for 5% of the time, Pallas kernels for 0%

profile of v4, /device:TPU:1, one launch (start us, length us, event | category | flops | bytes accessed | tf_op | source)
XLA Modules:
  0.0 152.9 jit_solution(15996526655721829198)
XLA Ops:
  2.9 1.2 pad_maximum_fusion
  4.1 9.4 %all-to-all-start = ((f32[16,34,512]{2,1,0:T(8,128)}), f32[16,34,512]{2,1,0:T(8,128)S(1)}, u32[]{:S(2)}, u32[]{:S(2)}) async-start(f32[16,34,512]{2,1,0:T(8,128)} %pad_maximum_fusion), calls=%async_computation | async-start | bytes 2621440 | tf_op jit(solution)/shard_map/all_to_all | solution.py:101
  14.2 19.5 %all-to-all-done = f32[16,34,512]{2,1,0:T(8,128)S(1)} async-done(((f32[16,34,512]{2,1,0:T(8,128)}), f32[16,34,512]{2,1,0:T(8,128)S(1)}, u32[]{:S(2)}, u32[]{:S(2)}) %all-to-all-start) | async-done | bytes 1114144 | tf_op jit(solution)/shard_map/all_to_all | solution.py:101
  35.7 2.0 %fusion.63 = f32[256,8,128]{0,2,1:T(8,128)} fusion(f32[256,64,1]{0,1,2:T(8,128)S(1)} %copy-done.8, f32[64,24,128]{2,0,1:T(8,128)S(1)} %bitcast.165), kind=kOutput, calls=%fused_computation.128 | convolution fusion | flops 201326592 | bytes 1376256 | tf_op jit(solution)/shard_map/kn,ncm->kcm/dot_general | solution.py:40
  37.8 2.0 %fusion.95 = f32[256,8,128]{0,2,1:T(8,128)} fusion(f32[256,64,1]{0,1,2:T(8,128)S(1)} %copy-done.8, f32[64,24,128]{2,0,1:T(8,128)S(1)} %bitcast.166, f32[64,8,128]{2,1,0:T(8,128)S(1)} %bitcast.177), kind=kOutput, calls=%fused_computation.192 | convolution fusion | flops 201392128 | bytes 1638400 | tf_op jit(solution)/shard_map/kn,ncm->kcm/dot_general | solution.py:40
  40.3 1.4 multiply_subtract_fusion.7
  42.4 1.8 %fusion.24 = f32[128,8,256]{2,0,1:T(8,128)S(1)} fusion(f32[256,256,1]{1,0,2:T(8,128)S(1)} %copy-done.2, f32[128,8,128]{0,2,1:T(8,128)S(1)} %get-tuple-element.37, f32[128,8,128]{0,2,1:T(8,128)S(1)} %get-tuple-element.36), kind=kOutput, calls=%fused_computation.35 | convolution fusion | flops 805568512 | bytes 2359296 | tf_op jit(solution)/shard_map/kcm,mj->kcj/dot_general | solution.py:44
  45.2 1.1 fusion.28
  47.2 1.1 convolution_add_fusion.1
  49.6 1.9 %fusion.2 = f32[128,8,256]{2,0,1:T(8,128)S(1)} fusion(f32[256,256,1]{1,0,2:T(8,128)S(1)} %copy-done.2, f32[128,8,128]{0,2,1:T(8,128)S(1)} %get-tuple-element.73, f32[128,8,128]{0,2,1:T(8,128)S(1)} %get-tuple-element.74), kind=kOutput, calls=%fused_computation.13 | convolution fusion | flops 805568512 | bytes 2359296 | tf_op jit(solution)/shard_map/kcm,mj->kcj/dot_general | solution.py:44
  51.5 2.1 %fusion.35 = f32[128,8,256]{2,0,1:T(8,128)S(1)} fusion(f32[256,256,1]{1,0,2:T(8,128)S(1)} %copy-done.2, f32[128,8,128]{0,2,1:T(8,128)S(1)} %get-tuple-element.31, f32[128,8,128]{0,2,1:T(8,128)S(1)} %get-tuple-element.30), kind=kOutput, calls=%fused_computation.46 | convolution fusion | flops 805568512 | bytes 2359296 | tf_op jit(solution)/shard_map/kcm,mj->kcj/dot_general | solution.py:44
  54.0 1.1 fusion.6
  55.1 1.1 fusion.39
  56.5 1.1 convolution_add_fusion.3
  58.8 1.9 %fusion.13 = f32[128,8,256]{2,0,1:T(8,128)S(1)} fusion(f32[256,256,1]{1,0,2:T(8,128)S(1)} %copy-done.2, f32[128,8,128]{0,2,1:T(8,128)S(1)} %get-tuple-element.43, f32[128,8,128]{0,2,1:T(8,128)S(1)} %get-tuple-element.42), kind=kOutput, calls=%fused_computation.24 | convolution fusion | flops 805568512 | bytes 2359296 | tf_op jit(solution)/shard_map/kcm,mj->kcj/dot_general | solution.py:44
  61.0 1.1 fusion.17
  62.3 1.1 convolution_add_fusion
  63.4 1.2 multiply_reduce_fusion.3
  67.9 4.0 %all-to-all-start.4 = ((f32[16,2,512]{2,1,0:T(2,128)}), f32[16,2,512]{2,1,0:T(2,128)S(1)}, u32[]{:S(2)}, u32[]{:S(2)}) async-start(f32[16,2,512]{2,1,0:T(2,128)} %bitcast.161), calls=%async_computation.4 | async-start | bytes 131072 | tf_op jit(solution)/shard_map/all_to_all | solution.py:190
  74.0 1.1 copy.208
  75.1 4.2 %all-to-all-done.4 = f32[16,2,512]{2,1,0:T(2,128)S(1)} async-done(((f32[16,2,512]{2,1,0:T(2,128)}), f32[16,2,512]{2,1,0:T(2,128)S(1)}, u32[]{:S(2)}, u32[]{:S(2)}) %all-to-all-start.4) | async-done | bytes 65568 | tf_op jit(solution)/shard_map/all_to_all | solution.py:190
  79.3 3.8 %all-to-all-start.1 = ((bf16[16,32,512]{2,1,0:T(8,128)(2,1)}), bf16[16,32,512]{2,1,0:T(8,128)(2,1)S(1)}, u32[]{:S(2)}, u32[]{:S(2)}) async-start(bf16[16,32,512]{2,1,0:T(8,128)(2,1)} %copy.208), calls=%async_computation.1 | async-start | bytes 1048576 | tf_op jit(solution)/shard_map/all_to_all | solution.py:161
  84.5 10.1 %all-to-all-done.1 = bf16[16,32,512]{2,1,0:T(8,128)(2,1)S(1)} async-done(((bf16[16,32,512]{2,1,0:T(8,128)(2,1)}), bf16[16,32,512]{2,1,0:T(8,128)(2,1)S(1)}, u32[]{:S(2)}, u32[]{:S(2)}) %all-to-all-start.1) | async-done | bytes 524320 | tf_op jit(solution)/shard_map/all_to_all | solution.py:161
  94.5 4.5 %all-to-all-start.5 = ((f32[8,2,512]{2,1,0:T(2,128)}), f32[8,2,512]{2,1,0:T(2,128)S(1)}, u32[]{:S(2)}, u32[]{:S(2)}) async-start(f32[8,2,512]{2,1,0:T(2,128)} %bitcast_reduce_fusion), calls=%async_computation.5 | async-start | bytes 65536 | tf_op jit(solution)/shard_map/all_to_all | solution.py:195
  100.2 1.2 all_to_all.33
  101.4 2.8 %all-to-all-done.5 = f32[8,2,512]{2,1,0:T(2,128)S(1)} async-done(((f32[8,2,512]{2,1,0:T(2,128)}), f32[8,2,512]{2,1,0:T(2,128)S(1)}, u32[]{:S(2)}, u32[]{:S(2)}) %all-to-all-start.5) | async-done | bytes 32800 | tf_op jit(solution)/shard_map/all_to_all | solution.py:195
  104.1 5.9 %all-to-all-start.2 = ((f32[128,1,524]{2,1,0:T(1,128)}), f32[128,1,524]{2,1,0:T(1,128)S(1)}, u32[]{:S(2)}, u32[]{:S(2)}) async-start(f32[128,1,524]{2,1,0:T(1,128)} %all_to_all.33), calls=%async_computation.2 | async-start | bytes 655360 | tf_op jit(solution)/shard_map/all_to_all | solution.py:193
  110.1 11.6 %all-to-all-done.2 = f32[128,1,524]{2,1,0:T(1,128)S(1)} async-done(((f32[128,1,524]{2,1,0:T(1,128)}), f32[128,1,524]{2,1,0:T(1,128)S(1)}, u32[]{:S(2)}, u32[]{:S(2)}) %all-to-all-start.2) | async-done | bytes 268320 | tf_op jit(solution)/shard_map/all_to_all | solution.py:193
  122.3 3.3 %all-to-all-start.6 = ((f32[8,2,512]{2,1,0:T(2,128)}), f32[8,2,512]{2,1,0:T(2,128)S(1)}, u32[]{:S(2)}, u32[]{:S(2)}) async-start(f32[8,2,512]{2,1,0:T(2,128)} %broadcast_in_dim.33), calls=%async_computation.6 | async-start | bytes 65536 | tf_op jit(solution)/shard_map/all_to_all | solution.py:197
  125.9 4.8 %all-to-all-done.6 = f32[8,2,512]{2,1,0:T(2,128)S(1)} async-done(((f32[8,2,512]{2,1,0:T(2,128)}), f32[8,2,512]{2,1,0:T(2,128)S(1)}, u32[]{:S(2)}, u32[]{:S(2)}) %all-to-all-start.6) | async-done | bytes 32800 | tf_op jit(solution)/shard_map/all_to_all | solution.py:197
  131.6 5.5 %all-to-all-start.3 = ((f32[128,1,524]{2,1,0:T(1,128)}), f32[128,1,524]{2,1,0:T(1,128)S(1)}, u32[]{:S(2)}, u32[]{:S(2)}) async-start(f32[128,1,524]{2,1,0:T(1,128)} %broadcast_in_dim.14), calls=%async_computation.3 | async-start | bytes 655360 | tf_op jit(solution)/shard_map/all_to_all | solution.py:199
  140.2 8.4 %all-to-all-done.3 = f32[128,1,524]{2,1,0:T(1,128)S(1)} async-done(((f32[128,1,524]{2,1,0:T(1,128)}), f32[128,1,524]{2,1,0:T(1,128)S(1)}, u32[]{:S(2)}, u32[]{:S(2)}) %all-to-all-start.3) | async-done | bytes 268320 | tf_op jit(solution)/shard_map/all_to_all | solution.py:199
  (128 shorter events, 28.2 us)
Async XLA Ops:
  0.6 1.1 copy-start
  1.7 0.7 copy-start.13
  1.7 0.7 copy-start.14
  1.7 0.9 copy-start.9
  1.8 0.9 copy-start.12
  4.1 9.4 %copy-start.15 = (f32[3,384]{1,0:T(4,128)S(1)}, f32[3,384]{1,0:T(4,128)}, u32[]{:S(2)}) copy-start(f32[3,384]{1,0:T(4,128)} %param.19) | copy-start | bytes 13828
  4.1 9.8 %copy-start.16 = (f32[128]{0:T(128)S(1)}, f32[128]{0:T(128)}, u32[]{:S(2)}) copy-start(f32[128]{0:T(128)} %param.20) | copy-start | bytes 1540
  4.1 9.9 %copy-start.17 = (f32[128]{0:T(128)S(1)}, f32[128]{0:T(128)}, u32[]{:S(2)}) copy-start(f32[128]{0:T(128)} %param.21) | copy-start | bytes 1540
  4.1 29.6 %all-to-all-start = ((f32[16,34,512]{2,1,0:T(8,128)}), f32[16,34,512]{2,1,0:T(8,128)S(1)}, u32[]{:S(2)}, u32[]{:S(2)}) async-start(f32[16,34,512]{2,1,0:T(8,128)} %pad_maximum_fusion), calls=%async_computation | async-start | bytes 2621440 | tf_op jit(solution)/shard_map/all_to_all | solution.py:101
  34.9 0.8 copy-start.8
  37.8 2.6 %copy-start.3 = (f32[128,128]{0,1:T(8,128)S(1)}, f32[128,128]{0,1:T(8,128)}, u32[]{:S(2)}) copy-start(f32[128,128]{0,1:T(8,128)} %constant.45.clone) | copy-start | bytes 196612
  37.8 2.6 %copy-start.4 = (f32[128,128]{0,1:T(8,128)S(1)}, f32[128,128]{0,1:T(8,128)}, u32[]{:S(2)}) copy-start(f32[128,128]{0,1:T(8,128)} %constant.46.clone) | copy-start | bytes 196612
  40.3 1.4 copy-start.2
  44.3 1.0 copy-start.1
  46.3 0.8 copy-start.7
  47.2 2.2 %copy-start.5 = (f32[256,8,128]{0,2,1:T(8,128)S(1)}, f32[256,8,128]{0,2,1:T(8,128)}, u32[]{:S(2)}) copy-start(f32[256,8,128]{0,2,1:T(8,128)} %fusion.63) | copy-start | bytes 3145732
  67.9 11.4 %all-to-all-start.4 = ((f32[16,2,512]{2,1,0:T(2,128)}), f32[16,2,512]{2,1,0:T(2,128)S(1)}, u32[]{:S(2)}, u32[]{:S(2)}) async-start(f32[16,2,512]{2,1,0:T(2,128)} %bitcast.161), calls=%async_computation.4 | async-start | bytes 131072 | tf_op jit(solution)/shard_map/all_to_all | solution.py:190
  72.4 1.1 copy-start.6
  79.3 15.2 %all-to-all-start.1 = ((bf16[16,32,512]{2,1,0:T(8,128)(2,1)}), bf16[16,32,512]{2,1,0:T(8,128)(2,1)S(1)}, u32[]{:S(2)}, u32[]{:S(2)}) async-start(bf16[16,32,512]{2,1,0:T(8,128)(2,1)} %copy.208), calls=%async_computation.1 | async-start | bytes 1048576 | tf_op jit(solution)/shard_map/all_to_all | solution.py:161
  94.5 9.6 %all-to-all-start.5 = ((f32[8,2,512]{2,1,0:T(2,128)}), f32[8,2,512]{2,1,0:T(2,128)S(1)}, u32[]{:S(2)}, u32[]{:S(2)}) async-start(f32[8,2,512]{2,1,0:T(2,128)} %bitcast_reduce_fusion), calls=%async_computation.5 | async-start | bytes 65536 | tf_op jit(solution)/shard_map/all_to_all | solution.py:195
  99.1 0.9 copy-start.10
  101.4 37.9 %copy-start.11 = (bf16[128,384]{1,0:T(8,128)(2,1)S(1)}, bf16[128,384]{1,0:T(8,128)(2,1)}, u32[]{:S(2)}) copy-start(bf16[128,384]{1,0:T(8,128)(2,1)} %param.17) | copy-start | bytes 294916
  104.1 17.6 %all-to-all-start.2 = ((f32[128,1,524]{2,1,0:T(1,128)}), f32[128,1,524]{2,1,0:T(1,128)S(1)}, u32[]{:S(2)}, u32[]{:S(2)}) async-start(f32[128,1,524]{2,1,0:T(1,128)} %all_to_all.33), calls=%async_computation.2 | async-start | bytes 655360 | tf_op jit(solution)/shard_map/all_to_all | solution.py:193
  122.3 8.4 %all-to-all-start.6 = ((f32[8,2,512]{2,1,0:T(2,128)}), f32[8,2,512]{2,1,0:T(2,128)S(1)}, u32[]{:S(2)}, u32[]{:S(2)}) async-start(f32[8,2,512]{2,1,0:T(2,128)} %broadcast_in_dim.33), calls=%async_computation.6 | async-start | bytes 65536 | tf_op jit(solution)/shard_map/all_to_all | solution.py:197
  131.6 17.0 %all-to-all-start.3 = ((f32[128,1,524]{2,1,0:T(1,128)}), f32[128,1,524]{2,1,0:T(1,128)S(1)}, u32[]{:S(2)}, u32[]{:S(2)}) async-start(f32[128,1,524]{2,1,0:T(1,128)} %broadcast_in_dim.14), calls=%async_computation.3 | async-start | bytes 655360 | tf_op jit(solution)/shard_map/all_to_all | solution.py:199

commit v5 on v3

--- a/solution.py
+++ b/solution.py
@@ -7,7 +7,7 @@
 from jax import lax
 from jax.sharding import PartitionSpec as P
 
-HIGHEST = lax.Precision.HIGHEST
+PRECISION = lax.Precision.HIGH
 LANES = 128
 
 
@@ -37,19 +37,19 @@
 
 def spectrum(x, tab):
     rows = tab["rows"]
-    a = jnp.einsum("kn,ncm->kcm", tab["fwd1"], x, precision=HIGHEST)
+    a = jnp.einsum("kn,ncm->kcm", tab["fwd1"], x, precision=PRECISION)
     ar, ai = a[:rows], a[rows:]
     tr, ti = tab["turn_r"], tab["turn_i"]
     cat = jnp.concatenate([ar * tr - ai * ti, ar * ti + ai * tr], axis=-1)
-    return jnp.einsum("kcm,mj->kcj", cat, tab["fwd2"], precision=HIGHEST)
+    return jnp.einsum("kcm,mj->kcj", cat, tab["fwd2"], precision=PRECISION)
 
 
 def signal(s, tab):
-    b = jnp.einsum("kcj,jm->kcm", s, tab["inv2"], precision=HIGHEST)
+    b = jnp.einsum("kcj,jm->kcm", s, tab["inv2"], precision=PRECISION)
     br, bi = b[..., :LANES], b[..., LANES:]
     tr, ti = tab["turn_r"], tab["turn_i"]
     stacked = jnp.concatenate([br * tr + bi * ti, bi * tr - br * ti], axis=0)
-    return jnp.einsum("nk,kcm->ncm", tab["inv1"], stacked, precision=HIGHEST)
+    return jnp.einsum("nk,kcm->ncm", tab["inv1"], stacked, precision=PRECISION)
 
 
 def cmul(a, b, conj=False):

time: 143 us -> 134 us (0.937)
  matrix products: 28.1 us -> 18.4 us
    dot_general x20, matrix products: 25.4 us -> 15.7 us  [the longest x5 4.78 us: spectrum(): a = jnp.einsum('kn,ncm->kcm', tab['fwd1'], x, precision=PRECISION)]
where the time goes in v5:
time: 134 us; the launch traced here: 133 us
  waiting for transfers between devices  40.2 us (30%)
  starting transfers between devices  23.9 us (18%)
  blocking collectives  22.4 us (17%)
  matrix products  18.4 us (14%)
  local copies, waits for them, and re-layouts  14.5 us (11%)
  other arithmetic  12.3 us (9%)
  between operations  1.48 us (1%)
    all_to_all x1, waiting for transfers between devices, shards(): lax.all_to_all(jnp.concatenate([proj_blk, dprod_blk, rows_sent], axis=1),...  18.5 us
    all_to_all x1, blocking collectives, shards(): lax.all_to_all(jnp.concatenate([params, fg_sent], axis=1), 'seq', 0, 0, t...  12.9 us
    all_to_all x1, waiting for transfers between devices, shards(): lax.all_to_all(jnp.concatenate([prod_sent, dp_sent], axis=1), 'seq', 0, 0...  10.3 us
    all_to_all x1, blocking collectives, shards(): lax.all_to_all(jnp.concatenate([p_part, f_part], axis=1), 'dp', 0, 0, til...  9.45 us
    all_to_all x1, starting transfers between devices, shards(): lax.all_to_all(jnp.concatenate([proj_blk, dprod_blk, rows_sent], axis=1),...  9.43 us
    all_to_all x1, waiting for transfers between devices, shards(): lax.all_to_all(jnp.broadcast_to(p_seq, (seq_n, dp_n * chunk)), 'seq', 0,...  7.23 us
    all_to_all x1, starting transfers between devices, shards(): lax.all_to_all(jnp.broadcast_to(p_seq, (seq_n, dp_n * chunk)), 'seq', 0,...  6.9 us
    unnamed x66, local copies, waits for them, and re-layouts  5.65 us
  transfers between devices with their start and end apart: 4, of which 4 were waited for; matrix products, arithmetic and copies ran while one was open for 4% of the time, Pallas kernels for 0%

profile of v5, /device:TPU:1, one launch (start us, length us, event | category | flops | bytes accessed | tf_op | source)
XLA Modules:
  0.0 133.1 jit_solution(18098470641968106432)
XLA Ops:
  0.7 1.0 copy.148
  2.9 1.2 pad_maximum_fusion
  4.1 9.4 %all-to-all-start = ((f32[16,34,512]{2,1,0:T(8,128)}), f32[16,34,512]{2,1,0:T(8,128)S(1)}, u32[]{:S(2)}, u32[]{:S(2)}) async-start(f32[16,34,512]{2,1,0:T(8,128)} %pad_maximum_fusion), calls=%async_computation | async-start | bytes 2621440 | tf_op jit(solution)/shard_map/all_to_all | solution.py:101
  15.2 18.5 %all-to-all-done = f32[16,34,512]{2,1,0:T(8,128)S(1)} async-done(((f32[16,34,512]{2,1,0:T(8,128)}), f32[16,34,512]{2,1,0:T(8,128)S(1)}, u32[]{:S(2)}, u32[]{:S(2)}) %all-to-all-start) | async-done | bytes 1114144 | tf_op jit(solution)/shard_map/all_to_all | solution.py:101
  33.7 1.1 slice_bitcast_fusion.1
  35.7 1.6 %fusion.63 = f32[256,8,128]{0,2,1:T(8,128)} fusion(f32[256,64,1]{0,1,2:T(8,128)S(1)} %copy-done.15, f32[64,24,128]{2,0,1:T(8,128)S(1)} %bitcast.169), kind=kOutput, calls=%fused_computation.131 | convolution fusion | flops 100663296 | bytes 1376256 | tf_op jit(solution)/shard_map/kn,ncm->kcm/dot_general | solution.py:40
  37.4 1.6 %fusion.97 = f32[256,8,128]{0,2,1:T(8,128)} fusion(f32[256,64,1]{0,1,2:T(8,128)S(1)} %copy-done.15, f32[64,24,128]{2,0,1:T(8,128)S(1)} %bitcast.170, f32[64,8,128]{2,1,0:T(8,128)S(1)} %bitcast.181), kind=kOutput, calls=%fused_computation.195 | convolution fusion | flops 100728832 | bytes 1638400 | tf_op jit(solution)/shard_map/kn,ncm->kcm/dot_general | solution.py:40
  39.4 1.4 %multiply_subtract_fusion.7 = (f32[128,8,128]{0,2,1:T(8,128)S(1)}, f32[128,8,128]{0,2,1:T(8,128)S(1)}) fusion(f32[256,8,128]{0,2,1:T(8,128)} %fusion.97, f32[128,128]{0,1:T(8,128)S(1)} %copy-done.4, f32[128,128]{0,1:T(8,128)S(1)} %copy-done.3), kind=kLoop, calls=%fused_computation.94 | loop fusion | flops 786432 | bytes 2228224 | tf_op jit(solution)/shard_map/sub | solution.py:43
  41.3 1.0 fusion.24
  42.5 0.8 copy-done.1
  44.0 0.7 copy-done.14
  46.2 1.0 fusion.2
  47.3 1.0 fusion.35
  48.3 1.3 multiply_subtract_fusion.1
  52.5 1.0 fusion.13
  53.6 1.4 %multiply_subtract_fusion = (f32[128,8,128]{2,0,1:T(8,128)}, f32[128,8,128]{2,0,1:T(8,128)}, f32[128,8,128]{2,0,1:T(8,128)S(1)}, f32[128,8,128]{2,0,1:T(8,128)S(1)}) fusion(f32[128,8,256]{2,0,1:T(8,128)S(1)} %fusion.24, f32[128,8,256]{2,0,1:T(8,128)S(1)} %fusion.13, f32[128,128]{1,0:T(8,128)S(1)} %get-tuple-element.68, f32[128,128]{1,0:T(8,128)S(1)} %get-tuple-element.67), kind=kLoop, calls=%fused_computation.80 | loop fusion | flops 1703936 | bytes 4325376 | tf_op jit(solution)/shard_map/sub | solution.py:60
  56.4 1.4 %multiply_reduce_fusion.3 = (f32[8]{0:T(128)S(1)}, f32[8]{0:T(128)S(1)}, bf16[64,8,128]{2,0,1:T(8,128)(2,1)}, f32[64,8,128]{2,0,1:T(8,128)S(1)}, f32[64,8,128]{2,0,1:T(8,128)S(1)}) fusion(f32[64,24,128]{2,0,1:T(8,128)S(1)} %bitcast.176, f32[64,8,128]{2,0,1:T(8,128)S(1)} %convolution_add_fusion.1, f32[64,8,128]{2,0,1:T(8,128)S(1)} %convolution_add_fusion.3, ...), kind=kOutput, calls=%fused_computation.125 | convolution fusion | flops 101777392 | bytes 3342432 | tf_op jit(solution)/shard_map/nk,kcm->ncm/dot_general | solution.py:52
  59.9 1.2 fusion.51
  62.3 1.1 copy.172
  63.4 4.2 %all-to-all-start.1 = ((bf16[16,32,512]{2,1,0:T(8,128)(2,1)}), bf16[16,32,512]{2,1,0:T(8,128)(2,1)S(1)}, u32[]{:S(2)}, u32[]{:S(2)}) async-start(bf16[16,32,512]{2,1,0:T(8,128)(2,1)} %copy.172), calls=%async_computation.1 | async-start | bytes 1048576 | tf_op jit(solution)/shard_map/all_to_all | solution.py:161
  68.7 10.3 %all-to-all-done.1 = bf16[16,32,512]{2,1,0:T(8,128)(2,1)S(1)} async-done(((bf16[16,32,512]{2,1,0:T(8,128)(2,1)}), bf16[16,32,512]{2,1,0:T(8,128)(2,1)S(1)}, u32[]{:S(2)}, u32[]{:S(2)}) %all-to-all-start.1) | async-done | bytes 524320 | tf_op jit(solution)/shard_map/all_to_all | solution.py:161
  80.7 12.9 %all_to_all.46 = f32[16,1,5216]{2,1,0:T(1,128)S(1)} all-to-all(f32[16,1,5216]{2,1,0:T(1,128)S(1)} %all_to_all.32), channel_id=1, replica_groups=mesh['dp'=8,'seq'=16] {'seq'}, dimensions={0} | all-to-all | bytes 667648 | tf_op jit(solution)/shard_map/all_to_all | solution.py:190
  94.2 9.4 %all_to_all.47 = f32[8,1,1548]{2,1,0:T(1,128)S(1)} all-to-all(f32[8,1,1548]{2,1,0:T(1,128)S(1)} %all_to_all.35), channel_id=1, replica_groups=mesh['dp'=8,'seq'=16] {'dp'}, dimensions={0} | all-to-all | bytes 99072 | tf_op jit(solution)/shard_map/all_to_all | solution.py:193
  103.7 0.7 broadcast_in_dim.30
  104.3 3.3 %all-to-all-start.4 = ((f32[8,1,1548]{2,1,0:T(1,128)}), f32[8,1,1548]{2,1,0:T(1,128)S(1)}, u32[]{:S(2)}, u32[]{:S(2)}) async-start(f32[8,1,1548]{2,1,0:T(1,128)} %broadcast_in_dim.30), calls=%async_computation.4 | async-start | bytes 106496 | tf_op jit(solution)/shard_map/all_to_all | solution.py:195
  107.7 1.0 fusion
  108.6 4.1 %all-to-all-done.4 = f32[8,1,1548]{2,1,0:T(1,128)S(1)} async-done(((f32[8,1,1548]{2,1,0:T(1,128)}), f32[8,1,1548]{2,1,0:T(1,128)S(1)}, u32[]{:S(2)}, u32[]{:S(2)}) %all-to-all-start.4) | async-done | bytes 49568 | tf_op jit(solution)/shard_map/all_to_all | solution.py:195
  112.9 0.8 broadcast_in_dim.32
  113.7 6.9 %all-to-all-start.5 = ((f32[16,1,4192]{2,1,0:T(1,128)}), f32[16,1,4192]{2,1,0:T(1,128)S(1)}, u32[]{:S(2)}, u32[]{:S(2)}) async-start(f32[16,1,4192]{2,1,0:T(1,128)} %broadcast_in_dim.32), calls=%async_computation.5 | async-start | bytes 540672 | tf_op jit(solution)/shard_map/all_to_all | solution.py:198
  120.6 0.9 fusion.1
  122.2 7.2 %all-to-all-done.5 = f32[16,1,4192]{2,1,0:T(1,128)S(1)} async-done(((f32[16,1,4192]{2,1,0:T(1,128)}), f32[16,1,4192]{2,1,0:T(1,128)S(1)}, u32[]{:S(2)}, u32[]{:S(2)}) %all-to-all-start.5) | async-done | bytes 268320 | tf_op jit(solution)/shard_map/all_to_all | solution.py:198
  131.2 0.7 mul.667
  (157 shorter events, 21.2 us)
Async XLA Ops:
  0.6 1.1 copy-start
  1.7 0.7 copy-start.22
  1.7 0.7 copy-start.23
  1.7 0.9 copy-start.17
  1.8 0.9 copy-start.20
  4.1 9.4 %copy-start.24 = (f32[3,384]{1,0:T(4,128)S(1)}, f32[3,384]{1,0:T(4,128)}, u32[]{:S(2)}) copy-start(f32[3,384]{1,0:T(4,128)} %param.19) | copy-start | bytes 13828
  4.1 9.8 %copy-start.26 = (f32[128]{0:T(128)S(1)}, f32[128]{0:T(128)}, u32[]{:S(2)}) copy-start(f32[128]{0:T(128)} %param.20) | copy-start | bytes 1540
  4.1 9.9 %copy-start.27 = (f32[128]{0:T(128)S(1)}, f32[128]{0:T(128)}, u32[]{:S(2)}) copy-start(f32[128]{0:T(128)} %param.21) | copy-start | bytes 1540
  4.1 29.6 %all-to-all-start = ((f32[16,34,512]{2,1,0:T(8,128)}), f32[16,34,512]{2,1,0:T(8,128)S(1)}, u32[]{:S(2)}, u32[]{:S(2)}) async-start(f32[16,34,512]{2,1,0:T(8,128)} %pad_maximum_fusion), calls=%async_computation | async-start | bytes 2621440 | tf_op jit(solution)/shard_map/all_to_all | solution.py:101
  34.9 0.8 copy-start.15
  37.3 2.0 %copy-start.3 = (f32[128,128]{0,1:T(8,128)S(1)}, f32[128,128]{0,1:T(8,128)}, u32[]{:S(2)}) copy-start(f32[128,128]{0,1:T(8,128)} %constant.45.clone) | copy-start | bytes 196612
  37.4 2.0 %copy-start.4 = (f32[128,128]{0,1:T(8,128)S(1)}, f32[128,128]{0,1:T(8,128)}, u32[]{:S(2)}) copy-start(f32[128,128]{0,1:T(8,128)} %constant.46.clone) | copy-start | bytes 196612
  39.4 1.4 %copy-start.2 = (f32[256,256,1]{1,0,2:T(8,128)S(1)}, f32[256,256,1]{1,0,2:T(8,128)}, u32[]{:S(2)}) copy-start(f32[256,256,1]{1,0,2:T(8,128)} %constant.59) | copy-start | bytes 786436
  42.3 1.0 copy-start.1
  43.9 0.8 copy-start.14
  43.9 0.8 copy-start.25
  44.7 1.2 copy-start.5
  56.4 2.6 %copy-start.9 = (f32[64,8,128]{2,0,1:T(8,128)}, f32[64,8,128]{2,0,1:T(8,128)S(1)}, u32[]{:S(2)}) copy-start(f32[64,8,128]{2,0,1:T(8,128)S(1)} %convolution_add_fusion) | copy-start | bytes 786436
  57.8 1.2 copy-start.6
  59.0 0.9 copy-start.8
  59.4 2.0 %copy-start.28 = (f32[3]{0:T(128)S(1)}, f32[3]{0:T(128)}, u32[]{:S(2)}) copy-start(f32[3]{0:T(128)} %pad.41.clone) | copy-start | bytes 40
  61.2 1.0 copy-start.16
  62.2 5.3 %copy-start.12 = (f32[128,8,128]{2,0,1:T(8,128)S(1)}, f32[128,8,128]{2,0,1:T(8,128)}, u32[]{:S(2)}) copy-start(f32[128,8,128]{2,0,1:T(8,128)} %get-tuple-element.16) | copy-start | bytes 1572868
  62.2 5.3 %copy-start.13 = (f32[128,8,128]{2,0,1:T(8,128)S(1)}, f32[128,8,128]{2,0,1:T(8,128)}, u32[]{:S(2)}) copy-start(f32[128,8,128]{2,0,1:T(8,128)} %get-tuple-element.17) | copy-start | bytes 1572868
  63.4 4.3 %copy-start.10 = (f32[128,8,128]{2,0,1:T(8,128)S(1)}, f32[128,8,128]{2,0,1:T(8,128)}, u32[]{:S(2)}) copy-start(f32[128,8,128]{2,0,1:T(8,128)} %get-tuple-element.18) | copy-start | bytes 1572868
  63.4 4.3 %copy-start.11 = (f32[128,8,128]{2,0,1:T(8,128)S(1)}, f32[128,8,128]{2,0,1:T(8,128)}, u32[]{:S(2)}) copy-start(f32[128,8,128]{2,0,1:T(8,128)} %get-tuple-element.19) | copy-start | bytes 1572868
  63.4 15.7 %all-to-all-start.1 = ((bf16[16,32,512]{2,1,0:T(8,128)(2,1)}), bf16[16,32,512]{2,1,0:T(8,128)(2,1)S(1)}, u32[]{:S(2)}, u32[]{:S(2)}) async-start(bf16[16,32,512]{2,1,0:T(8,128)(2,1)} %copy.172), calls=%async_computation.1 | async-start | bytes 1048576 | tf_op jit(solution)/shard_map/all_to_all | solution.py:161
  79.1 0.9 copy-start.18
  80.7 26.9 %copy-start.19 = (bf16[128,384]{1,0:T(8,128)(2,1)S(1)}, bf16[128,384]{1,0:T(8,128)(2,1)}, u32[]{:S(2)}) copy-start(bf16[128,384]{1,0:T(8,128)(2,1)} %param.17) | copy-start | bytes 294916
  93.8 26.8 %copy-start.21 = (bf16[128,128]{1,0:T(8,128)(2,1)S(1)}, bf16[128,128]{1,0:T(8,128)(2,1)}, u32[]{:S(2)}) copy-start(bf16[128,128]{1,0:T(8,128)(2,1)} %param.18) | copy-start | bytes 98308
  104.3 8.5 %all-to-all-start.4 = ((f32[8,1,1548]{2,1,0:T(1,128)}), f32[8,1,1548]{2,1,0:T(1,128)S(1)}, u32[]{:S(2)}, u32[]{:S(2)}) async-start(f32[8,1,1548]{2,1,0:T(1,128)} %broadcast_in_dim.30), calls=%async_computation.4 | async-start | bytes 106496 | tf_op jit(solution)/shard_map/all_to_all | solution.py:195
  113.7 15.7 %all-to-all-start.5 = ((f32[16,1,4192]{2,1,0:T(1,128)}), f32[16,1,4192]{2,1,0:T(1,128)S(1)}, u32[]{:S(2)}, u32[]{:S(2)}) async-start(f32[16,1,4192]{2,1,0:T(1,128)} %broadcast_in_dim.32), calls=%async_computation.5 | async-start | bytes 540672 | tf_op jit(solution)/shard_map/all_to_all | solution.py:198
  (1 other events, 0.7 us)

commit v6 on v5

--- a/solution.py
+++ b/solution.py
@@ -5,6 +5,8 @@
 import jax
 import jax.numpy as jnp
 from jax import lax
+from jax.experimental import pallas as pl
+from jax.experimental.pallas import tpu as pltpu
 from jax.sharding import PartitionSpec as P
 
 PRECISION = lax.Precision.HIGH
@@ -70,6 +72,55 @@
     return jnp.swapaxes(x, 0, 1).reshape(c, half * lanes)
 
 
+def exchange(x, axis, ident):
+    n = x.shape[0]
+    mesh_axes = ("dp", "seq")
+
+    def where(p):
+        return tuple(p if name == axis else lax.axis_index(name) for name in mesh_axes)
+
+    def kernel(x_ref, y_ref, send_sem, recv_sem):
+        me = lax.axis_index(axis)
+        barrier = pltpu.get_barrier_semaphore()
+        for k in range(1, n):
+            pl.semaphore_signal(
+                barrier, inc=1, device_id=where(lax.rem(me + k, n)),
+                device_id_type=pl.DeviceIdType.MESH,
+            )
+        pl.semaphore_wait(barrier, n - 1)
+        copies = []
+        for k in range(1, n):
+            p = lax.rem(me + k, n)
+            copy = pltpu.make_async_remote_copy(
+                src_ref=x_ref.at[p],
+                dst_ref=y_ref.at[me],
+                send_sem=send_sem.at[k],
+                recv_sem=recv_sem.at[k],
+                device_id=where(p),
+                device_id_type=pl.DeviceIdType.MESH,
+            )
+            copy.start()
+            copies.append(copy)
+        y_ref[pl.ds(me, 1)] = x_ref[pl.ds(me, 1)]
+        for copy in copies:
+            copy.wait()
+
+    return pl.pallas_call(
+        kernel,
+        out_shape=jax.ShapeDtypeStruct(x.shape, x.dtype),
+        in_specs=[pl.BlockSpec(memory_space=pltpu.VMEM)],
+        out_specs=pl.BlockSpec(memory_space=pltpu.VMEM),
+        scratch_shapes=[pltpu.SemaphoreType.DMA((n,)), pltpu.SemaphoreType.DMA((n,))],
+        compiler_params=pltpu.CompilerParams(collective_id=ident, has_side_effects=True),
+    )(x)
+
+
+def swap_blocks(x, axis, ident):
+    shape = x.shape
+    flat = x.reshape(shape[0], -1, LANES)
+    return exchange(flat, axis, ident).reshape(shape)
+
+
 def shards(series, cotangent, w_in, w_out, taps, skip_one, skip_two, filter_one, filter_two):
     _, block, width = series.shape
     seq_n = lax.axis_size("seq")
@@ -98,9 +149,7 @@
     dprod_blk = jnp.einsum("td,cd->ct", cotangent[0], w_out, preferred_element_type=jnp.float32)
     dprod_blk = dprod_blk.reshape(seq_n, per, block)
     rows_sent = jnp.repeat(jnp.swapaxes(jnp.stack([filter_one, filter_two]), 0, 1), per_group, axis=0)
-    got = lax.all_to_all(
-        jnp.concatenate([proj_blk, dprod_blk, rows_sent], axis=1), "seq", 0, 0, tiled=True
-    )
+    got = swap_blocks(jnp.concatenate([proj_blk, dprod_blk, rows_sent], axis=1), "seq", 0)
     proj = jnp.swapaxes(got[:, : 3 * per], 0, 1).reshape(3 * per, length)
     d_product = jnp.swapaxes(
         got[:, 3 * per : 4 * per].reshape(seq_n, per, block // LANES, LANES), 1, 2
@@ -158,7 +207,7 @@
     prod_sent = jnp.swapaxes(product.reshape(seq_n, half // seq_n, per, LANES), 1, 2)
     prod_sent = prod_sent.reshape(seq_n, per, block)
     dp_sent = jnp.swapaxes(d_proj.reshape(3 * per, seq_n, block), 0, 1)
-    back = lax.all_to_all(jnp.concatenate([prod_sent, dp_sent], axis=1), "seq", 0, 0, tiled=True)
+    back = swap_blocks(jnp.concatenate([prod_sent, dp_sent], axis=1), "seq", 1)
     prod_rows = jnp.transpose(back[:, :per], (2, 0, 1)).reshape(block, width)
     dp_rows = jnp.transpose(back[:, per:].reshape(seq_n, 3, per, block), (3, 1, 0, 2))
     dp_rows = dp_rows.reshape(block, 3 * width)
@@ -183,19 +232,19 @@
     )
     params = jnp.concatenate([local_w_in.reshape(-1), local_w_out.reshape(-1), small_full.reshape(-1)])
     n_params = params.shape[0]
-    chunk = -(-n_params // (seq_n * dp_n))
+    chunk = -(-n_params // (seq_n * dp_n * 8 * LANES)) * 8 * LANES
     params = jnp.pad(params, (0, chunk * seq_n * dp_n - n_params)).reshape(seq_n, dp_n * chunk)
 
     fg_sent = jnp.swapaxes(filt_grad.reshape(2, seq_n, block), 0, 1).reshape(seq_n, 2 * block)
-    got = lax.all_to_all(jnp.concatenate([params, fg_sent], axis=1), "seq", 0, 0, tiled=True)
+    got = swap_blocks(jnp.concatenate([params, fg_sent], axis=1), "seq", 2)
     p_part = jnp.sum(got[:, : dp_n * chunk], axis=0).reshape(dp_n, chunk)
     f_part = jnp.sum(got[:, dp_n * chunk :].reshape(filters, per_group, 2 * block), axis=1)
-    got = lax.all_to_all(jnp.concatenate([p_part, f_part], axis=1), "dp", 0, 0, tiled=True)
+    got = swap_blocks(jnp.concatenate([p_part, f_part], axis=1), "dp", 3)
     mine = jnp.sum(got, axis=0)
-    got = lax.all_to_all(jnp.broadcast_to(mine, (dp_n,) + mine.shape), "dp", 0, 0, tiled=True)
+    got = swap_blocks(jnp.broadcast_to(mine, (dp_n,) + mine.shape), "dp", 4)
     fg_blocks = jnp.swapaxes(got[:, chunk:].reshape(filters, 2, block), 0, 1)
     p_seq = got[:, :chunk].reshape(1, dp_n * chunk)
-    got = lax.all_to_all(jnp.broadcast_to(p_seq, (seq_n, dp_n * chunk)), "seq", 0, 0, tiled=True)
+    got = swap_blocks(jnp.broadcast_to(p_seq, (seq_n, dp_n * chunk)), "seq", 5)
     full = got.reshape(-1)
     sizes = [width * 3 * width, width * width, 3 * 4 * width]
     offsets = np.cumsum([0] + sizes)

time: 134 us -> 149 us (1.11)
  Pallas kernels: 0 us -> 85.6 us
  waiting for transfers between devices: 40.2 us -> 0 us
  starting transfers between devices: 23.9 us -> 0 us
  blocking collectives: 22.4 us -> 0 us
  local copies, waits for them, and re-layouts: 14.5 us -> 25 us
  other arithmetic: 12.3 us -> 17.6 us
    pallas_call x0 -> x6, Pallas kernels: none -> 85.6 us  [exchange(): pl.pallas_call(kernel, out_shape=jax.ShapeDtypeStruct(x.shape, x.dtype),...]
    all_to_all x4 -> x0, waiting for transfers between devices: 40.2 us -> none  [the longest x1 18.5 us: shards(): lax.all_to_all(jnp.concatenate([proj_blk, dprod_blk, rows_sent], axis=1),...]
    all_to_all x4 -> x0, starting transfers between devices: 23.9 us -> none  [the longest x1 9.43 us: shards(): lax.all_to_all(jnp.concatenate([proj_blk, dprod_blk, rows_sent], axis=1),...]
    all_to_all x2 -> x0, blocking collectives: 22.4 us -> none  [the longest x1 12.9 us: shards(): lax.all_to_all(jnp.concatenate([params, fg_sent], axis=1), 'seq', 0, 0, t...]
    reshape x2 -> x5, local copies, waits for them, and re-layouts: 0.22 us -> 5.03 us  [the longest x2 2.78 us: swap_blocks(): return exchange(flat, axis, ident).reshape(shape)]
    unnamed x66 -> x79, local copies, waits for them, and re-layouts: 5.65 us -> 9.19 us
    dot_general x5, matrix products: 4.78 us -> 2.8 us  [spectrum(): a = jnp.einsum('kn,ncm->kcm', tab['fwd1'], x, precision=PRECISION)]
    dot_general x5, matrix products: 3.53 us -> 5.48 us  [signal(): return jnp.einsum('nk,kcm->ncm', tab['inv1'], stacked, precision=PRECISION)]
  transfers between devices with their start and end apart: 4 -> 0, of which waited for: 4 -> 0; matrix products, arithmetic and copies ran while one was open for 4% -> 0% of each run, Pallas kernels for 0% -> 0%
where the time goes in v6:
time: 149 us; the launch traced here: 148 us
  Pallas kernels  85.6 us (57%)
  local copies, waits for them, and re-layouts  25 us (17%)
  matrix products  18.5 us (12%)
  other arithmetic  17.6 us (12%)
  between operations  1.64 us (1%)
    pallas_call x6, Pallas kernels, exchange(): pl.pallas_call(kernel, out_shape=jax.ShapeDtypeStruct(x.shape, x.dtype),...  85.6 us
    unnamed x79, local copies, waits for them, and re-layouts  9.19 us
    dot_general x5, matrix products, signal(): return jnp.einsum('nk,kcm->ncm', tab['inv1'], stacked, precision=PRECISION)  5.48 us
    dot_general x5, matrix products, spectrum(): return jnp.einsum('kcm,mj->kcj', cat, tab['fwd2'], precision=PRECISION)  4.63 us

profile of v6, /device:TPU:1, one launch (start us, length us, event | category | flops | bytes accessed | tf_op | source)
XLA Modules:
  0.0 148.3 jit_solution(8299102502661381175)
XLA Ops:
  1.8 1.0 copy.85
  4.2 1.1 reshape.192.x_ref
  5.3 26.5 %shard_map.214 = f32[16,136,128]{2,1,0:T(8,128)} custom-call(f32[16,136,128]{2,1,0:T(8,128)} %reshape.192.x_ref), custom_call_target="tpu_custom_call" | custom-call | tf_op jit(solution)/shard_map/pallas_call | solution.py:108
  31.8 1.4 reshape.193
  33.2 1.3 slice_bitcast_fusion.1
  35.2 1.0 fusion.98
  37.9 1.0 fusion.24
  38.9 1.0 slice_bitcast_fusion.8
  44.1 1.1 multiply_add_fusion.5
  46.1 1.9 %convolution_add_fusion.1 = f32[64,8,128]{2,0,1:T(8,128)S(1)} fusion(f32[64,256,1]{1,0,2:T(8,128)S(1)} %copy-done.11, f32[128,8,128]{0,2,1:T(8,128)} %get-tuple-element.33, f32[128,8,128]{0,2,1:T(8,128)} %get-tuple-element.32, f32[8]{0:T(128)S(1)} %get-tuple-element.80, f32[64,24,128]{2,0,1:T(8,128)S(1)} %bitcast.182, f32[64,8,128]{2,1,0:T(8,128)} %bitcast.194), kind=kOutput, calls=%fused_computation.4 | convolution fusion | flops 101122048 | bytes 1900576 | tf_op jit(solution)/shard_map/nk,kcm->ncm/dot_general | solution.py:54
  49.5 1.0 fusion.2
  50.6 1.0 fusion.35
  51.6 1.3 multiply_subtract_fusion.1
  54.5 1.3 convolution_add_fusion
  57.2 1.2 fusion.13
  58.4 1.2 multiply_subtract_fusion
  61.3 1.4 multiply_reduce_fusion.3
  63.2 1.2 fusion.51
  64.5 1.0 pad_maximum_fusion.1
  68.4 1.1 reshape.203.x_ref
  69.6 13.2 %shard_map.215 = bf16[16,128,128]{2,1,0:T(8,128)(2,1)} custom-call(bf16[16,128,128]{2,1,0:T(8,128)(2,1)} %reshape.203.x_ref), custom_call_target="tpu_custom_call" | custom-call | tf_op jit(solution)/shard_map/pallas_call | solution.py:108
  82.8 1.4 reshape.204
  85.5 1.3 maximum_reduce_fusion
  89.0 14.9 %shard_map.216 = f32[16,72,128]{2,1,0:T(8,128)} custom-call(f32[16,72,128]{2,1,0:T(8,128)} %bitcast.202), custom_call_target="tpu_custom_call" | custom-call | tf_op jit(solution)/shard_map/pallas_call | solution.py:108
  104.0 1.2 copy.164
  106.0 7.3 %shard_map.217 = f32[8,16,128]{2,1,0:T(8,128)} custom-call(f32[8,16,128]{2,1,0:T(8,128)} %pad_maximum_fusion.4.x_ref), custom_call_target="tpu_custom_call" | custom-call | tf_op jit(solution)/shard_map/pallas_call | solution.py:108
  114.9 7.0 %shard_map.218 = f32[8,16,128]{2,1,0:T(8,128)} custom-call(f32[8,16,128]{2,1,0:T(8,128)} %broadcast_in_dim.30.x_ref), custom_call_target="tpu_custom_call" | custom-call | tf_op jit(solution)/shard_map/pallas_call | solution.py:108
  123.6 16.6 %shard_map.219 = f32[16,64,128]{2,1,0:T(8,128)} custom-call(f32[16,64,128]{2,1,0:T(8,128)} %broadcast_in_dim.32.x_ref), custom_call_target="tpu_custom_call" | custom-call | tf_op jit(solution)/shard_map/pallas_call | solution.py:108
  140.2 0.9 slice_multiply_fusion.3
  141.9 1.5 slice_multiply_fusion.4
  144.6 1.2 fusion.78
  146.5 1.0 fusion
  (162 shorter events, 29.9 us)
Async XLA Ops:
  0.6 2.2 %copy-start = (bf16[1,512,128]{2,1,0:T(8,128)(2,1)S(1)}, bf16[1,512,128]{2,1,0:T(8,128)(2,1)}, u32[]{:S(2)}) copy-start(bf16[1,512,128]{2,1,0:T(8,128)(2,1)} %param.15) | copy-start | bytes 393220
  1.6 32.9 %copy-start.28 = (f32[24]{0:T(128)}, f32[24]{0:T(128)S(1)}, u32[]{:S(2)}) copy-start(f32[24]{0:T(128)S(1)} %mul.264) | copy-start | bytes 292
  1.7 32.8 %copy-start.30 = (f32[24]{0:T(128)}, f32[24]{0:T(128)S(1)}, u32[]{:S(2)}) copy-start(f32[24]{0:T(128)S(1)} %mul.267) | copy-start | bytes 292
  1.8 32.8 %copy-start.32 = (f32[24]{0:T(128)}, f32[24]{0:T(128)S(1)}, u32[]{:S(2)}) copy-start(f32[24]{0:T(128)S(1)} %mul.270) | copy-start | bytes 292
  2.8 0.9 copy-start.17
  2.8 1.1 copy-start.26
  2.9 1.1 copy-start.27
  33.2 1.3 copy-start.3
  35.1 1.2 copy-start.13
  35.2 1.7 %copy-start.4 = (f32[128,128]{0,1:T(8,128)S(1)}, f32[128,128]{0,1:T(8,128)}, u32[]{:S(2)}) copy-start(f32[128,128]{0,1:T(8,128)} %constant.45.clone) | copy-start | bytes 196612
  35.2 1.7 %copy-start.5 = (f32[128,128]{0,1:T(8,128)S(1)}, f32[128,128]{0,1:T(8,128)}, u32[]{:S(2)}) copy-start(f32[128,128]{0,1:T(8,128)} %constant.46.clone) | copy-start | bytes 196612
  36.3 5.5 %copy-start.6 = (f32[16,32,128]{2,1,0:T(8,128)}, f32[16,32,128]{2,1,0:T(8,128)S(1)}, u32[]{:S(2)}) copy-start(f32[16,32,128]{2,1,0:T(8,128)S(1)} %pad_maximum_fusion.3) | copy-start | bytes 786436
  36.9 1.0 copy-start.2
  42.1 1.3 copy-start.1
  44.1 1.2 copy-start.34
  44.1 2.0 %copy-start.11 = (f32[64,256,1]{1,0,2:T(8,128)S(1)}, f32[64,256,1]{1,0,2:T(8,128)}, u32[]{:S(2)}) copy-start(f32[64,256,1]{1,0,2:T(8,128)} %constant.59) | copy-start | bytes 196612
  50.5 1.1 copy-start.21
  50.5 1.1 copy-start.22
  50.5 1.1 copy-start.23
  57.2 1.2 copy-start.15
  57.2 1.2 copy-start.20
  60.3 1.0 copy-start.7
  61.3 1.4 copy-start.8
  66.1 1.0 copy-start.29
  66.1 1.0 copy-start.31
  66.1 1.0 copy-start.33
  67.1 0.9 copy-start.16
  84.2 0.9 copy-start.18
  85.3 1.5 copy-start.9
  85.4 1.5 %copy-start.10 = (f32[128,8,128]{2,0,1:T(8,128)S(1)}, f32[128,8,128]{2,0,1:T(8,128)}, u32[]{:S(2)}) copy-start(f32[128,8,128]{2,0,1:T(8,128)} %get-tuple-element.19) | copy-start | bytes 1572868
  122.8 23.7 %copy-start.19 = (bf16[128,384]{1,0:T(8,128)(2,1)S(1)}, bf16[128,384]{1,0:T(8,128)(2,1)}, u32[]{:S(2)}) copy-start(bf16[128,384]{1,0:T(8,128)(2,1)} %param.17) | copy-start | bytes 294916
  123.6 23.8 %copy-start.25 = (bf16[128,128]{1,0:T(8,128)(2,1)S(1)}, bf16[128,128]{1,0:T(8,128)(2,1)}, u32[]{:S(2)}) copy-start(bf16[128,128]{1,0:T(8,128)(2,1)} %param.18) | copy-start | bytes 98308
  (3 other events, 2.4 us)

commit v7 on v5

--- a/solution.py
+++ b/solution.py
@@ -98,14 +98,13 @@
     dprod_blk = jnp.einsum("td,cd->ct", cotangent[0], w_out, preferred_element_type=jnp.float32)
     dprod_blk = dprod_blk.reshape(seq_n, per, block)
     rows_sent = jnp.repeat(jnp.swapaxes(jnp.stack([filter_one, filter_two]), 0, 1), per_group, axis=0)
-    got = lax.all_to_all(
-        jnp.concatenate([proj_blk, dprod_blk, rows_sent], axis=1), "seq", 0, 0, tiled=True
-    )
+    got = lax.all_to_all(jnp.concatenate([proj_blk, rows_sent], axis=1), "seq", 0, 0, tiled=True)
     proj = jnp.swapaxes(got[:, : 3 * per], 0, 1).reshape(3 * per, length)
+    h_rows = jnp.swapaxes(got[:, 3 * per :], 0, 1).reshape(2, length)
+    dprod_got = lax.all_to_all(dprod_blk, "seq", 0, 0, tiled=True)
     d_product = jnp.swapaxes(
-        got[:, 3 * per : 4 * per].reshape(seq_n, per, block // LANES, LANES), 1, 2
+        dprod_got.reshape(seq_n, per, block // LANES, LANES), 1, 2
     ).reshape(half, per, LANES)
-    h_rows = jnp.swapaxes(got[:, 4 * per :], 0, 1).reshape(2, length)
     prev1 = jnp.pad(proj, ((0, 0), (1, 0)))[:, :length]
     prev2 = jnp.pad(proj, ((0, 0), (2, 0)))[:, :length]
     conv = taps_sel[0][:, None] * proj + taps_sel[1][:, None] * prev1 + taps_sel[2][:, None] * prev2
@@ -157,10 +156,11 @@
     local_skip2 = jnp.sum(grad_two * gated_mid, axis=(0, 2))
     prod_sent = jnp.swapaxes(product.reshape(seq_n, half // seq_n, per, LANES), 1, 2)
     prod_sent = prod_sent.reshape(seq_n, per, block)
+    prod_got = lax.all_to_all(prod_sent, "seq", 0, 0, tiled=True)
     dp_sent = jnp.swapaxes(d_proj.reshape(3 * per, seq_n, block), 0, 1)
-    back = lax.all_to_all(jnp.concatenate([prod_sent, dp_sent], axis=1), "seq", 0, 0, tiled=True)
-    prod_rows = jnp.transpose(back[:, :per], (2, 0, 1)).reshape(block, width)
-    dp_rows = jnp.transpose(back[:, per:].reshape(seq_n, 3, per, block), (3, 1, 0, 2))
+    dp_got = lax.all_to_all(dp_sent, "seq", 0, 0, tiled=True)
+    prod_rows = jnp.transpose(prod_got, (2, 0, 1)).reshape(block, width)
+    dp_rows = jnp.transpose(dp_got.reshape(seq_n, 3, per, block), (3, 1, 0, 2))
     dp_rows = dp_rows.reshape(block, 3 * width)
     output = jnp.dot(prod_rows, w_out, preferred_element_type=jnp.float32).astype(jnp.bfloat16)
     output = output.reshape(1, block, width)

time: 134 us -> 155 us (1.16)
  starting transfers between devices: 23.9 us -> 32 us
  local copies, waits for them, and re-layouts: 14.5 us -> 21.7 us
  waiting for transfers between devices: 40.2 us -> 45.9 us
    all_to_all x2 -> x4, starting transfers between devices: 13.6 us -> 21.5 us  [the longest x1 9.43 us: shards(): dprod_got = lax.all_to_all(dprod_blk, 'seq', 0, 0, tiled=True)]
    all_to_all x2 -> x4, waiting for transfers between devices: 28.8 us -> 34.5 us  [the longest x1 13.9 us: shards(): lax.all_to_all(jnp.concatenate([proj_blk, rows_sent], axis=1), 'seq', 0,...]
    unnamed x66 -> x61, local copies, waits for them, and re-layouts: 5.65 us -> 11.4 us
    dot_general x1, matrix products: 0.19 us -> 1.87 us  [shards(): jnp.einsum('td,cd->ct', cotangent[0], w_out, preferred_element_type=jnp.f...]
    transpose x4, local copies, waits for them, and re-layouts: 0.09 us -> 1.76 us  [the longest x2 0.98 us: shards(): h_rows = jnp.swapaxes(got[:, 3 * per:], 0, 1).reshape(2, length)]
  transfers between devices with their start and end apart: 4 -> 6, of which waited for: 4 -> 6; matrix products, arithmetic and copies ran while one was open for 4% -> 5% of each run, Pallas kernels for 0% -> 0%
where the time goes in v7:
time: 155 us; the launch traced here: 153 us
  waiting for transfers between devices  45.9 us (30%)
  starting transfers between devices  32 us (21%)
  blocking collectives  22.2 us (14%)
  local copies, waits for them, and re-layouts  21.7 us (14%)
  matrix products  19.2 us (12%)
  other arithmetic  10.9 us (7%)
    all_to_all x1, waiting for transfers between devices, shards(): lax.all_to_all(jnp.concatenate([proj_blk, rows_sent], axis=1), 'seq', 0,...  13.9 us
    all_to_all x1, blocking collectives, shards(): lax.all_to_all(jnp.concatenate([params, fg_sent], axis=1), 'seq', 0, 0, t...  12.8 us
    unnamed x61, local copies, waits for them, and re-layouts  11.4 us
    all_to_all x1, blocking collectives, shards(): lax.all_to_all(jnp.concatenate([p_part, f_part], axis=1), 'dp', 0, 0, til...  9.44 us
    all_to_all x1, starting transfers between devices, shards(): dprod_got = lax.all_to_all(dprod_blk, 'seq', 0, 0, tiled=True)  9.43 us
    all_to_all x1, waiting for transfers between devices, shards(): dp_got = lax.all_to_all(dp_sent, 'seq', 0, 0, tiled=True)  8.31 us
    all_to_all x1, waiting for transfers between devices, shards(): lax.all_to_all(jnp.broadcast_to(p_seq, (seq_n, dp_n * chunk)), 'seq', 0,...  7.14 us
    all_to_all x1, starting transfers between devices, shards(): lax.all_to_all(jnp.broadcast_to(p_seq, (seq_n, dp_n * chunk)), 'seq', 0,...  7.03 us
  transfers between devices with their start and end apart: 6, of which 6 were waited for; matrix products, arithmetic and copies ran while one was open for 5% of the time, Pallas kernels for 0%

profile of v7, /device:TPU:1, one launch (start us, length us, event | category | flops | bytes accessed | tf_op | source)
XLA Modules:
  0.0 153.2 jit_solution(17128866270849704938)
XLA Ops:
  0.7 1.9 %fusion.68 = f32[16,8,512]{2,1,0:T(8,128)} fusion(bf16[1,512,128]{2,1,0:T(8,128)(2,1)} %param.16, bf16[128,128]{1,0:T(8,128)(2,1)} %param.18), kind=kOutput, calls=%fused_computation.136 | convolution fusion | flops 16777216 | bytes 425984 | tf_op jit(solution)/shard_map/td,cd->ct/dot_general | solution.py:98
  2.5 9.4 %all-to-all-start.2 = ((f32[16,8,512]{2,1,0:T(8,128)}), f32[16,8,512]{2,1,0:T(8,128)S(1)}, u32[]{:S(2)}, u32[]{:S(2)}) async-start(f32[16,8,512]{2,1,0:T(8,128)} %fusion.68), calls=%async_computation.2 | async-start | bytes 524288 | tf_op jit(solution)/shard_map/all_to_all | solution.py:104
  13.2 1.1 pad_maximum_fusion
  14.3 6.4 %all-to-all-done.2 = f32[16,8,512]{2,1,0:T(8,128)S(1)} async-done(((f32[16,8,512]{2,1,0:T(8,128)}), f32[16,8,512]{2,1,0:T(8,128)S(1)}, u32[]{:S(2)}, u32[]{:S(2)}) %all-to-all-start.2) | async-done | bytes 262176 | tf_op jit(solution)/shard_map/all_to_all | solution.py:104
  20.6 4.2 %all-to-all-start = ((f32[16,26,512]{2,1,0:T(8,128)}), f32[16,26,512]{2,1,0:T(8,128)S(1)}, u32[]{:S(2)}, u32[]{:S(2)}) async-start(f32[16,26,512]{2,1,0:T(8,128)} %pad_maximum_fusion), calls=%async_computation | async-start | bytes 2097152 | tf_op jit(solution)/shard_map/all_to_all | solution.py:101
  28.4 13.9 %all-to-all-done = f32[16,26,512]{2,1,0:T(8,128)S(1)} async-done(((f32[16,26,512]{2,1,0:T(8,128)}), f32[16,26,512]{2,1,0:T(8,128)S(1)}, u32[]{:S(2)}, u32[]{:S(2)}) %all-to-all-start) | async-done | bytes 852000 | tf_op jit(solution)/shard_map/all_to_all | solution.py:101
  42.3 1.3 slice_bitcast_fusion.1
  45.0 1.6 %fusion.63 = f32[256,8,128]{0,2,1:T(8,128)} fusion(f32[256,64,1]{0,1,2:T(8,128)S(1)} %copy-done.14, f32[64,24,128]{2,0,1:T(8,128)S(1)} %bitcast.173), kind=kOutput, calls=%fused_computation.130 | convolution fusion | flops 100663296 | bytes 1376256 | tf_op jit(solution)/shard_map/kn,ncm->kcm/dot_general | solution.py:40
  47.3 1.0 slice_bitcast_fusion.4
  49.3 0.9 copy-done.2
  50.7 1.0 fusion.24
  56.2 1.0 fusion.2
  57.2 1.0 fusion.35
  58.3 1.3 multiply_subtract_fusion.1
  62.6 1.2 fusion.13
  63.8 1.3 multiply_subtract_fusion
  66.5 1.4 multiply_reduce_fusion.3
  70.2 1.2 fusion.51
  74.4 4.0 %all-to-all-start.1 = ((bf16[16,8,512]{2,1,0:T(8,128)(2,1)}), bf16[16,8,512]{2,1,0:T(8,128)(2,1)S(1)}, u32[]{:S(2)}, u32[]{:S(2)}) async-start(bf16[16,8,512]{2,1,0:T(8,128)(2,1)} %bitcast.170), calls=%async_computation.1 | async-start | bytes 262144 | tf_op jit(solution)/shard_map/all_to_all | solution.py:159
  78.5 1.0 copy-done.9
  80.1 6.0 %all-to-all-done.1 = bf16[16,8,512]{2,1,0:T(8,128)(2,1)S(1)} async-done(((bf16[16,8,512]{2,1,0:T(8,128)(2,1)}), bf16[16,8,512]{2,1,0:T(8,128)(2,1)S(1)}, u32[]{:S(2)}, u32[]{:S(2)}) %all-to-all-start.1) | async-done | bytes 131104 | tf_op jit(solution)/shard_map/all_to_all | solution.py:159
  86.1 3.8 %all-to-all-start.3 = ((bf16[16,24,512]{2,1,0:T(8,128)(2,1)}), bf16[16,24,512]{2,1,0:T(8,128)(2,1)S(1)}, u32[]{:S(2)}, u32[]{:S(2)}) async-start(bf16[16,24,512]{2,1,0:T(8,128)(2,1)} %bitcast.168), calls=%async_computation.3 | async-start | bytes 786432 | tf_op jit(solution)/shard_map/all_to_all | solution.py:161
  91.5 8.3 %all-to-all-done.3 = bf16[16,24,512]{2,1,0:T(8,128)(2,1)S(1)} async-done(((bf16[16,24,512]{2,1,0:T(8,128)(2,1)}), bf16[16,24,512]{2,1,0:T(8,128)(2,1)S(1)}, u32[]{:S(2)}, u32[]{:S(2)}) %all-to-all-start.3) | async-done | bytes 393248 | tf_op jit(solution)/shard_map/all_to_all | solution.py:161
  100.8 12.8 %all_to_all.56 = f32[16,1,5216]{2,1,0:T(1,128)S(1)} all-to-all(f32[16,1,5216]{2,1,0:T(1,128)S(1)} %all_to_all.40), channel_id=1, replica_groups=mesh['dp'=8,'seq'=16] {'seq'}, dimensions={0} | all-to-all | bytes 667648 | tf_op jit(solution)/shard_map/all_to_all | solution.py:190
  114.0 9.4 %all_to_all.57 = f32[8,1,1548]{2,1,0:T(1,128)S(1)} all-to-all(f32[8,1,1548]{2,1,0:T(1,128)S(1)} %all_to_all.43), channel_id=1, replica_groups=mesh['dp'=8,'seq'=16] {'dp'}, dimensions={0} | all-to-all | bytes 99072 | tf_op jit(solution)/shard_map/all_to_all | solution.py:193
  124.2 3.5 %all-to-all-start.6 = ((f32[8,1,1548]{2,1,0:T(1,128)}), f32[8,1,1548]{2,1,0:T(1,128)S(1)}, u32[]{:S(2)}, u32[]{:S(2)}) async-start(f32[8,1,1548]{2,1,0:T(1,128)} %broadcast_in_dim.30), calls=%async_computation.6 | async-start | bytes 106496 | tf_op jit(solution)/shard_map/all_to_all | solution.py:195
  127.7 0.9 fusion.1
  128.5 4.2 %all-to-all-done.6 = f32[8,1,1548]{2,1,0:T(1,128)S(1)} async-done(((f32[8,1,1548]{2,1,0:T(1,128)}), f32[8,1,1548]{2,1,0:T(1,128)S(1)}, u32[]{:S(2)}, u32[]{:S(2)}) %all-to-all-start.6) | async-done | bytes 49568 | tf_op jit(solution)/shard_map/all_to_all | solution.py:195
  132.9 0.8 broadcast_in_dim.32
  133.7 7.0 %all-to-all-start.7 = ((f32[16,1,4192]{2,1,0:T(1,128)}), f32[16,1,4192]{2,1,0:T(1,128)S(1)}, u32[]{:S(2)}, u32[]{:S(2)}) async-start(f32[16,1,4192]{2,1,0:T(1,128)} %broadcast_in_dim.32), calls=%async_computation.7 | async-start | bytes 540672 | tf_op jit(solution)/shard_map/all_to_all | solution.py:198
  140.7 1.0 fusion
  142.4 7.1 %all-to-all-done.7 = f32[16,1,4192]{2,1,0:T(1,128)S(1)} async-done(((f32[16,1,4192]{2,1,0:T(1,128)}), f32[16,1,4192]{2,1,0:T(1,128)S(1)}, u32[]{:S(2)}, u32[]{:S(2)}) %all-to-all-start.7) | async-done | bytes 268320 | tf_op jit(solution)/shard_map/all_to_all | solution.py:198
  (154 shorter events, 31.0 us)
Async XLA Ops:
  0.6 11.5 %copy-start = (bf16[1,512,128]{2,1,0:T(8,128)(2,1)S(1)}, bf16[1,512,128]{2,1,0:T(8,128)(2,1)}, u32[]{:S(2)}) copy-start(bf16[1,512,128]{2,1,0:T(8,128)(2,1)} %param.15) | copy-start | bytes 393220
  2.5 9.4 %copy-start.17 = (bf16[128,384]{1,0:T(8,128)(2,1)S(1)}, bf16[128,384]{1,0:T(8,128)(2,1)}, u32[]{:S(2)}) copy-start(bf16[128,384]{1,0:T(8,128)(2,1)} %param.17) | copy-start | bytes 294916
  2.5 18.1 %all-to-all-start.2 = ((f32[16,8,512]{2,1,0:T(8,128)}), f32[16,8,512]{2,1,0:T(8,128)S(1)}, u32[]{:S(2)}, u32[]{:S(2)}) async-start(f32[16,8,512]{2,1,0:T(8,128)} %fusion.68), calls=%async_computation.2 | async-start | bytes 524288 | tf_op jit(solution)/shard_map/all_to_all | solution.py:104
  12.4 0.7 copy-start.20
  12.4 0.7 copy-start.21
  20.6 21.7 %all-to-all-start = ((f32[16,26,512]{2,1,0:T(8,128)}), f32[16,26,512]{2,1,0:T(8,128)S(1)}, u32[]{:S(2)}, u32[]{:S(2)}) async-start(f32[16,26,512]{2,1,0:T(8,128)} %pad_maximum_fusion), calls=%async_computation | async-start | bytes 2097152 | tf_op jit(solution)/shard_map/all_to_all | solution.py:101
  24.9 0.7 copy-start.22
  25.9 0.7 copy-start.24
  42.3 1.3 copy-start.6
  44.2 0.8 copy-start.14
  48.3 0.8 copy-start.3
  48.3 0.9 copy-start.4
  49.3 1.0 copy-start.2
  51.7 1.0 copy-start.1
  53.3 0.8 copy-start.13
  53.4 0.7 copy-start.23
  54.7 1.2 copy-start.5
  66.5 1.4 copy-start.8
  68.5 1.1 copy-start.7
  71.6 0.7 copy-start.26
  72.4 1.3 copy-start.15
  72.9 5.5 %copy-start.11 = (f32[128,8,128]{2,0,1:T(8,128)S(1)}, f32[128,8,128]{2,0,1:T(8,128)}, u32[]{:S(2)}) copy-start(f32[128,8,128]{2,0,1:T(8,128)} %get-tuple-element.16) | copy-start | bytes 1572868
  72.9 5.5 %copy-start.12 = (f32[128,8,128]{2,0,1:T(8,128)S(1)}, f32[128,8,128]{2,0,1:T(8,128)}, u32[]{:S(2)}) copy-start(f32[128,8,128]{2,0,1:T(8,128)} %get-tuple-element.17) | copy-start | bytes 1572868
  74.4 11.7 %all-to-all-start.1 = ((bf16[16,8,512]{2,1,0:T(8,128)(2,1)}), bf16[16,8,512]{2,1,0:T(8,128)(2,1)S(1)}, u32[]{:S(2)}, u32[]{:S(2)}) async-start(bf16[16,8,512]{2,1,0:T(8,128)(2,1)} %bitcast.170), calls=%async_computation.1 | async-start | bytes 262144 | tf_op jit(solution)/shard_map/all_to_all | solution.py:159
  78.4 1.0 copy-start.9
  78.4 1.2 copy-start.10
  86.1 13.7 %all-to-all-start.3 = ((bf16[16,24,512]{2,1,0:T(8,128)(2,1)}), bf16[16,24,512]{2,1,0:T(8,128)(2,1)S(1)}, u32[]{:S(2)}, u32[]{:S(2)}) async-start(bf16[16,24,512]{2,1,0:T(8,128)(2,1)} %bitcast.168), calls=%async_computation.3 | async-start | bytes 786432 | tf_op jit(solution)/shard_map/all_to_all | solution.py:161
  90.4 0.9 copy-start.16
  124.2 3.5 %copy-start.19 = (bf16[128,128]{1,0:T(8,128)(2,1)S(1)}, bf16[128,128]{1,0:T(8,128)(2,1)}, u32[]{:S(2)}) copy-start(bf16[128,128]{1,0:T(8,128)(2,1)} %param.18) | copy-start | bytes 98308
  124.2 8.6 %all-to-all-start.6 = ((f32[8,1,1548]{2,1,0:T(1,128)}), f32[8,1,1548]{2,1,0:T(1,128)S(1)}, u32[]{:S(2)}, u32[]{:S(2)}) async-start(f32[8,1,1548]{2,1,0:T(1,128)} %broadcast_in_dim.30), calls=%async_computation.6 | async-start | bytes 106496 | tf_op jit(solution)/shard_map/all_to_all | solution.py:195
  133.7 7.0 %copy-start.18 = (bf16[128,384]{1,0:T(8,128)(2,1)S(1)}, bf16[128,384]{1,0:T(8,128)(2,1)}, u32[]{:S(2)}) copy-start(bf16[128,384]{1,0:T(8,128)(2,1)} %param.17) | copy-start | bytes 294916
  133.7 15.8 %all-to-all-start.7 = ((f32[16,1,4192]{2,1,0:T(1,128)}), f32[16,1,4192]{2,1,0:T(1,128)S(1)}, u32[]{:S(2)}, u32[]{:S(2)}) async-start(f32[16,1,4192]{2,1,0:T(1,128)} %broadcast_in_dim.32), calls=%async_computation.7 | async-start | bytes 540672 | tf_op jit(solution)/shard_map/all_to_all | solution.py:198
  (1 other events, 0.7 us)

commit v8 on v5

--- a/solution.py
+++ b/solution.py
@@ -190,9 +190,9 @@
     got = lax.all_to_all(jnp.concatenate([params, fg_sent], axis=1), "seq", 0, 0, tiled=True)
     p_part = jnp.sum(got[:, : dp_n * chunk], axis=0).reshape(dp_n, chunk)
     f_part = jnp.sum(got[:, dp_n * chunk :].reshape(filters, per_group, 2 * block), axis=1)
-    got = lax.all_to_all(jnp.concatenate([p_part, f_part], axis=1), "dp", 0, 0, tiled=True)
-    mine = jnp.sum(got, axis=0)
-    got = lax.all_to_all(jnp.broadcast_to(mine, (dp_n,) + mine.shape), "dp", 0, 0, tiled=True)
+    both = jnp.concatenate([p_part, f_part], axis=1)
+    got = lax.all_to_all(jnp.broadcast_to(both, (dp_n,) + both.shape), "dp", 0, 0, tiled=True)
+    got = jnp.sum(got.reshape((dp_n,) + both.shape), axis=0)
     fg_blocks = jnp.swapaxes(got[:, chunk:].reshape(filters, 2, block), 0, 1)
     p_seq = got[:, :chunk].reshape(1, dp_n * chunk)
     got = lax.all_to_all(jnp.broadcast_to(p_seq, (seq_n, dp_n * chunk)), "seq", 0, 0, tiled=True)

time: 134 us -> 128 us (0.955)
  blocking collectives: 22.4 us -> 12.8 us
  waiting for transfers between devices: 40.2 us -> 43.8 us
    all_to_all x1 -> x0, blocking collectives: 9.45 us -> none  [shards(): lax.all_to_all(jnp.concatenate([p_part, f_part], axis=1), 'dp', 0, 0, til...]
    all_to_all x1, waiting for transfers between devices: 4.13 us -> 7.83 us  [shards(): lax.all_to_all(jnp.broadcast_to(both, (dp_n,) + both.shape), 'dp', 0, 0,...]
    all_to_all x1, starting transfers between devices: 6.9 us -> 5.09 us  [shards(): lax.all_to_all(jnp.broadcast_to(p_seq, (seq_n, dp_n * chunk)), 'seq', 0,...]
    unnamed x66 -> x65, local copies, waits for them, and re-layouts: 5.65 us -> 5.64 us
where the time goes in v8:
time: 128 us; the launch traced here: 127 us
  waiting for transfers between devices  43.8 us (34%)
  starting transfers between devices  23.3 us (18%)
  matrix products  18.4 us (14%)
  local copies, waits for them, and re-layouts  14.6 us (11%)
  blocking collectives  12.8 us (10%)
  other arithmetic  12.3 us (10%)
  between operations  1.45 us (1%)
    all_to_all x1, waiting for transfers between devices, shards(): lax.all_to_all(jnp.concatenate([proj_blk, dprod_blk, rows_sent], axis=1),...  18.5 us
    all_to_all x1, blocking collectives, shards(): lax.all_to_all(jnp.concatenate([params, fg_sent], axis=1), 'seq', 0, 0, t...  12.8 us
    all_to_all x1, waiting for transfers between devices, shards(): lax.all_to_all(jnp.concatenate([prod_sent, dp_sent], axis=1), 'seq', 0, 0...  10.3 us
    all_to_all x1, starting transfers between devices, shards(): lax.all_to_all(jnp.concatenate([proj_blk, dprod_blk, rows_sent], axis=1),...  9.43 us
    all_to_all x1, waiting for transfers between devices, shards(): lax.all_to_all(jnp.broadcast_to(both, (dp_n,) + both.shape), 'dp', 0, 0,...  7.83 us
    all_to_all x1, waiting for transfers between devices, shards(): lax.all_to_all(jnp.broadcast_to(p_seq, (seq_n, dp_n * chunk)), 'seq', 0,...  7.16 us
    unnamed x65, local copies, waits for them, and re-layouts  5.64 us
    all_to_all x1, starting transfers between devices, shards(): lax.all_to_all(jnp.broadcast_to(p_seq, (seq_n, dp_n * chunk)), 'seq', 0,...  5.09 us
  transfers between devices with their start and end apart: 4, of which 4 were waited for; matrix products, arithmetic and copies ran while one was open for 4% of the time, Pallas kernels for 0%

profile of v8, /device:TPU:1, one launch (start us, length us, event | category | flops | bytes accessed | tf_op | source)
XLA Modules:
  0.0 126.7 jit_solution(1820061071110605380)
XLA Ops:
  0.7 1.0 copy.182
  2.9 1.2 pad_maximum_fusion
  4.1 9.4 %all-to-all-start = ((f32[16,34,512]{2,1,0:T(8,128)}), f32[16,34,512]{2,1,0:T(8,128)S(1)}, u32[]{:S(2)}, u32[]{:S(2)}) async-start(f32[16,34,512]{2,1,0:T(8,128)} %pad_maximum_fusion), calls=%async_computation | async-start | bytes 2621440 | tf_op jit(solution)/shard_map/all_to_all | solution.py:101
  15.2 18.5 %all-to-all-done = f32[16,34,512]{2,1,0:T(8,128)S(1)} async-done(((f32[16,34,512]{2,1,0:T(8,128)}), f32[16,34,512]{2,1,0:T(8,128)S(1)}, u32[]{:S(2)}, u32[]{:S(2)}) %all-to-all-start) | async-done | bytes 1114144 | tf_op jit(solution)/shard_map/all_to_all | solution.py:101
  33.7 1.1 slice_bitcast_fusion.1
  35.7 1.6 %fusion.63 = f32[256,8,128]{0,2,1:T(8,128)} fusion(f32[256,64,1]{0,1,2:T(8,128)S(1)} %copy-done.15, f32[64,24,128]{2,0,1:T(8,128)S(1)} %bitcast.166), kind=kOutput, calls=%fused_computation.131 | convolution fusion | flops 100663296 | bytes 1376256 | tf_op jit(solution)/shard_map/kn,ncm->kcm/dot_general | solution.py:40
  37.4 1.6 %fusion.97 = f32[256,8,128]{0,2,1:T(8,128)} fusion(f32[256,64,1]{0,1,2:T(8,128)S(1)} %copy-done.15, f32[64,24,128]{2,0,1:T(8,128)S(1)} %bitcast.167, f32[64,8,128]{2,1,0:T(8,128)S(1)} %bitcast.178), kind=kOutput, calls=%fused_computation.194 | convolution fusion | flops 100728832 | bytes 1638400 | tf_op jit(solution)/shard_map/kn,ncm->kcm/dot_general | solution.py:40
  39.4 1.4 %multiply_subtract_fusion.7 = (f32[128,8,128]{0,2,1:T(8,128)S(1)}, f32[128,8,128]{0,2,1:T(8,128)S(1)}) fusion(f32[256,8,128]{0,2,1:T(8,128)} %fusion.97, f32[128,128]{0,1:T(8,128)S(1)} %copy-done.4, f32[128,128]{0,1:T(8,128)S(1)} %copy-done.3), kind=kLoop, calls=%fused_computation.94 | loop fusion | flops 786432 | bytes 2228224 | tf_op jit(solution)/shard_map/sub | solution.py:43
  41.3 1.0 fusion.24
  42.5 0.8 copy-done.1
  44.0 0.7 copy-done.14
  46.2 1.0 fusion.2
  47.3 1.0 fusion.35
  48.3 1.3 %multiply_subtract_fusion.1 = (f32[128,8,128]{2,0,1:T(8,128)}, f32[128,8,128]{2,0,1:T(8,128)}, f32[128,8,128]{2,0,1:T(8,128)S(1)}, f32[128,8,128]{2,0,1:T(8,128)...) fusion(f32[128,8,256]{2,0,1:T(8,128)S(1)} %fusion.35, f32[128,8,256]{2,0,1:T(8,128)S(1)} %fusion.2, ...), kind=kLoop, calls=%fused_computation.82 | loop fusion | flops 2490368 | bytes 5439488 | tf_op jit(solution)/shard_map/sub | solution.py:60
  51.1 0.6 convolution_add_fusion.3
  52.5 1.0 fusion.13
  53.6 1.4 %multiply_subtract_fusion = (f32[128,8,128]{2,0,1:T(8,128)}, f32[128,8,128]{2,0,1:T(8,128)}, f32[128,8,128]{2,0,1:T(8,128)S(1)}, f32[128,8,128]{2,0,1:T(8,128)S(1)}) fusion(f32[128,8,256]{2,0,1:T(8,128)S(1)} %fusion.24, f32[128,8,256]{2,0,1:T(8,128)S(1)} %fusion.13, f32[128,128]{1,0:T(8,128)S(1)} %get-tuple-element.68, f32[128,128]{1,0:T(8,128)S(1)} %get-tuple-element.67), kind=kLoop, calls=%fused_computation.80 | loop fusion | flops 1703936 | bytes 4325376 | tf_op jit(solution)/shard_map/sub | solution.py:60
  56.4 1.4 %multiply_reduce_fusion.3 = (f32[8]{0:T(128)S(1)}, f32[8]{0:T(128)S(1)}, bf16[64,8,128]{2,0,1:T(8,128)(2,1)}, f32[64,8,128]{2,0,1:T(8,128)S(1)}, f32[64,8,128]{2,0,1:T(8,128)S(1)}) fusion(f32[64,24,128]{2,0,1:T(8,128)S(1)} %bitcast.173, f32[64,8,128]{2,0,1:T(8,128)S(1)} %convolution_add_fusion.1, f32[64,8,128]{2,0,1:T(8,128)S(1)} %convolution_add_fusion.3, ...), kind=kOutput, calls=%fused_computation.125 | convolution fusion | flops 101777392 | bytes 3342432 | tf_op jit(solution)/shard_map/nk,kcm->ncm/dot_general | solution.py:52
  59.9 1.2 fusion.51
  62.3 1.1 copy.206
  63.4 4.2 %all-to-all-start.1 = ((bf16[16,32,512]{2,1,0:T(8,128)(2,1)}), bf16[16,32,512]{2,1,0:T(8,128)(2,1)S(1)}, u32[]{:S(2)}, u32[]{:S(2)}) async-start(bf16[16,32,512]{2,1,0:T(8,128)(2,1)} %copy.206), calls=%async_computation.1 | async-start | bytes 1048576 | tf_op jit(solution)/shard_map/all_to_all | solution.py:161
  68.7 10.3 %all-to-all-done.1 = bf16[16,32,512]{2,1,0:T(8,128)(2,1)S(1)} async-done(((bf16[16,32,512]{2,1,0:T(8,128)(2,1)}), bf16[16,32,512]{2,1,0:T(8,128)(2,1)S(1)}, u32[]{:S(2)}, u32[]{:S(2)}) %all-to-all-start.1) | async-done | bytes 524320 | tf_op jit(solution)/shard_map/all_to_all | solution.py:161
  80.7 12.8 %all_to_all.33 = f32[16,1,5216]{2,1,0:T(1,128)S(1)} all-to-all(f32[16,1,5216]{2,1,0:T(1,128)S(1)} %all_to_all.23), channel_id=1, replica_groups=mesh['dp'=8,'seq'=16] {'seq'}, dimensions={0} | all-to-all | bytes 667648 | tf_op jit(solution)/shard_map/all_to_all | solution.py:190
  94.0 0.8 broadcast_in_dim.30
  94.8 4.6 %all-to-all-start.3 = ((f32[8,8,1548]{2,1,0:T(8,128)}), f32[8,8,1548]{2,1,0:T(8,128)S(1)}, u32[]{:S(2)}, u32[]{:S(2)}) async-start(f32[8,8,1548]{2,1,0:T(8,128)} %broadcast_in_dim.30), calls=%async_computation.3 | async-start | bytes 851968 | tf_op jit(solution)/shard_map/all_to_all | solution.py:194
  99.4 1.0 fusion
  100.3 7.8 %all-to-all-done.3 = f32[8,8,1548]{2,1,0:T(8,128)S(1)} async-done(((f32[8,8,1548]{2,1,0:T(8,128)}), f32[8,8,1548]{2,1,0:T(8,128)S(1)}, u32[]{:S(2)}, u32[]{:S(2)}) %all-to-all-start.3) | async-done | bytes 396320 | tf_op jit(solution)/shard_map/all_to_all | solution.py:194
  108.3 0.8 broadcast_in_dim.32
  109.1 5.1 %all-to-all-start.4 = ((f32[16,1,4192]{2,1,0:T(1,128)}), f32[16,1,4192]{2,1,0:T(1,128)S(1)}, u32[]{:S(2)}, u32[]{:S(2)}) async-start(f32[16,1,4192]{2,1,0:T(1,128)} %broadcast_in_dim.32), calls=%async_computation.4 | async-start | bytes 540672 | tf_op jit(solution)/shard_map/all_to_all | solution.py:198
  114.2 0.9 fusion.1
  115.8 7.2 %all-to-all-done.4 = f32[16,1,4192]{2,1,0:T(1,128)S(1)} async-done(((f32[16,1,4192]{2,1,0:T(1,128)}), f32[16,1,4192]{2,1,0:T(1,128)S(1)}, u32[]{:S(2)}, u32[]{:S(2)}) %all-to-all-start.4) | async-done | bytes 268320 | tf_op jit(solution)/shard_map/all_to_all | solution.py:198
  124.7 0.7 mul.667
  (154 shorter events, 20.5 us)
Async XLA Ops:
  0.6 1.1 copy-start
  1.7 0.7 copy-start.22
  1.7 0.7 copy-start.23
  1.7 0.9 copy-start.17
  1.8 0.9 copy-start.20
  4.1 9.4 %copy-start.24 = (f32[3,384]{1,0:T(4,128)S(1)}, f32[3,384]{1,0:T(4,128)}, u32[]{:S(2)}) copy-start(f32[3,384]{1,0:T(4,128)} %param.19) | copy-start | bytes 13828
  4.1 9.8 %copy-start.26 = (f32[128]{0:T(128)S(1)}, f32[128]{0:T(128)}, u32[]{:S(2)}) copy-start(f32[128]{0:T(128)} %param.20) | copy-start | bytes 1540
  4.1 9.9 %copy-start.27 = (f32[128]{0:T(128)S(1)}, f32[128]{0:T(128)}, u32[]{:S(2)}) copy-start(f32[128]{0:T(128)} %param.21) | copy-start | bytes 1540
  4.1 29.6 %all-to-all-start = ((f32[16,34,512]{2,1,0:T(8,128)}), f32[16,34,512]{2,1,0:T(8,128)S(1)}, u32[]{:S(2)}, u32[]{:S(2)}) async-start(f32[16,34,512]{2,1,0:T(8,128)} %pad_maximum_fusion), calls=%async_computation | async-start | bytes 2621440 | tf_op jit(solution)/shard_map/all_to_all | solution.py:101
  34.9 0.8 copy-start.15
  37.3 2.0 %copy-start.3 = (f32[128,128]{0,1:T(8,128)S(1)}, f32[128,128]{0,1:T(8,128)}, u32[]{:S(2)}) copy-start(f32[128,128]{0,1:T(8,128)} %constant.45.clone) | copy-start | bytes 196612
  37.4 2.0 %copy-start.4 = (f32[128,128]{0,1:T(8,128)S(1)}, f32[128,128]{0,1:T(8,128)}, u32[]{:S(2)}) copy-start(f32[128,128]{0,1:T(8,128)} %constant.46.clone) | copy-start | bytes 196612
  39.4 1.4 %copy-start.2 = (f32[256,256,1]{1,0,2:T(8,128)S(1)}, f32[256,256,1]{1,0,2:T(8,128)}, u32[]{:S(2)}) copy-start(f32[256,256,1]{1,0,2:T(8,128)} %constant.59) | copy-start | bytes 786436
  42.3 1.0 copy-start.1
  43.9 0.8 copy-start.14
  43.9 0.8 copy-start.25
  44.7 1.2 copy-start.5
  56.4 2.6 %copy-start.9 = (f32[64,8,128]{2,0,1:T(8,128)}, f32[64,8,128]{2,0,1:T(8,128)S(1)}, u32[]{:S(2)}) copy-start(f32[64,8,128]{2,0,1:T(8,128)S(1)} %convolution_add_fusion) | copy-start | bytes 786436
  57.8 1.2 copy-start.6
  59.0 0.9 copy-start.8
  59.4 2.0 %copy-start.28 = (f32[3]{0:T(128)S(1)}, f32[3]{0:T(128)}, u32[]{:S(2)}) copy-start(f32[3]{0:T(128)} %pad.41.clone) | copy-start | bytes 40
  61.2 1.0 copy-start.16
  62.2 5.3 %copy-start.12 = (f32[128,8,128]{2,0,1:T(8,128)S(1)}, f32[128,8,128]{2,0,1:T(8,128)}, u32[]{:S(2)}) copy-start(f32[128,8,128]{2,0,1:T(8,128)} %get-tuple-element.16) | copy-start | bytes 1572868
  62.2 5.3 %copy-start.13 = (f32[128,8,128]{2,0,1:T(8,128)S(1)}, f32[128,8,128]{2,0,1:T(8,128)}, u32[]{:S(2)}) copy-start(f32[128,8,128]{2,0,1:T(8,128)} %get-tuple-element.17) | copy-start | bytes 1572868
  63.4 4.3 %copy-start.10 = (f32[128,8,128]{2,0,1:T(8,128)S(1)}, f32[128,8,128]{2,0,1:T(8,128)}, u32[]{:S(2)}) copy-start(f32[128,8,128]{2,0,1:T(8,128)} %get-tuple-element.18) | copy-start | bytes 1572868
  63.4 4.3 %copy-start.11 = (f32[128,8,128]{2,0,1:T(8,128)S(1)}, f32[128,8,128]{2,0,1:T(8,128)}, u32[]{:S(2)}) copy-start(f32[128,8,128]{2,0,1:T(8,128)} %get-tuple-element.19) | copy-start | bytes 1572868
  63.4 15.7 %all-to-all-start.1 = ((bf16[16,32,512]{2,1,0:T(8,128)(2,1)}), bf16[16,32,512]{2,1,0:T(8,128)(2,1)S(1)}, u32[]{:S(2)}, u32[]{:S(2)}) async-start(bf16[16,32,512]{2,1,0:T(8,128)(2,1)} %copy.206), calls=%async_computation.1 | async-start | bytes 1048576 | tf_op jit(solution)/shard_map/all_to_all | solution.py:161
  79.1 0.9 copy-start.18
  93.5 5.9 %copy-start.19 = (bf16[128,384]{1,0:T(8,128)(2,1)S(1)}, bf16[128,384]{1,0:T(8,128)(2,1)}, u32[]{:S(2)}) copy-start(bf16[128,384]{1,0:T(8,128)(2,1)} %param.17) | copy-start | bytes 294916
  94.8 19.5 %copy-start.21 = (bf16[128,128]{1,0:T(8,128)(2,1)S(1)}, bf16[128,128]{1,0:T(8,128)(2,1)}, u32[]{:S(2)}) copy-start(bf16[128,128]{1,0:T(8,128)(2,1)} %param.18) | copy-start | bytes 98308
  94.8 13.4 %all-to-all-start.3 = ((f32[8,8,1548]{2,1,0:T(8,128)}), f32[8,8,1548]{2,1,0:T(8,128)S(1)}, u32[]{:S(2)}, u32[]{:S(2)}) async-start(f32[8,8,1548]{2,1,0:T(8,128)} %broadcast_in_dim.30), calls=%async_computation.3 | async-start | bytes 851968 | tf_op jit(solution)/shard_map/all_to_all | solution.py:194
  109.1 13.8 %all-to-all-start.4 = ((f32[16,1,4192]{2,1,0:T(1,128)}), f32[16,1,4192]{2,1,0:T(1,128)S(1)}, u32[]{:S(2)}, u32[]{:S(2)}) async-start(f32[16,1,4192]{2,1,0:T(1,128)} %broadcast_in_dim.32), calls=%async_computation.4 | async-start | bytes 540672 | tf_op jit(solution)/shard_map/all_to_all | solution.py:198
  (1 other events, 0.7 us)

commit v9 on v8

--- a/solution.py
+++ b/solution.py
@@ -5,6 +5,8 @@
 import jax
 import jax.numpy as jnp
 from jax import lax
+from jax.experimental import pallas as pl
+from jax.experimental.pallas import tpu as pltpu
 from jax.sharding import PartitionSpec as P
 
 PRECISION = lax.Precision.HIGH
@@ -70,6 +72,75 @@
     return jnp.swapaxes(x, 0, 1).reshape(c, half * lanes)
 
 
+def reduce_rounds(msg, param_rows, pair, dp_n):
+    seq_n, msg_rows, lanes = msg.shape
+    filter_rows = msg_rows - param_rows
+    groups = seq_n // pair
+    mesh = pl.DeviceIdType.MESH
+
+    def kernel(msg_ref, full_ref, fg_ref, rs_buf, ag_buf, sems):
+        ms = lax.axis_index("seq")
+        md = lax.axis_index("dp")
+        barrier = pltpu.get_barrier_semaphore()
+        for k in range(1, seq_n):
+            pl.semaphore_signal(barrier, inc=1, device_id=(md, lax.rem(ms + k, seq_n)), device_id_type=mesh)
+        for k in range(1, dp_n):
+            pl.semaphore_signal(barrier, inc=1, device_id=(lax.rem(md + k, dp_n), ms), device_id_type=mesh)
+        pl.semaphore_wait(barrier, seq_n + dp_n - 2)
+
+        def send_all(count, src, dst, stage, where):
+            copies = []
+            for k in range(1, count):
+                copy = pltpu.make_async_remote_copy(
+                    src_ref=src(k), dst_ref=dst, send_sem=sems.at[stage, 0, k],
+                    recv_sem=sems.at[stage, 1, k], device_id=where(k), device_id_type=mesh,
+                )
+                copy.start()
+                copies.append(copy)
+            return copies
+
+        seq_peer = lambda k: (md, lax.rem(ms + k, seq_n))
+        dp_peer = lambda k: (lax.rem(md + k, dp_n), ms)
+
+        copies = send_all(seq_n, lambda k: msg_ref.at[lax.rem(ms + k, seq_n)], rs_buf.at[ms], 0, seq_peer)
+        rs_buf[pl.ds(ms, 1)] = msg_ref[pl.ds(ms, 1)]
+        for copy in copies:
+            copy.wait()
+        got = rs_buf[...]
+        p_sum = jnp.sum(got[:, :param_rows], axis=0)
+        f_sum = jnp.sum(got[:, param_rows:].reshape(groups, pair, filter_rows, lanes), axis=1)
+        mine = jnp.concatenate([p_sum, f_sum.reshape(groups * filter_rows, lanes)], axis=0)
+
+        ag_buf[pl.ds(md, 1)] = mine[None]
+        copies = send_all(dp_n, lambda k: ag_buf.at[md], ag_buf.at[md], 1, dp_peer)
+        for copy in copies:
+            copy.wait()
+        total = jnp.sum(ag_buf[...], axis=0)
+        fg_ref[...] = total[param_rows:].reshape(groups, filter_rows, lanes)
+
+        full_ref[pl.ds(ms, 1)] = total[:param_rows][None]
+        copies = send_all(seq_n, lambda k: full_ref.at[ms], full_ref.at[ms], 2, seq_peer)
+        for copy in copies:
+            copy.wait()
+
+    ag_rows = param_rows + groups * filter_rows
+    return pl.pallas_call(
+        kernel,
+        out_shape=(
+            jax.ShapeDtypeStruct((seq_n, param_rows, lanes), msg.dtype),
+            jax.ShapeDtypeStruct((groups, filter_rows, lanes), msg.dtype),
+        ),
+        in_specs=[pl.BlockSpec(memory_space=pltpu.VMEM)],
+        out_specs=(pl.BlockSpec(memory_space=pltpu.VMEM), pl.BlockSpec(memory_space=pltpu.VMEM)),
+        scratch_shapes=[
+            pltpu.VMEM((seq_n, msg_rows, lanes), msg.dtype),
+            pltpu.VMEM((dp_n, ag_rows, lanes), msg.dtype),
+            pltpu.SemaphoreType.DMA((3, 2, max(seq_n, dp_n))),
+        ],
+        compiler_params=pltpu.CompilerParams(collective_id=0, has_side_effects=True),
+    )(msg)
+
+
 def shards(series, cotangent, w_in, w_out, taps, skip_one, skip_two, filter_one, filter_two):
     _, block, width = series.shape
     seq_n = lax.axis_size("seq")
@@ -183,20 +254,12 @@
     )
     params = jnp.concatenate([local_w_in.reshape(-1), local_w_out.reshape(-1), small_full.reshape(-1)])
     n_params = params.shape[0]
-    chunk = -(-n_params // (seq_n * dp_n))
-    params = jnp.pad(params, (0, chunk * seq_n * dp_n - n_params)).reshape(seq_n, dp_n * chunk)
-
-    fg_sent = jnp.swapaxes(filt_grad.reshape(2, seq_n, block), 0, 1).reshape(seq_n, 2 * block)
-    got = lax.all_to_all(jnp.concatenate([params, fg_sent], axis=1), "seq", 0, 0, tiled=True)
-    p_part = jnp.sum(got[:, : dp_n * chunk], axis=0).reshape(dp_n, chunk)
-    f_part = jnp.sum(got[:, dp_n * chunk :].reshape(filters, per_group, 2 * block), axis=1)
-    both = jnp.concatenate([p_part, f_part], axis=1)
-    got = lax.all_to_all(jnp.broadcast_to(both, (dp_n,) + both.shape), "dp", 0, 0, tiled=True)
-    got = jnp.sum(got.reshape((dp_n,) + both.shape), axis=0)
-    fg_blocks = jnp.swapaxes(got[:, chunk:].reshape(filters, 2, block), 0, 1)
-    p_seq = got[:, :chunk].reshape(1, dp_n * chunk)
-    got = lax.all_to_all(jnp.broadcast_to(p_seq, (seq_n, dp_n * chunk)), "seq", 0, 0, tiled=True)
-    full = got.reshape(-1)
+    chunk = -(-n_params // (seq_n * dp_n * 8 * LANES)) * 8 * LANES
+    params = jnp.pad(params, (0, chunk * seq_n * dp_n - n_params)).reshape(seq_n, -1, LANES)
+    fg_sent = jnp.swapaxes(filt_grad.reshape(2, seq_n, block), 0, 1).reshape(seq_n, -1, LANES)
+    full, fg = reduce_rounds(jnp.concatenate([params, fg_sent], axis=1), params.shape[1], per_group, dp_n)
+    fg_blocks = jnp.swapaxes(fg.reshape(filters, 2, block), 0, 1)
+    full = full.reshape(-1)
     sizes = [width * 3 * width, width * width, 3 * 4 * width]
     offsets = np.cumsum([0] + sizes)
     grad_w_in = full[offsets[0] : offsets[1]].reshape(width, 3 * width)

time: 128 us -> 124 us (0.969)
  Pallas kernels: 0 us -> 33.6 us
  waiting for transfers between devices: 43.8 us -> 28.8 us
  blocking collectives: 12.8 us -> 0 us
  starting transfers between devices: 23.3 us -> 13.6 us
  other arithmetic: 12.3 us -> 15.4 us
  local copies, waits for them, and re-layouts: 14.6 us -> 11.7 us
    pallas_call x0 -> x1, Pallas kernels: none -> 33.6 us  [reduce_rounds(): pl.pallas_call(kernel, out_shape=(jax.ShapeDtypeStruct((seq_n, param_rows...]
    all_to_all x2 -> x0, waiting for transfers between devices: 15 us -> none  [the longest x1 7.83 us: shards(): lax.all_to_all(jnp.broadcast_to(both, (dp_n,) + both.shape), 'dp', 0, 0,...]
    all_to_all x1 -> x0, blocking collectives: 12.8 us -> none  [shards(): lax.all_to_all(jnp.concatenate([params, fg_sent], axis=1), 'seq', 0, 0, t...]
    all_to_all x2 -> x0, starting transfers between devices: 9.7 us -> none  [the longest x1 5.09 us: shards(): lax.all_to_all(jnp.broadcast_to(p_seq, (seq_n, dp_n * chunk)), 'seq', 0,...]
    broadcast_in_dim x3 -> x0, local copies, waits for them, and re-layouts: 1.72 us -> none  [the longest x2 0.92 us: shards(): jnp.broadcast_to(p_seq, (seq_n, dp_n * chunk))]
  transfers between devices with their start and end apart: 4 -> 2, of which waited for: 4 -> 2; matrix products, arithmetic and copies ran while one was open for 4% -> 2% of each run, Pallas kernels for 0% -> 0%
where the time goes in v9:
time: 124 us; the launch traced here: 123 us
  Pallas kernels  33.6 us (27%)
  waiting for transfers between devices  28.8 us (23%)
  matrix products  18.3 us (15%)
  other arithmetic  15.4 us (12%)
  starting transfers between devices  13.6 us (11%)
  local copies, waits for them, and re-layouts  11.7 us (9%)
  between operations  1.41 us (1%)
    pallas_call x1, Pallas kernels, reduce_rounds(): pl.pallas_call(kernel, out_shape=(jax.ShapeDtypeStruct((seq_n, param_rows...  33.6 us
    all_to_all x1, waiting for transfers between devices, shards(): lax.all_to_all(jnp.concatenate([proj_blk, dprod_blk, rows_sent], axis=1),...  18.5 us
    all_to_all x1, waiting for transfers between devices, shards(): lax.all_to_all(jnp.concatenate([prod_sent, dp_sent], axis=1), 'seq', 0, 0...  10.3 us
    all_to_all x1, starting transfers between devices, shards(): lax.all_to_all(jnp.concatenate([proj_blk, dprod_blk, rows_sent], axis=1),...  9.43 us
    unnamed x65, local copies, waits for them, and re-layouts  5.59 us
    dot_general x5, matrix products, spectrum(): a = jnp.einsum('kn,ncm->kcm', tab['fwd1'], x, precision=PRECISION)  4.77 us
    dot_general x5, matrix products, spectrum(): return jnp.einsum('kcm,mj->kcj', cat, tab['fwd2'], precision=PRECISION)  4.48 us
    all_to_all x1, starting transfers between devices, shards(): lax.all_to_all(jnp.concatenate([prod_sent, dp_sent], axis=1), 'seq', 0, 0...  4.21 us
  transfers between devices with their start and end apart: 2, of which 2 were waited for; matrix products, arithmetic and copies ran while one was open for 2% of the time, Pallas kernels for 0%

profile of v9, /device:TPU:1, one launch (start us, length us, event | category | flops | bytes accessed | tf_op | source)
XLA Modules:
  0.0 122.8 jit_solution(3479706917198049863)
XLA Ops:
  0.7 1.0 copy.153
  2.9 1.2 pad_maximum_fusion
  4.1 9.4 %all-to-all-start = ((f32[16,34,512]{2,1,0:T(8,128)}), f32[16,34,512]{2,1,0:T(8,128)S(1)}, u32[]{:S(2)}, u32[]{:S(2)}) async-start(f32[16,34,512]{2,1,0:T(8,128)} %pad_maximum_fusion), calls=%async_computation | async-start | bytes 2621440 | tf_op jit(solution)/shard_map/all_to_all | solution.py:172
  15.2 18.5 %all-to-all-done = f32[16,34,512]{2,1,0:T(8,128)S(1)} async-done(((f32[16,34,512]{2,1,0:T(8,128)}), f32[16,34,512]{2,1,0:T(8,128)S(1)}, u32[]{:S(2)}, u32[]{:S(2)}) %all-to-all-start) | async-done | bytes 1114144 | tf_op jit(solution)/shard_map/all_to_all | solution.py:172
  33.7 1.1 slice_bitcast_fusion.1
  35.7 1.6 %fusion.63 = f32[256,8,128]{0,2,1:T(8,128)} fusion(f32[256,64,1]{0,1,2:T(8,128)S(1)} %copy-done.15, f32[64,24,128]{2,0,1:T(8,128)S(1)} %bitcast.166), kind=kOutput, calls=%fused_computation.131 | convolution fusion | flops 100663296 | bytes 1376256 | tf_op jit(solution)/shard_map/kn,ncm->kcm/dot_general | solution.py:42
  37.4 1.6 %fusion.97 = f32[256,8,128]{0,2,1:T(8,128)} fusion(f32[256,64,1]{0,1,2:T(8,128)S(1)} %copy-done.15, f32[64,24,128]{2,0,1:T(8,128)S(1)} %bitcast.167, f32[64,8,128]{2,1,0:T(8,128)S(1)} %bitcast.178), kind=kOutput, calls=%fused_computation.195 | convolution fusion | flops 100728832 | bytes 1638400 | tf_op jit(solution)/shard_map/kn,ncm->kcm/dot_general | solution.py:42
  39.4 1.4 %multiply_subtract_fusion.7 = (f32[128,8,128]{0,2,1:T(8,128)S(1)}, f32[128,8,128]{0,2,1:T(8,128)S(1)}) fusion(f32[256,8,128]{0,2,1:T(8,128)} %fusion.97, f32[128,128]{0,1:T(8,128)S(1)} %copy-done.4, f32[128,128]{0,1:T(8,128)S(1)} %copy-done.3), kind=kLoop, calls=%fused_computation.98 | loop fusion | flops 786432 | bytes 2228224 | tf_op jit(solution)/shard_map/sub | solution.py:45
  41.3 1.0 fusion.24
  42.4 0.8 copy-done.1
  44.0 0.7 copy-done.14
  46.2 1.0 fusion.2
  47.2 1.0 fusion.35
  48.3 1.4 %multiply_subtract_fusion.1 = (f32[128,8,128]{2,0,1:T(8,128)}, f32[128,8,128]{2,0,1:T(8,128)}, f32[128,8,128]{2,0,1:T(8,128)S(1)}, f32[128,8,128]{2,0,1:T(8,128)...) fusion(f32[128,8,256]{2,0,1:T(8,128)S(1)} %fusion.35, f32[128,8,256]{2,0,1:T(8,128)S(1)} %fusion.2, ...), kind=kLoop, calls=%fused_computation.86 | loop fusion | flops 2490368 | bytes 5439488 | tf_op jit(solution)/shard_map/sub | solution.py:62
  51.1 0.6 convolution_add_fusion.3
  52.5 1.0 fusion.13
  53.6 1.4 %multiply_subtract_fusion = (f32[128,8,128]{2,0,1:T(8,128)}, f32[128,8,128]{2,0,1:T(8,128)}, f32[128,8,128]{2,0,1:T(8,128)S(1)}, f32[128,8,128]{2,0,1:T(8,128)S(1)}) fusion(f32[128,8,256]{2,0,1:T(8,128)S(1)} %fusion.24, f32[128,8,256]{2,0,1:T(8,128)S(1)} %fusion.13, f32[128,128]{1,0:T(8,128)S(1)} %get-tuple-element.72, f32[128,128]{1,0:T(8,128)S(1)} %get-tuple-element.71), kind=kLoop, calls=%fused_computation.84 | loop fusion | flops 1703936 | bytes 4325376 | tf_op jit(solution)/shard_map/sub | solution.py:62
  54.9 0.6 fusion.17
  56.3 1.4 %multiply_reduce_fusion.3 = (f32[8]{0:T(128)S(1)}, f32[8]{0:T(128)S(1)}, bf16[64,8,128]{2,0,1:T(8,128)(2,1)}, f32[64,8,128]{2,0,1:T(8,128)S(1)}, f32[64,8,128]{2,0,1:T(8,128)S(1)}) fusion(f32[64,24,128]{2,0,1:T(8,128)S(1)} %bitcast.173, f32[64,8,128]{2,0,1:T(8,128)S(1)} %convolution_add_fusion.1, f32[64,8,128]{2,0,1:T(8,128)S(1)} %convolution_add_fusion.3, ...), kind=kOutput, calls=%fused_computation.125 | convolution fusion | flops 101777392 | bytes 3342432 | tf_op jit(solution)/shard_map/nk,kcm->ncm/dot_general | solution.py:54
  59.9 1.2 fusion.51
  62.2 1.1 copy.177
  63.3 4.2 %all-to-all-start.1 = ((bf16[16,32,512]{2,1,0:T(8,128)(2,1)}), bf16[16,32,512]{2,1,0:T(8,128)(2,1)S(1)}, u32[]{:S(2)}, u32[]{:S(2)}) async-start(bf16[16,32,512]{2,1,0:T(8,128)(2,1)} %copy.177), calls=%async_computation.1 | async-start | bytes 1048576 | tf_op jit(solution)/shard_map/all_to_all | solution.py:232
  68.7 10.3 %all-to-all-done.1 = bf16[16,32,512]{2,1,0:T(8,128)(2,1)S(1)} async-done(((bf16[16,32,512]{2,1,0:T(8,128)(2,1)}), bf16[16,32,512]{2,1,0:T(8,128)(2,1)S(1)}, u32[]{:S(2)}, u32[]{:S(2)}) %all-to-all-start.1) | async-done | bytes 524320 | tf_op jit(solution)/shard_map/all_to_all | solution.py:232
  80.2 0.9 pad_maximum_fusion.2.msg_ref
  81.1 33.6 %shard_map.214 = (f32[16,64,128]{2,1,0:T(8,128)}, f32[8,8,128]{2,1,0:T(8,128)}) custom-call(f32[16,72,128]{2,1,0:T(8,128)} %pad_maximum_fusion.2.msg_ref), custom_call_target="tpu_custom_call" | custom-call | tf_op jit(solution)/shard_map/pallas_call | solution.py:127
  114.7 0.9 slice_multiply_fusion.3
  115.6 1.5 %slice_multiply_fusion.4 = f32[2,64,128]{2,1,0:T(8,128)} fusion(f32[16,64,128]{2,1,0:T(8,128)} %get-tuple-element.11), kind=kLoop, calls=%fused_computation.150 | loop fusion | flops 16384 | bytes 131072 | tf_op jit(solution)/shard_map/mul | solution.py:276
  117.1 0.7 fusion.75
  117.8 1.2 fusion.78
  119.0 1.0 fusion
  120.0 0.7 mul.670
  121.9 0.9 fusion.1
  (135 shorter events, 16.5 us)
Async XLA Ops:
  0.6 1.1 copy-start
  1.7 0.7 copy-start.23
  1.7 0.7 copy-start.24
  1.7 0.9 copy-start.17
  1.8 0.9 copy-start.20
  4.1 9.4 %copy-start.25 = (f32[3,384]{1,0:T(4,128)S(1)}, f32[3,384]{1,0:T(4,128)}, u32[]{:S(2)}) copy-start(f32[3,384]{1,0:T(4,128)} %param.19) | copy-start | bytes 13828
  4.1 9.8 %copy-start.27 = (f32[128]{0:T(128)S(1)}, f32[128]{0:T(128)}, u32[]{:S(2)}) copy-start(f32[128]{0:T(128)} %param.20) | copy-start | bytes 1540
  4.1 9.9 %copy-start.28 = (f32[128]{0:T(128)S(1)}, f32[128]{0:T(128)}, u32[]{:S(2)}) copy-start(f32[128]{0:T(128)} %param.21) | copy-start | bytes 1540
  4.1 29.6 %all-to-all-start = ((f32[16,34,512]{2,1,0:T(8,128)}), f32[16,34,512]{2,1,0:T(8,128)S(1)}, u32[]{:S(2)}, u32[]{:S(2)}) async-start(f32[16,34,512]{2,1,0:T(8,128)} %pad_maximum_fusion), calls=%async_computation | async-start | bytes 2621440 | tf_op jit(solution)/shard_map/all_to_all | solution.py:172
  34.8 0.8 copy-start.15
  37.3 2.0 %copy-start.3 = (f32[128,128]{0,1:T(8,128)S(1)}, f32[128,128]{0,1:T(8,128)}, u32[]{:S(2)}) copy-start(f32[128,128]{0,1:T(8,128)} %constant.45.clone) | copy-start | bytes 196612
  37.4 2.0 %copy-start.4 = (f32[128,128]{0,1:T(8,128)S(1)}, f32[128,128]{0,1:T(8,128)}, u32[]{:S(2)}) copy-start(f32[128,128]{0,1:T(8,128)} %constant.46.clone) | copy-start | bytes 196612
  39.4 1.4 %copy-start.2 = (f32[256,256,1]{1,0,2:T(8,128)S(1)}, f32[256,256,1]{1,0,2:T(8,128)}, u32[]{:S(2)}) copy-start(f32[256,256,1]{1,0,2:T(8,128)} %constant.61) | copy-start | bytes 786436
  42.3 1.0 copy-start.1
  43.9 0.8 copy-start.14
  43.9 0.8 copy-start.26
  44.7 1.2 %copy-start.5 = (f32[256,8,128]{0,2,1:T(8,128)S(1)}, f32[256,8,128]{0,2,1:T(8,128)}, u32[]{:S(2)}) copy-start(f32[256,8,128]{0,2,1:T(8,128)} %fusion.63) | copy-start | bytes 3145732
  56.3 2.6 %copy-start.9 = (f32[64,8,128]{2,0,1:T(8,128)}, f32[64,8,128]{2,0,1:T(8,128)S(1)}, u32[]{:S(2)}) copy-start(f32[64,8,128]{2,0,1:T(8,128)S(1)} %convolution_add_fusion) | copy-start | bytes 786436
  57.7 0.7 copy-start.7
  57.8 1.2 copy-start.6
  58.9 0.9 copy-start.8
  59.4 2.0 %copy-start.29 = (f32[3]{0:T(128)S(1)}, f32[3]{0:T(128)}, u32[]{:S(2)}) copy-start(f32[3]{0:T(128)} %pad.44.clone) | copy-start | bytes 40
  61.1 1.0 copy-start.16
  62.2 5.3 %copy-start.12 = (f32[128,8,128]{2,0,1:T(8,128)S(1)}, f32[128,8,128]{2,0,1:T(8,128)}, u32[]{:S(2)}) copy-start(f32[128,8,128]{2,0,1:T(8,128)} %get-tuple-element.20) | copy-start | bytes 1572868
  62.2 5.3 %copy-start.13 = (f32[128,8,128]{2,0,1:T(8,128)S(1)}, f32[128,8,128]{2,0,1:T(8,128)}, u32[]{:S(2)}) copy-start(f32[128,8,128]{2,0,1:T(8,128)} %get-tuple-element.21) | copy-start | bytes 1572868
  63.3 4.3 %copy-start.10 = (f32[128,8,128]{2,0,1:T(8,128)S(1)}, f32[128,8,128]{2,0,1:T(8,128)}, u32[]{:S(2)}) copy-start(f32[128,8,128]{2,0,1:T(8,128)} %get-tuple-element.22) | copy-start | bytes 1572868
  63.3 4.3 %copy-start.11 = (f32[128,8,128]{2,0,1:T(8,128)S(1)}, f32[128,8,128]{2,0,1:T(8,128)}, u32[]{:S(2)}) copy-start(f32[128,8,128]{2,0,1:T(8,128)} %get-tuple-element.23) | copy-start | bytes 1572868
  63.3 15.7 %all-to-all-start.1 = ((bf16[16,32,512]{2,1,0:T(8,128)(2,1)}), bf16[16,32,512]{2,1,0:T(8,128)(2,1)S(1)}, u32[]{:S(2)}, u32[]{:S(2)}) async-start(bf16[16,32,512]{2,1,0:T(8,128)(2,1)} %copy.177), calls=%async_computation.1 | async-start | bytes 1048576 | tf_op jit(solution)/shard_map/all_to_all | solution.py:232
  79.0 0.9 copy-start.18
  80.2 38.8 %copy-start.19 = (bf16[128,384]{1,0:T(8,128)(2,1)S(1)}, bf16[128,384]{1,0:T(8,128)(2,1)}, u32[]{:S(2)}) copy-start(bf16[128,384]{1,0:T(8,128)(2,1)} %param.17) | copy-start | bytes 294916
  81.1 40.9 %copy-start.21 = (bf16[128,128]{1,0:T(8,128)(2,1)S(1)}, bf16[128,128]{1,0:T(8,128)(2,1)}, u32[]{:S(2)}) copy-start(bf16[128,128]{1,0:T(8,128)(2,1)} %param.18) | copy-start | bytes 98308
  114.7 6.0 %copy-start.22 = (f32[8,8,128]{2,1,0:T(8,128)S(1)}, f32[8,8,128]{2,1,0:T(8,128)}, u32[]{:S(2)}) copy-start(f32[8,8,128]{2,1,0:T(8,128)} %get-tuple-element.12) | copy-start | bytes 98308

commit v10 on v9

--- a/solution.py
+++ b/solution.py
@@ -254,8 +254,8 @@
     )
     params = jnp.concatenate([local_w_in.reshape(-1), local_w_out.reshape(-1), small_full.reshape(-1)])
     n_params = params.shape[0]
-    chunk = -(-n_params // (seq_n * dp_n * 8 * LANES)) * 8 * LANES
-    params = jnp.pad(params, (0, chunk * seq_n * dp_n - n_params)).reshape(seq_n, -1, LANES)
+    chunk = -(-n_params // (seq_n * 8 * LANES)) * 8 * LANES
+    params = jnp.pad(params, (0, chunk * seq_n - n_params)).reshape(seq_n, -1, LANES)
     fg_sent = jnp.swapaxes(filt_grad.reshape(2, seq_n, block), 0, 1).reshape(seq_n, -1, LANES)
     full, fg = reduce_rounds(jnp.concatenate([params, fg_sent], axis=1), params.shape[1], per_group, dp_n)
     fg_blocks = jnp.swapaxes(fg.reshape(filters, 2, block), 0, 1)

time: 124 us -> 117 us (0.944)
  Pallas kernels: 33.6 us -> 27.4 us
    pallas_call x1, Pallas kernels: 33.6 us -> 27.4 us  [reduce_rounds(): pl.pallas_call(kernel, out_shape=(jax.ShapeDtypeStruct((seq_n, param_rows...]
where the time goes in v10:
time: 117 us; the launch traced here: 116 us
  waiting for transfers between devices  28.8 us (25%)
  Pallas kernels  27.4 us (23%)
  matrix products  18.3 us (16%)
  other arithmetic  15.2 us (13%)
  starting transfers between devices  13.6 us (12%)
  local copies, waits for them, and re-layouts  11.7 us (10%)
  between operations  1.41 us (1%)
    pallas_call x1, Pallas kernels, reduce_rounds(): pl.pallas_call(kernel, out_shape=(jax.ShapeDtypeStruct((seq_n, param_rows...  27.4 us
    all_to_all x1, waiting for transfers between devices, shards(): lax.all_to_all(jnp.concatenate([proj_blk, dprod_blk, rows_sent], axis=1),...  18.5 us
    all_to_all x1, waiting for transfers between devices, shards(): lax.all_to_all(jnp.concatenate([prod_sent, dp_sent], axis=1), 'seq', 0, 0...  10.3 us
    all_to_all x1, starting transfers between devices, shards(): lax.all_to_all(jnp.concatenate([proj_blk, dprod_blk, rows_sent], axis=1),...  9.43 us
    unnamed x65, local copies, waits for them, and re-layouts  5.59 us
    dot_general x5, matrix products, spectrum(): a = jnp.einsum('kn,ncm->kcm', tab['fwd1'], x, precision=PRECISION)  4.77 us
    dot_general x5, matrix products, spectrum(): return jnp.einsum('kcm,mj->kcj', cat, tab['fwd2'], precision=PRECISION)  4.48 us
    all_to_all x1, starting transfers between devices, shards(): lax.all_to_all(jnp.concatenate([prod_sent, dp_sent], axis=1), 'seq', 0, 0...  4.21 us
  transfers between devices with their start and end apart: 2, of which 2 were waited for; matrix products, arithmetic and copies ran while one was open for 2% of the time, Pallas kernels for 0%

profile of v10, /device:TPU:1, one launch (start us, length us, event | category | flops | bytes accessed | tf_op | source)
XLA Modules:
  0.0 116.4 jit_solution(18168429252764986801)
XLA Ops:
  0.7 1.0 copy.153
  2.9 1.2 %pad_maximum_fusion = f32[16,34,512]{2,1,0:T(8,128)} fusion(f32[16,2,512]{2,1,0:T(2,128)S(1)} %bitcast.193, f32[16,8,512]{2,1,0:T(8,128)S(1)} %fusion.66, f32[16,24,512]{2,1,0:T(8,128)S(1)} %bitcast.185), kind=kLoop, calls=%fused_computation.1 | loop fusion | flops 557056 | bytes 2228224 | tf_op jit(solution)/shard_map/concatenate | solution.py:173
  4.1 9.4 %all-to-all-start = ((f32[16,34,512]{2,1,0:T(8,128)}), f32[16,34,512]{2,1,0:T(8,128)S(1)}, u32[]{:S(2)}, u32[]{:S(2)}) async-start(f32[16,34,512]{2,1,0:T(8,128)} %pad_maximum_fusion), calls=%async_computation | async-start | bytes 2621440 | tf_op jit(solution)/shard_map/all_to_all | solution.py:172
  15.2 18.5 %all-to-all-done = f32[16,34,512]{2,1,0:T(8,128)S(1)} async-done(((f32[16,34,512]{2,1,0:T(8,128)}), f32[16,34,512]{2,1,0:T(8,128)S(1)}, u32[]{:S(2)}, u32[]{:S(2)}) %all-to-all-start) | async-done | bytes 1114144 | tf_op jit(solution)/shard_map/all_to_all | solution.py:172
  33.7 1.1 slice_bitcast_fusion.1
  35.7 1.6 %fusion.63 = f32[256,8,128]{0,2,1:T(8,128)} fusion(f32[256,64,1]{0,1,2:T(8,128)S(1)} %copy-done.15, f32[64,24,128]{2,0,1:T(8,128)S(1)} %bitcast.167), kind=kOutput, calls=%fused_computation.131 | convolution fusion | flops 100663296 | bytes 1376256 | tf_op jit(solution)/shard_map/kn,ncm->kcm/dot_general | solution.py:42
  37.4 1.6 %fusion.97 = f32[256,8,128]{0,2,1:T(8,128)} fusion(f32[256,64,1]{0,1,2:T(8,128)S(1)} %copy-done.15, f32[64,24,128]{2,0,1:T(8,128)S(1)} %bitcast.168, f32[64,8,128]{2,1,0:T(8,128)S(1)} %bitcast.179), kind=kOutput, calls=%fused_computation.195 | convolution fusion | flops 100728832 | bytes 1638400 | tf_op jit(solution)/shard_map/kn,ncm->kcm/dot_general | solution.py:42
  39.4 1.4 %multiply_subtract_fusion.7 = (f32[128,8,128]{0,2,1:T(8,128)S(1)}, f32[128,8,128]{0,2,1:T(8,128)S(1)}) fusion(f32[256,8,128]{0,2,1:T(8,128)} %fusion.97, f32[128,128]{0,1:T(8,128)S(1)} %copy-done.4, f32[128,128]{0,1:T(8,128)S(1)} %copy-done.3), kind=kLoop, calls=%fused_computation.94 | loop fusion | flops 786432 | bytes 2228224 | tf_op jit(solution)/shard_map/sub | solution.py:45
  41.3 1.0 fusion.24
  42.4 0.8 copy-done.1
  44.0 0.7 copy-done.14
  46.2 1.0 fusion.2
  47.2 1.0 fusion.35
  48.3 1.4 %multiply_subtract_fusion.1 = (f32[128,8,128]{2,0,1:T(8,128)}, f32[128,8,128]{2,0,1:T(8,128)}, f32[128,8,128]{2,0,1:T(8,128)S(1)}, f32[128,8,128]{2,0,1:T(8,128)...) fusion(f32[128,8,256]{2,0,1:T(8,128)S(1)} %fusion.35, f32[128,8,256]{2,0,1:T(8,128)S(1)} %fusion.2, ...), kind=kLoop, calls=%fused_computation.82 | loop fusion | flops 2490368 | bytes 5439488 | tf_op jit(solution)/shard_map/sub | solution.py:62
  51.1 0.6 convolution_add_fusion.3
  52.5 1.0 fusion.13
  53.6 1.4 %multiply_subtract_fusion = (f32[128,8,128]{2,0,1:T(8,128)}, f32[128,8,128]{2,0,1:T(8,128)}, f32[128,8,128]{2,0,1:T(8,128)S(1)}, f32[128,8,128]{2,0,1:T(8,128)S(1)}) fusion(f32[128,8,256]{2,0,1:T(8,128)S(1)} %fusion.24, f32[128,8,256]{2,0,1:T(8,128)S(1)} %fusion.13, f32[128,128]{1,0:T(8,128)S(1)} %get-tuple-element.72, f32[128,128]{1,0:T(8,128)S(1)} %get-tuple-element.71), kind=kLoop, calls=%fused_computation.80 | loop fusion | flops 1703936 | bytes 4325376 | tf_op jit(solution)/shard_map/sub | solution.py:62
  54.9 0.6 fusion.17
  56.3 1.4 %multiply_reduce_fusion.3 = (f32[8]{0:T(128)S(1)}, f32[8]{0:T(128)S(1)}, bf16[64,8,128]{2,0,1:T(8,128)(2,1)}, f32[64,8,128]{2,0,1:T(8,128)S(1)}, f32[64,8,128]{2,0,1:T(8,128)S(1)}) fusion(f32[64,24,128]{2,0,1:T(8,128)S(1)} %bitcast.174, f32[64,8,128]{2,0,1:T(8,128)S(1)} %convolution_add_fusion.1, f32[64,8,128]{2,0,1:T(8,128)S(1)} %convolution_add_fusion.3, ...), kind=kOutput, calls=%fused_computation.125 | convolution fusion | flops 101777392 | bytes 3342432 | tf_op jit(solution)/shard_map/nk,kcm->ncm/dot_general | solution.py:54
  59.9 1.2 %fusion.51 = f32[24]{0:T(128)S(1)} fusion(f32[24,64,128]{2,1,0:T(8,128)S(1)} %reshape.164, f32[64,8,128]{2,0,1:T(8,128)S(1)} %get-tuple-element.61, f32[64,8,128]{2,0,1:T(8,128)S(1)} %copy-done.8, f32[64,8,128]{2,0,1:T(8,128)} %copy-done.9), kind=kLoop, calls=%fused_computation.71 | loop fusion | flops 786408 | bytes 1572960 | tf_op jit(solution)/shard_map/reduce_sum | solution.py:225
  62.2 1.1 copy.177
  63.3 4.2 %all-to-all-start.1 = ((bf16[16,32,512]{2,1,0:T(8,128)(2,1)}), bf16[16,32,512]{2,1,0:T(8,128)(2,1)S(1)}, u32[]{:S(2)}, u32[]{:S(2)}) async-start(bf16[16,32,512]{2,1,0:T(8,128)(2,1)} %copy.177), calls=%async_computation.1 | async-start | bytes 1048576 | tf_op jit(solution)/shard_map/all_to_all | solution.py:232
  68.7 10.3 %all-to-all-done.1 = bf16[16,32,512]{2,1,0:T(8,128)(2,1)S(1)} async-done(((bf16[16,32,512]{2,1,0:T(8,128)(2,1)}), bf16[16,32,512]{2,1,0:T(8,128)(2,1)S(1)}, u32[]{:S(2)}, u32[]{:S(2)}) %all-to-all-start.1) | async-done | bytes 524320 | tf_op jit(solution)/shard_map/all_to_all | solution.py:232
  80.2 0.8 pad_maximum_fusion.3.msg_ref
  80.9 27.4 %shard_map.214 = (f32[16,40,128]{2,1,0:T(8,128)}, f32[8,8,128]{2,1,0:T(8,128)}) custom-call(f32[16,48,128]{2,1,0:T(8,128)} %pad_maximum_fusion.3.msg_ref), custom_call_target="tpu_custom_call" | custom-call | tf_op jit(solution)/shard_map/pallas_call | solution.py:127
  108.3 0.7 fusion.75
  109.0 1.2 %fusion.78 = (f32[128]{0:T(128)}, f32[128]{0:T(128)}) fusion(f32[160,4,128]{2,1,0:T(4,128)} %bitcast.196), kind=kLoop, calls=%fused_computation.175 | loop fusion | flops 256 | bytes 2048 | tf_op jit(solution)/shard_map/mul | solution.py:279
  110.2 1.0 fusion
  111.2 0.9 slice_multiply_fusion.3
  112.1 0.7 mul.667
  113.5 1.5 %slice_multiply_fusion.4 = f32[128,128]{1,0:T(8,128)} fusion(f32[640,128]{1,0:T(8,128)} %bitcast.198), kind=kLoop, calls=%fused_computation.144 | loop fusion | flops 16384 | bytes 131072 | tf_op jit(solution)/shard_map/mul | solution.py:276
  115.6 0.9 fusion.1
  (135 shorter events, 16.5 us)
Async XLA Ops:
  0.6 1.1 copy-start
  1.7 0.7 copy-start.23
  1.7 0.7 copy-start.24
  1.7 0.9 copy-start.17
  1.8 0.9 copy-start.20
  4.1 9.4 %copy-start.25 = (f32[3,384]{1,0:T(4,128)S(1)}, f32[3,384]{1,0:T(4,128)}, u32[]{:S(2)}) copy-start(f32[3,384]{1,0:T(4,128)} %param.19) | copy-start | bytes 13828
  4.1 9.8 %copy-start.27 = (f32[128]{0:T(128)S(1)}, f32[128]{0:T(128)}, u32[]{:S(2)}) copy-start(f32[128]{0:T(128)} %param.20) | copy-start | bytes 1540
  4.1 9.9 %copy-start.28 = (f32[128]{0:T(128)S(1)}, f32[128]{0:T(128)}, u32[]{:S(2)}) copy-start(f32[128]{0:T(128)} %param.21) | copy-start | bytes 1540
  4.1 29.6 %all-to-all-start = ((f32[16,34,512]{2,1,0:T(8,128)}), f32[16,34,512]{2,1,0:T(8,128)S(1)}, u32[]{:S(2)}, u32[]{:S(2)}) async-start(f32[16,34,512]{2,1,0:T(8,128)} %pad_maximum_fusion), calls=%async_computation | async-start | bytes 2621440 | tf_op jit(solution)/shard_map/all_to_all | solution.py:172
  34.8 0.8 copy-start.15
  37.3 2.0 %copy-start.3 = (f32[128,128]{0,1:T(8,128)S(1)}, f32[128,128]{0,1:T(8,128)}, u32[]{:S(2)}) copy-start(f32[128,128]{0,1:T(8,128)} %constant.45.clone) | copy-start | bytes 196612
  37.4 2.0 %copy-start.4 = (f32[128,128]{0,1:T(8,128)S(1)}, f32[128,128]{0,1:T(8,128)}, u32[]{:S(2)}) copy-start(f32[128,128]{0,1:T(8,128)} %constant.46.clone) | copy-start | bytes 196612
  39.4 1.4 %copy-start.2 = (f32[256,256,1]{1,0,2:T(8,128)S(1)}, f32[256,256,1]{1,0,2:T(8,128)}, u32[]{:S(2)}) copy-start(f32[256,256,1]{1,0,2:T(8,128)} %constant.61) | copy-start | bytes 786436
  42.3 1.0 copy-start.1
  43.9 0.8 copy-start.14
  43.9 0.8 copy-start.26
  44.7 1.2 %copy-start.5 = (f32[256,8,128]{0,2,1:T(8,128)S(1)}, f32[256,8,128]{0,2,1:T(8,128)}, u32[]{:S(2)}) copy-start(f32[256,8,128]{0,2,1:T(8,128)} %fusion.63) | copy-start | bytes 3145732
  56.3 2.6 %copy-start.9 = (f32[64,8,128]{2,0,1:T(8,128)}, f32[64,8,128]{2,0,1:T(8,128)S(1)}, u32[]{:S(2)}) copy-start(f32[64,8,128]{2,0,1:T(8,128)S(1)} %convolution_add_fusion) | copy-start | bytes 786436
  57.7 0.7 copy-start.7
  57.8 1.2 %copy-start.6 = (f32[24,16,512]{2,0,1:T(8,128)S(1)}, f32[24,16,512]{2,0,1:T(8,128)}, u32[]{:S(2)}) copy-start(f32[24,16,512]{2,0,1:T(8,128)} %get-tuple-element.24) | copy-start | bytes 2359300
  58.9 0.9 copy-start.8
  59.4 2.0 %copy-start.29 = (f32[3]{0:T(128)S(1)}, f32[3]{0:T(128)}, u32[]{:S(2)}) copy-start(f32[3]{0:T(128)} %pad.44.clone) | copy-start | bytes 40
  61.1 1.0 copy-start.16
  62.2 5.3 %copy-start.12 = (f32[128,8,128]{2,0,1:T(8,128)S(1)}, f32[128,8,128]{2,0,1:T(8,128)}, u32[]{:S(2)}) copy-start(f32[128,8,128]{2,0,1:T(8,128)} %get-tuple-element.20) | copy-start | bytes 1572868
  62.2 5.3 %copy-start.13 = (f32[128,8,128]{2,0,1:T(8,128)S(1)}, f32[128,8,128]{2,0,1:T(8,128)}, u32[]{:S(2)}) copy-start(f32[128,8,128]{2,0,1:T(8,128)} %get-tuple-element.21) | copy-start | bytes 1572868
  63.3 4.3 %copy-start.10 = (f32[128,8,128]{2,0,1:T(8,128)S(1)}, f32[128,8,128]{2,0,1:T(8,128)}, u32[]{:S(2)}) copy-start(f32[128,8,128]{2,0,1:T(8,128)} %get-tuple-element.22) | copy-start | bytes 1572868
  63.3 4.3 %copy-start.11 = (f32[128,8,128]{2,0,1:T(8,128)S(1)}, f32[128,8,128]{2,0,1:T(8,128)}, u32[]{:S(2)}) copy-start(f32[128,8,128]{2,0,1:T(8,128)} %get-tuple-element.23) | copy-start | bytes 1572868
  63.3 15.7 %all-to-all-start.1 = ((bf16[16,32,512]{2,1,0:T(8,128)(2,1)}), bf16[16,32,512]{2,1,0:T(8,128)(2,1)S(1)}, u32[]{:S(2)}, u32[]{:S(2)}) async-start(bf16[16,32,512]{2,1,0:T(8,128)(2,1)} %copy.177), calls=%async_computation.1 | async-start | bytes 1048576 | tf_op jit(solution)/shard_map/all_to_all | solution.py:232
  79.0 0.9 copy-start.18
  79.5 30.7 %copy-start.19 = (bf16[128,384]{1,0:T(8,128)(2,1)S(1)}, bf16[128,384]{1,0:T(8,128)(2,1)}, u32[]{:S(2)}) copy-start(bf16[128,384]{1,0:T(8,128)(2,1)} %param.17) | copy-start | bytes 294916
  80.2 35.4 %copy-start.21 = (bf16[128,128]{1,0:T(8,128)(2,1)S(1)}, bf16[128,128]{1,0:T(8,128)(2,1)}, u32[]{:S(2)}) copy-start(bf16[128,128]{1,0:T(8,128)(2,1)} %param.18) | copy-start | bytes 98308
  108.3 4.5 %copy-start.22 = (f32[8,8,128]{2,1,0:T(8,128)S(1)}, f32[8,8,128]{2,1,0:T(8,128)}, u32[]{:S(2)}) copy-start(f32[8,8,128]{2,1,0:T(8,128)} %get-tuple-element.12) | copy-start | bytes 98308

commit v11 on v10

--- a/solution.py
+++ b/solution.py
@@ -72,6 +72,55 @@
     return jnp.swapaxes(x, 0, 1).reshape(c, half * lanes)
 
 
+def exchange(x, axis, ident):
+    n = x.shape[0]
+    mesh_axes = ("dp", "seq")
+
+    def where(p):
+        return tuple(p if name == axis else lax.axis_index(name) for name in mesh_axes)
+
+    def kernel(x_ref, y_ref, send_sem, recv_sem):
+        me = lax.axis_index(axis)
+        barrier = pltpu.get_barrier_semaphore()
+        for k in range(1, n):
+            pl.semaphore_signal(
+                barrier, inc=1, device_id=where(lax.rem(me + k, n)),
+                device_id_type=pl.DeviceIdType.MESH,
+            )
+        pl.semaphore_wait(barrier, n - 1)
+        copies = []
+        for k in range(1, n):
+            p = lax.rem(me + k, n)
+            copy = pltpu.make_async_remote_copy(
+                src_ref=x_ref.at[p],
+                dst_ref=y_ref.at[me],
+                send_sem=send_sem.at[k],
+                recv_sem=recv_sem.at[k],
+                device_id=where(p),
+                device_id_type=pl.DeviceIdType.MESH,
+            )
+            copy.start()
+            copies.append(copy)
+        y_ref[pl.ds(me, 1)] = x_ref[pl.ds(me, 1)]
+        for copy in copies:
+            copy.wait()
+
+    return pl.pallas_call(
+        kernel,
+        out_shape=jax.ShapeDtypeStruct(x.shape, x.dtype),
+        in_specs=[pl.BlockSpec(memory_space=pltpu.VMEM)],
+        out_specs=pl.BlockSpec(memory_space=pltpu.VMEM),
+        scratch_shapes=[pltpu.SemaphoreType.DMA((n,)), pltpu.SemaphoreType.DMA((n,))],
+        compiler_params=pltpu.CompilerParams(collective_id=ident, has_side_effects=True),
+    )(x)
+
+
+def swap_blocks(x, axis, ident):
+    shape = x.shape
+    flat = x.reshape(shape[0], -1, LANES)
+    return exchange(flat, axis, ident).reshape(shape)
+
+
 def reduce_rounds(msg, param_rows, pair, dp_n):
     seq_n, msg_rows, lanes = msg.shape
     filter_rows = msg_rows - param_rows
@@ -169,9 +218,7 @@
     dprod_blk = jnp.einsum("td,cd->ct", cotangent[0], w_out, preferred_element_type=jnp.float32)
     dprod_blk = dprod_blk.reshape(seq_n, per, block)
     rows_sent = jnp.repeat(jnp.swapaxes(jnp.stack([filter_one, filter_two]), 0, 1), per_group, axis=0)
-    got = lax.all_to_all(
-        jnp.concatenate([proj_blk, dprod_blk, rows_sent], axis=1), "seq", 0, 0, tiled=True
-    )
+    got = swap_blocks(jnp.concatenate([proj_blk, dprod_blk, rows_sent], axis=1), "seq", 1)
     proj = jnp.swapaxes(got[:, : 3 * per], 0, 1).reshape(3 * per, length)
     d_product = jnp.swapaxes(
         got[:, 3 * per : 4 * per].reshape(seq_n, per, block // LANES, LANES), 1, 2
@@ -229,7 +276,7 @@
     prod_sent = jnp.swapaxes(product.reshape(seq_n, half // seq_n, per, LANES), 1, 2)
     prod_sent = prod_sent.reshape(seq_n, per, block)
     dp_sent = jnp.swapaxes(d_proj.reshape(3 * per, seq_n, block), 0, 1)
-    back = lax.all_to_all(jnp.concatenate([prod_sent, dp_sent], axis=1), "seq", 0, 0, tiled=True)
+    back = swap_blocks(jnp.concatenate([prod_sent, dp_sent], axis=1), "seq", 2)
     prod_rows = jnp.transpose(back[:, :per], (2, 0, 1)).reshape(block, width)
     dp_rows = jnp.transpose(back[:, per:].reshape(seq_n, 3, per, block), (3, 1, 0, 2))
     dp_rows = dp_rows.reshape(block, 3 * width)

time: 117 us -> 130 us (1.11)
  Pallas kernels: 27.4 us -> 69 us
  waiting for transfers between devices: 28.8 us -> 0 us
  starting transfers between devices: 13.6 us -> 0 us
  local copies, waits for them, and re-layouts: 11.7 us -> 21.6 us
  other arithmetic: 15.2 us -> 17.2 us
    pallas_call x0 -> x2, Pallas kernels: none -> 39.7 us  [exchange(): pl.pallas_call(kernel, out_shape=jax.ShapeDtypeStruct(x.shape, x.dtype),...]
    all_to_all x2 -> x0, waiting for transfers between devices: 28.8 us -> none  [the longest x1 18.5 us: shards(): lax.all_to_all(jnp.concatenate([proj_blk, dprod_blk, rows_sent], axis=1),...]
    all_to_all x2 -> x0, starting transfers between devices: 13.6 us -> none  [the longest x1 9.43 us: shards(): lax.all_to_all(jnp.concatenate([proj_blk, dprod_blk, rows_sent], axis=1),...]
    reshape x0 -> x4, local copies, waits for them, and re-layouts: none -> 5 us  [the longest x2 2.78 us: swap_blocks(): return exchange(flat, axis, ident).reshape(shape)]
    pallas_call x1, Pallas kernels: 27.4 us -> 29.4 us  [reduce_rounds(): pl.pallas_call(kernel, out_shape=(jax.ShapeDtypeStruct((seq_n, param_rows...]
    dot_general x5, matrix products: 4.77 us -> 2.8 us  [spectrum(): a = jnp.einsum('kn,ncm->kcm', tab['fwd1'], x, precision=PRECISION)]
    dot_general x5, matrix products: 3.53 us -> 5.47 us  [signal(): return jnp.einsum('nk,kcm->ncm', tab['inv1'], stacked, precision=PRECISION)]
    reshape x1, local copies, waits for them, and re-layouts: 0.01 us -> 1.71 us  [shards(): local_w_in.reshape(-1)]
  transfers between devices with their start and end apart: 2 -> 0, of which waited for: 2 -> 0; matrix products, arithmetic and copies ran while one was open for 2% -> 0% of each run, Pallas kernels for 0% -> 0%
where the time goes in v11:
time: 130 us; the launch traced here: 129 us
  Pallas kernels  69 us (53%)
  local copies, waits for them, and re-layouts  21.6 us (17%)
  matrix products  19.4 us (15%)
  other arithmetic  17.2 us (13%)
  between operations  1.6 us (1%)
    pallas_call x2, Pallas kernels, exchange(): pl.pallas_call(kernel, out_shape=jax.ShapeDtypeStruct(x.shape, x.dtype),...  39.7 us
    pallas_call x1, Pallas kernels, reduce_rounds(): pl.pallas_call(kernel, out_shape=(jax.ShapeDtypeStruct((seq_n, param_rows...  29.4 us
    unnamed x79, local copies, waits for them, and re-layouts  5.69 us
    dot_general x5, matrix products, signal(): return jnp.einsum('nk,kcm->ncm', tab['inv1'], stacked, precision=PRECISION)  5.47 us
    dot_general x5, matrix products, spectrum(): return jnp.einsum('kcm,mj->kcj', cat, tab['fwd2'], precision=PRECISION)  4.63 us
    dot_general x5, matrix products, signal(): b = jnp.einsum('kcj,jm->kcm', s, tab['inv2'], precision=PRECISION)  2.87 us
    dot_general x5, matrix products, spectrum(): a = jnp.einsum('kn,ncm->kcm', tab['fwd1'], x, precision=PRECISION)  2.8 us
    reshape x2, local copies, waits for them, and re-layouts, swap_blocks(): return exchange(flat, axis, ident).reshape(shape)  2.78 us

profile of v11, /device:TPU:1, one launch (start us, length us, event | category | flops | bytes accessed | tf_op | source)
XLA Modules:
  0.0 128.8 jit_solution(15966666035018433939)
XLA Ops:
  0.7 0.8 reshape.157
  1.8 1.0 copy.87
  4.2 1.1 reshape.160.x_ref
  5.3 26.5 %shard_map.214 = f32[16,136,128]{2,1,0:T(8,128)} custom-call(f32[16,136,128]{2,1,0:T(8,128)} %reshape.160.x_ref), custom_call_target="tpu_custom_call" | custom-call | tf_op jit(solution)/shard_map/pallas_call | solution.py:108
  31.7 1.4 %reshape.161 = f32[16,34,512]{2,1,0:T(8,128)S(1)} reshape(f32[16,136,128]{2,1,0:T(8,128)} %shard_map.214) | data formatting | bytes 2228224 | tf_op jit(solution)/shard_map/reshape | solution.py:121
  33.2 1.3 slice_bitcast_fusion.1
  35.2 1.0 fusion.98
  37.9 1.0 fusion.24
  38.9 1.0 slice_bitcast_fusion.8
  42.7 1.2 multiply_add_fusion.5
  44.7 1.9 %convolution_add_fusion.1 = f32[64,8,128]{2,0,1:T(8,128)S(1)} fusion(f32[64,256,1]{1,0,2:T(8,128)S(1)} %copy-done.13, f32[128,8,128]{0,2,1:T(8,128)} %get-tuple-element.37, f32[128,8,128]{0,2,1:T(8,128)} %get-tuple-element.36, f32[8]{0:T(128)S(1)} %get-tuple-element.82, f32[64,24,128]{2,0,1:T(8,128)S(1)} %bitcast.168, f32[64,8,128]{2,1,0:T(8,128)} %bitcast.180), kind=kOutput, calls=%fused_computation.4 | convolution fusion | flops 101122048 | bytes 1900576 | tf_op jit(solution)/shard_map/nk,kcm->ncm/dot_general | solution.py:54
  48.0 1.0 fusion.2
  49.1 1.0 fusion.35
  50.2 1.4 %multiply_subtract_fusion.1 = (f32[128,8,128]{2,0,1:T(8,128)}, f32[128,8,128]{2,0,1:T(8,128)}, f32[128,8,128]{2,0,1:T(8,128)S(1)}, f32[128,8,128]{2,0,1:T(8,128)...) fusion(f32[128,8,256]{2,0,1:T(8,128)S(1)} %fusion.35, f32[128,8,256]{2,0,1:T(8,128)S(1)} %fusion.2, ...), kind=kLoop, calls=%fused_computation.82 | loop fusion | flops 2490368 | bytes 5439488 | tf_op jit(solution)/shard_map/sub | solution.py:62
  53.0 1.3 %convolution_add_fusion = f32[64,8,128]{2,0,1:T(8,128)} fusion(f32[64,256,1]{1,0,2:T(8,128)S(1)} %copy-done.13, f32[128,8,128]{0,2,1:T(8,128)S(1)} %get-tuple-element.31, f32[128,8,128]{0,2,1:T(8,128)S(1)} %get-tuple-element.30, f32[8]{0:T(128)S(1)} %get-tuple-element.81, f32[64,8,128]{2,0,1:T(8,128)S(1)} %convolution_add_fusion.1, ...), kind=kOutput, calls=%fused_computation.3 | convolution fusion | flops 101122048 | bytes 1900576 | tf_op jit(solution)/shard_map/nk,kcm->ncm/dot_general | solution.py:54
  55.8 1.2 fusion.13
  57.0 1.3 multiply_subtract_fusion
  59.9 1.4 %multiply_reduce_fusion.3 = (f32[8]{0:T(128)S(1)}, f32[8]{0:T(128)S(1)}, bf16[64,8,128]{2,0,1:T(8,128)(2,1)}, f32[64,8,128]{2,0,1:T(8,128)S(1)}, f32[64,8,128]{2,0,1:T(8,128)S(1)}) fusion(f32[64,24,128]{2,0,1:T(8,128)S(1)} %bitcast.174, f32[64,8,128]{2,0,1:T(8,128)S(1)} %convolution_add_fusion.1, f32[64,8,128]{2,0,1:T(8,128)S(1)} %convolution_add_fusion.3, ...), kind=kOutput, calls=%fused_computation.125 | convolution fusion | flops 101777392 | bytes 3342432 | tf_op jit(solution)/shard_map/nk,kcm->ncm/dot_general | solution.py:54
  61.7 1.2 fusion.51
  63.0 1.0 pad_maximum_fusion.1
  67.0 1.1 reshape.171.x_ref
  68.1 13.2 %shard_map.215 = bf16[16,128,128]{2,1,0:T(8,128)(2,1)} custom-call(bf16[16,128,128]{2,1,0:T(8,128)(2,1)} %reshape.171.x_ref), custom_call_target="tpu_custom_call" | custom-call | tf_op jit(solution)/shard_map/pallas_call | solution.py:108
  81.3 1.4 %reshape.172 = bf16[16,32,512]{2,1,0:T(8,128)(2,1)S(1)} reshape(bf16[16,128,128]{2,1,0:T(8,128)(2,1)} %shard_map.215) | data formatting | bytes 1048576 | tf_op jit(solution)/shard_map/reshape | solution.py:121
  83.9 1.7 %reshape.178 = f32[49152]{0:T(1024)} reshape(f32[128,384]{1,0:T(8,128)} %copy.113) | data formatting | bytes 393216 | tf_op jit(solution)/shard_map/reshape | solution.py:302
  85.6 1.1 convolution_bitcast_fusion
  86.7 1.7 %select_maximum_fusion = f32[81920]{0:T(1024)} fusion(f32[1536]{0:T(1024)S(1)} %reshape.182, f32[16384]{0:T(1024)S(1)} %convolution_bitcast_fusion, f32[49152]{0:T(1024)} %reshape.178), kind=kLoop, calls=%fused_computation.109 | loop fusion | flops 491520 | bytes 595968 | tf_op jit(solution)/shard_map/concatenate | solution.py:302
  90.5 29.4 %shard_map.216 = (f32[16,40,128]{2,1,0:T(8,128)}, f32[8,8,128]{2,1,0:T(8,128)}) custom-call(f32[16,48,128]{2,1,0:T(8,128)} %pad_maximum_fusion.3.msg_ref), custom_call_target="tpu_custom_call" | custom-call | tf_op jit(solution)/shard_map/pallas_call | solution.py:176
  119.9 0.9 slice_multiply_fusion.3
  123.0 1.5 %slice_multiply_fusion.4 = f32[128,128]{1,0:T(8,128)} fusion(f32[640,128]{1,0:T(8,128)} %bitcast.196), kind=kLoop, calls=%fused_computation.144 | loop fusion | flops 16384 | bytes 131072 | tf_op jit(solution)/shard_map/mul | solution.py:323
  125.7 1.2 fusion.78
  126.9 1.0 fusion
  127.9 0.9 fusion.1
  (151 shorter events, 23.3 us)
Async XLA Ops:
  0.6 2.2 %copy-start = (bf16[1,512,128]{2,1,0:T(8,128)(2,1)S(1)}, bf16[1,512,128]{2,1,0:T(8,128)(2,1)}, u32[]{:S(2)}) copy-start(bf16[1,512,128]{2,1,0:T(8,128)(2,1)} %param.15) | copy-start | bytes 393220
  1.6 32.9 %copy-start.30 = (f32[24]{0:T(128)}, f32[24]{0:T(128)S(1)}, u32[]{:S(2)}) copy-start(f32[24]{0:T(128)S(1)} %mul.261) | copy-start | bytes 292
  1.7 32.8 %copy-start.32 = (f32[24]{0:T(128)}, f32[24]{0:T(128)S(1)}, u32[]{:S(2)}) copy-start(f32[24]{0:T(128)S(1)} %mul.264) | copy-start | bytes 292
  1.8 32.8 %copy-start.34 = (f32[24]{0:T(128)}, f32[24]{0:T(128)S(1)}, u32[]{:S(2)}) copy-start(f32[24]{0:T(128)S(1)} %mul.267) | copy-start | bytes 292
  2.8 0.9 copy-start.20
  2.8 1.1 copy-start.28
  2.9 1.1 copy-start.29
  33.2 1.4 %copy-start.3 = (f32[16,34,512]{2,1,0:T(8,128)}, f32[16,34,512]{2,1,0:T(8,128)S(1)}, u32[]{:S(2)}) copy-start(f32[16,34,512]{2,1,0:T(8,128)S(1)} %reshape.161) | copy-start | bytes 3342340
  35.0 1.2 copy-start.15
  35.2 1.7 %copy-start.4 = (f32[128,128]{0,1:T(8,128)S(1)}, f32[128,128]{0,1:T(8,128)}, u32[]{:S(2)}) copy-start(f32[128,128]{0,1:T(8,128)} %constant.45.clone) | copy-start | bytes 196612
  35.2 1.7 %copy-start.5 = (f32[128,128]{0,1:T(8,128)S(1)}, f32[128,128]{0,1:T(8,128)}, u32[]{:S(2)}) copy-start(f32[128,128]{0,1:T(8,128)} %constant.46.clone) | copy-start | bytes 196612
  36.9 1.0 copy-start.2
  40.7 1.3 %copy-start.1 = (f32[256,256,1]{1,0,2:T(8,128)S(1)}, f32[256,256,1]{1,0,2:T(8,128)}, u32[]{:S(2)}) copy-start(f32[256,256,1]{1,0,2:T(8,128)} %constant.62) | copy-start | bytes 786436
  42.6 1.2 copy-start.36
  42.6 2.0 %copy-start.13 = (f32[64,256,1]{1,0,2:T(8,128)S(1)}, f32[64,256,1]{1,0,2:T(8,128)}, u32[]{:S(2)}) copy-start(f32[64,256,1]{1,0,2:T(8,128)} %constant.59) | copy-start | bytes 196612
  49.1 1.1 copy-start.23
  49.1 1.1 copy-start.24
  49.1 1.1 copy-start.25
  55.8 1.2 copy-start.18
  55.8 1.2 copy-start.22
  58.9 1.0 copy-start.7
  59.8 1.4 %copy-start.8 = (f32[24,16,512]{2,0,1:T(8,128)S(1)}, f32[24,16,512]{2,0,1:T(8,128)}, u32[]{:S(2)}) copy-start(f32[24,16,512]{2,0,1:T(8,128)} %get-tuple-element.24) | copy-start | bytes 2359300
  64.7 1.0 copy-start.31
  64.7 1.0 copy-start.33
  64.7 1.0 copy-start.35
  82.8 5.6 %copy-start.11 = (f32[128,8,128]{2,0,1:T(8,128)S(1)}, f32[128,8,128]{2,0,1:T(8,128)}, u32[]{:S(2)}) copy-start(f32[128,8,128]{2,0,1:T(8,128)} %get-tuple-element.20) | copy-start | bytes 1572868
  82.8 5.6 %copy-start.12 = (f32[128,8,128]{2,0,1:T(8,128)S(1)}, f32[128,8,128]{2,0,1:T(8,128)}, u32[]{:S(2)}) copy-start(f32[128,8,128]{2,0,1:T(8,128)} %get-tuple-element.21) | copy-start | bytes 1572868
  83.9 4.5 %copy-start.9 = (f32[128,8,128]{2,0,1:T(8,128)S(1)}, f32[128,8,128]{2,0,1:T(8,128)}, u32[]{:S(2)}) copy-start(f32[128,8,128]{2,0,1:T(8,128)} %get-tuple-element.22) | copy-start | bytes 1572868
  83.9 4.5 %copy-start.10 = (f32[128,8,128]{2,0,1:T(8,128)S(1)}, f32[128,8,128]{2,0,1:T(8,128)}, u32[]{:S(2)}) copy-start(f32[128,8,128]{2,0,1:T(8,128)} %get-tuple-element.23) | copy-start | bytes 1572868
  88.5 1.2 copy-start.16
  89.6 37.4 %copy-start.21 = (bf16[128,384]{1,0:T(8,128)(2,1)S(1)}, bf16[128,384]{1,0:T(8,128)(2,1)}, u32[]{:S(2)}) copy-start(bf16[128,384]{1,0:T(8,128)(2,1)} %param.17) | copy-start | bytes 294916
  89.7 38.2 %copy-start.27 = (bf16[128,128]{1,0:T(8,128)(2,1)S(1)}, bf16[128,128]{1,0:T(8,128)(2,1)}, u32[]{:S(2)}) copy-start(bf16[128,128]{1,0:T(8,128)(2,1)} %param.18) | copy-start | bytes 98308
  (5 other events, 4.1 us)

commit v12 on v10

--- a/solution.py
+++ b/solution.py
@@ -252,11 +252,14 @@
     small_full = lax.dynamic_update_slice(
         jnp.zeros((3, 4, seq_n, per), jnp.float32), small, (0, 0, me, 0)
     )
-    params = jnp.concatenate([local_w_in.reshape(-1), local_w_out.reshape(-1), small_full.reshape(-1)])
+    params = grad_scale * jnp.concatenate(
+        [local_w_in.reshape(-1), local_w_out.reshape(-1), small_full.reshape(-1)]
+    )
     n_params = params.shape[0]
     chunk = -(-n_params // (seq_n * 8 * LANES)) * 8 * LANES
     params = jnp.pad(params, (0, chunk * seq_n - n_params)).reshape(seq_n, -1, LANES)
-    fg_sent = jnp.swapaxes(filt_grad.reshape(2, seq_n, block), 0, 1).reshape(seq_n, -1, LANES)
+    fg_sent = jnp.swapaxes(grad_scale * filt_grad.reshape(2, seq_n, block), 0, 1)
+    fg_sent = fg_sent.reshape(seq_n, -1, LANES)
     full, fg = reduce_rounds(jnp.concatenate([params, fg_sent], axis=1), params.shape[1], per_group, dp_n)
     fg_blocks = jnp.swapaxes(fg.reshape(filters, 2, block), 0, 1)
     full = full.reshape(-1)
@@ -272,13 +275,13 @@
     return (
         output,
         d_series,
-        grad_scale * grad_w_in,
-        grad_scale * grad_w_out,
-        grad_scale * grad_taps,
-        grad_scale * grad_skip_one,
-        grad_scale * grad_skip_two,
-        grad_scale * fg_blocks[0],
-        grad_scale * fg_blocks[1],
+        grad_w_in,
+        grad_w_out,
+        grad_taps,
+        grad_skip_one,
+        grad_skip_two,
+        fg_blocks[0],
+        fg_blocks[1],
     )
 
 

time: 117 us -> 117 us (level)
  local copies, waits for them, and re-layouts: 11.7 us -> 16.6 us
  other arithmetic: 15.2 us -> 10.3 us
    mul x4 -> x1, other arithmetic: 4.22 us -> 0.02 us  [shards(): grad_scale * jnp.concatenate([local_w_in.reshape(-1), local_w_out.reshape...]
    slice x0 -> x2, local copies, waits for them, and re-layouts: none -> 2.41 us  [the longest x1 1.47 us: shards(): grad_w_out = full[offsets[1]:offsets[2]].reshape(width, width)]
    squeeze x0 -> x2, local copies, waits for them, and re-layouts: none -> 1.81 us  [the longest x1 1.19 us: shards(): grad_skip_two = small_full[1, 3]]
    unnamed x65 -> x66, local copies, waits for them, and re-layouts: 5.59 us -> 6.29 us
where the time goes in v12:
time: 117 us; the launch traced here: 116 us
  waiting for transfers between devices  28.8 us (25%)
  Pallas kernels  27.4 us (23%)
  matrix products  18.4 us (16%)
  local copies, waits for them, and re-layouts  16.6 us (14%)
  starting transfers between devices  13.6 us (12%)
  other arithmetic  10.3 us (9%)
  between operations  1.41 us (1%)
    pallas_call x1, Pallas kernels, reduce_rounds(): pl.pallas_call(kernel, out_shape=(jax.ShapeDtypeStruct((seq_n, param_rows...  27.4 us
    all_to_all x1, waiting for transfers between devices, shards(): lax.all_to_all(jnp.concatenate([proj_blk, dprod_blk, rows_sent], axis=1),...  18.5 us
    all_to_all x1, waiting for transfers between devices, shards(): lax.all_to_all(jnp.concatenate([prod_sent, dp_sent], axis=1), 'seq', 0, 0...  10.3 us
    all_to_all x1, starting transfers between devices, shards(): lax.all_to_all(jnp.concatenate([proj_blk, dprod_blk, rows_sent], axis=1),...  9.43 us
    unnamed x66, local copies, waits for them, and re-layouts  6.29 us
    dot_general x5, matrix products, spectrum(): a = jnp.einsum('kn,ncm->kcm', tab['fwd1'], x, precision=PRECISION)  4.77 us
    dot_general x5, matrix products, spectrum(): return jnp.einsum('kcm,mj->kcj', cat, tab['fwd2'], precision=PRECISION)  4.48 us
    all_to_all x1, starting transfers between devices, shards(): lax.all_to_all(jnp.concatenate([prod_sent, dp_sent], axis=1), 'seq', 0, 0...  4.21 us
  transfers between devices with their start and end apart: 2, of which 2 were waited for; matrix products, arithmetic and copies ran while one was open for 2% of the time, Pallas kernels for 0%

profile of v12, /device:TPU:1, one launch (start us, length us, event | category | flops | bytes accessed | tf_op | source)
XLA Modules:
  0.0 116.5 jit_solution(17046183000212737467)
XLA Ops:
  0.7 1.0 copy.153
  2.9 1.2 %pad_maximum_fusion = f32[16,34,512]{2,1,0:T(8,128)} fusion(f32[16,2,512]{2,1,0:T(2,128)S(1)} %bitcast.193, f32[16,8,512]{2,1,0:T(8,128)S(1)} %fusion.67, f32[16,24,512]{2,1,0:T(8,128)S(1)} %bitcast.185), kind=kLoop, calls=%fused_computation.1 | loop fusion | flops 557056 | bytes 2228224 | tf_op jit(solution)/shard_map/concatenate | solution.py:173
  4.1 9.4 %all-to-all-start = ((f32[16,34,512]{2,1,0:T(8,128)}), f32[16,34,512]{2,1,0:T(8,128)S(1)}, u32[]{:S(2)}, u32[]{:S(2)}) async-start(f32[16,34,512]{2,1,0:T(8,128)} %pad_maximum_fusion), calls=%async_computation | async-start | bytes 2621440 | tf_op jit(solution)/shard_map/all_to_all | solution.py:172
  15.2 18.5 %all-to-all-done = f32[16,34,512]{2,1,0:T(8,128)S(1)} async-done(((f32[16,34,512]{2,1,0:T(8,128)}), f32[16,34,512]{2,1,0:T(8,128)S(1)}, u32[]{:S(2)}, u32[]{:S(2)}) %all-to-all-start) | async-done | bytes 1114144 | tf_op jit(solution)/shard_map/all_to_all | solution.py:172
  33.7 1.1 slice_bitcast_fusion.1
  35.7 1.6 %fusion.64 = f32[256,8,128]{0,2,1:T(8,128)} fusion(f32[256,64,1]{0,1,2:T(8,128)S(1)} %copy-done.15, f32[64,24,128]{2,0,1:T(8,128)S(1)} %bitcast.167), kind=kOutput, calls=%fused_computation.130 | convolution fusion | flops 100663296 | bytes 1376256 | tf_op jit(solution)/shard_map/kn,ncm->kcm/dot_general | solution.py:42
  37.4 1.6 %fusion.93 = f32[256,8,128]{0,2,1:T(8,128)} fusion(f32[256,64,1]{0,1,2:T(8,128)S(1)} %copy-done.15, f32[64,24,128]{2,0,1:T(8,128)S(1)} %bitcast.168, f32[64,8,128]{2,1,0:T(8,128)S(1)} %bitcast.179), kind=kOutput, calls=%fused_computation.187 | convolution fusion | flops 100728832 | bytes 1638400 | tf_op jit(solution)/shard_map/kn,ncm->kcm/dot_general | solution.py:42
  39.4 1.4 %multiply_subtract_fusion.7 = (f32[128,8,128]{0,2,1:T(8,128)S(1)}, f32[128,8,128]{0,2,1:T(8,128)S(1)}) fusion(f32[256,8,128]{0,2,1:T(8,128)} %fusion.93, f32[128,128]{0,1:T(8,128)S(1)} %copy-done.4, f32[128,128]{0,1:T(8,128)S(1)} %copy-done.3), kind=kLoop, calls=%fused_computation.95 | loop fusion | flops 786432 | bytes 2228224 | tf_op jit(solution)/shard_map/sub | solution.py:45
  41.3 1.0 fusion.25
  42.4 0.8 copy-done.1
  44.0 0.7 copy-done.14
  46.2 1.0 fusion.3
  47.2 1.0 fusion.36
  48.3 1.4 %multiply_subtract_fusion.1 = (f32[128,8,128]{2,0,1:T(8,128)}, f32[128,8,128]{2,0,1:T(8,128)}, f32[128,8,128]{2,0,1:T(8,128)S(1)}, f32[128,8,128]{2,0,1:T(8,128)...) fusion(f32[128,8,256]{2,0,1:T(8,128)S(1)} %fusion.36, f32[128,8,256]{2,0,1:T(8,128)S(1)} %fusion.3, ...), kind=kLoop, calls=%fused_computation.83 | loop fusion | flops 2490368 | bytes 5439488 | tf_op jit(solution)/shard_map/sub | solution.py:62
  51.1 0.6 convolution_add_fusion.3
  52.5 1.0 fusion.14
  53.6 1.4 %multiply_subtract_fusion = (f32[128,8,128]{2,0,1:T(8,128)}, f32[128,8,128]{2,0,1:T(8,128)}, f32[128,8,128]{2,0,1:T(8,128)S(1)}, f32[128,8,128]{2,0,1:T(8,128)S(1)}) fusion(f32[128,8,256]{2,0,1:T(8,128)S(1)} %fusion.25, f32[128,8,256]{2,0,1:T(8,128)S(1)} %fusion.14, f32[128,128]{1,0:T(8,128)S(1)} %get-tuple-element.72, f32[128,128]{1,0:T(8,128)S(1)} %get-tuple-element.71), kind=kLoop, calls=%fused_computation.81 | loop fusion | flops 1703936 | bytes 4325376 | tf_op jit(solution)/shard_map/sub | solution.py:62
  54.9 0.6 fusion.18
  56.3 1.4 %multiply_reduce_fusion.3 = (f32[8]{0:T(128)S(1)}, f32[8]{0:T(128)S(1)}, bf16[64,8,128]{2,0,1:T(8,128)(2,1)}, f32[64,8,128]{2,0,1:T(8,128)S(1)}, f32[64,8,128]{2,0,1:T(8,128)S(1)}) fusion(f32[64,24,128]{2,0,1:T(8,128)S(1)} %bitcast.174, f32[64,8,128]{2,0,1:T(8,128)S(1)} %convolution_add_fusion.1, f32[64,8,128]{2,0,1:T(8,128)S(1)} %convolution_add_fusion.3, ...), kind=kOutput, calls=%fused_computation.124 | convolution fusion | flops 101777392 | bytes 3342432 | tf_op jit(solution)/shard_map/nk,kcm->ncm/dot_general | solution.py:54
  59.9 1.2 %fusion.52 = f32[24]{0:T(128)S(1)} fusion(f32[24,64,128]{2,1,0:T(8,128)S(1)} %reshape.158, f32[64,8,128]{2,0,1:T(8,128)S(1)} %get-tuple-element.61, f32[64,8,128]{2,0,1:T(8,128)S(1)} %copy-done.8, f32[64,8,128]{2,0,1:T(8,128)} %copy-done.9), kind=kLoop, calls=%fused_computation.72 | loop fusion | flops 786408 | bytes 1572960 | tf_op jit(solution)/shard_map/reduce_sum | solution.py:225
  62.2 1.1 copy.177
  63.3 4.2 %all-to-all-start.1 = ((bf16[16,32,512]{2,1,0:T(8,128)(2,1)}), bf16[16,32,512]{2,1,0:T(8,128)(2,1)S(1)}, u32[]{:S(2)}, u32[]{:S(2)}) async-start(bf16[16,32,512]{2,1,0:T(8,128)(2,1)} %copy.177), calls=%async_computation.1 | async-start | bytes 1048576 | tf_op jit(solution)/shard_map/all_to_all | solution.py:232
  68.7 10.3 %all-to-all-done.1 = bf16[16,32,512]{2,1,0:T(8,128)(2,1)S(1)} async-done(((bf16[16,32,512]{2,1,0:T(8,128)(2,1)}), bf16[16,32,512]{2,1,0:T(8,128)(2,1)S(1)}, u32[]{:S(2)}, u32[]{:S(2)}) %all-to-all-start.1) | async-done | bytes 524320 | tf_op jit(solution)/shard_map/all_to_all | solution.py:232
  80.2 0.8 pad_maximum_fusion.3.msg_ref
  81.0 27.4 %shard_map.214 = (f32[16,40,128]{2,1,0:T(8,128)}, f32[8,8,128]{2,1,0:T(8,128)}) custom-call(f32[16,48,128]{2,1,0:T(8,128)} %pad_maximum_fusion.3.msg_ref), custom_call_target="tpu_custom_call" | custom-call | tf_op jit(solution)/shard_map/pallas_call | solution.py:127
  108.3 0.7 slice_bitcast_fusion.13
  109.0 1.2 %slice_bitcast_fusion.14 = (f32[128]{0:T(128)}, f32[128]{0:T(128)}) fusion(f32[160,4,128]{2,1,0:T(4,128)} %bitcast.196), kind=kLoop, calls=%fused_computation.168 | loop fusion | bytes 2048 | tf_op jit(solution)/shard_map/squeeze | solution.py:273
  110.2 1.0 fusion
  111.2 0.9 slice.312
  112.1 0.7 reshape.164
  113.5 1.5 %slice.313 = f32[128,128]{1,0:T(8,128)} slice(f32[640,128]{1,0:T(8,128)} %bitcast.198), slice={[384:512], [0:128]} | slice | bytes 131072 | tf_op jit(solution)/shard_map/slice | solution.py:269
  115.6 0.9 fusion.1
  (136 shorter events, 16.5 us)
Async XLA Ops:
  0.6 1.1 copy-start
  1.7 0.7 copy-start.23
  1.7 0.7 copy-start.24
  1.7 0.9 copy-start.17
  1.8 0.9 copy-start.20
  4.1 9.4 %copy-start.25 = (f32[3,384]{1,0:T(4,128)S(1)}, f32[3,384]{1,0:T(4,128)}, u32[]{:S(2)}) copy-start(f32[3,384]{1,0:T(4,128)} %param.19) | copy-start | bytes 13828
  4.1 9.8 %copy-start.27 = (f32[128]{0:T(128)S(1)}, f32[128]{0:T(128)}, u32[]{:S(2)}) copy-start(f32[128]{0:T(128)} %param.20) | copy-start | bytes 1540
  4.1 9.9 %copy-start.28 = (f32[128]{0:T(128)S(1)}, f32[128]{0:T(128)}, u32[]{:S(2)}) copy-start(f32[128]{0:T(128)} %param.21) | copy-start | bytes 1540
  4.1 29.6 %all-to-all-start = ((f32[16,34,512]{2,1,0:T(8,128)}), f32[16,34,512]{2,1,0:T(8,128)S(1)}, u32[]{:S(2)}, u32[]{:S(2)}) async-start(f32[16,34,512]{2,1,0:T(8,128)} %pad_maximum_fusion), calls=%async_computation | async-start | bytes 2621440 | tf_op jit(solution)/shard_map/all_to_all | solution.py:172
  34.8 0.8 copy-start.15
  37.3 2.0 %copy-start.3 = (f32[128,128]{0,1:T(8,128)S(1)}, f32[128,128]{0,1:T(8,128)}, u32[]{:S(2)}) copy-start(f32[128,128]{0,1:T(8,128)} %constant.42.clone) | copy-start | bytes 196612
  37.4 2.0 %copy-start.4 = (f32[128,128]{0,1:T(8,128)S(1)}, f32[128,128]{0,1:T(8,128)}, u32[]{:S(2)}) copy-start(f32[128,128]{0,1:T(8,128)} %constant.43.clone) | copy-start | bytes 196612
  39.4 1.4 %copy-start.2 = (f32[256,256,1]{1,0,2:T(8,128)S(1)}, f32[256,256,1]{1,0,2:T(8,128)}, u32[]{:S(2)}) copy-start(f32[256,256,1]{1,0,2:T(8,128)} %constant.58) | copy-start | bytes 786436
  42.3 1.0 copy-start.1
  43.9 0.8 copy-start.14
  43.9 0.8 copy-start.26
  44.7 1.2 %copy-start.5 = (f32[256,8,128]{0,2,1:T(8,128)S(1)}, f32[256,8,128]{0,2,1:T(8,128)}, u32[]{:S(2)}) copy-start(f32[256,8,128]{0,2,1:T(8,128)} %fusion.64) | copy-start | bytes 3145732
  56.3 2.6 %copy-start.9 = (f32[64,8,128]{2,0,1:T(8,128)}, f32[64,8,128]{2,0,1:T(8,128)S(1)}, u32[]{:S(2)}) copy-start(f32[64,8,128]{2,0,1:T(8,128)S(1)} %convolution_add_fusion) | copy-start | bytes 786436
  57.7 0.7 copy-start.7
  57.8 1.2 %copy-start.6 = (f32[24,16,512]{2,0,1:T(8,128)S(1)}, f32[24,16,512]{2,0,1:T(8,128)}, u32[]{:S(2)}) copy-start(f32[24,16,512]{2,0,1:T(8,128)} %get-tuple-element.24) | copy-start | bytes 2359300
  58.9 0.9 copy-start.8
  59.4 2.0 %copy-start.29 = (f32[3]{0:T(128)S(1)}, f32[3]{0:T(128)}, u32[]{:S(2)}) copy-start(f32[3]{0:T(128)} %pad.44.clone) | copy-start | bytes 40
  61.1 1.0 copy-start.16
  62.2 5.3 %copy-start.12 = (f32[128,8,128]{2,0,1:T(8,128)S(1)}, f32[128,8,128]{2,0,1:T(8,128)}, u32[]{:S(2)}) copy-start(f32[128,8,128]{2,0,1:T(8,128)} %get-tuple-element.20) | copy-start | bytes 1572868
  62.2 5.3 %copy-start.13 = (f32[128,8,128]{2,0,1:T(8,128)S(1)}, f32[128,8,128]{2,0,1:T(8,128)}, u32[]{:S(2)}) copy-start(f32[128,8,128]{2,0,1:T(8,128)} %get-tuple-element.21) | copy-start | bytes 1572868
  63.3 4.3 %copy-start.10 = (f32[128,8,128]{2,0,1:T(8,128)S(1)}, f32[128,8,128]{2,0,1:T(8,128)}, u32[]{:S(2)}) copy-start(f32[128,8,128]{2,0,1:T(8,128)} %get-tuple-element.22) | copy-start | bytes 1572868
  63.3 4.3 %copy-start.11 = (f32[128,8,128]{2,0,1:T(8,128)S(1)}, f32[128,8,128]{2,0,1:T(8,128)}, u32[]{:S(2)}) copy-start(f32[128,8,128]{2,0,1:T(8,128)} %get-tuple-element.23) | copy-start | bytes 1572868
  63.3 15.7 %all-to-all-start.1 = ((bf16[16,32,512]{2,1,0:T(8,128)(2,1)}), bf16[16,32,512]{2,1,0:T(8,128)(2,1)S(1)}, u32[]{:S(2)}, u32[]{:S(2)}) async-start(bf16[16,32,512]{2,1,0:T(8,128)(2,1)} %copy.177), calls=%async_computation.1 | async-start | bytes 1048576 | tf_op jit(solution)/shard_map/all_to_all | solution.py:232
  79.0 0.9 copy-start.18
  80.0 30.3 %copy-start.19 = (bf16[128,384]{1,0:T(8,128)(2,1)S(1)}, bf16[128,384]{1,0:T(8,128)(2,1)}, u32[]{:S(2)}) copy-start(bf16[128,384]{1,0:T(8,128)(2,1)} %param.17) | copy-start | bytes 294916
  80.2 35.4 %copy-start.21 = (bf16[128,128]{1,0:T(8,128)(2,1)S(1)}, bf16[128,128]{1,0:T(8,128)(2,1)}, u32[]{:S(2)}) copy-start(bf16[128,128]{1,0:T(8,128)(2,1)} %param.18) | copy-start | bytes 98308
  108.3 4.5 %copy-start.22 = (f32[8,8,128]{2,1,0:T(8,128)S(1)}, f32[8,8,128]{2,1,0:T(8,128)}, u32[]{:S(2)}) copy-start(f32[8,8,128]{2,1,0:T(8,128)} %get-tuple-element.12) | copy-start | bytes 98308

commit v13 on v12

--- a/solution.py
+++ b/solution.py
@@ -72,13 +72,20 @@
     return jnp.swapaxes(x, 0, 1).reshape(c, half * lanes)
 
 
-def reduce_rounds(msg, param_rows, pair, dp_n):
-    seq_n, msg_rows, lanes = msg.shape
-    filter_rows = msg_rows - param_rows
+def tail_rounds(out_msg, series_blk, cot_blk, side, scale, pair, dp_n):
+    seq_n, out_rows, block = out_msg.shape
+    per = out_rows // 4
+    width = series_blk.shape[1]
+    side_rows = side.shape[1]
+    filter_rows = side_rows // 2
+    param_rows = 3 * per + per + filter_rows
+    msg_rows = param_rows + filter_rows
     groups = seq_n // pair
+    ag_rows = param_rows + groups * filter_rows
     mesh = pl.DeviceIdType.MESH
 
-    def kernel(msg_ref, full_ref, fg_ref, rs_buf, ag_buf, sems):
+    def kernel(out_ref, ser_ref, cot_ref, side_ref, back_ref, full_ref, fg_ref,
+               msg_buf, rs_buf, ag_buf, sems):
         ms = lax.axis_index("seq")
         md = lax.axis_index("dp")
         barrier = pltpu.get_barrier_semaphore()
@@ -102,43 +109,57 @@
         seq_peer = lambda k: (md, lax.rem(ms + k, seq_n))
         dp_peer = lambda k: (lax.rem(md + k, dp_n), ms)
 
-        copies = send_all(seq_n, lambda k: msg_ref.at[lax.rem(ms + k, seq_n)], rs_buf.at[ms], 0, seq_peer)
-        rs_buf[pl.ds(ms, 1)] = msg_ref[pl.ds(ms, 1)]
+        copies = send_all(seq_n, lambda k: out_ref.at[lax.rem(ms + k, seq_n)], back_ref.at[ms], 3, seq_peer)
+        back_ref[pl.ds(ms, 1)] = out_ref[pl.ds(ms, 1)]
+        for copy in copies:
+            copy.wait()
+        ser = ser_ref[...].astype(jnp.float32)
+        cot = cot_ref[...].astype(jnp.float32)
+        for j in range(seq_n):
+            rows = back_ref[j].astype(jnp.float32)
+            msg_buf[j, : 3 * per] = scale * jnp.dot(rows[per:], ser, preferred_element_type=jnp.float32)
+            msg_buf[j, 3 * per : 4 * per] = scale * jnp.dot(rows[:per], cot, preferred_element_type=jnp.float32)
+        msg_buf[:, 4 * per :] = side_ref[...]
+
+        copies = send_all(seq_n, lambda k: msg_buf.at[lax.rem(ms + k, seq_n)], rs_buf.at[ms], 0, seq_peer)
+        rs_buf[pl.ds(ms, 1)] = msg_buf[pl.ds(ms, 1)]
         for copy in copies:
             copy.wait()
         got = rs_buf[...]
         p_sum = jnp.sum(got[:, :param_rows], axis=0)
-        f_sum = jnp.sum(got[:, param_rows:].reshape(groups, pair, filter_rows, lanes), axis=1)
-        mine = jnp.concatenate([p_sum, f_sum.reshape(groups * filter_rows, lanes)], axis=0)
+        f_sum = jnp.sum(got[:, param_rows:].reshape(groups, pair, filter_rows, width), axis=1)
+        mine = jnp.concatenate([p_sum, f_sum.reshape(groups * filter_rows, width)], axis=0)
 
         ag_buf[pl.ds(md, 1)] = mine[None]
         copies = send_all(dp_n, lambda k: ag_buf.at[md], ag_buf.at[md], 1, dp_peer)
         for copy in copies:
             copy.wait()
         total = jnp.sum(ag_buf[...], axis=0)
-        fg_ref[...] = total[param_rows:].reshape(groups, filter_rows, lanes)
+        fg_ref[...] = total[param_rows:].reshape(groups, filter_rows, width)
 
         full_ref[pl.ds(ms, 1)] = total[:param_rows][None]
         copies = send_all(seq_n, lambda k: full_ref.at[ms], full_ref.at[ms], 2, seq_peer)
         for copy in copies:
             copy.wait()
 
-    ag_rows = param_rows + groups * filter_rows
+    vmem = pl.BlockSpec(memory_space=pltpu.VMEM)
     return pl.pallas_call(
         kernel,
         out_shape=(
-            jax.ShapeDtypeStruct((seq_n, param_rows, lanes), msg.dtype),
-            jax.ShapeDtypeStruct((groups, filter_rows, lanes), msg.dtype),
+            jax.ShapeDtypeStruct(out_msg.shape, out_msg.dtype),
+            jax.ShapeDtypeStruct((seq_n, param_rows, width), jnp.float32),
+            jax.ShapeDtypeStruct((groups, filter_rows, width), jnp.float32),
         ),
-        in_specs=[pl.BlockSpec(memory_space=pltpu.VMEM)],
-        out_specs=(pl.BlockSpec(memory_space=pltpu.VMEM), pl.BlockSpec(memory_space=pltpu.VMEM)),
+        in_specs=[vmem] * 4,
+        out_specs=(vmem, vmem, vmem),
         scratch_shapes=[
-            pltpu.VMEM((seq_n, msg_rows, lanes), msg.dtype),
-            pltpu.VMEM((dp_n, ag_rows, lanes), msg.dtype),
-            pltpu.SemaphoreType.DMA((3, 2, max(seq_n, dp_n))),
+            pltpu.VMEM((seq_n, msg_rows, width), jnp.float32),
+            pltpu.VMEM((seq_n, msg_rows, width), jnp.float32),
+            pltpu.VMEM((dp_n, ag_rows, width), jnp.float32),
+            pltpu.SemaphoreType.DMA((4, 2, max(seq_n, dp_n))),
         ],
         compiler_params=pltpu.CompilerParams(collective_id=0, has_side_effects=True),
-    )(msg)
+    )(out_msg, series_blk, cot_blk, side)
 
 
 def shards(series, cotangent, w_in, w_out, taps, skip_one, skip_two, filter_one, filter_two):
@@ -229,7 +250,24 @@
     prod_sent = jnp.swapaxes(product.reshape(seq_n, half // seq_n, per, LANES), 1, 2)
     prod_sent = prod_sent.reshape(seq_n, per, block)
     dp_sent = jnp.swapaxes(d_proj.reshape(3 * per, seq_n, block), 0, 1)
-    back = lax.all_to_all(jnp.concatenate([prod_sent, dp_sent], axis=1), "seq", 0, 0, tiled=True)
+    small = jnp.concatenate(
+        [
+            local_taps.reshape(3, 3, 1, per),
+            jnp.stack([local_skip1, local_skip2, jnp.zeros_like(local_skip1)]).reshape(3, 1, 1, per),
+        ],
+        axis=1,
+    )
+    small_full = lax.dynamic_update_slice(
+        jnp.zeros((3, 4, seq_n, per), jnp.float32), small, (0, 0, me, 0)
+    )
+    small_sent = jnp.transpose(grad_scale * small_full, (2, 0, 1, 3)).reshape(seq_n, -1)
+    small_sent = jnp.pad(small_sent, ((0, 0), (0, 2 * block - small_sent.shape[1])))
+    fg_sent = jnp.swapaxes(grad_scale * filt_grad.reshape(2, seq_n, block), 0, 1)
+    side = jnp.concatenate([small_sent, fg_sent.reshape(seq_n, -1)], axis=1).reshape(seq_n, -1, LANES)
+    back, full, fg = tail_rounds(
+        jnp.concatenate([prod_sent, dp_sent], axis=1), series[0], cotangent[0], side,
+        grad_scale, per_group, dp_n,
+    )
     prod_rows = jnp.transpose(back[:, :per], (2, 0, 1)).reshape(block, width)
     dp_rows = jnp.transpose(back[:, per:].reshape(seq_n, 3, per, block), (3, 1, 0, 2))
     dp_rows = dp_rows.reshape(block, 3 * width)
@@ -240,37 +278,15 @@
     ).astype(jnp.bfloat16)
     d_series = d_series.reshape(1, block, width)
 
-    local_w_in = jnp.einsum("td,tc->dc", series[0], dp_rows, preferred_element_type=jnp.float32)
-    local_w_out = jnp.einsum("tc,td->cd", prod_rows, cotangent[0], preferred_element_type=jnp.float32)
-    small = jnp.concatenate(
-        [
-            local_taps.reshape(3, 3, 1, per),
-            jnp.stack([local_skip1, local_skip2, jnp.zeros_like(local_skip1)]).reshape(3, 1, 1, per),
-        ],
-        axis=1,
-    )
-    small_full = lax.dynamic_update_slice(
-        jnp.zeros((3, 4, seq_n, per), jnp.float32), small, (0, 0, me, 0)
-    )
-    params = grad_scale * jnp.concatenate(
-        [local_w_in.reshape(-1), local_w_out.reshape(-1), small_full.reshape(-1)]
-    )
-    n_params = params.shape[0]
-    chunk = -(-n_params // (seq_n * 8 * LANES)) * 8 * LANES
-    params = jnp.pad(params, (0, chunk * seq_n - n_params)).reshape(seq_n, -1, LANES)
-    fg_sent = jnp.swapaxes(grad_scale * filt_grad.reshape(2, seq_n, block), 0, 1)
-    fg_sent = fg_sent.reshape(seq_n, -1, LANES)
-    full, fg = reduce_rounds(jnp.concatenate([params, fg_sent], axis=1), params.shape[1], per_group, dp_n)
     fg_blocks = jnp.swapaxes(fg.reshape(filters, 2, block), 0, 1)
-    full = full.reshape(-1)
-    sizes = [width * 3 * width, width * width, 3 * 4 * width]
-    offsets = np.cumsum([0] + sizes)
-    grad_w_in = full[offsets[0] : offsets[1]].reshape(width, 3 * width)
-    grad_w_out = full[offsets[1] : offsets[2]].reshape(width, width)
-    small_full = full[offsets[2] : offsets[3]].reshape(3, 4, width)
-    grad_taps = small_full[:, :3].reshape(3, 3 * width)
-    grad_skip_one = small_full[0, 3]
-    grad_skip_two = small_full[1, 3]
+    grad_w_in = jnp.transpose(full[:, : 3 * per].reshape(seq_n, 3, per, width), (3, 1, 0, 2))
+    grad_w_in = grad_w_in.reshape(width, 3 * width)
+    grad_w_out = full[:, 3 * per : 4 * per].reshape(width, width)
+    small_all = full[:, 4 * per :].reshape(seq_n, -1)[:, : 3 * 4 * per].reshape(seq_n, 3, 4, per)
+    small_all = jnp.transpose(small_all, (1, 2, 0, 3)).reshape(3, 4, width)
+    grad_taps = small_all[:, :3].reshape(3, 3 * width)
+    grad_skip_one = small_all[0, 3]
+    grad_skip_two = small_all[1, 3]
 
     return (
         output,

time: 117 us -> 112 us (0.957)
  Pallas kernels: 27.4 us -> 36.8 us
  waiting for transfers between devices: 28.8 us -> 19.5 us
  starting transfers between devices: 13.6 us -> 9.43 us
  local copies, waits for them, and re-layouts: 16.6 us -> 13.4 us
  other arithmetic: 10.3 us -> 12.2 us
    all_to_all x1 -> x0, waiting for transfers between devices: 10.3 us -> none  [shards(): lax.all_to_all(jnp.concatenate([prod_sent, dp_sent], axis=1), 'seq', 0, 0...]
    pallas_call x1, Pallas kernels: 27.4 us -> 36.8 us  [tail_rounds(): pl.pallas_call(kernel, out_shape=(jax.ShapeDtypeStruct(out_msg.shape, out...]
    all_to_all x1 -> x0, starting transfers between devices: 4.21 us -> none  [shards(): lax.all_to_all(jnp.concatenate([prod_sent, dp_sent], axis=1), 'seq', 0, 0...]
    reduce_sum x1, other arithmetic: 0.05 us -> 1.26 us  [shards(): jnp.sum(cmul(g1_spec, v_spec, conj=True), axis=1, keepdims=True)]
    unnamed x66 -> x56, local copies, waits for them, and re-layouts: 6.29 us -> 5.37 us
  transfers between devices with their start and end apart: 2 -> 1, of which waited for: 2 -> 1; matrix products, arithmetic and copies ran while one was open for 2% -> 1% of each run, Pallas kernels for 0% -> 0%
where the time goes in v13:
time: 112 us; the launch traced here: 111 us
  Pallas kernels  36.8 us (33%)
  waiting for transfers between devices  19.5 us (17%)
  matrix products  18.2 us (16%)
  local copies, waits for them, and re-layouts  13.4 us (12%)
  other arithmetic  12.2 us (11%)
  starting transfers between devices  9.43 us (8%)
  between operations  1.43 us (1%)
    pallas_call x1, Pallas kernels, tail_rounds(): pl.pallas_call(kernel, out_shape=(jax.ShapeDtypeStruct(out_msg.shape, out...  36.8 us
    all_to_all x1, waiting for transfers between devices, shards(): lax.all_to_all(jnp.concatenate([proj_blk, dprod_blk, rows_sent], axis=1),...  19.5 us
    all_to_all x1, starting transfers between devices, shards(): lax.all_to_all(jnp.concatenate([proj_blk, dprod_blk, rows_sent], axis=1),...  9.43 us
    unnamed x56, local copies, waits for them, and re-layouts  5.37 us
    dot_general x5, matrix products, spectrum(): a = jnp.einsum('kn,ncm->kcm', tab['fwd1'], x, precision=PRECISION)  4.77 us
    dot_general x5, matrix products, spectrum(): return jnp.einsum('kcm,mj->kcj', cat, tab['fwd2'], precision=PRECISION)  4.48 us
    sub x3, other arithmetic, cmul(): return jnp.concatenate([ar * br - ai * bi, ar * bi + ai * br], axis=-1)  2.87 us
    dot_general x5, matrix products, signal(): return jnp.einsum('nk,kcm->ncm', tab['inv1'], stacked, precision=PRECISION)  2.87 us
  transfers between devices with their start and end apart: 1, of which 1 were waited for; matrix products, arithmetic and copies ran while one was open for 1% of the time, Pallas kernels for 0%

profile of v13, /device:TPU:1, one launch (start us, length us, event | category | flops | bytes accessed | tf_op | source)
XLA Modules:
  0.0 111.0 jit_solution(5063101138711638122)
XLA Ops:
  0.7 1.0 copy.93
  1.7 1.2 %convolution_bitcast_fusion = f32[16,3,8,512]{3,2,0,1:T(8,128)S(1)} fusion(bf16[3,16,8,128]{3,2,1,0:T(8,128)(2,1)S(1)} %bitcast.200, bf16[1,512,128]{2,1,0:T(8,128)(2,1)} %param.15), kind=kOutput, calls=%fused_computation.1 | convolution fusion | flops 50331648 | bytes 1015808 | tf_op jit(solution)/shard_map/td,dc->ct/dot_general | solution.py:188
  3.3 1.2 %pad_maximum_fusion = f32[16,34,512]{2,1,0:T(8,128)} fusion(f32[16,2,512]{2,1,0:T(2,128)S(1)} %bitcast.201, f32[16,8,512]{2,1,0:T(8,128)S(1)} %fusion.68, f32[16,24,512]{2,1,0:T(8,128)S(1)} %bitcast.187), kind=kLoop, calls=%fused_computation | loop fusion | flops 557056 | bytes 2228224 | tf_op jit(solution)/shard_map/concatenate | solution.py:194
  4.5 9.4 %all-to-all-start = ((f32[16,34,512]{2,1,0:T(8,128)}), f32[16,34,512]{2,1,0:T(8,128)S(1)}, u32[]{:S(2)}, u32[]{:S(2)}) async-start(f32[16,34,512]{2,1,0:T(8,128)} %pad_maximum_fusion), calls=%async_computation | async-start | bytes 2621440 | tf_op jit(solution)/shard_map/all_to_all | solution.py:193
  14.6 19.5 %all-to-all-done = f32[16,34,512]{2,1,0:T(8,128)S(1)} async-done(((f32[16,34,512]{2,1,0:T(8,128)}), f32[16,34,512]{2,1,0:T(8,128)S(1)}, u32[]{:S(2)}, u32[]{:S(2)}) %all-to-all-start) | async-done | bytes 1114144 | tf_op jit(solution)/shard_map/all_to_all | solution.py:193
  34.1 1.1 slice_bitcast_fusion.1
  36.1 1.6 %fusion.64 = f32[256,8,128]{0,2,1:T(8,128)} fusion(f32[256,64,1]{0,1,2:T(8,128)S(1)} %copy-done.13, f32[64,24,128]{2,0,1:T(8,128)S(1)} %bitcast.171), kind=kOutput, calls=%fused_computation.127 | convolution fusion | flops 100663296 | bytes 1376256 | tf_op jit(solution)/shard_map/kn,ncm->kcm/dot_general | solution.py:42
  37.8 1.6 %fusion.93 = f32[256,8,128]{0,2,1:T(8,128)} fusion(f32[256,64,1]{0,1,2:T(8,128)S(1)} %copy-done.13, f32[64,24,128]{2,0,1:T(8,128)S(1)} %bitcast.172, f32[64,8,128]{2,1,0:T(8,128)S(1)} %bitcast.183), kind=kOutput, calls=%fused_computation.188 | convolution fusion | flops 100728832 | bytes 1638400 | tf_op jit(solution)/shard_map/kn,ncm->kcm/dot_general | solution.py:42
  39.8 1.4 %multiply_subtract_fusion.7 = (f32[128,8,128]{0,2,1:T(8,128)S(1)}, f32[128,8,128]{0,2,1:T(8,128)S(1)}) fusion(f32[256,8,128]{0,2,1:T(8,128)} %fusion.93, f32[128,128]{0,1:T(8,128)S(1)} %copy-done.4, f32[128,128]{0,1:T(8,128)S(1)} %copy-done.3), kind=kLoop, calls=%fused_computation.93 | loop fusion | flops 786432 | bytes 2228224 | tf_op jit(solution)/shard_map/sub | solution.py:45
  41.7 1.0 fusion.25
  42.9 0.8 copy-done.1
  44.5 0.7 copy-done.12
  46.6 1.0 fusion.3
  47.7 1.0 fusion.36
  48.7 1.3 %multiply_subtract_fusion.1 = (f32[128,8,128]{2,0,1:T(8,128)}, f32[128,8,128]{2,0,1:T(8,128)}, f32[128,8,128]{2,0,1:T(8,128)S(1)}, f32[128,8,128]{2,0,1:T(8,128)...) fusion(f32[128,8,256]{2,0,1:T(8,128)S(1)} %fusion.36, f32[128,8,256]{2,0,1:T(8,128)S(1)} %fusion.3, ...), kind=kLoop, calls=%fused_computation.81 | loop fusion | flops 2490368 | bytes 5439488 | tf_op jit(solution)/shard_map/sub | solution.py:62
  51.5 0.6 convolution_add_fusion.3
  52.9 1.0 fusion.14
  54.0 1.4 %multiply_subtract_fusion = (f32[128,8,128]{2,0,1:T(8,128)}, f32[128,8,128]{2,0,1:T(8,128)}, f32[128,8,128]{2,0,1:T(8,128)S(1)}, f32[128,8,128]{2,0,1:T(8,128)S(1)}) fusion(f32[128,8,256]{2,0,1:T(8,128)S(1)} %fusion.25, f32[128,8,256]{2,0,1:T(8,128)S(1)} %fusion.14, f32[128,128]{1,0:T(8,128)S(1)} %get-tuple-element.92, f32[128,128]{1,0:T(8,128)S(1)} %get-tuple-element.91), kind=kLoop, calls=%fused_computation.79 | loop fusion | flops 1703936 | bytes 4325376 | tf_op jit(solution)/shard_map/sub | solution.py:62
  55.4 0.6 fusion.18
  56.1 0.6 convolution_add_fusion
  56.8 0.7 multiply_reduce_fusion.3
  59.7 1.2 %fusion.52 = f32[24]{0:T(128)S(1)} fusion(f32[24,64,128]{2,1,0:T(8,128)S(1)} %reshape.150, f32[64,8,128]{2,0,1:T(8,128)S(1)} %get-tuple-element.81, f32[64,8,128]{2,0,1:T(8,128)S(1)} %copy-done.8, f32[64,8,128]{2,0,1:T(8,128)} %copy-done.9), kind=kLoop, calls=%fused_computation.70 | loop fusion | flops 786408 | bytes 1572960 | tf_op jit(solution)/shard_map/reduce_sum | solution.py:246
  61.4 0.9 dynamic_update_slice.3
  62.4 0.8 copy.149
  63.2 1.3 %maximum_reduce_fusion = f32[128,256]{1,0:T(8,128)S(1)} fusion(f32[128,8,128]{2,0,1:T(8,128)} %get-tuple-element.41, f32[128,8,128]{2,0,1:T(8,128)} %get-tuple-element.40), kind=kLoop, calls=%fused_computation.56 | loop fusion | flops 491520 | bytes 1179648 | tf_op jit(solution)/shard_map/reduce_sum | solution.py:231
  66.1 0.7 pad_maximum_fusion.4.side_ref
  66.8 0.9 pad_maximum_fusion.2.out_ref
  67.6 36.8 %shard_map.214 = (bf16[16,32,512]{2,1,0:T(8,128)(2,1)}, f32[16,40,128]{2,1,0:T(8,128)}, f32[8,8,128]{2,1,0:T(8,128)}) custom-call(bf16[16,32,512]{2,1,0:T(8,128)(2,1)} %pad_maximum_fusion.2.out_ref, bf16[512,128]{1,0:T(8,128)(2,1)} %bitcast.198, bf16[512,128]{1,0:T(8,128)(2,1)} %bitcast.194, f32[16,16,128]{2,1,0:T(8,128)} %pad_maximum_fusion.4.side_ref), custom_call_target="tpu_custom_call" | custom-call | tf_op jit(solution)/shard_map/pallas_call | solution.py:146
  104.4 1.6 %fusion.95 = (f32[16,8,128]{2,1,0:T(8,128)S(1)}, f32[128,128]{1,0:T(8,128)}) fusion(f32[16,40,128]{2,1,0:T(8,128)} %get-tuple-element.13), kind=kLoop, calls=%fused_computation.190 | loop fusion | bytes 262144 | tf_op jit(solution)/shard_map/slice | solution.py:285
  107.1 0.9 fusion.1
  108.0 1.0 fusion
  109.5 0.8 copy.132
  (125 shorter events, 13.9 us)
Async XLA Ops:
  0.6 2.4 %copy-start = (bf16[128,128]{1,0:T(8,128)(2,1)S(1)}, bf16[128,128]{1,0:T(8,128)(2,1)}, u32[]{:S(2)}) copy-start(bf16[128,128]{1,0:T(8,128)(2,1)} %param.18) | copy-start | bytes 98308
  1.7 1.3 %copy-start.20 = (f32[8,512]{1,0:T(8,128)S(1)}, f32[8,512]{1,0:T(8,128)}, u32[]{:S(2)}) copy-start(f32[8,512]{1,0:T(8,128)} %param.23) | copy-start | bytes 49156
  1.7 1.3 %copy-start.21 = (f32[8,512]{1,0:T(8,128)S(1)}, f32[8,512]{1,0:T(8,128)}, u32[]{:S(2)}) copy-start(f32[8,512]{1,0:T(8,128)} %param.22) | copy-start | bytes 49156
  1.7 1.4 %copy-start.14 = (bf16[1,512,128]{2,1,0:T(8,128)(2,1)S(1)}, bf16[1,512,128]{2,1,0:T(8,128)(2,1)}, u32[]{:S(2)}) copy-start(bf16[1,512,128]{2,1,0:T(8,128)(2,1)} %param.16) | copy-start | bytes 393220
  4.5 9.4 %copy-start.22 = (f32[3,384]{1,0:T(4,128)S(1)}, f32[3,384]{1,0:T(4,128)}, u32[]{:S(2)}) copy-start(f32[3,384]{1,0:T(4,128)} %param.19) | copy-start | bytes 13828
  4.5 9.8 %copy-start.23 = (f32[128]{0:T(128)S(1)}, f32[128]{0:T(128)}, u32[]{:S(2)}) copy-start(f32[128]{0:T(128)} %param.20) | copy-start | bytes 1540
  4.5 9.9 %copy-start.24 = (f32[128]{0:T(128)S(1)}, f32[128]{0:T(128)}, u32[]{:S(2)}) copy-start(f32[128]{0:T(128)} %param.21) | copy-start | bytes 1540
  4.5 29.6 %all-to-all-start = ((f32[16,34,512]{2,1,0:T(8,128)}), f32[16,34,512]{2,1,0:T(8,128)S(1)}, u32[]{:S(2)}, u32[]{:S(2)}) async-start(f32[16,34,512]{2,1,0:T(8,128)} %pad_maximum_fusion), calls=%async_computation | async-start | bytes 2621440 | tf_op jit(solution)/shard_map/all_to_all | solution.py:193
  35.3 0.8 copy-start.13
  37.8 2.0 %copy-start.3 = (f32[128,128]{0,1:T(8,128)S(1)}, f32[128,128]{0,1:T(8,128)}, u32[]{:S(2)}) copy-start(f32[128,128]{0,1:T(8,128)} %constant.42.clone) | copy-start | bytes 196612
  37.8 2.0 %copy-start.4 = (f32[128,128]{0,1:T(8,128)S(1)}, f32[128,128]{0,1:T(8,128)}, u32[]{:S(2)}) copy-start(f32[128,128]{0,1:T(8,128)} %constant.43.clone) | copy-start | bytes 196612
  39.8 1.4 %copy-start.2 = (f32[256,256,1]{1,0,2:T(8,128)S(1)}, f32[256,256,1]{1,0,2:T(8,128)}, u32[]{:S(2)}) copy-start(f32[256,256,1]{1,0,2:T(8,128)} %constant.58) | copy-start | bytes 786436
  42.7 1.0 copy-start.1
  44.3 0.8 copy-start.12
  45.1 1.2 %copy-start.5 = (f32[256,8,128]{0,2,1:T(8,128)S(1)}, f32[256,8,128]{0,2,1:T(8,128)}, u32[]{:S(2)}) copy-start(f32[256,8,128]{0,2,1:T(8,128)} %fusion.64) | copy-start | bytes 3145732
  56.8 1.9 %copy-start.9 = (f32[64,8,128]{2,0,1:T(8,128)}, f32[64,8,128]{2,0,1:T(8,128)S(1)}, u32[]{:S(2)}) copy-start(f32[64,8,128]{2,0,1:T(8,128)S(1)} %convolution_add_fusion) | copy-start | bytes 786436
  57.5 0.7 copy-start.7
  57.6 1.2 %copy-start.6 = (f32[24,16,512]{2,0,1:T(8,128)S(1)}, f32[24,16,512]{2,0,1:T(8,128)}, u32[]{:S(2)}) copy-start(f32[24,16,512]{2,0,1:T(8,128)} %get-tuple-element.44) | copy-start | bytes 2359300
  58.7 0.9 copy-start.8
  61.4 3.1 %copy-start.10 = (f32[128,8,128]{2,0,1:T(8,128)S(1)}, f32[128,8,128]{2,0,1:T(8,128)}, u32[]{:S(2)}) copy-start(f32[128,8,128]{2,0,1:T(8,128)} %get-tuple-element.42) | copy-start | bytes 1572868
  61.4 3.1 %copy-start.11 = (f32[128,8,128]{2,0,1:T(8,128)S(1)}, f32[128,8,128]{2,0,1:T(8,128)}, u32[]{:S(2)}) copy-start(f32[128,8,128]{2,0,1:T(8,128)} %get-tuple-element.43) | copy-start | bytes 1572868
  65.2 0.8 copy-start.18
  104.4 2.6 %copy-start.17 = (f32[16,40,128]{2,1,0:T(8,128)S(1)}, f32[16,40,128]{2,1,0:T(8,128)}, u32[]{:S(2)}) copy-start(f32[16,40,128]{2,1,0:T(8,128)} %get-tuple-element.13) | copy-start | bytes 983044
  104.4 2.6 %copy-start.15 = (bf16[16,32,512]{2,1,0:T(8,128)(2,1)S(1)}, bf16[16,32,512]{2,1,0:T(8,128)(2,1)}, u32[]{:S(2)}) copy-start(bf16[16,32,512]{2,1,0:T(8,128)(2,1)} %get-tuple-element.12) | copy-start | bytes 1572868
  106.2 1.7 %copy-start.16 = (bf16[128,384]{1,0:T(8,128)(2,1)S(1)}, bf16[128,384]{1,0:T(8,128)(2,1)}, u32[]{:S(2)}) copy-start(bf16[128,384]{1,0:T(8,128)(2,1)} %param.17) | copy-start | bytes 294916
  107.1 3.3 %copy-start.19 = (f32[8,8,128]{2,1,0:T(8,128)S(1)}, f32[8,8,128]{2,1,0:T(8,128)}, u32[]{:S(2)}) copy-start(f32[8,8,128]{2,1,0:T(8,128)} %get-tuple-element.14) | copy-start | bytes 98308

commit v14 on v13

--- a/solution.py
+++ b/solution.py
@@ -72,6 +72,55 @@
     return jnp.swapaxes(x, 0, 1).reshape(c, half * lanes)
 
 
+def exchange(x, axis, ident):
+    n = x.shape[0]
+    mesh_axes = ("dp", "seq")
+
+    def where(p):
+        return tuple(p if name == axis else lax.axis_index(name) for name in mesh_axes)
+
+    def kernel(x_ref, y_ref, send_sem, recv_sem):
+        me = lax.axis_index(axis)
+        barrier = pltpu.get_barrier_semaphore()
+        for k in range(1, n):
+            pl.semaphore_signal(
+                barrier, inc=1, device_id=where(lax.rem(me + k, n)),
+                device_id_type=pl.DeviceIdType.MESH,
+            )
+        pl.semaphore_wait(barrier, n - 1)
+        copies = []
+        for k in range(1, n):
+            p = lax.rem(me + k, n)
+            copy = pltpu.make_async_remote_copy(
+                src_ref=x_ref.at[p],
+                dst_ref=y_ref.at[me],
+                send_sem=send_sem.at[k],
+                recv_sem=recv_sem.at[k],
+                device_id=where(p),
+                device_id_type=pl.DeviceIdType.MESH,
+            )
+            copy.start()
+            copies.append(copy)
+        y_ref[pl.ds(me, 1)] = x_ref[pl.ds(me, 1)]
+        for copy in copies:
+            copy.wait()
+
+    return pl.pallas_call(
+        kernel,
+        out_shape=jax.ShapeDtypeStruct(x.shape, x.dtype),
+        in_specs=[pl.BlockSpec(memory_space=pltpu.VMEM)],
+        out_specs=pl.BlockSpec(memory_space=pltpu.VMEM),
+        scratch_shapes=[pltpu.SemaphoreType.DMA((n,)), pltpu.SemaphoreType.DMA((n,))],
+        compiler_params=pltpu.CompilerParams(collective_id=ident, has_side_effects=True),
+    )(x)
+
+
+def swap_blocks(x, axis, ident):
+    shape = x.shape
+    flat = x.reshape(shape[0], -1, LANES)
+    return exchange(flat, axis, ident).reshape(shape)
+
+
 def tail_rounds(out_msg, series_blk, cot_blk, side, scale, pair, dp_n):
     seq_n, out_rows, block = out_msg.shape
     per = out_rows // 4
@@ -190,9 +239,7 @@
     dprod_blk = jnp.einsum("td,cd->ct", cotangent[0], w_out, preferred_element_type=jnp.float32)
     dprod_blk = dprod_blk.reshape(seq_n, per, block)
     rows_sent = jnp.repeat(jnp.swapaxes(jnp.stack([filter_one, filter_two]), 0, 1), per_group, axis=0)
-    got = lax.all_to_all(
-        jnp.concatenate([proj_blk, dprod_blk, rows_sent], axis=1), "seq", 0, 0, tiled=True
-    )
+    got = swap_blocks(jnp.concatenate([proj_blk, dprod_blk, rows_sent], axis=1), "seq", 1)
     proj = jnp.swapaxes(got[:, : 3 * per], 0, 1).reshape(3 * per, length)
     d_product = jnp.swapaxes(
         got[:, 3 * per : 4 * per].reshape(seq_n, per, block // LANES, LANES), 1, 2

time: 112 us -> 116 us (1.036)
  Pallas kernels: 36.8 us -> 64.3 us
  waiting for transfers between devices: 19.5 us -> 0 us
  starting transfers between devices: 9.43 us -> 0 us
  local copies, waits for them, and re-layouts: 13.4 us -> 18.2 us
    pallas_call x0 -> x1, Pallas kernels: none -> 26.5 us  [exchange(): pl.pallas_call(kernel, out_shape=jax.ShapeDtypeStruct(x.shape, x.dtype),...]
    all_to_all x1 -> x0, waiting for transfers between devices: 19.5 us -> none  [shards(): lax.all_to_all(jnp.concatenate([proj_blk, dprod_blk, rows_sent], axis=1),...]
    all_to_all x1 -> x0, starting transfers between devices: 9.43 us -> none  [shards(): lax.all_to_all(jnp.concatenate([proj_blk, dprod_blk, rows_sent], axis=1),...]
    reshape x0 -> x2, local copies, waits for them, and re-layouts: none -> 2.53 us  [the longest x1 1.42 us: swap_blocks(): return exchange(flat, axis, ident).reshape(shape)]
    dot_general x5, matrix products: 4.77 us -> 2.81 us  [spectrum(): a = jnp.einsum('kn,ncm->kcm', tab['fwd1'], x, precision=PRECISION)]
    dot_general x5, matrix products: 2.87 us -> 4.83 us  [signal(): return jnp.einsum('nk,kcm->ncm', tab['inv1'], stacked, precision=PRECISION)]
    sub x4, other arithmetic: 1.76 us -> 0.56 us  [spectrum(): cat = jnp.concatenate([ar * tr - ai * ti, ar * ti + ai * tr], axis=-1)]
  transfers between devices with their start and end apart: 1 -> 0, of which waited for: 1 -> 0; matrix products, arithmetic and copies ran while one was open for 1% -> 0% of each run, Pallas kernels for 0% -> 0%
where the time goes in v14:
time: 116 us
  Pallas kernels  64.3 us (55%)
  matrix products  19.3 us (17%)
  local copies, waits for them, and re-layouts  18.2 us (16%)
  other arithmetic  12.4 us (11%)
  between operations  1.5 us (1%)
    pallas_call x1, Pallas kernels, tail_rounds(): pl.pallas_call(kernel, out_shape=(jax.ShapeDtypeStruct(out_msg.shape, out...  37.8 us
    pallas_call x1, Pallas kernels, exchange(): pl.pallas_call(kernel, out_shape=jax.ShapeDtypeStruct(x.shape, x.dtype),...  26.5 us
    unnamed x56, local copies, waits for them, and re-layouts  5.37 us
    dot_general x5, matrix products, signal(): return jnp.einsum('nk,kcm->ncm', tab['inv1'], stacked, precision=PRECISION)  4.83 us
    dot_general x5, matrix products, spectrum(): return jnp.einsum('kcm,mj->kcj', cat, tab['fwd2'], precision=PRECISION)  4.64 us
    dot_general x5, matrix products, signal(): b = jnp.einsum('kcj,jm->kcm', s, tab['inv2'], precision=PRECISION)  2.86 us
    dot_general x5, matrix products, spectrum(): a = jnp.einsum('kn,ncm->kcm', tab['fwd1'], x, precision=PRECISION)  2.81 us
    sub x3, other arithmetic, cmul(): return jnp.concatenate([ar * br - ai * bi, ar * bi + ai * br], axis=-1)  2.71 us

profile of v14, /device:TPU:1, one launch (start us, length us, event | category | flops | bytes accessed | tf_op | source)
XLA Modules:
  0.0 115.7 jit_solution(10301451196992451639)
XLA Ops:
  0.7 0.8 reshape.144
  1.7 1.0 copy.56
  2.8 1.2 %convolution_bitcast_fusion = f32[16,3,8,512]{3,2,0,1:T(8,128)S(1)} fusion(bf16[3,16,8,128]{3,2,1,0:T(8,128)(2,1)S(1)} %bitcast.200, bf16[1,512,128]{2,1,0:T(8,128)(2,1)} %param.15), kind=kOutput, calls=%fused_computation.1 | convolution fusion | flops 50331648 | bytes 1015808 | tf_op jit(solution)/shard_map/td,dc->ct/dot_general | solution.py:237
  4.6 1.1 reshape.147.x_ref
  5.7 26.5 %shard_map.214 = f32[16,136,128]{2,1,0:T(8,128)} custom-call(f32[16,136,128]{2,1,0:T(8,128)} %reshape.147.x_ref), custom_call_target="tpu_custom_call" | custom-call | tf_op jit(solution)/shard_map/pallas_call | solution.py:108
  32.2 1.4 %reshape.148 = f32[16,34,512]{2,1,0:T(8,128)S(1)} reshape(f32[16,136,128]{2,1,0:T(8,128)} %shard_map.214) | data formatting | bytes 2228224 | tf_op jit(solution)/shard_map/reshape | solution.py:121
  33.6 1.3 %slice_bitcast_fusion.1 = (f32[24,16,512]{2,0,1:T(8,128)}, f32[16,3,8,512]{3,2,1,0:T(8,128)S(1)}) fusion(f32[16,34,512]{2,1,0:T(8,128)S(1)} %reshape.148), kind=kLoop, calls=%fused_computation.76 | loop fusion | bytes 2359296 | tf_op jit(solution)/shard_map/transpose | solution.py:243
  35.6 1.0 fusion.94
  37.5 0.8 copy-done.2
  38.3 1.0 fusion.25
  39.3 1.0 slice_bitcast_fusion.6
  41.1 0.7 negate_bitcast_fusion
  42.8 1.1 multiply_add_fusion.5
  44.1 1.9 %convolution_add_fusion.1 = f32[64,8,128]{2,0,1:T(8,128)S(1)} fusion(f32[64,256,1]{1,0,2:T(8,128)S(1)} %copy-done.11, f32[128,8,128]{0,2,1:T(8,128)} %get-tuple-element.48, f32[128,8,128]{0,2,1:T(8,128)} %get-tuple-element.47, f32[8]{0:T(128)S(1)} %get-tuple-element.95, f32[64,24,128]{2,0,1:T(8,128)S(1)} %bitcast.172, f32[64,8,128]{2,1,0:T(8,128)} %bitcast.184), kind=kOutput, calls=%fused_computation.3 | convolution fusion | flops 101122048 | bytes 1900576 | tf_op jit(solution)/shard_map/nk,kcm->ncm/dot_general | solution.py:54
  47.5 1.0 fusion.3
  48.6 1.0 fusion.36
  49.6 1.3 %multiply_subtract_fusion.1 = (f32[128,8,128]{2,0,1:T(8,128)}, f32[128,8,128]{2,0,1:T(8,128)}, f32[128,8,128]{2,0,1:T(8,128)S(1)}, f32[128,8,128]{2,0,1:T(8,128)...) fusion(f32[128,8,256]{2,0,1:T(8,128)S(1)} %fusion.36, f32[128,8,256]{2,0,1:T(8,128)S(1)} %fusion.3, ...), kind=kLoop, calls=%fused_computation.81 | loop fusion | flops 2490368 | bytes 5439488 | tf_op jit(solution)/shard_map/sub | solution.py:62
  52.4 1.3 %convolution_add_fusion = f32[64,8,128]{2,0,1:T(8,128)} fusion(f32[64,256,1]{1,0,2:T(8,128)S(1)} %copy-done.11, f32[128,8,128]{0,2,1:T(8,128)S(1)} %get-tuple-element.42, f32[128,8,128]{0,2,1:T(8,128)S(1)} %get-tuple-element.41, f32[8]{0:T(128)S(1)} %get-tuple-element.94, f32[64,8,128]{2,0,1:T(8,128)S(1)} %convolution_add_fusion.1, ...), kind=kOutput, calls=%fused_computation.2 | convolution fusion | flops 101122048 | bytes 1900576 | tf_op jit(solution)/shard_map/nk,kcm->ncm/dot_general | solution.py:54
  55.2 1.2 %fusion.14 = f32[128,8,256]{2,0,1:T(8,128)S(1)} fusion(f32[256,256,1]{1,0,2:T(8,128)S(1)} %copy-done.2, f32[128,8,128]{0,2,1:T(8,128)S(1)} %get-tuple-element.58, f32[128,8,128]{0,2,1:T(8,128)S(1)} %get-tuple-element.57), kind=kOutput, calls=%fused_computation.23 | convolution fusion | flops 402915328 | bytes 2359296 | tf_op jit(solution)/shard_map/kcm,mj->kcj/dot_general | solution.py:46
  56.4 1.2 %multiply_subtract_fusion = (f32[128,8,128]{2,0,1:T(8,128)}, f32[128,8,128]{2,0,1:T(8,128)}, f32[128,8,128]{2,0,1:T(8,128)S(1)}, f32[128,8,128]{2,0,1:T(8,128)S(1)}) fusion(f32[128,8,256]{2,0,1:T(8,128)S(1)} %fusion.25, f32[128,8,256]{2,0,1:T(8,128)S(1)} %fusion.14, f32[128,128]{1,0:T(8,128)S(1)} %get-tuple-element.83, f32[128,128]{1,0:T(8,128)S(1)} %copy-done.16), kind=kLoop, calls=%fused_computation.79 | loop fusion | flops 1703936 | bytes 4325376 | tf_op jit(solution)/shard_map/sub | solution.py:62
  58.4 0.8 copy-done.7
  59.2 0.7 multiply_reduce_fusion.3
  60.9 1.2 %fusion.52 = f32[24]{0:T(128)S(1)} fusion(f32[24,64,128]{2,1,0:T(8,128)S(1)} %reshape.158, f32[64,8,128]{2,0,1:T(8,128)S(1)} %get-tuple-element.72, f32[64,8,128]{2,0,1:T(8,128)S(1)} %get-tuple-element.73, f32[64,8,128]{2,0,1:T(8,128)} %convolution_add_fusion), kind=kLoop, calls=%fused_computation.70 | loop fusion | flops 786408 | bytes 1572960 | tf_op jit(solution)/shard_map/reduce_sum | solution.py:293
  62.2 1.0 pad_maximum_fusion.1
  64.3 0.9 dynamic_update_slice.3
  65.5 1.3 %maximum_reduce_fusion = f32[128,256]{1,0:T(8,128)S(1)} fusion(f32[128,8,128]{2,0,1:T(8,128)} %get-tuple-element.32, f32[128,8,128]{2,0,1:T(8,128)} %get-tuple-element.31), kind=kLoop, calls=%fused_computation.56 | loop fusion | flops 491520 | bytes 1179648 | tf_op jit(solution)/shard_map/reduce_sum | solution.py:278
  69.5 0.9 pad_maximum_fusion.2.out_ref
  70.3 37.8 %shard_map.215 = (bf16[16,32,512]{2,1,0:T(8,128)(2,1)}, f32[16,40,128]{2,1,0:T(8,128)}, f32[8,8,128]{2,1,0:T(8,128)}) custom-call(bf16[16,32,512]{2,1,0:T(8,128)(2,1)} %pad_maximum_fusion.2.out_ref, bf16[512,128]{1,0:T(8,128)(2,1)} %bitcast.198, bf16[512,128]{1,0:T(8,128)(2,1)} %bitcast.194, f32[16,16,128]{2,1,0:T(8,128)} %pad_maximum_fusion.4.side_ref), custom_call_target="tpu_custom_call" | custom-call | tf_op jit(solution)/shard_map/pallas_call | solution.py:195
  108.1 1.1 slice_bitcast_fusion.2
  109.2 1.0 fusion
  112.4 0.8 copy.95
  113.2 1.8 %fusion.1 = bf16[1,512,128]{2,1,0:T(8,128)(2,1)} fusion(bf16[128,128]{1,0:T(8,128)(2,1)S(1)} %copy-done, bf16[16,32,512]{2,1,0:T(8,128)(2,1)} %get-tuple-element.12), kind=kOutput, calls=%fused_computation.9 | convolution fusion | flops 16842752 | bytes 294912 | tf_op jit(solution)/shard_map/dot_general | solution.py:321
  (126 shorter events, 17.0 us)
Async XLA Ops:
  0.6 3.5 %copy-start = (bf16[128,128]{1,0:T(8,128)(2,1)S(1)}, bf16[128,128]{1,0:T(8,128)(2,1)}, u32[]{:S(2)}) copy-start(bf16[128,128]{1,0:T(8,128)(2,1)} %param.18) | copy-start | bytes 98308
  2.8 1.3 %copy-start.13 = (bf16[1,512,128]{2,1,0:T(8,128)(2,1)S(1)}, bf16[1,512,128]{2,1,0:T(8,128)(2,1)}, u32[]{:S(2)}) copy-start(bf16[1,512,128]{2,1,0:T(8,128)(2,1)} %param.16) | copy-start | bytes 393220
  2.8 1.5 %copy-start.21 = (f32[8,512]{1,0:T(8,128)S(1)}, f32[8,512]{1,0:T(8,128)}, u32[]{:S(2)}) copy-start(f32[8,512]{1,0:T(8,128)} %param.23) | copy-start | bytes 49156
  2.8 1.5 %copy-start.22 = (f32[8,512]{1,0:T(8,128)S(1)}, f32[8,512]{1,0:T(8,128)}, u32[]{:S(2)}) copy-start(f32[8,512]{1,0:T(8,128)} %param.22) | copy-start | bytes 49156
  33.6 1.3 %copy-start.3 = (f32[16,34,512]{2,1,0:T(8,128)}, f32[16,34,512]{2,1,0:T(8,128)S(1)}, u32[]{:S(2)}) copy-start(f32[16,34,512]{2,1,0:T(8,128)S(1)} %reshape.148) | copy-start | bytes 3342340
  35.4 1.2 %copy-start.12 = (f32[256,64,1]{0,1,2:T(8,128)S(1)}, f32[256,64,1]{0,1,2:T(8,128)}, u32[]{:S(2)}) copy-start(f32[256,64,1]{0,1,2:T(8,128)} %constant.57) | copy-start | bytes 196612
  35.6 1.7 %copy-start.4 = (f32[128,128]{0,1:T(8,128)S(1)}, f32[128,128]{0,1:T(8,128)}, u32[]{:S(2)}) copy-start(f32[128,128]{0,1:T(8,128)} %constant.42.clone) | copy-start | bytes 196612
  35.6 1.7 %copy-start.5 = (f32[128,128]{0,1:T(8,128)S(1)}, f32[128,128]{0,1:T(8,128)}, u32[]{:S(2)}) copy-start(f32[128,128]{0,1:T(8,128)} %constant.43.clone) | copy-start | bytes 196612
  36.6 4.0 %copy-start.6 = (f32[16,32,128]{2,1,0:T(8,128)}, f32[16,32,128]{2,1,0:T(8,128)S(1)}, u32[]{:S(2)}) copy-start(f32[16,32,128]{2,1,0:T(8,128)S(1)} %pad_maximum_fusion.3) | copy-start | bytes 786436
  37.3 1.0 copy-start.2
  41.1 1.0 copy-start.1
  42.7 1.2 %copy-start.23 = (f32[128]{0:T(128)S(1)}, f32[128]{0:T(128)}, u32[]{:S(2)}) copy-start(f32[128]{0:T(128)} %param.20) | copy-start | bytes 1540
  42.7 1.2 %copy-start.24 = (f32[128]{0:T(128)S(1)}, f32[128]{0:T(128)}, u32[]{:S(2)}) copy-start(f32[128]{0:T(128)} %param.21) | copy-start | bytes 1540
  42.8 1.3 %copy-start.11 = (f32[64,256,1]{1,0,2:T(8,128)S(1)}, f32[64,256,1]{1,0,2:T(8,128)}, u32[]{:S(2)}) copy-start(f32[64,256,1]{1,0,2:T(8,128)} %constant.56) | copy-start | bytes 196612
  48.5 1.1 copy-start.17
  48.5 1.1 copy-start.18
  48.5 1.1 copy-start.19
  55.2 1.2 %copy-start.16 = (f32[128,128]{1,0:T(8,128)S(1)}, f32[128,128]{1,0:T(8,128)}, u32[]{:S(2)}) copy-start(f32[128,128]{1,0:T(8,128)} %get-tuple-element.82) | copy-start | bytes 196612
  58.3 1.0 copy-start.7
  59.2 1.1 copy-start.8
  64.3 2.4 %copy-start.9 = (f32[128,8,128]{2,0,1:T(8,128)S(1)}, f32[128,8,128]{2,0,1:T(8,128)}, u32[]{:S(2)}) copy-start(f32[128,8,128]{2,0,1:T(8,128)} %get-tuple-element.33) | copy-start | bytes 1572868
  64.3 2.4 %copy-start.10 = (f32[128,8,128]{2,0,1:T(8,128)S(1)}, f32[128,8,128]{2,0,1:T(8,128)}, u32[]{:S(2)}) copy-start(f32[128,8,128]{2,0,1:T(8,128)} %get-tuple-element.34) | copy-start | bytes 1572868
  70.3 38.9 %copy-start.14 = (bf16[128,384]{1,0:T(8,128)(2,1)S(1)}, bf16[128,384]{1,0:T(8,128)(2,1)}, u32[]{:S(2)}) copy-start(bf16[128,384]{1,0:T(8,128)(2,1)} %param.17) | copy-start | bytes 294916
  108.1 2.1 %copy-start.15 = (f32[16,40,128]{2,1,0:T(8,128)S(1)}, f32[16,40,128]{2,1,0:T(8,128)}, u32[]{:S(2)}) copy-start(f32[16,40,128]{2,1,0:T(8,128)} %get-tuple-element.13) | copy-start | bytes 983044
  110.2 4.8 %copy-start.20 = (f32[8,8,128]{2,1,0:T(8,128)S(1)}, f32[8,8,128]{2,1,0:T(8,128)}, u32[]{:S(2)}) copy-start(f32[8,8,128]{2,1,0:T(8,128)} %get-tuple-element.14) | copy-start | bytes 98308

commit v15 on v13

--- a/solution.py
+++ b/solution.py
@@ -72,7 +72,7 @@
     return jnp.swapaxes(x, 0, 1).reshape(c, half * lanes)
 
 
-def tail_rounds(out_msg, series_blk, cot_blk, side, scale, pair, dp_n):
+def tail_rounds(out_msg, series_blk, cot_blk, side, w_out, w_in_rows, scale, pair, dp_n):
     seq_n, out_rows, block = out_msg.shape
     per = out_rows // 4
     width = series_blk.shape[1]
@@ -84,8 +84,8 @@
     ag_rows = param_rows + groups * filter_rows
     mesh = pl.DeviceIdType.MESH
 
-    def kernel(out_ref, ser_ref, cot_ref, side_ref, back_ref, full_ref, fg_ref,
-               msg_buf, rs_buf, ag_buf, sems):
+    def kernel(out_ref, ser_ref, cot_ref, side_ref, wo_ref, wi_ref, back_ref, full_ref, fg_ref,
+               o_ref, ds_ref, msg_buf, rs_buf, ag_buf, sems):
         ms = lax.axis_index("seq")
         md = lax.axis_index("dp")
         barrier = pltpu.get_barrier_semaphore()
@@ -120,6 +120,15 @@
             msg_buf[j, : 3 * per] = scale * jnp.dot(rows[per:], ser, preferred_element_type=jnp.float32)
             msg_buf[j, 3 * per : 4 * per] = scale * jnp.dot(rows[:per], cot, preferred_element_type=jnp.float32)
         msg_buf[:, 4 * per :] = side_ref[...]
+        every = back_ref[...].astype(jnp.float32)
+        prod_t = every[:, :per].reshape(seq_n * per, block).T
+        o_ref[...] = jnp.dot(
+            prod_t, wo_ref[...].astype(jnp.float32), preferred_element_type=jnp.float32
+        ).astype(o_ref.dtype)
+        dp_t = every[:, per:].reshape(seq_n * 3 * per, block).T
+        ds_ref[...] = jnp.dot(
+            dp_t, wi_ref[...].astype(jnp.float32), preferred_element_type=jnp.float32
+        ).astype(ds_ref.dtype)
 
         copies = send_all(seq_n, lambda k: msg_buf.at[lax.rem(ms + k, seq_n)], rs_buf.at[ms], 0, seq_peer)
         rs_buf[pl.ds(ms, 1)] = msg_buf[pl.ds(ms, 1)]
@@ -149,9 +158,11 @@
             jax.ShapeDtypeStruct(out_msg.shape, out_msg.dtype),
             jax.ShapeDtypeStruct((seq_n, param_rows, width), jnp.float32),
             jax.ShapeDtypeStruct((groups, filter_rows, width), jnp.float32),
+            jax.ShapeDtypeStruct((block, width), jnp.bfloat16),
+            jax.ShapeDtypeStruct((block, width), jnp.bfloat16),
         ),
-        in_specs=[vmem] * 4,
-        out_specs=(vmem, vmem, vmem),
+        in_specs=[vmem] * 6,
+        out_specs=(vmem, vmem, vmem, vmem, vmem),
         scratch_shapes=[
             pltpu.VMEM((seq_n, msg_rows, width), jnp.float32),
             pltpu.VMEM((seq_n, msg_rows, width), jnp.float32),
@@ -159,7 +170,7 @@
             pltpu.SemaphoreType.DMA((4, 2, max(seq_n, dp_n))),
         ],
         compiler_params=pltpu.CompilerParams(collective_id=0, has_side_effects=True),
-    )(out_msg, series_blk, cot_blk, side)
+    )(out_msg, series_blk, cot_blk, side, w_out, w_in_rows)
 
 
 def shards(series, cotangent, w_in, w_out, taps, skip_one, skip_two, filter_one, filter_two):
@@ -264,18 +275,12 @@
     small_sent = jnp.pad(small_sent, ((0, 0), (0, 2 * block - small_sent.shape[1])))
     fg_sent = jnp.swapaxes(grad_scale * filt_grad.reshape(2, seq_n, block), 0, 1)
     side = jnp.concatenate([small_sent, fg_sent.reshape(seq_n, -1)], axis=1).reshape(seq_n, -1, LANES)
-    back, full, fg = tail_rounds(
+    w_in_rows = jnp.transpose(w_in.reshape(width, 3, seq_n, per), (2, 1, 3, 0)).reshape(3 * width, width)
+    _, full, fg, output, d_series = tail_rounds(
         jnp.concatenate([prod_sent, dp_sent], axis=1), series[0], cotangent[0], side,
-        grad_scale, per_group, dp_n,
-    )
-    prod_rows = jnp.transpose(back[:, :per], (2, 0, 1)).reshape(block, width)
-    dp_rows = jnp.transpose(back[:, per:].reshape(seq_n, 3, per, block), (3, 1, 0, 2))
-    dp_rows = dp_rows.reshape(block, 3 * width)
-    output = jnp.dot(prod_rows, w_out, preferred_element_type=jnp.float32).astype(jnp.bfloat16)
+        w_out, w_in_rows, grad_scale, per_group, dp_n,
+    )
     output = output.reshape(1, block, width)
-    d_series = jnp.einsum(
-        "tc,dc->td", dp_rows, w_in, preferred_element_type=jnp.float32
-    ).astype(jnp.bfloat16)
     d_series = d_series.reshape(1, block, width)
 
     fg_blocks = jnp.swapaxes(fg.reshape(filters, 2, block), 0, 1)

time: 112 us -> 111 us (level)
  local copies, waits for them, and re-layouts: 13.4 us -> 15.8 us
  waiting for transfers between devices: 19.5 us -> 17.8 us
    dot_general x2 -> x0, matrix products: 1.83 us -> none  [the longest x1 0.96 us: shards(): jnp.einsum('tc,dc->td', dp_rows, w_in, preferred_element_type=jnp.float32)]
    all_to_all x1, waiting for transfers between devices: 19.5 us -> 17.8 us  [shards(): lax.all_to_all(jnp.concatenate([proj_blk, dprod_blk, rows_sent], axis=1),...]
    unnamed x56 -> x68, local copies, waits for them, and re-layouts: 5.37 us -> 6.75 us
    dot_general x5, matrix products: 2.87 us -> 4.02 us  [signal(): return jnp.einsum('nk,kcm->ncm', tab['inv1'], stacked, precision=PRECISION)]
  transfers between devices with their start and end apart: 1 -> 1, of which waited for: 1 -> 1; matrix products, arithmetic and copies ran while one was open for 1% -> 2% of each run, Pallas kernels for 0% -> 0%
where the time goes in v15:
time: 111 us
  Pallas kernels  37.2 us (34%)
  waiting for transfers between devices  17.8 us (16%)
  matrix products  17.7 us (16%)
  local copies, waits for them, and re-layouts  15.8 us (14%)
  other arithmetic  11.5 us (10%)
  starting transfers between devices  9.42 us (8%)
  between operations  1.42 us (1%)
    pallas_call x1, Pallas kernels, tail_rounds(): pl.pallas_call(kernel, out_shape=(jax.ShapeDtypeStruct(out_msg.shape, out...  37.2 us
    all_to_all x1, waiting for transfers between devices, shards(): lax.all_to_all(jnp.concatenate([proj_blk, dprod_blk, rows_sent], axis=1),...  17.8 us
    all_to_all x1, starting transfers between devices, shards(): lax.all_to_all(jnp.concatenate([proj_blk, dprod_blk, rows_sent], axis=1),...  9.42 us
    unnamed x68, local copies, waits for them, and re-layouts  6.75 us
    dot_general x5, matrix products, spectrum(): a = jnp.einsum('kn,ncm->kcm', tab['fwd1'], x, precision=PRECISION)  4.78 us
    dot_general x5, matrix products, spectrum(): return jnp.einsum('kcm,mj->kcj', cat, tab['fwd2'], precision=PRECISION)  4.65 us
    dot_general x5, matrix products, signal(): return jnp.einsum('nk,kcm->ncm', tab['inv1'], stacked, precision=PRECISION)  4.02 us
    dot_general x5, matrix products, signal(): b = jnp.einsum('kcj,jm->kcm', s, tab['inv2'], precision=PRECISION)  2.86 us
  transfers between devices with their start and end apart: 1, of which 1 were waited for; matrix products, arithmetic and copies ran while one was open for 2% of the time, Pallas kernels for 0%

profile of v15, /device:TPU:1, one launch (start us, length us, event | category | flops | bytes accessed | tf_op | source)
XLA Modules:
  0.0 110.8 jit_solution(3786965241739164532)
XLA Ops:
  0.6 1.0 copy.95
  1.7 1.2 %convolution_bitcast_fusion = f32[16,3,8,512]{3,2,0,1:T(8,128)S(1)} fusion(bf16[3,16,8,128]{3,2,1,0:T(8,128)(2,1)S(1)} %bitcast.180, bf16[1,512,128]{2,1,0:T(8,128)(2,1)} %param.15), kind=kOutput, calls=%fused_computation.1 | convolution fusion | flops 50331648 | bytes 1015808 | tf_op jit(solution)/shard_map/td,dc->ct/dot_general | solution.py:199
  3.3 1.2 %pad_maximum_fusion = f32[16,34,512]{2,1,0:T(8,128)} fusion(f32[16,2,512]{2,1,0:T(2,128)S(1)} %bitcast.191, f32[16,8,512]{2,1,0:T(8,128)S(1)} %fusion.65, f32[16,24,512]{2,1,0:T(8,128)S(1)} %bitcast.176), kind=kLoop, calls=%fused_computation | loop fusion | flops 557056 | bytes 2228224 | tf_op jit(solution)/shard_map/concatenate | solution.py:205
  4.5 9.4 %all-to-all-start = ((f32[16,34,512]{2,1,0:T(8,128)}), f32[16,34,512]{2,1,0:T(8,128)S(1)}, u32[]{:S(2)}, u32[]{:S(2)}) async-start(f32[16,34,512]{2,1,0:T(8,128)} %pad_maximum_fusion), calls=%async_computation | async-start | bytes 2621440 | tf_op jit(solution)/shard_map/all_to_all | solution.py:204
  14.5 0.7 copy.130
  16.3 17.8 %all-to-all-done = f32[16,34,512]{2,1,0:T(8,128)S(1)} async-done(((f32[16,34,512]{2,1,0:T(8,128)}), f32[16,34,512]{2,1,0:T(8,128)S(1)}, u32[]{:S(2)}, u32[]{:S(2)}) %all-to-all-start) | async-done | bytes 1114144 | tf_op jit(solution)/shard_map/all_to_all | solution.py:204
  34.1 1.1 slice_bitcast_fusion.1
  36.1 1.6 %fusion.62 = f32[256,8,128]{0,2,1:T(8,128)} fusion(f32[256,64,1]{0,1,2:T(8,128)S(1)} %copy-done.11, f32[64,24,128]{2,0,1:T(8,128)S(1)} %bitcast.160), kind=kOutput, calls=%fused_computation.122 | convolution fusion | flops 100663296 | bytes 1376256 | tf_op jit(solution)/shard_map/kn,ncm->kcm/dot_general | solution.py:42
  37.8 1.6 %fusion.89 = f32[256,8,128]{0,2,1:T(8,128)} fusion(f32[256,64,1]{0,1,2:T(8,128)S(1)} %copy-done.11, f32[64,24,128]{2,0,1:T(8,128)S(1)} %bitcast.161, f32[64,8,128]{2,1,0:T(8,128)S(1)} %bitcast.172), kind=kOutput, calls=%fused_computation.181 | convolution fusion | flops 100728832 | bytes 1638400 | tf_op jit(solution)/shard_map/kn,ncm->kcm/dot_general | solution.py:42
  39.8 1.4 %multiply_subtract_fusion.7 = (f32[128,8,128]{0,2,1:T(8,128)S(1)}, f32[128,8,128]{0,2,1:T(8,128)S(1)}) fusion(f32[256,8,128]{0,2,1:T(8,128)} %fusion.89, f32[128,128]{0,1:T(8,128)S(1)} %copy-done.3, f32[128,128]{0,1:T(8,128)S(1)} %copy-done.2), kind=kLoop, calls=%fused_computation.89 | loop fusion | flops 786432 | bytes 2228224 | tf_op jit(solution)/shard_map/sub | solution.py:45
  41.7 1.0 fusion.23
  42.9 0.8 copy-done
  44.4 0.7 copy-done.9
  45.1 0.6 convolution_add_fusion.1
  45.8 0.6 fusion.88
  46.6 1.0 fusion.1
  47.7 1.0 fusion.34
  48.7 1.3 %multiply_subtract_fusion.1 = (f32[128,8,128]{2,0,1:T(8,128)}, f32[128,8,128]{2,0,1:T(8,128)}, f32[128,8,128]{2,0,1:T(8,128)S(1)}, f32[128,8,128]{2,0,1:T(8,128)...) fusion(f32[128,8,256]{2,0,1:T(8,128)S(1)} %fusion.34, f32[128,8,256]{2,0,1:T(8,128)S(1)} %fusion.1, ...), kind=kLoop, calls=%fused_computation.77 | loop fusion | flops 2490368 | bytes 5439488 | tf_op jit(solution)/shard_map/sub | solution.py:62
  52.2 0.6 fusion.87
  52.9 1.2 %fusion.12 = f32[128,8,256]{2,0,1:T(8,128)S(1)} fusion(f32[256,256,1]{1,0,2:T(8,128)S(1)} %copy-done.1, f32[128,8,128]{0,2,1:T(8,128)S(1)} %get-tuple-element.69, f32[128,8,128]{0,2,1:T(8,128)S(1)} %get-tuple-element.68), kind=kOutput, calls=%fused_computation.19 | convolution fusion | flops 402915328 | bytes 2359296 | tf_op jit(solution)/shard_map/kcm,mj->kcj/dot_general | solution.py:46
  54.2 1.2 %multiply_subtract_fusion = (f32[128,8,128]{2,0,1:T(8,128)}, f32[128,8,128]{2,0,1:T(8,128)}, f32[128,8,128]{2,0,1:T(8,128)S(1)}, f32[128,8,128]{2,0,1:T(8,128)S(1)}) fusion(f32[128,8,256]{2,0,1:T(8,128)S(1)} %fusion.23, f32[128,8,256]{2,0,1:T(8,128)S(1)} %fusion.12, f32[128,128]{1,0:T(8,128)S(1)} %get-tuple-element.94, f32[128,128]{1,0:T(8,128)S(1)} %get-tuple-element.93), kind=kLoop, calls=%fused_computation.75 | loop fusion | flops 1703936 | bytes 4325376 | tf_op jit(solution)/shard_map/sub | solution.py:62
  56.8 1.9 %multiply_reduce_fusion.3 = (f32[8]{0:T(128)}, f32[8]{0:T(128)}, bf16[64,8,128]{2,0,1:T(8,128)(2,1)}, f32[64,8,128]{2,0,1:T(8,128)S(1)}, f32[64,8,128]{2,0,1:T(8,128)S(1)}) fusion(f32[64,24,128]{2,0,1:T(8,128)S(1)} %bitcast.167, f32[64,8,128]{2,0,1:T(8,128)S(1)} %convolution_add_fusion.1, f32[64,8,128]{2,0,1:T(8,128)S(1)} %convolution_add_fusion.3, ...), kind=kOutput, calls=%fused_computation.116 | convolution fusion | flops 101777392 | bytes 3342432 | tf_op jit(solution)/shard_map/nk,kcm->ncm/dot_general | solution.py:54
  58.7 1.1 %multiply_reduce_fusion.1 = (f32[24]{0:T(128)}, f32[24]{0:T(128)S(1)}) fusion(f32[24,8192]{1,0:T(8,128)S(1)} %bitcast.169, f32[3,8,64,128]{3,2,1,0:T(8,128)S(1)} %bitcast.170), kind=kLoop, calls=%fused_computation.69 | loop fusion | flops 786384 | bytes 1573056 | tf_op jit(solution)/shard_map/reduce_sum | solution.py:257
  62.0 0.9 dynamic_update_slice.3
  63.1 1.1 maximum_reduce_fusion
  66.1 0.7 pad_maximum_fusion.4.side_ref
  66.8 0.9 pad_maximum_fusion.2.out_ref
  67.7 37.2 %shard_map.214 = (bf16[16,32,512]{2,1,0:T(8,128)(2,1)}, f32[16,40,128]{2,1,0:T(8,128)}, f32[8,8,128]{2,1,0:T(8,128)}, bf16[512,128]{1,0:T(8,128)(2,1)}, bf16[512,128]{1,0:T(8,128)(2,1)}) custom-call(bf16[16,32,512]{2,1,0:T(8,128)(2,1)} %pad_maximum_fusion.2.out_ref, bf16[512,128]{1,0:T(8,128)(2,1)} %bitcast.189, bf16[512,128]{1,0:T(8,128)(2,1)} %bitcast.187, ...), custom_call_target="tpu_custom_call" | custom-call | tf_op jit(solution)/shard_map/pallas_call | solution.py:155
  104.9 1.6 %fusion.91 = (f32[16,8,128]{2,1,0:T(8,128)S(1)}, f32[128,128]{1,0:T(8,128)}) fusion(f32[16,40,128]{2,1,0:T(8,128)} %get-tuple-element.15), kind=kLoop, calls=%fused_computation.183 | loop fusion | bytes 262144 | tf_op jit(solution)/shard_map/slice | solution.py:290
  108.1 0.8 copy.135
  109.5 0.7 copy.187
  110.2 0.7 copy.188
  (134 shorter events, 14.8 us)
Async XLA Ops:
  1.7 1.3 %copy-start.20 = (f32[8,512]{1,0:T(8,128)S(1)}, f32[8,512]{1,0:T(8,128)}, u32[]{:S(2)}) copy-start(f32[8,512]{1,0:T(8,128)} %param.23) | copy-start | bytes 49156
  1.7 1.3 %copy-start.21 = (f32[8,512]{1,0:T(8,128)S(1)}, f32[8,512]{1,0:T(8,128)}, u32[]{:S(2)}) copy-start(f32[8,512]{1,0:T(8,128)} %param.22) | copy-start | bytes 49156
  1.7 1.4 %copy-start.14 = (bf16[1,512,128]{2,1,0:T(8,128)(2,1)S(1)}, bf16[1,512,128]{2,1,0:T(8,128)(2,1)}, u32[]{:S(2)}) copy-start(bf16[1,512,128]{2,1,0:T(8,128)(2,1)} %param.16) | copy-start | bytes 393220
  1.7 1.4 %copy-start.18 = (bf16[128,128]{1,0:T(8,128)(2,1)S(1)}, bf16[128,128]{1,0:T(8,128)(2,1)}, u32[]{:S(2)}) copy-start(bf16[128,128]{1,0:T(8,128)(2,1)} %wo_ref.1) | copy-start | bytes 98308
  4.5 9.4 %copy-start.22 = (f32[3,384]{1,0:T(4,128)S(1)}, f32[3,384]{1,0:T(4,128)}, u32[]{:S(2)}) copy-start(f32[3,384]{1,0:T(4,128)} %param.19) | copy-start | bytes 13828
  4.5 9.8 %copy-start.27 = (f32[128]{0:T(128)S(1)}, f32[128]{0:T(128)}, u32[]{:S(2)}) copy-start(f32[128]{0:T(128)} %param.20) | copy-start | bytes 1540
  4.5 9.9 %copy-start.28 = (f32[128]{0:T(128)S(1)}, f32[128]{0:T(128)}, u32[]{:S(2)}) copy-start(f32[128]{0:T(128)} %param.21) | copy-start | bytes 1540
  4.5 29.6 %all-to-all-start = ((f32[16,34,512]{2,1,0:T(8,128)}), f32[16,34,512]{2,1,0:T(8,128)S(1)}, u32[]{:S(2)}, u32[]{:S(2)}) async-start(f32[16,34,512]{2,1,0:T(8,128)} %pad_maximum_fusion), calls=%async_computation | async-start | bytes 2621440 | tf_op jit(solution)/shard_map/all_to_all | solution.py:204
  35.2 0.8 copy-start.11
  37.7 2.0 %copy-start.2 = (f32[128,128]{0,1:T(8,128)S(1)}, f32[128,128]{0,1:T(8,128)}, u32[]{:S(2)}) copy-start(f32[128,128]{0,1:T(8,128)} %constant.42.clone) | copy-start | bytes 196612
  37.8 2.0 %copy-start.3 = (f32[128,128]{0,1:T(8,128)S(1)}, f32[128,128]{0,1:T(8,128)}, u32[]{:S(2)}) copy-start(f32[128,128]{0,1:T(8,128)} %constant.43.clone) | copy-start | bytes 196612
  39.8 1.4 %copy-start.1 = (f32[256,256,1]{1,0,2:T(8,128)S(1)}, f32[256,256,1]{1,0,2:T(8,128)}, u32[]{:S(2)}) copy-start(f32[256,256,1]{1,0,2:T(8,128)} %constant.58) | copy-start | bytes 786436
  42.7 1.0 copy-start
  44.3 0.8 copy-start.9
  44.3 0.8 copy-start.23
  44.4 1.3 %copy-start.12 = (f32[256,64,1]{0,1,2:T(8,128)S(1)}, f32[256,64,1]{0,1,2:T(8,128)}, u32[]{:S(2)}) copy-start(f32[256,64,1]{0,1,2:T(8,128)} %constant.57) | copy-start | bytes 196612
  45.1 1.3 %copy-start.4 = (f32[256,8,128]{0,2,1:T(8,128)S(1)}, f32[256,8,128]{0,2,1:T(8,128)}, u32[]{:S(2)}) copy-start(f32[256,8,128]{0,2,1:T(8,128)} %fusion.62) | copy-start | bytes 3145732
  58.7 1.6 %copy-start.5 = (f32[24,16,512]{2,0,1:T(8,128)S(1)}, f32[24,16,512]{2,0,1:T(8,128)}, u32[]{:S(2)}) copy-start(f32[24,16,512]{2,0,1:T(8,128)} %get-tuple-element.46) | copy-start | bytes 2359300
  60.9 0.7 copy-start.24
  60.9 0.8 copy-start.25
  60.9 0.8 copy-start.26
  60.9 0.8 copy-start.29
  61.2 1.9 %copy-start.8 = (f32[128,8,128]{2,0,1:T(8,128)S(1)}, f32[128,8,128]{2,0,1:T(8,128)}, u32[]{:S(2)}) copy-start(f32[128,8,128]{2,0,1:T(8,128)} %get-tuple-element.42) | copy-start | bytes 1572868
  61.9 2.3 %copy-start.6 = (f32[128,8,128]{2,0,1:T(8,128)S(1)}, f32[128,8,128]{2,0,1:T(8,128)}, u32[]{:S(2)}) copy-start(f32[128,8,128]{2,0,1:T(8,128)} %get-tuple-element.44) | copy-start | bytes 1572868
  61.9 2.3 %copy-start.7 = (f32[128,8,128]{2,0,1:T(8,128)S(1)}, f32[128,8,128]{2,0,1:T(8,128)}, u32[]{:S(2)}) copy-start(f32[128,8,128]{2,0,1:T(8,128)} %get-tuple-element.45) | copy-start | bytes 1572868
  64.2 0.8 copy-start.10
  65.1 1.0 copy-start.13
  104.9 2.5 %copy-start.15 = (f32[16,40,128]{2,1,0:T(8,128)S(1)}, f32[16,40,128]{2,1,0:T(8,128)}, u32[]{:S(2)}) copy-start(f32[16,40,128]{2,1,0:T(8,128)} %get-tuple-element.15) | copy-start | bytes 983044
  104.9 4.0 %copy-start.19 = (f32[8,8,128]{2,1,0:T(8,128)S(1)}, f32[8,8,128]{2,1,0:T(8,128)}, u32[]{:S(2)}) copy-start(f32[8,8,128]{2,1,0:T(8,128)} %get-tuple-element.16) | copy-start | bytes 98308
  104.9 4.6 %copy-start.17 = (bf16[512,128]{1,0:T(8,128)(2,1)S(1)}, bf16[512,128]{1,0:T(8,128)(2,1)}, u32[]{:S(2)}) copy-start(bf16[512,128]{1,0:T(8,128)(2,1)} %get-tuple-element.13) | copy-start | bytes 393220
  106.5 3.7 %copy-start.16 = (bf16[512,128]{1,0:T(8,128)(2,1)S(1)}, bf16[512,128]{1,0:T(8,128)(2,1)}, u32[]{:S(2)}) copy-start(bf16[512,128]{1,0:T(8,128)(2,1)} %get-tuple-element.14) | copy-start | bytes 393220

commit v16 on v13

--- a/solution.py
+++ b/solution.py
@@ -206,11 +206,11 @@
     gate_one = conv_f[:, per : 2 * per]
     gate_two = conv_f[:, 2 * per :]
 
-    h_spec = spectrum(fold(h_rows), tab)
-    h_one = h_spec[:, 0:1]
-    h_two = h_spec[:, 1:2]
-
-    v_spec = spectrum(value, tab)
+
+    both_spec = spectrum(jnp.concatenate([value, fold(h_rows)], axis=1), tab)
+    v_spec = both_spec[:, :per]
+    h_one = both_spec[:, per : per + 1]
+    h_two = both_spec[:, per + 1 : per + 2]
     y_one = signal(cmul(v_spec, h_one), tab) + skip1 * value
     gated_mid = gate_one * y_one
     m_spec = spectrum(gated_mid, tab)
@@ -224,8 +224,6 @@
     grad_one = d_mid * gate_one
     d_gate_one = d_mid * y_one
     g1_spec = spectrum(grad_one, tab)
-    d_value = signal(cmul(g1_spec, h_one, conj=True), tab) + skip1 * grad_one
-
     corr = jnp.concatenate(
         [
             jnp.sum(cmul(g1_spec, v_spec, conj=True), axis=1, keepdims=True),
@@ -233,7 +231,9 @@
         ],
         axis=1,
     )
-    filt_grad = unfold(signal(corr, tab))
+    last = signal(jnp.concatenate([cmul(g1_spec, h_one, conj=True), corr], axis=1), tab)
+    d_value = last[:, :per] + skip1 * grad_one
+    filt_grad = unfold(last[:, per:])
 
     d_conv = unfold(jnp.concatenate([d_value, d_gate_one, d_gate_two], axis=1))
     next1 = jnp.pad(d_conv, ((0, 0), (0, 1)))[:, 1:]

time: 112 us -> 102 us (0.911)
  other arithmetic: 12.2 us -> 6.93 us
  matrix products: 18.2 us -> 13.7 us
    dot_general x5 -> x4, matrix products: 4.77 us -> 2.58 us  [spectrum(): a = jnp.einsum('kn,ncm->kcm', tab['fwd1'], x, precision=PRECISION)]
    sub x3, other arithmetic: 2.87 us -> 0.85 us  [cmul(): return jnp.concatenate([ar * br - ai * bi, ar * bi + ai * br], axis=-1)]
    dot_general x5 -> x4, matrix products: 4.48 us -> 2.98 us  [spectrum(): return jnp.einsum('kcm,mj->kcj', cat, tab['fwd2'], precision=PRECISION)]
    reduce_sum x1, other arithmetic: 1.26 us -> 0.05 us  [shards(): jnp.sum(cmul(g1_spec, v_spec, conj=True), axis=1, keepdims=True)]
    sub x4, other arithmetic: 1.76 us -> 0.59 us  [spectrum(): cat = jnp.concatenate([ar * tr - ai * ti, ar * ti + ai * tr], axis=-1)]
    unnamed x56 -> x46, local copies, waits for them, and re-layouts: 5.37 us -> 6.09 us
    dot_general x5 -> x4, matrix products: 2.87 us -> 2.46 us  [signal(): return jnp.einsum('nk,kcm->ncm', tab['inv1'], stacked, precision=PRECISION)]
    dot_general x5 -> x4, matrix products: 2.86 us -> 2.47 us  [signal(): b = jnp.einsum('kcj,jm->kcm', s, tab['inv2'], precision=PRECISION)]
where the time goes in v16:
time: 102 us; the launch traced here: 101 us
  Pallas kernels  36.8 us (36%)
  waiting for transfers between devices  19.5 us (19%)
  matrix products  13.7 us (13%)
  local copies, waits for them, and re-layouts  13.5 us (13%)
  starting transfers between devices  9.43 us (9%)
  other arithmetic  6.93 us (7%)
  between operations  1.39 us (1%)
    pallas_call x1, Pallas kernels, tail_rounds(): pl.pallas_call(kernel, out_shape=(jax.ShapeDtypeStruct(out_msg.shape, out...  36.8 us
    all_to_all x1, waiting for transfers between devices, shards(): lax.all_to_all(jnp.concatenate([proj_blk, dprod_blk, rows_sent], axis=1),...  19.5 us
    all_to_all x1, starting transfers between devices, shards(): lax.all_to_all(jnp.concatenate([proj_blk, dprod_blk, rows_sent], axis=1),...  9.43 us
    unnamed x46, local copies, waits for them, and re-layouts  6.09 us
    dot_general x4, matrix products, spectrum(): return jnp.einsum('kcm,mj->kcj', cat, tab['fwd2'], precision=PRECISION)  2.98 us
    dot_general x4, matrix products, spectrum(): a = jnp.einsum('kn,ncm->kcm', tab['fwd1'], x, precision=PRECISION)  2.58 us
    dot_general x4, matrix products, signal(): b = jnp.einsum('kcj,jm->kcm', s, tab['inv2'], precision=PRECISION)  2.47 us
    dot_general x4, matrix products, signal(): return jnp.einsum('nk,kcm->ncm', tab['inv1'], stacked, precision=PRECISION)  2.46 us
  transfers between devices with their start and end apart: 1, of which 1 were waited for; matrix products, arithmetic and copies ran while one was open for 1% of the time, Pallas kernels for 0%

profile of v16, /device:TPU:1, one launch (start us, length us, event | category | flops | bytes accessed | tf_op | source)
XLA Modules:
  0.0 101.3 jit_solution(15574858966129283665)
XLA Ops:
  0.7 1.0 %copy.77 = bf16[128,384]{0,1:T(8,128)(2,1)S(1)} copy(bf16[128,384]{1,0:T(8,128)(2,1)} %param.17) | data formatting | bytes 196608 | tf_op args[2]
  1.7 1.2 %convolution_bitcast_fusion = f32[16,3,8,512]{3,2,0,1:T(8,128)S(1)} fusion(bf16[3,16,8,128]{3,2,1,0:T(8,128)(2,1)S(1)} %bitcast.193, bf16[1,512,128]{2,1,0:T(8,128)(2,1)} %param.15), kind=kOutput, calls=%fused_computation.17 | convolution fusion | flops 50331648 | bytes 1015808 | tf_op jit(solution)/shard_map/td,dc->ct/dot_general | solution.py:188
  3.3 1.2 %pad_maximum_fusion = f32[16,34,512]{2,1,0:T(8,128)} fusion(f32[16,2,512]{2,1,0:T(2,128)S(1)} %bitcast.194, f32[16,8,512]{2,1,0:T(8,128)S(1)} %fusion.63, f32[16,24,512]{2,1,0:T(8,128)S(1)} %bitcast.180), kind=kLoop, calls=%fused_computation | loop fusion | flops 557056 | bytes 2228224 | tf_op jit(solution)/shard_map/concatenate | solution.py:194
  4.5 9.4 %all-to-all-start = ((f32[16,34,512]{2,1,0:T(8,128)}), f32[16,34,512]{2,1,0:T(8,128)S(1)}, u32[]{:S(2)}, u32[]{:S(2)}) async-start(f32[16,34,512]{2,1,0:T(8,128)} %pad_maximum_fusion), calls=%async_computation | async-start | bytes 2621440 | tf_op jit(solution)/shard_map/all_to_all | solution.py:193
  14.6 19.5 %all-to-all-done = f32[16,34,512]{2,1,0:T(8,128)S(1)} async-done(((f32[16,34,512]{2,1,0:T(8,128)}), f32[16,34,512]{2,1,0:T(8,128)S(1)}, u32[]{:S(2)}, u32[]{:S(2)}) %all-to-all-start) | async-done | bytes 1114144 | tf_op jit(solution)/shard_map/all_to_all | solution.py:193
  34.1 1.1 %slice_bitcast_fusion.1 = (f32[24,16,512]{2,0,1:T(8,128)}, f32[16,3,8,512]{3,2,1,0:T(8,128)S(1)}) fusion(f32[16,34,512]{2,1,0:T(8,128)S(1)} %all-to-all-done), kind=kLoop, calls=%fused_computation.78 | loop fusion | bytes 2359296 | tf_op jit(solution)/shard_map/transpose | solution.py:196
  36.1 0.7 copy-done.7
  36.8 0.6 fusion.85
  37.4 0.7 fusion.57
  38.3 0.8 copy-done.2
  39.1 1.2 %fusion = f32[128,10,256]{2,0,1:T(8,128)S(1)} fusion(f32[256,256,1]{1,0,2:T(8,128)S(1)} %copy-done.2, f32[128,10,128]{0,2,1:T(8,128)S(1)} %get-tuple-element.49, f32[128,10,128]{0,2,1:T(8,128)S(1)} %get-tuple-element.48), kind=kOutput, calls=%fused_computation.1 | convolution fusion | flops 503644160 | bytes 2883584 | tf_op jit(solution)/shard_map/kcm,mj->kcj/dot_general | solution.py:46
  40.5 0.6 fusion.36
  41.3 0.8 copy-done.1
  42.8 0.7 copy-done.6
  44.0 0.6 fusion.84
  44.8 0.6 fusion.47
  47.0 0.6 fusion.83
  47.8 0.6 fusion.25
  49.5 0.7 fusion.4
  50.4 0.7 fusion.12
  51.2 0.8 multiply_reduce_fusion.3
  52.1 0.6 multiply_reduce_fusion.1
  54.5 0.9 dynamic_update_slice.3
  56.4 0.7 pad_maximum_fusion.4.side_ref
  57.1 0.9 pad_maximum_fusion.2.out_ref
  57.9 36.8 %shard_map.214 = (bf16[16,32,512]{2,1,0:T(8,128)(2,1)}, f32[16,40,128]{2,1,0:T(8,128)}, f32[8,8,128]{2,1,0:T(8,128)}) custom-call(bf16[16,32,512]{2,1,0:T(8,128)(2,1)} %pad_maximum_fusion.2.out_ref, bf16[512,128]{1,0:T(8,128)(2,1)} %bitcast.191, bf16[512,128]{1,0:T(8,128)(2,1)} %bitcast.189, f32[16,16,128]{2,1,0:T(8,128)} %pad_maximum_fusion.4.side_ref), custom_call_target="tpu_custom_call" | custom-call | tf_op jit(solution)/shard_map/pallas_call | solution.py:146
  94.7 1.6 %fusion.87 = (f32[16,8,128]{2,1,0:T(8,128)S(1)}, f32[128,128]{1,0:T(8,128)}) fusion(f32[16,40,128]{2,1,0:T(8,128)} %get-tuple-element.13), kind=kLoop, calls=%fused_computation.178 | loop fusion | bytes 262144 | tf_op jit(solution)/shard_map/slice | solution.py:285
  97.4 0.9 fusion.17
  98.3 1.0 fusion.16
  99.2 0.6 copy.147
  99.9 0.8 copy.108
  100.7 0.6 slice_bitcast_fusion.10
  (113 shorter events, 10.5 us)
Async XLA Ops:
  0.6 2.4 %copy-start = (bf16[128,128]{1,0:T(8,128)(2,1)S(1)}, bf16[128,128]{1,0:T(8,128)(2,1)}, u32[]{:S(2)}) copy-start(bf16[128,128]{1,0:T(8,128)(2,1)} %param.18) | copy-start | bytes 98308
  1.7 1.3 %copy-start.15 = (f32[8,512]{1,0:T(8,128)S(1)}, f32[8,512]{1,0:T(8,128)}, u32[]{:S(2)}) copy-start(f32[8,512]{1,0:T(8,128)} %param.23) | copy-start | bytes 49156
  1.7 1.3 %copy-start.16 = (f32[8,512]{1,0:T(8,128)S(1)}, f32[8,512]{1,0:T(8,128)}, u32[]{:S(2)}) copy-start(f32[8,512]{1,0:T(8,128)} %param.22) | copy-start | bytes 49156
  1.7 1.4 %copy-start.8 = (bf16[1,512,128]{2,1,0:T(8,128)(2,1)S(1)}, bf16[1,512,128]{2,1,0:T(8,128)(2,1)}, u32[]{:S(2)}) copy-start(bf16[1,512,128]{2,1,0:T(8,128)(2,1)} %param.16) | copy-start | bytes 393220
  4.5 9.4 %copy-start.17 = (f32[3,384]{1,0:T(4,128)S(1)}, f32[3,384]{1,0:T(4,128)}, u32[]{:S(2)}) copy-start(f32[3,384]{1,0:T(4,128)} %param.19) | copy-start | bytes 13828
  4.5 9.8 %copy-start.18 = (f32[128]{0:T(128)S(1)}, f32[128]{0:T(128)}, u32[]{:S(2)}) copy-start(f32[128]{0:T(128)} %param.20) | copy-start | bytes 1540
  4.5 9.9 %copy-start.19 = (f32[128]{0:T(128)S(1)}, f32[128]{0:T(128)}, u32[]{:S(2)}) copy-start(f32[128]{0:T(128)} %param.21) | copy-start | bytes 1540
  4.5 29.6 %all-to-all-start = ((f32[16,34,512]{2,1,0:T(8,128)}), f32[16,34,512]{2,1,0:T(8,128)S(1)}, u32[]{:S(2)}, u32[]{:S(2)}) async-start(f32[16,34,512]{2,1,0:T(8,128)} %pad_maximum_fusion), calls=%async_computation | async-start | bytes 2621440 | tf_op jit(solution)/shard_map/all_to_all | solution.py:193
  35.9 0.8 copy-start.7
  36.8 1.4 %copy-start.12 = (f32[128,128]{0,1:T(8,128)S(1)}, f32[128,128]{0,1:T(8,128)}, u32[]{:S(2)}) copy-start(f32[128,128]{0,1:T(8,128)} %constant.42.clone) | copy-start | bytes 196612
  36.8 1.4 %copy-start.13 = (f32[128,128]{0,1:T(8,128)S(1)}, f32[128,128]{0,1:T(8,128)}, u32[]{:S(2)}) copy-start(f32[128,128]{0,1:T(8,128)} %constant.43.clone) | copy-start | bytes 196612
  38.1 1.0 copy-start.2
  39.1 1.3 %copy-start.4 = (f32[128,128]{1,0:T(8,128)S(1)}, f32[128,128]{1,0:T(8,128)}, u32[]{:S(2)}) copy-start(f32[128,128]{1,0:T(8,128)} %constant.60) | copy-start | bytes 196612
  39.1 1.3 %copy-start.5 = (f32[128,128]{1,0:T(8,128)S(1)}, f32[128,128]{1,0:T(8,128)}, u32[]{:S(2)}) copy-start(f32[128,128]{1,0:T(8,128)} %constant.61) | copy-start | bytes 196612
  41.1 1.0 copy-start.1
  42.7 0.8 copy-start.6
  52.1 1.1 %copy-start.3 = (f32[24,16,512]{2,0,1:T(8,128)S(1)}, f32[24,16,512]{2,0,1:T(8,128)}, u32[]{:S(2)}) copy-start(f32[24,16,512]{2,0,1:T(8,128)} %get-tuple-element.50) | copy-start | bytes 2359300
  94.7 2.6 %copy-start.11 = (f32[16,40,128]{2,1,0:T(8,128)S(1)}, f32[16,40,128]{2,1,0:T(8,128)}, u32[]{:S(2)}) copy-start(f32[16,40,128]{2,1,0:T(8,128)} %get-tuple-element.13) | copy-start | bytes 983044
  94.7 2.6 %copy-start.9 = (bf16[16,32,512]{2,1,0:T(8,128)(2,1)S(1)}, bf16[16,32,512]{2,1,0:T(8,128)(2,1)}, u32[]{:S(2)}) copy-start(bf16[16,32,512]{2,1,0:T(8,128)(2,1)} %get-tuple-element.12) | copy-start | bytes 1572868
  96.5 1.7 %copy-start.10 = (bf16[128,384]{1,0:T(8,128)(2,1)S(1)}, bf16[128,384]{1,0:T(8,128)(2,1)}, u32[]{:S(2)}) copy-start(bf16[128,384]{1,0:T(8,128)(2,1)} %param.17) | copy-start | bytes 294916
  97.4 3.3 %copy-start.14 = (f32[8,8,128]{2,1,0:T(8,128)S(1)}, f32[8,8,128]{2,1,0:T(8,128)}, u32[]{:S(2)}) copy-start(f32[8,8,128]{2,1,0:T(8,128)} %get-tuple-element.14) | copy-start | bytes 98308

commit v17 on v13

--- a/solution.py
+++ b/solution.py
@@ -206,26 +206,24 @@
     gate_one = conv_f[:, per : 2 * per]
     gate_two = conv_f[:, 2 * per :]
 
-    h_spec = spectrum(fold(h_rows), tab)
-    h_one = h_spec[:, 0:1]
-    h_two = h_spec[:, 1:2]
-
-    v_spec = spectrum(value, tab)
-    y_one = signal(cmul(v_spec, h_one), tab) + skip1 * value
+
+    grad_two = d_product * gate_two
+    first = spectrum(jnp.concatenate([value, grad_two, fold(h_rows)], axis=1), tab)
+    v_spec = first[:, :per]
+    g2_spec = first[:, per : 2 * per]
+    h_one = first[:, 2 * per : 2 * per + 1]
+    h_two = first[:, 2 * per + 1 : 2 * per + 2]
+    second = signal(
+        jnp.concatenate([cmul(v_spec, h_one), cmul(g2_spec, h_two, conj=True)], axis=1), tab
+    )
+    y_one = second[:, :per] + skip1 * value
+    d_mid = second[:, per:] + skip2 * grad_two
     gated_mid = gate_one * y_one
-    m_spec = spectrum(gated_mid, tab)
-    y_two = signal(cmul(m_spec, h_two), tab) + skip2 * gated_mid
-    product = (gate_two * y_two).astype(jnp.bfloat16)
-
-    grad_two = d_product * gate_two
-    d_gate_two = d_product * y_two
-    g2_spec = spectrum(grad_two, tab)
-    d_mid = signal(cmul(g2_spec, h_two, conj=True), tab) + skip2 * grad_two
     grad_one = d_mid * gate_one
     d_gate_one = d_mid * y_one
-    g1_spec = spectrum(grad_one, tab)
-    d_value = signal(cmul(g1_spec, h_one, conj=True), tab) + skip1 * grad_one
-
+    third = spectrum(jnp.concatenate([gated_mid, grad_one], axis=1), tab)
+    m_spec = third[:, :per]
+    g1_spec = third[:, per:]
     corr = jnp.concatenate(
         [
             jnp.sum(cmul(g1_spec, v_spec, conj=True), axis=1, keepdims=True),
@@ -233,7 +231,14 @@
         ],
         axis=1,
     )
-    filt_grad = unfold(signal(corr, tab))
+    last = signal(
+        jnp.concatenate([cmul(m_spec, h_two), cmul(g1_spec, h_one, conj=True), corr], axis=1), tab
+    )
+    y_two = last[:, :per] + skip2 * gated_mid
+    product = (gate_two * y_two).astype(jnp.bfloat16)
+    d_gate_two = d_product * y_two
+    d_value = last[:, per : 2 * per] + skip1 * grad_one
+    filt_grad = unfold(last[:, 2 * per :])
 
     d_conv = unfold(jnp.concatenate([d_value, d_gate_one, d_gate_two], axis=1))
     next1 = jnp.pad(d_conv, ((0, 0), (0, 1)))[:, 1:]

time: 112 us -> 105 us (0.938)
  matrix products: 18.2 us -> 13.6 us
  other arithmetic: 12.2 us -> 8.37 us
  local copies, waits for them, and re-layouts: 13.4 us -> 15.5 us
    dot_general x5 -> x2, matrix products: 4.77 us -> 2.16 us  [spectrum(): a = jnp.einsum('kn,ncm->kcm', tab['fwd1'], x, precision=PRECISION)]
    sub x3, other arithmetic: 2.87 us -> 0.74 us  [cmul(): return jnp.concatenate([ar * br - ai * bi, ar * bi + ai * br], axis=-1)]
    dot_general x5 -> x2, matrix products: 4.48 us -> 3.08 us  [spectrum(): return jnp.einsum('kcm,mj->kcj', cat, tab['fwd2'], precision=PRECISION)]
    reduce_sum x1, other arithmetic: 1.26 us -> 0.05 us  [shards(): jnp.sum(cmul(g1_spec, v_spec, conj=True), axis=1, keepdims=True)]
    sub x4 -> x2, other arithmetic: 1.76 us -> 0.56 us  [spectrum(): cat = jnp.concatenate([ar * tr - ai * ti, ar * ti + ai * tr], axis=-1)]
    dot_general x5 -> x2, matrix products: 2.87 us -> 2.11 us  [signal(): return jnp.einsum('nk,kcm->ncm', tab['inv1'], stacked, precision=PRECISION)]
    dot_general x5 -> x2, matrix products: 2.86 us -> 2.2 us  [signal(): b = jnp.einsum('kcj,jm->kcm', s, tab['inv2'], precision=PRECISION)]
    unnamed x56 -> x40, local copies, waits for them, and re-layouts: 5.37 us -> 5.47 us
where the time goes in v17:
time: 105 us; the launch traced here: 104 us
  Pallas kernels  36.8 us (35%)
  waiting for transfers between devices  19.5 us (19%)
  local copies, waits for them, and re-layouts  15.5 us (15%)
  matrix products  13.6 us (13%)
  starting transfers between devices  9.3 us (9%)
  other arithmetic  8.37 us (8%)
  between operations  1.26 us (1%)
    pallas_call x1, Pallas kernels, tail_rounds(): pl.pallas_call(kernel, out_shape=(jax.ShapeDtypeStruct(out_msg.shape, out...  36.8 us
    all_to_all x1, waiting for transfers between devices, shards(): lax.all_to_all(jnp.concatenate([proj_blk, dprod_blk, rows_sent], axis=1),...  19.5 us
    all_to_all x1, starting transfers between devices, shards(): lax.all_to_all(jnp.concatenate([proj_blk, dprod_blk, rows_sent], axis=1),...  9.3 us
    unnamed x40, local copies, waits for them, and re-layouts  5.47 us
    dot_general x2, matrix products, spectrum(): return jnp.einsum('kcm,mj->kcj', cat, tab['fwd2'], precision=PRECISION)  3.08 us
    dot_general x2, matrix products, signal(): b = jnp.einsum('kcj,jm->kcm', s, tab['inv2'], precision=PRECISION)  2.2 us
    dot_general x2, matrix products, spectrum(): a = jnp.einsum('kn,ncm->kcm', tab['fwd1'], x, precision=PRECISION)  2.16 us
    dot_general x2, matrix products, signal(): return jnp.einsum('nk,kcm->ncm', tab['inv1'], stacked, precision=PRECISION)  2.11 us
  transfers between devices with their start and end apart: 1, of which 1 were waited for; matrix products, arithmetic and copies ran while one was open for 1% of the time, Pallas kernels for 0%

profile of v17, /device:TPU:1, one launch (start us, length us, event | category | flops | bytes accessed | tf_op | source)
XLA Modules:
  0.0 104.4 jit_solution(2771860723035473500)
XLA Ops:
  0.7 0.8 maximum_bitcast_fusion
  1.5 1.0 copy.69
  2.5 1.2 %convolution_bitcast_fusion = f32[16,3,8,512]{3,2,0,1:T(8,128)S(1)} fusion(bf16[3,16,8,128]{3,2,1,0:T(8,128)(2,1)S(1)} %bitcast.178, bf16[1,512,128]{2,1,0:T(8,128)(2,1)} %param.15), kind=kOutput, calls=%fused_computation.37 | convolution fusion | flops 50331648 | bytes 1015808 | tf_op jit(solution)/shard_map/td,dc->ct/dot_general | solution.py:188
  4.0 1.2 %pad_maximum_fusion = f32[16,34,512]{2,1,0:T(8,128)} fusion(f32[16,2,512]{2,1,0:T(2,128)S(1)} %bitcast.180, f32[16,8,512]{2,1,0:T(8,128)S(1)} %fusion.56, f32[16,24,512]{2,1,0:T(8,128)S(1)} %bitcast.165), kind=kLoop, calls=%fused_computation.36 | loop fusion | flops 557056 | bytes 2228224 | tf_op jit(solution)/shard_map/concatenate | solution.py:194
  5.2 9.3 %all-to-all-start = ((f32[16,34,512]{2,1,0:T(8,128)}), f32[16,34,512]{2,1,0:T(8,128)S(1)}, u32[]{:S(2)}, u32[]{:S(2)}) async-start(f32[16,34,512]{2,1,0:T(8,128)} %pad_maximum_fusion), calls=%async_computation | async-start | bytes 2621440 | tf_op jit(solution)/shard_map/all_to_all | solution.py:193
  15.2 19.5 %all-to-all-done = f32[16,34,512]{2,1,0:T(8,128)S(1)} async-done(((f32[16,34,512]{2,1,0:T(8,128)}), f32[16,34,512]{2,1,0:T(8,128)S(1)}, u32[]{:S(2)}, u32[]{:S(2)}) %all-to-all-start) | async-done | bytes 1114144 | tf_op jit(solution)/shard_map/all_to_all | solution.py:193
  34.7 1.1 %slice_bitcast_fusion.1 = (f32[24,16,512]{2,0,1:T(8,128)}, f32[16,3,8,512]{3,2,1,0:T(8,128)S(1)}) fusion(f32[16,34,512]{2,1,0:T(8,128)S(1)} %all-to-all-done), kind=kLoop, calls=%fused_computation.70 | loop fusion | bytes 2359296 | tf_op jit(solution)/shard_map/transpose | solution.py:196
  37.2 1.1 %fusion.44 = f32[256,18,128]{0,2,1:T(8,128)S(1)} fusion(f32[256,64,1]{0,1,2:T(8,128)S(1)} %copy-done.12, f32[64,2,128]{2,0,1:T(8,128)S(1)} %bitcast.179, f32[64,8,128]{2,0,1:T(8,128)S(1)} %get-tuple-element.84, f32[64,8,128]{2,0,1:T(8,128)S(1)} %get-tuple-element.83), kind=kOutput, calls=%fused_computation.71 | convolution fusion | flops 226787328 | bytes 3014656 | tf_op jit(solution)/shard_map/kn,ncm->kcm/dot_general | solution.py:42
  38.7 0.6 copy-done.3
  39.3 2.1 %fusion = f32[128,18,256]{2,0,1:T(8,128)S(1)} fusion(f32[256,256,1]{1,0,2:T(8,128)S(1)} %copy-done.3, f32[128,18,128]{0,2,1:T(8,128)S(1)} %get-tuple-element.53, f32[128,18,128]{0,2,1:T(8,128)S(1)} %get-tuple-element.52), kind=kOutput, calls=%fused_computation | convolution fusion | flops 906559488 | bytes 4980736 | tf_op jit(solution)/shard_map/kcm,mj->kcj/dot_general | solution.py:46
  41.6 0.7 copy-done.10
  42.3 1.0 fusion.20
  43.6 0.6 copy-done.11
  44.2 0.8 fusion.28
  45.4 1.0 fusion.50
  46.7 1.0 fusion.32
  48.3 1.2 %fusion.4 = f32[128,18,256]{0,2,1:T(8,128)S(1)} fusion(f32[256,256,1]{1,0,2:T(8,128)S(1)} %copy-done.10, f32[128,1,256]{2,0,1:T(8,128)S(1)} %bitcast.184, f32[128,1,256]{2,0,1:T(8,128)S(1)} %bitcast.185, f32[128,8,128]{2,0,1:T(8,128)S(1)} %get-tuple-element.70, f32[128,8,128]{2,0,1:T(8,128)S(1)} %get-tuple-element.71, ...), kind=kOutput, calls=%fused_computation.4 | convolution fusion | flops 908918784 | bytes 4980736 | tf_op jit(solution)/shard_map/kcj,jm->kcm/dot_general | solution.py:50
  49.9 1.3 %fusion.16 = f32[64,18,128]{2,0,1:T(8,128)S(1)} fusion(f32[64,256,1]{1,0,2:T(8,128)S(1)} %copy-done.11, f32[128,18,128]{0,2,1:T(8,128)S(1)} %get-tuple-element.47, f32[128,18,128]{0,2,1:T(8,128)S(1)} %get-tuple-element.46), kind=kOutput, calls=%fused_computation.16 | convolution fusion | flops 227082240 | bytes 3014656 | tf_op jit(solution)/shard_map/nk,kcm->ncm/dot_general | solution.py:54
  52.1 0.6 multiply_reduce_fusion.1
  53.2 0.8 copy.124
  55.6 0.9 dynamic_update_slice.3
  56.7 0.9 pad_maximum_fusion.2.out_ref
  57.6 0.7 pad_maximum_fusion.4.side_ref
  58.2 36.8 %shard_map.214 = (bf16[16,32,512]{2,1,0:T(8,128)(2,1)}, f32[16,40,128]{2,1,0:T(8,128)}, f32[8,8,128]{2,1,0:T(8,128)}) custom-call(bf16[16,32,512]{2,1,0:T(8,128)(2,1)} %pad_maximum_fusion.2.out_ref, bf16[512,128]{1,0:T(8,128)(2,1)} %bitcast.176, bf16[512,128]{1,0:T(8,128)(2,1)} %bitcast.174, f32[16,16,128]{2,1,0:T(8,128)} %pad_maximum_fusion.4.side_ref), custom_call_target="tpu_custom_call" | custom-call | tf_op jit(solution)/shard_map/pallas_call | solution.py:146
  95.1 1.8 %fusion.37 = bf16[1,512,128]{2,1,0:T(8,128)(2,1)} fusion(bf16[128,128]{1,0:T(8,128)(2,1)S(1)} %copy-done, bf16[16,32,512]{2,1,0:T(8,128)(2,1)} %get-tuple-element.12), kind=kOutput, calls=%fused_computation.45 | convolution fusion | flops 16842752 | bytes 294912 | tf_op jit(solution)/shard_map/dot_general | solution.py:279
  96.8 1.0 slice_bitcast_fusion.2
  97.9 0.9 slice_bitcast_fusion.3
  98.8 1.5 %fusion.74 = (f32[16,8,128]{2,1,0:T(8,128)S(1)}, f32[128,128]{1,0:T(8,128)}) fusion(f32[16,40,128]{2,1,0:T(8,128)} %get-tuple-element.13), kind=kLoop, calls=%fused_computation.157 | loop fusion | bytes 262144 | tf_op jit(solution)/shard_map/slice | solution.py:290
  101.3 1.0 fusion.36
  102.3 0.8 copy.96
  103.1 0.6 copy.128
  103.8 0.6 slice_bitcast_fusion.10
  (97 shorter events, 8.7 us)
Async XLA Ops:
  0.6 3.1 %copy-start = (bf16[128,128]{1,0:T(8,128)(2,1)S(1)}, bf16[128,128]{1,0:T(8,128)(2,1)}, u32[]{:S(2)}) copy-start(bf16[128,128]{1,0:T(8,128)(2,1)} %param.18) | copy-start | bytes 98308
  0.7 3.1 %copy-start.4 = (bf16[1,512,128]{2,1,0:T(8,128)(2,1)S(1)}, bf16[1,512,128]{2,1,0:T(8,128)(2,1)}, u32[]{:S(2)}) copy-start(bf16[1,512,128]{2,1,0:T(8,128)(2,1)} %param.16) | copy-start | bytes 393220
  4.0 10.6 %copy-start.14 = (f32[3,384]{1,0:T(4,128)S(1)}, f32[3,384]{1,0:T(4,128)}, u32[]{:S(2)}) copy-start(f32[3,384]{1,0:T(4,128)} %param.19) | copy-start | bytes 13828
  4.0 11.0 %copy-start.15 = (f32[128]{0:T(128)S(1)}, f32[128]{0:T(128)}, u32[]{:S(2)}) copy-start(f32[128]{0:T(128)} %param.20) | copy-start | bytes 1540
  4.0 11.0 %copy-start.16 = (f32[128]{0:T(128)S(1)}, f32[128]{0:T(128)}, u32[]{:S(2)}) copy-start(f32[128]{0:T(128)} %param.21) | copy-start | bytes 1540
  5.2 29.5 %all-to-all-start = ((f32[16,34,512]{2,1,0:T(8,128)}), f32[16,34,512]{2,1,0:T(8,128)S(1)}, u32[]{:S(2)}, u32[]{:S(2)}) async-start(f32[16,34,512]{2,1,0:T(8,128)} %pad_maximum_fusion), calls=%async_computation | async-start | bytes 2621440 | tf_op jit(solution)/shard_map/all_to_all | solution.py:193
  36.3 0.8 copy-start.12
  36.6 1.7 %copy-start.6 = (f32[128,128]{0,1:T(8,128)S(1)}, f32[128,128]{0,1:T(8,128)}, u32[]{:S(2)}) copy-start(f32[128,128]{0,1:T(8,128)} %constant.43.clone) | copy-start | bytes 196612
  36.6 1.7 %copy-start.7 = (f32[128,128]{0,1:T(8,128)S(1)}, f32[128,128]{0,1:T(8,128)}, u32[]{:S(2)}) copy-start(f32[128,128]{0,1:T(8,128)} %constant.42.clone) | copy-start | bytes 196612
  38.3 1.0 copy-start.3
  41.4 1.0 copy-start.10
  42.3 1.0 copy-start.8
  42.3 1.0 copy-start.9
  43.4 0.8 copy-start.11
  52.1 2.4 %copy-start.1 = (f32[24,16,512]{2,0,1:T(8,128)S(1)}, f32[24,16,512]{2,0,1:T(8,128)}, u32[]{:S(2)}) copy-start(f32[24,16,512]{2,0,1:T(8,128)} %get-tuple-element.75) | copy-start | bytes 2359300
  55.0 1.7 %copy-start.2 = (bf16[3,16,8,512]{3,2,0,1:T(8,128)(2,1)S(1)}, bf16[3,16,8,512]{3,2,0,1:T(8,128)(2,1)}, u32[]{:S(2)}) copy-start(bf16[3,16,8,512]{3,2,0,1:T(8,128)(2,1)} %copy.124) | copy-start | bytes 1179652
  58.2 43.1 %copy-start.5 = (bf16[128,384]{1,0:T(8,128)(2,1)S(1)}, bf16[128,384]{1,0:T(8,128)(2,1)}, u32[]{:S(2)}) copy-start(bf16[128,384]{1,0:T(8,128)(2,1)} %param.17) | copy-start | bytes 294916
  97.9 5.9 %copy-start.13 = (f32[8,8,128]{2,1,0:T(8,128)S(1)}, f32[8,8,128]{2,1,0:T(8,128)}, u32[]{:S(2)}) copy-start(f32[8,8,128]{2,1,0:T(8,128)} %get-tuple-element.14) | copy-start | bytes 98308

commit v18 on v17

--- a/solution.py
+++ b/solution.py
@@ -208,11 +208,12 @@
 
 
     grad_two = d_product * gate_two
-    first = spectrum(jnp.concatenate([value, grad_two, fold(h_rows)], axis=1), tab)
+    h_spec = spectrum(fold(h_rows), tab)
+    h_one = h_spec[:, 0:1]
+    h_two = h_spec[:, 1:2]
+    first = spectrum(jnp.concatenate([value, grad_two], axis=1), tab)
     v_spec = first[:, :per]
-    g2_spec = first[:, per : 2 * per]
-    h_one = first[:, 2 * per : 2 * per + 1]
-    h_two = first[:, 2 * per + 1 : 2 * per + 2]
+    g2_spec = first[:, per:]
     second = signal(
         jnp.concatenate([cmul(v_spec, h_one), cmul(g2_spec, h_two, conj=True)], axis=1), tab
     )
@@ -231,14 +232,12 @@
         ],
         axis=1,
     )
-    last = signal(
-        jnp.concatenate([cmul(m_spec, h_two), cmul(g1_spec, h_one, conj=True), corr], axis=1), tab
-    )
+    last = signal(jnp.concatenate([cmul(m_spec, h_two), cmul(g1_spec, h_one, conj=True)], axis=1), tab)
     y_two = last[:, :per] + skip2 * gated_mid
     product = (gate_two * y_two).astype(jnp.bfloat16)
     d_gate_two = d_product * y_two
     d_value = last[:, per : 2 * per] + skip1 * grad_one
-    filt_grad = unfold(last[:, 2 * per :])
+    filt_grad = unfold(signal(corr, tab))
 
     d_conv = unfold(jnp.concatenate([d_value, d_gate_one, d_gate_two], axis=1))
     next1 = jnp.pad(d_conv, ((0, 0), (0, 1)))[:, 1:]

time: 105 us -> 109 us (1.038)
  other arithmetic: 8.37 us -> 12.8 us
  local copies, waits for them, and re-layouts: 15.5 us -> 12.8 us
  matrix products: 13.6 us -> 15.6 us
    sub x3, other arithmetic: 0.74 us -> 2.01 us  [cmul(): return jnp.concatenate([ar * br - ai * bi, ar * bi + ai * br], axis=-1)]
    reduce_sum x1, other arithmetic: 0.05 us -> 1.27 us  [shards(): jnp.sum(cmul(g1_spec, v_spec, conj=True), axis=1, keepdims=True)]
    unnamed x40 -> x36, local copies, waits for them, and re-layouts: 5.47 us -> 4.4 us
    dot_general x2 -> x3, matrix products: 3.08 us -> 4.12 us  [spectrum(): return jnp.einsum('kcm,mj->kcj', cat, tab['fwd2'], precision=PRECISION)]
    dot_general x2 -> x3, matrix products: 2.11 us -> 2.51 us  [signal(): return jnp.einsum('nk,kcm->ncm', tab['inv1'], stacked, precision=PRECISION)]
    dot_general x2 -> x3, matrix products: 2.2 us -> 2.49 us  [signal(): b = jnp.einsum('kcj,jm->kcm', s, tab['inv2'], precision=PRECISION)]
    dot_general x2 -> x3, matrix products: 2.16 us -> 2.37 us  [spectrum(): a = jnp.einsum('kn,ncm->kcm', tab['fwd1'], x, precision=PRECISION)]
where the time goes in v18:
time: 109 us; the launch traced here: 108 us
  Pallas kernels  36.8 us (34%)
  waiting for transfers between devices  19.5 us (18%)
  matrix products  15.6 us (14%)
  local copies, waits for them, and re-layouts  12.8 us (12%)
  other arithmetic  12.8 us (12%)
  starting transfers between devices  9.45 us (9%)
  between operations  1.26 us (1%)
    pallas_call x1, Pallas kernels, tail_rounds(): pl.pallas_call(kernel, out_shape=(jax.ShapeDtypeStruct(out_msg.shape, out...  36.8 us
    all_to_all x1, waiting for transfers between devices, shards(): lax.all_to_all(jnp.concatenate([proj_blk, dprod_blk, rows_sent], axis=1),...  19.5 us
    all_to_all x1, starting transfers between devices, shards(): lax.all_to_all(jnp.concatenate([proj_blk, dprod_blk, rows_sent], axis=1),...  9.45 us
    unnamed x36, local copies, waits for them, and re-layouts  4.4 us
    dot_general x3, matrix products, spectrum(): return jnp.einsum('kcm,mj->kcj', cat, tab['fwd2'], precision=PRECISION)  4.12 us
    dot_general x3, matrix products, signal(): return jnp.einsum('nk,kcm->ncm', tab['inv1'], stacked, precision=PRECISION)  2.51 us
    dot_general x3, matrix products, signal(): b = jnp.einsum('kcj,jm->kcm', s, tab['inv2'], precision=PRECISION)  2.49 us
    dot_general x3, matrix products, spectrum(): a = jnp.einsum('kn,ncm->kcm', tab['fwd1'], x, precision=PRECISION)  2.37 us
  transfers between devices with their start and end apart: 1, of which 1 were waited for; matrix products, arithmetic and copies ran while one was open for 1% of the time, Pallas kernels for 0%

profile of v18, /device:TPU:1, one launch (start us, length us, event | category | flops | bytes accessed | tf_op | source)
XLA Modules:
  0.0 108.1 jit_solution(2603294800185317801)
XLA Ops:
  0.7 0.8 maximum_bitcast_fusion
  1.5 1.0 copy.77
  2.5 1.2 %convolution_bitcast_fusion = f32[16,3,8,512]{3,2,0,1:T(8,128)S(1)} fusion(bf16[3,16,8,128]{3,2,1,0:T(8,128)(2,1)S(1)} %bitcast.186, bf16[1,512,128]{2,1,0:T(8,128)(2,1)} %param.15), kind=kOutput, calls=%fused_computation.33 | convolution fusion | flops 50331648 | bytes 1015808 | tf_op jit(solution)/shard_map/td,dc->ct/dot_general | solution.py:188
  4.0 1.2 %pad_maximum_fusion = f32[16,34,512]{2,1,0:T(8,128)} fusion(f32[16,2,512]{2,1,0:T(2,128)S(1)} %bitcast.187, f32[16,8,512]{2,1,0:T(8,128)S(1)} %fusion.62, f32[16,24,512]{2,1,0:T(8,128)S(1)} %bitcast.171), kind=kLoop, calls=%fused_computation.32 | loop fusion | flops 557056 | bytes 2228224 | tf_op jit(solution)/shard_map/concatenate | solution.py:194
  5.2 9.4 %all-to-all-start = ((f32[16,34,512]{2,1,0:T(8,128)}), f32[16,34,512]{2,1,0:T(8,128)S(1)}, u32[]{:S(2)}, u32[]{:S(2)}) async-start(f32[16,34,512]{2,1,0:T(8,128)} %pad_maximum_fusion), calls=%async_computation | async-start | bytes 2621440 | tf_op jit(solution)/shard_map/all_to_all | solution.py:193
  15.4 19.5 %all-to-all-done = f32[16,34,512]{2,1,0:T(8,128)S(1)} async-done(((f32[16,34,512]{2,1,0:T(8,128)}), f32[16,34,512]{2,1,0:T(8,128)S(1)}, u32[]{:S(2)}, u32[]{:S(2)}) %all-to-all-start) | async-done | bytes 1114144 | tf_op jit(solution)/shard_map/all_to_all | solution.py:193
  36.8 1.0 fusion.41
  38.1 1.9 %fusion = f32[128,16,256]{2,0,1:T(8,128)S(1)} fusion(f32[256,256,1]{1,0,2:T(8,128)S(1)} %copy-done.4, f32[128,16,128]{0,2,1:T(8,128)S(1)} %get-tuple-element.61, f32[128,16,128]{0,2,1:T(8,128)S(1)} %get-tuple-element.60), kind=kOutput, calls=%fused_computation | convolution fusion | flops 805830656 | bytes 4456448 | tf_op jit(solution)/shard_map/kcm,mj->kcj/dot_general | solution.py:46
  40.2 0.7 copy-done.3
  40.9 1.1 fusion.4
  42.2 0.6 copy-done.7
  42.8 1.1 %fusion.12 = f32[64,16,128]{2,0,1:T(8,128)S(1)} fusion(f32[64,256,1]{1,0,2:T(8,128)S(1)} %copy-done.7, f32[128,16,128]{0,2,1:T(8,128)S(1)} %get-tuple-element.55, f32[128,16,128]{0,2,1:T(8,128)S(1)} %get-tuple-element.54), kind=kOutput, calls=%fused_computation.12 | convolution fusion | flops 201850880 | bytes 2686976 | tf_op jit(solution)/shard_map/nk,kcm->ncm/dot_general | solution.py:54
  44.2 1.0 fusion.45
  45.5 1.9 %fusion.16 = f32[128,16,256]{2,0,1:T(8,128)S(1)} fusion(f32[256,256,1]{1,0,2:T(8,128)S(1)} %copy-done.4, f32[128,16,128]{0,2,1:T(8,128)S(1)} %get-tuple-element.53, f32[128,16,128]{0,2,1:T(8,128)S(1)} %get-tuple-element.52), kind=kOutput, calls=%fused_computation.16 | convolution fusion | flops 805830656 | bytes 4456448 | tf_op jit(solution)/shard_map/kcm,mj->kcj/dot_general | solution.py:46
  47.4 1.6 %multiply_subtract_fusion.5 = (f32[128,8,128]{2,0,1:T(8,128)}, f32[128,8,128]{2,0,1:T(8,128)}, f32[128,8,128]{2,0,1:T(8,128)}, f32[128,8,128]{2,0,1:T(8,128)}) fusion(f32[128,16,256]{2,0,1:T(8,128)S(1)} %fusion.16, f32[128,16,256]{2,0,1:T(8,128)S(1)} %fusion), kind=kLoop, calls=%fused_computation.81 | loop fusion | flops 1835008 | bytes 6291456 | tf_op jit(solution)/shard_map/sub | solution.py:62
  49.2 1.0 fusion.20
  50.7 1.1 %fusion.28 = f32[64,16,128]{2,0,1:T(8,128)S(1)} fusion(f32[64,256,1]{1,0,2:T(8,128)S(1)} %copy-done.7, f32[128,16,128]{0,2,1:T(8,128)S(1)} %get-tuple-element.47, f32[128,16,128]{0,2,1:T(8,128)S(1)} %get-tuple-element.46), kind=kOutput, calls=%fused_computation.28 | convolution fusion | flops 201850880 | bytes 2686976 | tf_op jit(solution)/shard_map/nk,kcm->ncm/dot_general | solution.py:54
  52.1 0.6 multiply_reduce_fusion.1
  53.8 1.3 %fusion.40 = f32[24]{0:T(128)S(1)} fusion(f32[24,64,128]{2,1,0:T(8,128)S(1)} %reshape.150, f32[64,8,128]{2,0,1:T(8,128)S(1)} %get-tuple-element.76, f32[64,8,128]{2,0,1:T(8,128)S(1)} %get-tuple-element.66, f32[64,8,128]{2,0,1:T(8,128)} %copy-done.5), kind=kLoop, calls=%fused_computation.62 | loop fusion | flops 786408 | bytes 1572960 | tf_op jit(solution)/shard_map/reduce_sum | solution.py:250
  55.2 1.3 %maximum_reduce_fusion = f32[128,256]{1,0:T(8,128)S(1)} fusion(f32[128,8,128]{2,0,1:T(8,128)} %get-tuple-element.45, f32[128,8,128]{2,0,1:T(8,128)} %get-tuple-element.42), kind=kLoop, calls=%fused_computation.40 | loop fusion | flops 491520 | bytes 1179648 | tf_op jit(solution)/shard_map/reduce_sum | solution.py:230
  56.5 1.1 %maximum_reduce_fusion.1 = f32[128,256]{1,0:T(8,128)S(1)} fusion(f32[128,8,128]{2,0,1:T(8,128)} %get-tuple-element.44, f32[128,8,128]{2,0,1:T(8,128)S(1)} %copy-done.6), kind=kLoop, calls=%fused_computation.41 | loop fusion | flops 491520 | bytes 1179648 | tf_op jit(solution)/shard_map/reduce_sum | solution.py:231
  59.3 0.9 dynamic_update_slice.3
  60.5 0.9 pad_maximum_fusion.2.out_ref
  61.3 0.7 pad_maximum_fusion.4.side_ref
  62.0 36.8 %shard_map.214 = (bf16[16,32,512]{2,1,0:T(8,128)(2,1)}, f32[16,40,128]{2,1,0:T(8,128)}, f32[8,8,128]{2,1,0:T(8,128)}) custom-call(bf16[16,32,512]{2,1,0:T(8,128)(2,1)} %pad_maximum_fusion.2.out_ref, bf16[512,128]{1,0:T(8,128)(2,1)} %bitcast.184, bf16[512,128]{1,0:T(8,128)(2,1)} %bitcast.180, f32[16,16,128]{2,1,0:T(8,128)} %pad_maximum_fusion.4.side_ref), custom_call_target="tpu_custom_call" | custom-call | tf_op jit(solution)/shard_map/pallas_call | solution.py:146
  98.9 1.8 %fusion.33 = bf16[1,512,128]{2,1,0:T(8,128)(2,1)} fusion(bf16[128,128]{1,0:T(8,128)(2,1)S(1)} %copy-done, bf16[16,32,512]{2,1,0:T(8,128)(2,1)} %get-tuple-element.12), kind=kOutput, calls=%fused_computation.37 | convolution fusion | flops 16842752 | bytes 294912 | tf_op jit(solution)/shard_map/dot_general | solution.py:278
  100.6 1.0 slice_bitcast_fusion.2
  101.7 1.5 %fusion.84 = (f32[16,8,128]{2,1,0:T(8,128)S(1)}, f32[128,128]{1,0:T(8,128)}) fusion(f32[16,40,128]{2,1,0:T(8,128)} %get-tuple-element.13), kind=kLoop, calls=%fused_computation.171 | loop fusion | bytes 262144 | tf_op jit(solution)/shard_map/slice | solution.py:289
  103.2 0.9 slice_bitcast_fusion.3
  105.1 0.6 slice_bitcast_fusion.10
  105.8 1.0 fusion.32
  106.7 0.8 copy.108
  (98 shorter events, 9.6 us)
Async XLA Ops:
  0.6 3.1 %copy-start = (bf16[128,128]{1,0:T(8,128)(2,1)S(1)}, bf16[128,128]{1,0:T(8,128)(2,1)}, u32[]{:S(2)}) copy-start(bf16[128,128]{1,0:T(8,128)(2,1)} %param.18) | copy-start | bytes 98308
  0.7 3.1 %copy-start.9 = (bf16[1,512,128]{2,1,0:T(8,128)(2,1)S(1)}, bf16[1,512,128]{2,1,0:T(8,128)(2,1)}, u32[]{:S(2)}) copy-start(bf16[1,512,128]{2,1,0:T(8,128)(2,1)} %param.16) | copy-start | bytes 393220
  4.0 10.7 %copy-start.13 = (f32[128]{0:T(128)S(1)}, f32[128]{0:T(128)}, u32[]{:S(2)}) copy-start(f32[128]{0:T(128)} %param.20) | copy-start | bytes 1540
  4.0 10.8 %copy-start.14 = (f32[128]{0:T(128)S(1)}, f32[128]{0:T(128)}, u32[]{:S(2)}) copy-start(f32[128]{0:T(128)} %param.21) | copy-start | bytes 1540
  4.0 10.9 %copy-start.12 = (f32[3,384]{1,0:T(4,128)S(1)}, f32[3,384]{1,0:T(4,128)}, u32[]{:S(2)}) copy-start(f32[3,384]{1,0:T(4,128)} %param.19) | copy-start | bytes 13828
  5.2 29.7 %copy-start.8 = (f32[256,64,1]{0,1,2:T(8,128)S(1)}, f32[256,64,1]{0,1,2:T(8,128)}, u32[]{:S(2)}) copy-start(f32[256,64,1]{0,1,2:T(8,128)} %constant.57) | copy-start | bytes 196612
  5.2 30.0 %copy-start.1 = (f32[128,128]{0,1:T(8,128)S(1)}, f32[128,128]{0,1:T(8,128)}, u32[]{:S(2)}) copy-start(f32[128,128]{0,1:T(8,128)} %constant.43.clone) | copy-start | bytes 196612
  5.2 30.0 %copy-start.2 = (f32[128,128]{0,1:T(8,128)S(1)}, f32[128,128]{0,1:T(8,128)}, u32[]{:S(2)}) copy-start(f32[128,128]{0,1:T(8,128)} %constant.42.clone) | copy-start | bytes 196612
  5.2 30.1 %copy-start.4 = (f32[256,256,1]{1,0,2:T(8,128)S(1)}, f32[256,256,1]{1,0,2:T(8,128)}, u32[]{:S(2)}) copy-start(f32[256,256,1]{1,0,2:T(8,128)} %constant.58) | copy-start | bytes 786436
  5.2 29.6 %all-to-all-start = ((f32[16,34,512]{2,1,0:T(8,128)}), f32[16,34,512]{2,1,0:T(8,128)S(1)}, u32[]{:S(2)}, u32[]{:S(2)}) async-start(f32[16,34,512]{2,1,0:T(8,128)} %pad_maximum_fusion), calls=%async_computation | async-start | bytes 2621440 | tf_op jit(solution)/shard_map/all_to_all | solution.py:193
  39.9 1.0 copy-start.3
  42.0 0.8 copy-start.7
  52.0 1.2 %copy-start.5 = (f32[64,8,128]{2,0,1:T(8,128)}, f32[64,8,128]{2,0,1:T(8,128)S(1)}, u32[]{:S(2)}) copy-start(f32[64,8,128]{2,0,1:T(8,128)S(1)} %get-tuple-element.79) | copy-start | bytes 786436
  53.7 2.8 %copy-start.6 = (f32[128,8,128]{2,0,1:T(8,128)S(1)}, f32[128,8,128]{2,0,1:T(8,128)}, u32[]{:S(2)}) copy-start(f32[128,8,128]{2,0,1:T(8,128)} %get-tuple-element.43) | copy-start | bytes 1572868
  62.0 43.7 %copy-start.10 = (bf16[128,384]{1,0:T(8,128)(2,1)S(1)}, bf16[128,384]{1,0:T(8,128)(2,1)}, u32[]{:S(2)}) copy-start(bf16[128,384]{1,0:T(8,128)(2,1)} %param.17) | copy-start | bytes 294916
  98.8 6.2 %copy-start.11 = (f32[8,8,128]{2,1,0:T(8,128)S(1)}, f32[8,8,128]{2,1,0:T(8,128)}, u32[]{:S(2)}) copy-start(f32[8,8,128]{2,1,0:T(8,128)} %get-tuple-element.14) | copy-start | bytes 98308

commit v19 on v16

--- a/solution.py
+++ b/solution.py
@@ -213,14 +213,17 @@
     h_two = both_spec[:, per + 1 : per + 2]
     y_one = signal(cmul(v_spec, h_one), tab) + skip1 * value
     gated_mid = gate_one * y_one
-    m_spec = spectrum(gated_mid, tab)
-    y_two = signal(cmul(m_spec, h_two), tab) + skip2 * gated_mid
+    grad_two = d_product * gate_two
+    pair_spec = spectrum(jnp.concatenate([gated_mid, grad_two], axis=1), tab)
+    m_spec = pair_spec[:, :per]
+    g2_spec = pair_spec[:, per:]
+    pair_sig = signal(
+        jnp.concatenate([cmul(m_spec, h_two), cmul(g2_spec, h_two, conj=True)], axis=1), tab
+    )
+    y_two = pair_sig[:, :per] + skip2 * gated_mid
     product = (gate_two * y_two).astype(jnp.bfloat16)
-
-    grad_two = d_product * gate_two
     d_gate_two = d_product * y_two
-    g2_spec = spectrum(grad_two, tab)
-    d_mid = signal(cmul(g2_spec, h_two, conj=True), tab) + skip2 * grad_two
+    d_mid = pair_sig[:, per:] + skip2 * grad_two
     grad_one = d_mid * gate_one
     d_gate_one = d_mid * y_one
     g1_spec = spectrum(grad_one, tab)

time: 102 us -> 106 us (1.039)
  local copies, waits for them, and re-layouts: 13.5 us -> 15.2 us
  matrix products: 13.7 us -> 15.2 us
  other arithmetic: 6.93 us -> 8.03 us
    dot_general x4 -> x3, matrix products: 2.98 us -> 3.68 us  [spectrum(): return jnp.einsum('kcm,mj->kcj', cat, tab['fwd2'], precision=PRECISION)]
    dot_general x4 -> x3, matrix products: 2.58 us -> 2.36 us  [spectrum(): a = jnp.einsum('kn,ncm->kcm', tab['fwd1'], x, precision=PRECISION)]
    unnamed x46 -> x38, local copies, waits for them, and re-layouts: 6.09 us -> 5.91 us
    dot_general x4 -> x3, matrix products: 2.47 us -> 2.55 us  [signal(): b = jnp.einsum('kcj,jm->kcm', s, tab['inv2'], precision=PRECISION)]
    dot_general x4 -> x3, matrix products: 2.46 us -> 2.49 us  [signal(): return jnp.einsum('nk,kcm->ncm', tab['inv1'], stacked, precision=PRECISION)]
where the time goes in v19:
time: 106 us; the launch traced here: 105 us
  Pallas kernels  36.8 us (35%)
  waiting for transfers between devices  19.5 us (18%)
  local copies, waits for them, and re-layouts  15.2 us (14%)
  matrix products  15.2 us (14%)
  starting transfers between devices  9.43 us (9%)
  other arithmetic  8.03 us (8%)
  between operations  1.3 us (1%)
    pallas_call x1, Pallas kernels, tail_rounds(): pl.pallas_call(kernel, out_shape=(jax.ShapeDtypeStruct(out_msg.shape, out...  36.8 us
    all_to_all x1, waiting for transfers between devices, shards(): lax.all_to_all(jnp.concatenate([proj_blk, dprod_blk, rows_sent], axis=1),...  19.5 us
    all_to_all x1, starting transfers between devices, shards(): lax.all_to_all(jnp.concatenate([proj_blk, dprod_blk, rows_sent], axis=1),...  9.43 us
    unnamed x38, local copies, waits for them, and re-layouts  5.91 us
    dot_general x3, matrix products, spectrum(): return jnp.einsum('kcm,mj->kcj', cat, tab['fwd2'], precision=PRECISION)  3.68 us
    dot_general x3, matrix products, signal(): b = jnp.einsum('kcj,jm->kcm', s, tab['inv2'], precision=PRECISION)  2.55 us
    dot_general x3, matrix products, signal(): return jnp.einsum('nk,kcm->ncm', tab['inv1'], stacked, precision=PRECISION)  2.49 us
    dot_general x3, matrix products, spectrum(): a = jnp.einsum('kn,ncm->kcm', tab['fwd1'], x, precision=PRECISION)  2.36 us
  transfers between devices with their start and end apart: 1, of which 1 were waited for; matrix products, arithmetic and copies ran while one was open for 1% of the time, Pallas kernels for 0%

profile of v19, /device:TPU:1, one launch (start us, length us, event | category | flops | bytes accessed | tf_op | source)
XLA Modules:
  0.0 105.5 jit_solution(13044688128075091132)
XLA Ops:
  0.7 0.7 maximum_bitcast_fusion
  1.4 1.0 copy.77
  2.5 1.2 %convolution_bitcast_fusion = f32[16,3,8,512]{3,2,0,1:T(8,128)S(1)} fusion(bf16[3,16,8,128]{3,2,1,0:T(8,128)(2,1)S(1)} %bitcast.185, bf16[1,512,128]{2,1,0:T(8,128)(2,1)} %param.15), kind=kOutput, calls=%fused_computation.33 | convolution fusion | flops 50331648 | bytes 1015808 | tf_op jit(solution)/shard_map/td,dc->ct/dot_general | solution.py:188
  4.0 1.2 %pad_maximum_fusion = f32[16,34,512]{2,1,0:T(8,128)} fusion(f32[16,2,512]{2,1,0:T(2,128)S(1)} %bitcast.186, f32[16,8,512]{2,1,0:T(8,128)S(1)} %fusion.61, f32[16,24,512]{2,1,0:T(8,128)S(1)} %bitcast.170), kind=kLoop, calls=%fused_computation.16 | loop fusion | flops 557056 | bytes 2228224 | tf_op jit(solution)/shard_map/concatenate | solution.py:194
  5.2 9.4 %all-to-all-start = ((f32[16,34,512]{2,1,0:T(8,128)}), f32[16,34,512]{2,1,0:T(8,128)S(1)}, u32[]{:S(2)}, u32[]{:S(2)}) async-start(f32[16,34,512]{2,1,0:T(8,128)} %pad_maximum_fusion), calls=%async_computation | async-start | bytes 2621440 | tf_op jit(solution)/shard_map/all_to_all | solution.py:193
  15.3 19.5 %all-to-all-done = f32[16,34,512]{2,1,0:T(8,128)S(1)} async-done(((f32[16,34,512]{2,1,0:T(8,128)}), f32[16,34,512]{2,1,0:T(8,128)S(1)}, u32[]{:S(2)}, u32[]{:S(2)}) %all-to-all-start) | async-done | bytes 1114144 | tf_op jit(solution)/shard_map/all_to_all | solution.py:193
  34.8 1.1 %slice_bitcast_fusion.1 = (f32[24,16,512]{2,0,1:T(8,128)}, f32[16,3,8,512]{3,2,1,0:T(8,128)S(1)}) fusion(f32[16,34,512]{2,1,0:T(8,128)S(1)} %all-to-all-done), kind=kLoop, calls=%fused_computation.74 | loop fusion | bytes 2359296 | tf_op jit(solution)/shard_map/transpose | solution.py:196
  37.3 0.7 fusion.55
  38.2 0.8 copy-done.3
  39.0 1.2 %fusion.16 = f32[128,10,256]{2,0,1:T(8,128)S(1)} fusion(f32[256,256,1]{1,0,2:T(8,128)S(1)} %copy-done.3, f32[128,10,128]{0,2,1:T(8,128)S(1)} %get-tuple-element.66, f32[128,10,128]{0,2,1:T(8,128)S(1)} %get-tuple-element.65), kind=kOutput, calls=%fused_computation.17 | convolution fusion | flops 503644160 | bytes 2883584 | tf_op jit(solution)/shard_map/kcm,mj->kcj/dot_general | solution.py:46
  40.4 0.7 copy-done.2
  42.0 0.6 copy-done.6
  42.6 0.6 multiply_reduce_fusion.2
  43.2 1.0 fusion.51
  44.5 1.9 %fusion = f32[128,16,256]{2,0,1:T(8,128)S(1)} fusion(f32[256,256,1]{1,0,2:T(8,128)S(1)} %copy-done.3, f32[128,16,128]{0,2,1:T(8,128)S(1)} %get-tuple-element.52, f32[128,16,128]{0,2,1:T(8,128)S(1)} %get-tuple-element.51), kind=kOutput, calls=%fused_computation | convolution fusion | flops 805830656 | bytes 4456448 | tf_op jit(solution)/shard_map/kcm,mj->kcj/dot_general | solution.py:46
  46.9 1.0 fusion.4
  48.1 1.1 %fusion.12 = f32[64,16,128]{2,0,1:T(8,128)S(1)} fusion(f32[64,256,1]{1,0,2:T(8,128)S(1)} %copy-done.6, f32[128,16,128]{0,2,1:T(8,128)S(1)} %get-tuple-element.46, f32[128,16,128]{0,2,1:T(8,128)S(1)} %get-tuple-element.45), kind=kOutput, calls=%fused_computation.12 | convolution fusion | flops 201850880 | bytes 2686976 | tf_op jit(solution)/shard_map/nk,kcm->ncm/dot_general | solution.py:54
  49.6 0.6 fusion.82
  51.3 0.9 fusion.20
  52.4 0.7 fusion.28
  53.8 0.6 multiply_reduce_fusion.1
  56.7 0.9 dynamic_update_slice.3
  57.8 0.9 pad_maximum_fusion.2.out_ref
  58.7 0.7 pad_maximum_fusion.4.side_ref
  59.3 36.8 %shard_map.214 = (bf16[16,32,512]{2,1,0:T(8,128)(2,1)}, f32[16,40,128]{2,1,0:T(8,128)}, f32[8,8,128]{2,1,0:T(8,128)}) custom-call(bf16[16,32,512]{2,1,0:T(8,128)(2,1)} %pad_maximum_fusion.2.out_ref, bf16[512,128]{1,0:T(8,128)(2,1)} %bitcast.183, bf16[512,128]{1,0:T(8,128)(2,1)} %bitcast.181, f32[16,16,128]{2,1,0:T(8,128)} %pad_maximum_fusion.4.side_ref), custom_call_target="tpu_custom_call" | custom-call | tf_op jit(solution)/shard_map/pallas_call | solution.py:146
  96.1 1.8 %fusion.33 = bf16[1,512,128]{2,1,0:T(8,128)(2,1)} fusion(bf16[128,128]{1,0:T(8,128)(2,1)S(1)} %copy-done, bf16[16,32,512]{2,1,0:T(8,128)(2,1)} %get-tuple-element.12), kind=kOutput, calls=%fused_computation.38 | convolution fusion | flops 16842752 | bytes 294912 | tf_op jit(solution)/shard_map/dot_general | solution.py:277
  97.9 1.0 slice_bitcast_fusion.2
  98.9 1.0 slice_bitcast_fusion.3
  99.9 1.5 %fusion.81 = (f32[16,8,128]{2,1,0:T(8,128)S(1)}, f32[128,128]{1,0:T(8,128)}) fusion(f32[16,40,128]{2,1,0:T(8,128)} %get-tuple-element.13), kind=kLoop, calls=%fused_computation.168 | loop fusion | bytes 262144 | tf_op jit(solution)/shard_map/slice | solution.py:288
  102.4 1.0 fusion.32
  103.4 0.8 copy.108
  104.9 0.6 slice_bitcast_fusion.10
  (101 shorter events, 10.4 us)
Async XLA Ops:
  0.6 3.1 %copy-start = (bf16[128,128]{1,0:T(8,128)(2,1)S(1)}, bf16[128,128]{1,0:T(8,128)(2,1)}, u32[]{:S(2)}) copy-start(bf16[128,128]{1,0:T(8,128)(2,1)} %param.18) | copy-start | bytes 98308
  2.4 1.3 %copy-start.8 = (bf16[1,512,128]{2,1,0:T(8,128)(2,1)S(1)}, bf16[1,512,128]{2,1,0:T(8,128)(2,1)}, u32[]{:S(2)}) copy-start(bf16[1,512,128]{2,1,0:T(8,128)(2,1)} %param.16) | copy-start | bytes 393220
  5.2 9.4 %copy-start.13 = (f32[3,384]{1,0:T(4,128)S(1)}, f32[3,384]{1,0:T(4,128)}, u32[]{:S(2)}) copy-start(f32[3,384]{1,0:T(4,128)} %param.19) | copy-start | bytes 13828
  5.2 9.8 %copy-start.14 = (f32[128]{0:T(128)S(1)}, f32[128]{0:T(128)}, u32[]{:S(2)}) copy-start(f32[128]{0:T(128)} %param.20) | copy-start | bytes 1540
  5.2 9.9 %copy-start.15 = (f32[128]{0:T(128)S(1)}, f32[128]{0:T(128)}, u32[]{:S(2)}) copy-start(f32[128]{0:T(128)} %param.21) | copy-start | bytes 1540
  5.2 29.6 %all-to-all-start = ((f32[16,34,512]{2,1,0:T(8,128)}), f32[16,34,512]{2,1,0:T(8,128)S(1)}, u32[]{:S(2)}, u32[]{:S(2)}) async-start(f32[16,34,512]{2,1,0:T(8,128)} %pad_maximum_fusion), calls=%async_computation | async-start | bytes 2621440 | tf_op jit(solution)/shard_map/all_to_all | solution.py:193
  36.4 0.8 copy-start.7
  36.6 1.4 %copy-start.4 = (f32[128,128]{0,1:T(8,128)S(1)}, f32[128,128]{0,1:T(8,128)}, u32[]{:S(2)}) copy-start(f32[128,128]{0,1:T(8,128)} %constant.43.clone) | copy-start | bytes 196612
  36.6 1.4 %copy-start.5 = (f32[128,128]{0,1:T(8,128)S(1)}, f32[128,128]{0,1:T(8,128)}, u32[]{:S(2)}) copy-start(f32[128,128]{0,1:T(8,128)} %constant.42.clone) | copy-start | bytes 196612
  38.0 1.0 copy-start.3
  40.2 1.0 copy-start.2
  40.4 1.4 %copy-start.10 = (f32[128,128]{1,0:T(8,128)S(1)}, f32[128,128]{1,0:T(8,128)}, u32[]{:S(2)}) copy-start(f32[128,128]{1,0:T(8,128)} %constant.61) | copy-start | bytes 196612
  40.4 1.3 %copy-start.11 = (f32[128,128]{1,0:T(8,128)S(1)}, f32[128,128]{1,0:T(8,128)}, u32[]{:S(2)}) copy-start(f32[128,128]{1,0:T(8,128)} %constant.60) | copy-start | bytes 196612
  41.8 0.8 copy-start.6
  54.5 1.1 %copy-start.1 = (f32[24,16,512]{2,0,1:T(8,128)S(1)}, f32[24,16,512]{2,0,1:T(8,128)}, u32[]{:S(2)}) copy-start(f32[24,16,512]{2,0,1:T(8,128)} %get-tuple-element.68) | copy-start | bytes 2359300
  98.9 3.5 %copy-start.9 = (bf16[128,384]{1,0:T(8,128)(2,1)S(1)}, bf16[128,384]{1,0:T(8,128)(2,1)}, u32[]{:S(2)}) copy-start(bf16[128,384]{1,0:T(8,128)(2,1)} %param.17) | copy-start | bytes 294916
  101.7 3.2 %copy-start.12 = (f32[8,8,128]{2,1,0:T(8,128)S(1)}, f32[8,8,128]{2,1,0:T(8,128)}, u32[]{:S(2)}) copy-start(f32[8,8,128]{2,1,0:T(8,128)} %get-tuple-element.14) | copy-start | bytes 98308

commit v20 on v16

--- a/solution.py
+++ b/solution.py
@@ -113,12 +113,14 @@
         back_ref[pl.ds(ms, 1)] = out_ref[pl.ds(ms, 1)]
         for copy in copies:
             copy.wait()
-        ser = ser_ref[...].astype(jnp.float32)
-        cot = cot_ref[...].astype(jnp.float32)
+        ser = ser_ref[...]
+        cot = cot_ref[...]
         for j in range(seq_n):
             rows = back_ref[j].astype(jnp.float32)
-            msg_buf[j, : 3 * per] = scale * jnp.dot(rows[per:], ser, preferred_element_type=jnp.float32)
-            msg_buf[j, 3 * per : 4 * per] = scale * jnp.dot(rows[:per], cot, preferred_element_type=jnp.float32)
+            dp_rows = rows[per:].astype(ser.dtype)
+            pr_rows = rows[:per].astype(cot.dtype)
+            msg_buf[j, : 3 * per] = scale * jnp.dot(dp_rows, ser, preferred_element_type=jnp.float32)
+            msg_buf[j, 3 * per : 4 * per] = scale * jnp.dot(pr_rows, cot, preferred_element_type=jnp.float32)
         msg_buf[:, 4 * per :] = side_ref[...]
 
         copies = send_all(seq_n, lambda k: msg_buf.at[lax.rem(ms + k, seq_n)], rs_buf.at[ms], 0, seq_peer)

time: 102 us -> 102 us (level)
  no operation moved by 1% of the time
where the time goes in v20:
time: 102 us; the launch traced here: 101 us
  Pallas kernels  36.8 us (36%)
  waiting for transfers between devices  19.5 us (19%)
  matrix products  13.7 us (13%)
  local copies, waits for them, and re-layouts  13.5 us (13%)
  starting transfers between devices  9.43 us (9%)
  other arithmetic  6.93 us (7%)
  between operations  1.39 us (1%)
    pallas_call x1, Pallas kernels, tail_rounds(): pl.pallas_call(kernel, out_shape=(jax.ShapeDtypeStruct(out_msg.shape, out...  36.8 us
    all_to_all x1, waiting for transfers between devices, shards(): lax.all_to_all(jnp.concatenate([proj_blk, dprod_blk, rows_sent], axis=1),...  19.5 us
    all_to_all x1, starting transfers between devices, shards(): lax.all_to_all(jnp.concatenate([proj_blk, dprod_blk, rows_sent], axis=1),...  9.43 us
    unnamed x46, local copies, waits for them, and re-layouts  6.09 us
    dot_general x4, matrix products, spectrum(): return jnp.einsum('kcm,mj->kcj', cat, tab['fwd2'], precision=PRECISION)  2.98 us
    dot_general x4, matrix products, spectrum(): a = jnp.einsum('kn,ncm->kcm', tab['fwd1'], x, precision=PRECISION)  2.58 us
    dot_general x4, matrix products, signal(): b = jnp.einsum('kcj,jm->kcm', s, tab['inv2'], precision=PRECISION)  2.47 us
    dot_general x4, matrix products, signal(): return jnp.einsum('nk,kcm->ncm', tab['inv1'], stacked, precision=PRECISION)  2.46 us
  transfers between devices with their start and end apart: 1, of which 1 were waited for; matrix products, arithmetic and copies ran while one was open for 1% of the time, Pallas kernels for 0%

profile of v20, /device:TPU:1, one launch (start us, length us, event | category | flops | bytes accessed | tf_op | source)
XLA Modules:
  0.0 101.3 jit_solution(3787087855395557044)
XLA Ops:
  0.7 1.0 %copy.77 = bf16[128,384]{0,1:T(8,128)(2,1)S(1)} copy(bf16[128,384]{1,0:T(8,128)(2,1)} %param.17) | data formatting | bytes 196608 | tf_op args[2]
  1.7 1.2 %convolution_bitcast_fusion = f32[16,3,8,512]{3,2,0,1:T(8,128)S(1)} fusion(bf16[3,16,8,128]{3,2,1,0:T(8,128)(2,1)S(1)} %bitcast.193, bf16[1,512,128]{2,1,0:T(8,128)(2,1)} %param.15), kind=kOutput, calls=%fused_computation.17 | convolution fusion | flops 50331648 | bytes 1015808 | tf_op jit(solution)/shard_map/td,dc->ct/dot_general | solution.py:190
  3.3 1.2 %pad_maximum_fusion = f32[16,34,512]{2,1,0:T(8,128)} fusion(f32[16,2,512]{2,1,0:T(2,128)S(1)} %bitcast.194, f32[16,8,512]{2,1,0:T(8,128)S(1)} %fusion.63, f32[16,24,512]{2,1,0:T(8,128)S(1)} %bitcast.180), kind=kLoop, calls=%fused_computation | loop fusion | flops 557056 | bytes 2228224 | tf_op jit(solution)/shard_map/concatenate | solution.py:196
  4.5 9.4 %all-to-all-start = ((f32[16,34,512]{2,1,0:T(8,128)}), f32[16,34,512]{2,1,0:T(8,128)S(1)}, u32[]{:S(2)}, u32[]{:S(2)}) async-start(f32[16,34,512]{2,1,0:T(8,128)} %pad_maximum_fusion), calls=%async_computation | async-start | bytes 2621440 | tf_op jit(solution)/shard_map/all_to_all | solution.py:195
  14.6 19.5 %all-to-all-done = f32[16,34,512]{2,1,0:T(8,128)S(1)} async-done(((f32[16,34,512]{2,1,0:T(8,128)}), f32[16,34,512]{2,1,0:T(8,128)S(1)}, u32[]{:S(2)}, u32[]{:S(2)}) %all-to-all-start) | async-done | bytes 1114144 | tf_op jit(solution)/shard_map/all_to_all | solution.py:195
  34.1 1.1 %slice_bitcast_fusion.1 = (f32[24,16,512]{2,0,1:T(8,128)}, f32[16,3,8,512]{3,2,1,0:T(8,128)S(1)}) fusion(f32[16,34,512]{2,1,0:T(8,128)S(1)} %all-to-all-done), kind=kLoop, calls=%fused_computation.78 | loop fusion | bytes 2359296 | tf_op jit(solution)/shard_map/transpose | solution.py:198
  36.1 0.7 copy-done.7
  36.8 0.6 fusion.85
  37.4 0.7 fusion.57
  38.3 0.8 copy-done.2
  39.1 1.2 %fusion = f32[128,10,256]{2,0,1:T(8,128)S(1)} fusion(f32[256,256,1]{1,0,2:T(8,128)S(1)} %copy-done.2, f32[128,10,128]{0,2,1:T(8,128)S(1)} %get-tuple-element.49, f32[128,10,128]{0,2,1:T(8,128)S(1)} %get-tuple-element.48), kind=kOutput, calls=%fused_computation.1 | convolution fusion | flops 503644160 | bytes 2883584 | tf_op jit(solution)/shard_map/kcm,mj->kcj/dot_general | solution.py:46
  40.5 0.6 fusion.36
  41.3 0.8 copy-done.1
  42.8 0.7 copy-done.6
  44.0 0.6 fusion.84
  44.8 0.6 fusion.47
  47.0 0.6 fusion.83
  47.8 0.6 fusion.25
  49.5 0.7 fusion.4
  50.4 0.7 fusion.12
  51.2 0.8 multiply_reduce_fusion.3
  52.1 0.6 multiply_reduce_fusion.1
  54.5 0.9 dynamic_update_slice.3
  56.4 0.7 pad_maximum_fusion.4.side_ref
  57.1 0.9 pad_maximum_fusion.2.out_ref
  57.9 36.8 %shard_map.214 = (bf16[16,32,512]{2,1,0:T(8,128)(2,1)}, f32[16,40,128]{2,1,0:T(8,128)}, f32[8,8,128]{2,1,0:T(8,128)}) custom-call(bf16[16,32,512]{2,1,0:T(8,128)(2,1)} %pad_maximum_fusion.2.out_ref, bf16[512,128]{1,0:T(8,128)(2,1)} %bitcast.191, bf16[512,128]{1,0:T(8,128)(2,1)} %bitcast.189, f32[16,16,128]{2,1,0:T(8,128)} %pad_maximum_fusion.4.side_ref), custom_call_target="tpu_custom_call" | custom-call | tf_op jit(solution)/shard_map/pallas_call | solution.py:148
  94.8 1.6 %fusion.87 = (f32[16,8,128]{2,1,0:T(8,128)S(1)}, f32[128,128]{1,0:T(8,128)}) fusion(f32[16,40,128]{2,1,0:T(8,128)} %get-tuple-element.13), kind=kLoop, calls=%fused_computation.178 | loop fusion | bytes 262144 | tf_op jit(solution)/shard_map/slice | solution.py:287
  97.4 0.9 fusion.17
  98.3 1.0 fusion.16
  99.3 0.6 copy.147
  99.9 0.8 copy.108
  100.7 0.6 slice_bitcast_fusion.10
  (113 shorter events, 10.5 us)
Async XLA Ops:
  0.6 2.4 %copy-start = (bf16[128,128]{1,0:T(8,128)(2,1)S(1)}, bf16[128,128]{1,0:T(8,128)(2,1)}, u32[]{:S(2)}) copy-start(bf16[128,128]{1,0:T(8,128)(2,1)} %param.18) | copy-start | bytes 98308
  1.7 1.3 %copy-start.15 = (f32[8,512]{1,0:T(8,128)S(1)}, f32[8,512]{1,0:T(8,128)}, u32[]{:S(2)}) copy-start(f32[8,512]{1,0:T(8,128)} %param.23) | copy-start | bytes 49156
  1.7 1.3 %copy-start.16 = (f32[8,512]{1,0:T(8,128)S(1)}, f32[8,512]{1,0:T(8,128)}, u32[]{:S(2)}) copy-start(f32[8,512]{1,0:T(8,128)} %param.22) | copy-start | bytes 49156
  1.7 1.4 %copy-start.8 = (bf16[1,512,128]{2,1,0:T(8,128)(2,1)S(1)}, bf16[1,512,128]{2,1,0:T(8,128)(2,1)}, u32[]{:S(2)}) copy-start(bf16[1,512,128]{2,1,0:T(8,128)(2,1)} %param.16) | copy-start | bytes 393220
  4.5 9.4 %copy-start.17 = (f32[3,384]{1,0:T(4,128)S(1)}, f32[3,384]{1,0:T(4,128)}, u32[]{:S(2)}) copy-start(f32[3,384]{1,0:T(4,128)} %param.19) | copy-start | bytes 13828
  4.5 9.8 %copy-start.18 = (f32[128]{0:T(128)S(1)}, f32[128]{0:T(128)}, u32[]{:S(2)}) copy-start(f32[128]{0:T(128)} %param.20) | copy-start | bytes 1540
  4.5 9.9 %copy-start.19 = (f32[128]{0:T(128)S(1)}, f32[128]{0:T(128)}, u32[]{:S(2)}) copy-start(f32[128]{0:T(128)} %param.21) | copy-start | bytes 1540
  4.5 29.6 %all-to-all-start = ((f32[16,34,512]{2,1,0:T(8,128)}), f32[16,34,512]{2,1,0:T(8,128)S(1)}, u32[]{:S(2)}, u32[]{:S(2)}) async-start(f32[16,34,512]{2,1,0:T(8,128)} %pad_maximum_fusion), calls=%async_computation | async-start | bytes 2621440 | tf_op jit(solution)/shard_map/all_to_all | solution.py:195
  35.9 0.8 copy-start.7
  36.8 1.4 %copy-start.12 = (f32[128,128]{0,1:T(8,128)S(1)}, f32[128,128]{0,1:T(8,128)}, u32[]{:S(2)}) copy-start(f32[128,128]{0,1:T(8,128)} %constant.42.clone) | copy-start | bytes 196612
  36.8 1.4 %copy-start.13 = (f32[128,128]{0,1:T(8,128)S(1)}, f32[128,128]{0,1:T(8,128)}, u32[]{:S(2)}) copy-start(f32[128,128]{0,1:T(8,128)} %constant.43.clone) | copy-start | bytes 196612
  38.1 1.0 copy-start.2
  39.1 1.3 %copy-start.4 = (f32[128,128]{1,0:T(8,128)S(1)}, f32[128,128]{1,0:T(8,128)}, u32[]{:S(2)}) copy-start(f32[128,128]{1,0:T(8,128)} %constant.60) | copy-start | bytes 196612
  39.1 1.3 %copy-start.5 = (f32[128,128]{1,0:T(8,128)S(1)}, f32[128,128]{1,0:T(8,128)}, u32[]{:S(2)}) copy-start(f32[128,128]{1,0:T(8,128)} %constant.61) | copy-start | bytes 196612
  41.1 1.0 copy-start.1
  42.7 0.8 copy-start.6
  52.1 1.1 %copy-start.3 = (f32[24,16,512]{2,0,1:T(8,128)S(1)}, f32[24,16,512]{2,0,1:T(8,128)}, u32[]{:S(2)}) copy-start(f32[24,16,512]{2,0,1:T(8,128)} %get-tuple-element.50) | copy-start | bytes 2359300
  94.7 2.6 %copy-start.11 = (f32[16,40,128]{2,1,0:T(8,128)S(1)}, f32[16,40,128]{2,1,0:T(8,128)}, u32[]{:S(2)}) copy-start(f32[16,40,128]{2,1,0:T(8,128)} %get-tuple-element.13) | copy-start | bytes 983044
  94.8 2.6 %copy-start.9 = (bf16[16,32,512]{2,1,0:T(8,128)(2,1)S(1)}, bf16[16,32,512]{2,1,0:T(8,128)(2,1)}, u32[]{:S(2)}) copy-start(bf16[16,32,512]{2,1,0:T(8,128)(2,1)} %get-tuple-element.12) | copy-start | bytes 1572868
  96.6 1.7 %copy-start.10 = (bf16[128,384]{1,0:T(8,128)(2,1)S(1)}, bf16[128,384]{1,0:T(8,128)(2,1)}, u32[]{:S(2)}) copy-start(bf16[128,384]{1,0:T(8,128)(2,1)} %param.17) | copy-start | bytes 294916
  97.4 3.3 %copy-start.14 = (f32[8,8,128]{2,1,0:T(8,128)S(1)}, f32[8,8,128]{2,1,0:T(8,128)}, u32[]{:S(2)}) copy-start(f32[8,8,128]{2,1,0:T(8,128)} %get-tuple-element.14) | copy-start | bytes 98308
